TPU v7x, 32 devices: a whole 2x2x4 slice. The times are simulated.
32 devices in a mesh: rep: 4 (over y, x), shard: 8 (over z, core).
Axes of the slice: x: 2, y: 2, z: 4, core: 2. Of those that a mesh axis runs over, the one named last changes fastest.
Arguments:
- tokens: bfloat16 [4096, 2048], P(('rep', 'shard')), may hold values from -6 to 6
- seq_lengths: int32 [4, 32], P('rep'), may hold values from 1 to 64, as said below
- deal_order: int32 [4, 32], P('rep'), may hold values from 0 to 31, as said below
- attn_gain: bfloat16 [2048], P('shard'), may hold values from 0.099609375 to 1.8984375
- mlp_gain: bfloat16 [2048], P('shard'), may hold values from 0.099609375 to 1.8984375
- q_weight: bfloat16 [2048, 2048], P('shard'), may hold values from -0.125 to 0.125
- k_weight: bfloat16 [2048, 256], P('shard'), may hold values from -0.125 to 0.125
- v_weight: bfloat16 [2048, 256], P('shard'), may hold values from -0.125 to 0.125
- o_weight: bfloat16 [2048, 2048], P('shard'), may hold values from -0.5 to 0.5
- gate_weight: bfloat16 [2048, 5632], P('shard'), may hold values from -0.125 to 0.125
- up_weight: bfloat16 [2048, 5632], P('shard'), may hold values from -0.125 to 0.125
- down_weight: bfloat16 [5632, 2048], P('shard'), may hold values from -0.078125 to 0.078125
- cotangent: bfloat16 [4096, 2048], P(('rep', 'shard')), may hold values from -6 to 6
Outputs:
- layer_out: bfloat16 [4096, 2048], P(('rep', 'shard'))
- input_grad: bfloat16 [4096, 2048], P(('rep', 'shard'))
- attn_gain_grad: float32 [2048], P('shard')
- mlp_gain_grad: float32 [2048], P('shard')
- q_weight_grad: float32 [2048, 2048], P('shard')
- k_weight_grad: float32 [2048, 256], P('shard')
- v_weight_grad: float32 [2048, 256], P('shard')
- o_weight_grad: float32 [2048, 2048], P('shard')
- gate_weight_grad: float32 [2048, 5632], P('shard')
- up_weight_grad: float32 [2048, 5632], P('shard')
- down_weight_grad: float32 [5632, 2048], P('shard')
Inputs may be any that keep to these rules, and one draw needn't show every extreme that they name: seq_lengths[g] are the lengths of group g's sequences in initial order and add up to 1024; in every group one sequence has exactly 64 tokens. deal_order[g] is a permutation of the group's 32 sequences; dealt places s * 4 to s * 4 + 3 hold sequences whose lengths add up to exactly 128, so that index s of shard receives whole sequences.
All inputs are finite; a program needn't handle non-finite values.
Results may differ from a plain program's by a relative error of at most 0.014.
Values may be sent and summed in bfloat16 or wider, within the bound.
No kernel may reach another device: no remote copies, remote signals or barrier semaphores. Data moves between devices by JAX's collectives and lax.ppermute only.
A program may use at most 256 MiB of HBM per device.

v0:
```python
from functools import partial

import jax
import jax.numpy as jnp
from jax import lax
from jax.experimental import pallas as pl
from jax.experimental.pallas import tpu as pltpu
from jax.sharding import PartitionSpec as P


H = 32
KVH = 4
HD = 64
HALO = 64
LANES = 128

EPSILON = 1e-05
ROPE_BASE = 10000.0
NEG_FILL = -1e30

BF = jnp.bfloat16
F32 = jnp.float32


def dot(left, right, contract):
    return lax.dot_general(left, right, (contract, ((), ())), preferred_element_type=F32)


def rows_cols(left, right):
    return dot(left, right, ((1,), (0,)))


def rows_rows(left, right):
    return dot(left, right, ((0,), (0,)))


def cols_cols(left, right):
    return dot(left, right, ((1,), (1,)))


def spread(value, axis, count):
    wide = jnp.broadcast_to(value[None], (count,) + value.shape)
    return lax.all_to_all(wide, axis, split_axis=0, concat_axis=0, tiled=True)


def swap(value, axis):
    return lax.all_to_all(value, axis, split_axis=0, concat_axis=0, tiled=True)


def pairs(count, step):
    return [(i, i ^ step) for i in range(count)]


def send(value, axis, count, step):
    return lax.ppermute(value, axis, pairs(count, step))


def sum_rep(chunks, count):
    wide = lambda value: value.astype(F32)
    go = lambda value, step: send(value, "rep", count, step)
    if count != 4:
        return tuple(
            sum([wide(go(chunks[k][h], k)) for k in range(1, count)], wide(chunks[0][h]))
            for h in range(2)
        )
    first_one = go(chunks[1][0], 1)
    first_two = go(chunks[3][0], 1)
    second_one = go(chunks[2][1], 2)
    second_two = go(chunks[3][1], 2)
    joint_one = (wide(chunks[2][0]) + wide(first_two)).astype(BF)
    joint_two = (wide(chunks[1][1]) + wide(second_two)).astype(BF)
    last_one = go(joint_one, 2)
    last_two = go(joint_two, 1)
    return (
        wide(chunks[0][0]) + wide(first_one) + wide(last_one),
        wide(chunks[0][1]) + wide(second_one) + wide(last_two),
    )


def gather_rep(halves, count):
    go = lambda value, step: send(value, "rep", count, step)
    if count != 4:
        return [halves] + [tuple(go(v, k) for v in halves) for k in range(1, count)]
    one = tuple(go(v, 1) for v in halves)
    two = tuple(go(v, 2) for v in halves)
    return [halves, one, two, (go(one[0], 2), go(two[1], 1))]


def place_kernel(count, me_ref, *refs):
    parts, out_ref = refs[:-1], refs[-1]
    at = pl.program_id(0)
    size = len(parts) // count
    for k in range(count):

        @pl.when(at == jnp.bitwise_xor(me_ref[0], k))
        def _(k=k):
            row = 0
            for part in parts[k * size : (k + 1) * size]:
                out_ref[0, row : row + part.shape[0]] = part[...].astype(F32)
                row += part.shape[0]


def place(pieces, me):
    count = len(pieces)
    flat = [part for piece in pieces for part in piece]
    rows = sum(part.shape[0] for part in pieces[0])
    width = flat[0].shape[1]
    grid = pltpu.PrefetchScalarGridSpec(
        num_scalar_prefetch=1,
        grid=(count,),
        in_specs=[
            pl.BlockSpec(part.shape, lambda g, me: (0, 0), pipeline_mode=pl.Buffered(1))
            for part in flat
        ],
        out_specs=pl.BlockSpec((1, rows, width), lambda g, me: (g, 0, 0)),
    )
    return pl.pallas_call(
        partial(place_kernel, count),
        out_shape=shape((count, rows, width), F32),
        grid_spec=grid,
        compiler_params=pltpu.CompilerParams(vmem_limit_bytes=56 * 1024 * 1024),
    )(me.astype(jnp.int32).reshape(1), *flat).reshape(count * rows, width)


def norm_scale(value):
    return lax.rsqrt(jnp.mean(value * value, axis=1, keepdims=True) + EPSILON)


def turn(tile, cosine, sine):
    lane = lax.broadcasted_iota(jnp.int32, tile.shape, 1)
    swapped = jnp.where(
        lane % HD < HD // 2,
        -pltpu.roll(tile, LANES - HD // 2, 1),
        pltpu.roll(tile, HD // 2, 1),
    )
    return tile * cosine + swapped * sine


def turn_first(tile, cosine, sine):
    lane = lax.broadcasted_iota(jnp.int32, tile.shape, 1)
    return jnp.where(lane < HD, turn(tile, cosine, sine), tile)


def in_kernel(x_ref, gain_ref, w_ref, cos_ref, sin_ref, normed_ref, q_ref, kv_ref):
    x = x_ref[0].astype(F32)
    normed = (x * norm_scale(x) * gain_ref[...]).astype(BF)
    normed_ref[0] = normed
    qkv = rows_cols(normed, w_ref[...])
    cosine, sine = cos_ref[0], sin_ref[0]
    q_cols = q_ref.shape[2]
    for at in range(0, q_cols, LANES):
        q_ref[0, :, at : at + LANES] = turn(qkv[:, at : at + LANES], cosine, sine).astype(BF)
    kv_ref[0] = turn_first(qkv[:, q_cols:], cosine, sine).astype(BF)


def stack_heads(value):
    return jnp.concatenate(
        [value[:, at : at + HD] for at in range(0, value.shape[1], HD)], axis=0
    )


def unstack_heads(value, rows):
    return jnp.concatenate(
        [value[at : at + rows] for at in range(0, value.shape[0], rows)], axis=1
    )


def attend_kernel(fine, q_ref, own_ref, halo_ref, pos_ref, probs_ref, out_ref):
    rows, q_cols = q_ref.shape[1:]
    heads = q_cols // HD
    count = out_ref.shape[0]
    kv = jnp.concatenate([halo_ref[0], own_ref[0]], axis=0)
    keys, values = kv[:, :HD], kv[:, HD:]
    span = kv.shape[0]
    scores = cols_cols(stack_heads(q_ref[0]), keys) * (HD**-0.5)
    query = lax.broadcasted_iota(jnp.int32, (rows, span), 0) + HALO
    key = lax.broadcasted_iota(jnp.int32, (rows, span), 1)
    first = query - pos_ref[0][:, :1].astype(jnp.int32)
    allowed = (key >= first) & (key <= query)
    scores = jnp.where(allowed[None], scores.reshape(heads, rows, span), NEG_FILL)
    grown = jnp.exp(scores - jnp.max(scores, axis=-1, keepdims=True))
    probs = grown / jnp.sum(grown, axis=-1, keepdims=True)
    probs_ref[0] = probs
    mixed = rows_cols(probs.reshape(heads * rows, span).astype(BF), values)
    mixed = unstack_heads(mixed, rows).astype(BF)
    for to in range(count):
        out_ref[to, 0] = jnp.concatenate(
            [
                mixed[:, at + to * fine : at + (to + 1) * fine]
                for at in range(0, q_cols, count * fine)
            ],
            axis=1,
        )


def attend_back_kernel(
    fine, grad_ref, probs_ref, q_ref, own_ref, halo_ref, cos_ref, sin_ref, q_out, kv_out
):
    rows, q_cols = q_ref.shape[1:]
    heads = q_cols // HD
    count = grad_ref.shape[0]
    kv = jnp.concatenate([halo_ref[0], own_ref[0]], axis=0)
    keys, values = kv[:, :HD], kv[:, HD:]
    span = kv.shape[0]
    grad = jnp.concatenate(
        [
            grad_ref[source, 0][:, at * fine : (at + 1) * fine]
            for at in range(q_cols // (count * fine))
            for source in range(count)
        ],
        axis=1,
    )
    grad = stack_heads(grad)
    probs = probs_ref[0].reshape(heads * rows, span)
    probs_grad = cols_cols(grad, values)
    inner = jnp.sum(probs * probs_grad, axis=-1, keepdims=True)
    score_grad = (probs * (probs_grad - inner)).astype(BF)
    scale = HD**-0.5
    key_grad = rows_rows(score_grad, stack_heads(q_ref[0])) * scale
    value_grad = rows_rows(probs.astype(BF), grad)
    kv_out[0] = jnp.concatenate([key_grad, value_grad], axis=1)
    query_grad = unstack_heads(rows_cols(score_grad, keys) * scale, rows)
    cosine, sine = cos_ref[0], -sin_ref[0]
    for at in range(0, q_cols, LANES):
        q_out[0, :, at : at + LANES] = turn(
            query_grad[:, at : at + LANES], cosine, sine
        ).astype(BF)


def in_back_kernel(
    dq_ref, dkv_ref, back_ref, cos_ref, sin_ref, normed_ref, x_ref, two_ref, w_ref,
    part_ref, grad_ref, total_ref,
):
    at = pl.program_id(0)
    rows = dq_ref.shape[1]
    own = dkv_ref[0, HALO:]
    tail = own[rows - HALO :] + back_ref[0]
    own = jnp.concatenate([own[: rows - HALO], tail], axis=0)
    own = turn_first(own, cos_ref[0], -sin_ref[0]).astype(BF)
    qkv_grad = jnp.concatenate([dq_ref[0], own], axis=1)
    normed_grad = cols_cols(qkv_grad, w_ref[...])
    part_ref[0] = normed_grad.astype(BF)
    x = x_ref[0].astype(F32)
    one = (normed_grad * x * norm_scale(x)).astype(BF)
    cols = qkv_grad.shape[1]
    lane = lax.broadcasted_iota(jnp.int32, (rows, LANES), 1)

    @pl.when(at == 0)
    def _():
        total_ref[:, :cols] = rows_rows(normed_ref[0], qkv_grad)
        total_ref[:, cols:] = rows_rows(one, (lane < HD).astype(BF)) + rows_rows(
            two_ref[...], (lane >= HD).astype(BF)
        )

    @pl.when(at > 0)
    def _():
        total_ref[:, :cols] += rows_rows(normed_ref[0], qkv_grad)
        total_ref[:, cols:] += rows_rows(one, (lane < HD).astype(BF))

    @pl.when(at == pl.num_programs(0) - 1)
    def _():
        grad_ref[...] = total_ref[...].astype(BF)


def middle_kernel(part_ref, x_ref, gain_ref, mid_ref, normed_ref):
    mid = x_ref[...].astype(F32)
    for at in range(part_ref.shape[0]):
        mid += part_ref[at].astype(F32)
    mid_ref[...] = mid
    normed_ref[...] = (mid * norm_scale(mid) * gain_ref[...]).astype(BF)


def middle_back_kernel(grad_ref, mid_ref, gain_ref, cot_ref, out_ref, low_ref, gain_out_ref):
    mid = mid_ref[...]
    scale = norm_scale(mid)
    grad = grad_ref[...].astype(F32)
    gain_out_ref[...] = (grad * mid * scale).astype(BF)
    scaled = grad * gain_ref[...]
    out = (
        cot_ref[...].astype(F32)
        + scale * scaled
        - mid * scale**3 * jnp.mean(scaled * mid, axis=1, keepdims=True)
    )
    out_ref[...] = out
    low_ref[...] = out.astype(BF)


def last_kernel(part_ref, x_ref, gain_ref, mid_ref, out_ref):
    x = x_ref[...].astype(F32)
    scale = norm_scale(x)
    grad = part_ref[0].astype(F32)
    for at in range(1, part_ref.shape[0]):
        grad += part_ref[at].astype(F32)
    scaled = grad * gain_ref[...]
    out = (
        mid_ref[...]
        + scale * scaled
        - x * scale**3 * jnp.mean(scaled * x, axis=1, keepdims=True)
    )
    out_ref[...] = out.astype(BF)


def forward_back_kernel(
    x_ref, cot_ref, pair_ref, down_ref, mixed_ref, gate_out, up_out, part_ref
):
    x = x_ref[...]
    gate = rows_cols(x, pair_ref[0])
    up = rows_cols(x, pair_ref[1])
    mixed_grad = cols_cols(cot_ref[...], down_ref[...])
    sigma = jax.nn.sigmoid(gate)
    silu = gate * sigma
    mixed_ref[...] = (silu * up).astype(BF)
    gate_grad = (mixed_grad * up * sigma * (1.0 + gate * (1.0 - sigma))).astype(BF)
    up_grad = (mixed_grad * silu).astype(BF)
    gate_out[...] = gate_grad
    up_out[...] = up_grad
    part_ref[...] = (
        cols_cols(gate_grad, pair_ref[0]) + cols_cols(up_grad, pair_ref[1])
    ).astype(BF)


def shape(dims, kind):
    return jax.ShapeDtypeStruct(dims, kind)


def call(kernel, out_shape, grid=None, in_specs=None, out_specs=None, scratch=()):
    options = {}
    if grid is not None:
        options = {"grid": grid, "in_specs": in_specs, "out_specs": out_specs}
    return pl.pallas_call(
        kernel,
        out_shape=out_shape,
        scratch_shapes=list(scratch),
        compiler_params=pltpu.CompilerParams(vmem_limit_bytes=56 * 1024 * 1024),
        **options,
    )


def by_block(dims):
    return pl.BlockSpec((1,) + dims, lambda g: (g,) + (0,) * len(dims))


def whole(dims):
    return pl.BlockSpec(dims, lambda g: (0,) * len(dims), pipeline_mode=pl.Buffered(1))


def body(
    n_rep,
    n_shard,
    tokens,
    seq_lengths,
    deal_order,
    attn_gain,
    mlp_gain,
    q_weight,
    k_weight,
    v_weight,
    o_weight,
    gate_weight,
    up_weight,
    down_weight,
    cotangent,
):
    rows, width = tokens.shape
    r = lax.axis_index("rep")
    s = lax.axis_index("shard")
    own = width // n_shard
    fine = own // n_rep
    hidden = down_weight.shape[0]
    q_cols = width // n_rep
    heads = H // n_rep
    pair = n_shard // n_rep
    share = max(n_rep // KVH, 1)
    kv_at = (r * KVH) // n_rep
    all_rows = n_rep * rows
    span = HALO + rows
    qkv_cols = q_cols + 2 * HD

    starts = jnp.cumsum(seq_lengths[0]) - seq_lengths[0]
    places = s * rows + jnp.arange(rows, dtype=jnp.int32)
    first = jnp.max(
        jnp.where(starts[None, :] <= places[:, None], starts[None, :], 0), axis=1, keepdims=True
    )
    offset = jnp.broadcast_to((places[:, None] - first).astype(BF), (rows, LANES))

    w_qkv_own = jnp.concatenate(
        [
            lax.dynamic_slice_in_dim(q_weight, r * q_cols, q_cols, 1),
            lax.dynamic_slice_in_dim(k_weight, kv_at * HD, HD, 1),
            lax.dynamic_slice_in_dim(v_weight, kv_at * HD, HD, 1),
        ],
        axis=1,
    )
    w_qkv = lax.all_gather(w_qkv_own, "shard", axis=0, tiled=True)
    w_o = lax.all_gather(
        lax.dynamic_slice_in_dim(o_weight, r * fine, fine, 0), "shard", axis=0, tiled=True
    )
    x_all = spread(jnp.concatenate([tokens, offset], axis=1), "rep", n_rep)
    gains = lax.all_gather(jnp.stack([attn_gain, mlp_gain]), "shard", axis=1, tiled=True)
    gain_one = gains[0:1].astype(F32)
    gain_two = gains[1:2].astype(F32)

    def exchange_shard(value):
        total = jnp.zeros_like(value)
        for k in range(n_shard):
            piece = lax.dynamic_slice_in_dim(value, s ^ k, 1, 0)
            if k:
                piece = send(piece, "shard", n_shard, k)
            total = lax.dynamic_update_slice_in_dim(total, piece, s ^ k, 0)
        return total

    def quarter(weight):
        part = lax.dynamic_slice_in_dim(weight, r * fine, fine, 0)
        return part.reshape(fine, n_shard, hidden).transpose(1, 0, 2)

    w_pair = jnp.stack([quarter(gate_weight), quarter(up_weight)], axis=1)
    w_pair = exchange_shard(w_pair).transpose(1, 0, 2, 3)
    w_pair = gather_rep((w_pair[0], w_pair[1]), n_rep)
    grown = jnp.zeros((2, n_shard, n_rep, fine, hidden), BF)
    for k, piece in enumerate(w_pair):
        for h in range(2):
            grown = lax.dynamic_update_slice(
                grown, piece[h][None, :, None], (h, 0, r ^ k, 0, 0)
            )
    w_pair = grown.reshape(2, width, hidden)
    cot_all = lax.all_gather(cotangent, "shard", axis=0, tiled=True)

    half = HD // 2
    inverse = ROPE_BASE ** (-2.0 * (jnp.arange(LANES) % half).astype(F32) / HD)
    angles = x_all[:, :, width:].astype(F32) * inverse[None, None, :]
    cosine, sine = jnp.cos(angles), jnp.sin(angles)
    x_block = by_block((rows, width))
    table = by_block((rows, LANES))
    normed_one, queries, kv_own = call(
        in_kernel,
        (
            shape((n_rep, rows, width), BF),
            shape((n_rep, rows, q_cols), BF),
            shape((n_rep, rows, LANES), BF),
        ),
        (n_rep,),
        [x_block, whole((1, width)), whole((width, qkv_cols)), table, table],
        (x_block, by_block((rows, q_cols)), table),
    )(x_all, gain_one, w_qkv, cosine, sine)
    kv_halo = lax.ppermute(
        kv_own[:, rows - HALO :], "shard", [(i, i + 1) for i in range(n_shard - 1)]
    )
    head_block = pl.BlockSpec((n_rep, 1, rows, pair * fine), lambda g: (0, g, 0, 0))
    probs_block = by_block((heads, rows, span))
    probs, out_in = call(
        partial(attend_kernel, fine),
        (
            shape((n_rep, heads, rows, span), F32),
            shape((n_rep, n_rep, rows, pair * fine), BF),
        ),
        (n_rep,),
        [
            by_block((rows, q_cols)),
            table,
            by_block((HALO, LANES)),
            pl.BlockSpec((1, rows, LANES), lambda g: (g, 0, width // LANES)),
        ],
        (probs_block, head_block),
    )(queries, kv_own, kv_halo, x_all)
    out_in = swap(out_in, "rep").reshape(n_rep, all_rows, pair * fine)
    out_in = out_in.transpose(1, 0, 2).reshape(all_rows, q_cols)
    mid_part = rows_cols(out_in, w_o).astype(BF).reshape(n_rep, rows, width)
    x_mid, normed_two = call(
        middle_kernel, (shape((rows, width), F32), shape((rows, width), BF))
    )(swap(mid_part, "rep"), tokens, gain_two)

    two_all = lax.all_gather(normed_two, "shard", axis=0, tiled=True)
    step = 256
    group = two_all.shape[0]
    token_block = pl.BlockSpec((step, width), lambda g: (g, 0))
    hidden_block = pl.BlockSpec((step, hidden), lambda g: (g, 0))
    mixed, gate_grad, up_grad, two_grad_part = call(
        forward_back_kernel,
        (shape((group, hidden), BF),) * 3 + (shape((group, width), BF),),
        (group // step,),
        [token_block, token_block, whole((2, width, hidden)), whole((hidden, width))],
        (hidden_block,) * 3 + (token_block,),
    )(two_all, cot_all, w_pair, down_weight)
    two_grad = lax.psum_scatter(two_grad_part, "shard", scatter_dimension=0, tiled=True)
    mixed, two_grad_part = lax.optimization_barrier((mixed, two_grad_part))
    down_part = rows_cols(mixed, down_weight).astype(BF)
    down_rows = lax.psum_scatter(down_part, "shard", scatter_dimension=0, tiled=True)
    layer_out = (x_mid + down_rows.astype(F32)).astype(BF)

    mid_grad, branch, gain_two_rows = call(
        middle_back_kernel,
        (shape((rows, width), F32), shape((rows, width), BF), shape((rows, width), BF)),
    )(two_grad, x_mid, gain_two, cotangent)

    part_rows = hidden // n_rep
    cut = (part_rows // 2 + 15) // 16 * 16
    w_down_grad = rows_rows(mixed, cot_all).astype(BF)
    chunks = []
    for k in range(n_rep):
        at = (r ^ k) * part_rows
        chunks.append(
            (
                lax.dynamic_slice_in_dim(w_down_grad, at, cut, 0),
                lax.dynamic_slice_in_dim(w_down_grad, at + cut, part_rows - cut, 0),
            )
        )
    low = lambda values: tuple(value.astype(BF) for value in values)
    w_down_grad = low(sum_rep(chunks, n_rep))
    down_out = place(gather_rep(w_down_grad, n_rep), r)
    halves = [
        rows_rows(two_all, part).astype(BF).reshape(n_shard, n_rep, fine, hidden)
        for part in (gate_grad, up_grad)
    ]
    chunks = [
        tuple(lax.dynamic_index_in_dim(half, r ^ k, 1, False) for half in halves)
        for k in range(n_rep)
    ]
    w_pair_grad = low(sum_rep(chunks, n_rep))
    w_pair_grad = exchange_shard(jnp.stack(w_pair_grad, axis=1))
    w_pair_grad = w_pair_grad.transpose(1, 2, 0, 3).reshape(2, fine, n_shard * hidden)
    w_pair_grad = gather_rep((w_pair_grad[0], w_pair_grad[1]), n_rep)
    gate_out = place([piece[:1] for piece in w_pair_grad], r)
    up_out = place([piece[1:] for piece in w_pair_grad], r)

    branch_all = spread(branch, "rep", n_rep).reshape(all_rows, width)
    in_grad = cols_cols(branch_all, w_o).astype(BF)
    in_grad = in_grad.reshape(all_rows, n_rep, pair * fine).transpose(1, 0, 2)
    in_grad = swap(in_grad, "rep").reshape(n_rep, n_rep, rows, pair * fine)
    w_o_grad = rows_rows(out_in, branch_all).astype(BF)
    w_o_grad = lax.psum_scatter(w_o_grad, "shard", scatter_dimension=0, tiled=True)
    w_o_grad = (w_o_grad[: fine // 2], w_o_grad[fine // 2 :])
    o_out = place(gather_rep(w_o_grad, n_rep), r)
    query_grad, kv_grad = call(
        partial(attend_back_kernel, fine),
        (shape((n_rep, rows, q_cols), BF), shape((n_rep, span, LANES), F32)),
        (n_rep,),
        [
            head_block,
            probs_block,
            by_block((rows, q_cols)),
            table,
            by_block((HALO, LANES)),
            table,
            table,
        ],
        (by_block((rows, q_cols)), by_block((span, LANES))),
    )(in_grad, probs, queries, kv_own, kv_halo, cosine, sine)
    kv_back = lax.ppermute(
        kv_grad[:, :HALO], "shard", [(i + 1, i) for i in range(n_shard - 1)]
    )
    grad_cols = qkv_cols + LANES
    one_grad_part, w_qkv_grad = call(
        in_back_kernel,
        (shape((n_rep, rows, width), BF), shape((width, grad_cols), BF)),
        (n_rep,),
        [
            by_block((rows, q_cols)),
            by_block((span, LANES)),
            by_block((HALO, LANES)),
            table,
            table,
            x_block,
            x_block,
            whole((rows, width)),
            whole((width, qkv_cols)),
        ],
        (x_block, pl.BlockSpec((width, grad_cols), lambda g: (0, 0))),
        [pltpu.VMEM((width, grad_cols), F32)],
    )(
        query_grad, kv_grad, kv_back, cosine, sine, normed_one, x_all, gain_two_rows, w_qkv
    )
    w_qkv_grad = lax.psum_scatter(w_qkv_grad, "shard", scatter_dimension=0, tiled=True)
    input_grad = call(last_kernel, shape((rows, width), BF))(
        swap(one_grad_part, "rep"), tokens, gain_one, mid_grad
    )
    w_qkv_grad = spread(w_qkv_grad, "rep", n_rep).astype(F32)

    def columns(part):
        return part.transpose(1, 0, 2).reshape(own, -1)

    def kv_columns(part):
        return columns(jnp.sum(part.reshape(-1, share, own, HD), axis=1))

    q_out = columns(w_qkv_grad[..., :q_cols])
    k_out = kv_columns(w_qkv_grad[..., q_cols : q_cols + HD])
    v_out = kv_columns(w_qkv_grad[..., q_cols + HD : qkv_cols])
    gain_sums = jnp.sum(w_qkv_grad[..., qkv_cols:], axis=0)
    return (
        layer_out,
        input_grad,
        gain_sums[:, 0],
        gain_sums[:, HD],
        q_out,
        k_out,
        v_out,
        o_out,
        gate_out,
        up_out,
        down_out,
    )


def solution(mesh):
    split = P("shard", None)
    by_token = P(("rep", "shard"), None)
    return jax.shard_map(
        partial(body, mesh.shape["rep"], mesh.shape["shard"]),
        mesh=mesh,
        in_specs=(by_token, P("rep", None), P("rep", None), P("shard"), P("shard"))
        + (split,) * 7
        + (by_token,),
        out_specs=(by_token, by_token, P("shard"), P("shard")) + (split,) * 7,
        check_vma=False,
    )
```

profile of v0, /device:TPU:0, one launch (start us, length us, event | category | flops | bytes accessed | tf_op | source)
XLA Modules:
  0.0 798.5 jit_solution(5346101643871583406)
XLA Ops:
  14.8 5.3 all-to-all-start
  20.1 12.3 %all_gather.15 = bf16[2,2048]{1,0:T(2,128)(2,1)S(1)} all-gather(bf16[2,256]{1,0:T(2,128)(2,1)S(1)} %pad_maximum_fusion.2), channel_id=1, replica_groups=mesh['rep'=4,'shard'=8] {'shard'}, dimensions={1}, use_global_device_ids=true | all-gather | bytes 9216 | tf_op jit(solution)/shard_map/all_gather | solution.py:399
  33.1 13.3 %all-to-all-done.x_ref.pos_ref = bf16[4,128,2176]{2,1,0:T(8,128)(2,1)S(1)} async-done(((bf16[4,128,2176]{2,1,0:T(8,128)(2,1)}), bf16[4,128,2176]{2,1,0:T(8,128)(2,1)S(1)}, u32[]{:S(2)}, u32[]{:S(2)}) %all-to-all-start) | async-done | bytes 2228256 | tf_op jit(solution)/shard_map/all_to_all | solution.py:43
  48.0 6.2 shard_map.203
  57.9 6.4 shard_map.204
  64.3 10.6 %all_to_all.35 = bf16[4,4,128,128]{3,2,1,0:T(8,128)(2,1)S(1)} all-to-all(bf16[4,4,128,128]{3,2,1,0:T(8,128)(2,1)} %get-tuple-element.32), channel_id=1, replica_groups=mesh['rep'=4,'shard'=8] {'rep'}, dimensions={0} | all-to-all | bytes 1048576 | tf_op jit(solution)/shard_map/all_to_all | solution.py:47
  80.3 30.0 %all_to_all.36.part_ref = bf16[4,128,2048]{2,1,0:T(8,128)(2,1)} all-to-all(bf16[4,128,2048]{2,1,0:T(8,128)(2,1)S(1)} %bitcast.120), channel_id=1, replica_groups=mesh['rep'=4,'shard'=8] {'rep'}, dimensions={0} | all-to-all | bytes 4194304 | tf_op jit(solution)/shard_map/all_to_all | solution.py:47
  131.5 30.7 %collective-permute-done.2 = bf16[1,2,64,704]{3,0,2,1:T(2,128)(2,1)S(1)} collective-permute-done((bf16[1,2,64,704]{3,0,2,1:T(2,128)(2,1)}, bf16[1,2,64,704]{3,0,2,1:T(2,128)(2,1)S(1)}, u32[]{:S(2)}, u32[]{:S(2)}) %collective-permute-start.2) | collective-permute-done | bytes 180256 | tf_op jit(solution)/shard_map/ppermute | solution.py:55
  162.6 8.1 %dynamic_update_slice.72 = bf16[8,2,64,704]{3,0,2,1:T(8,128)(2,1)S(1)} dynamic-update-slice(bf16[8,2,64,704]{3,0,2,1:T(8,128)(2,1)S(1)} %broadcast.46.clone, bf16[1,2,64,704]{3,0,2,1:T(2,128)(2,1)S(1)} %get-tuple-element.98, s32[]{:T(128)S(6)} %select_n.134, s32[]{:T(128)} %constant.82.clone.1, s32[]{:T(128)} %constant.82.clone.1, s32[]{:T(128)} %constant.82.clone.1) | dynamic-update-slice | bytes 360452 | tf_op jit(solution)/shard_map/dynamic_update_slice | solution.py:409
  170.6 8.1 %dynamic_update_slice.73 = bf16[8,2,64,704]{3,0,2,1:T(8,128)(2,1)S(1)} dynamic-update-slice(bf16[8,2,64,704]{3,0,2,1:T(8,128)(2,1)S(1)} %dynamic_update_slice.72, bf16[1,2,64,704]{3,0,2,1:T(2,128)(2,1)S(1)} %collective-permute-done.1, s32[]{:T(128)S(6)} %select_n.135, s32[]{:T(128)} %constant.82.clone.1, s32[]{:T(128)} %constant.82.clone.1, s32[]{:T(128)} %constant.82.clone.1) | dynamic-update-slice | bytes 360452 | tf_op jit(solution)/shard_map/dynamic_update_slice | solution.py:409
  178.7 8.1 %dynamic_update_slice.74 = bf16[8,2,64,704]{3,0,2,1:T(8,128)(2,1)S(1)} dynamic-update-slice(bf16[8,2,64,704]{3,0,2,1:T(8,128)(2,1)S(1)} %dynamic_update_slice.73, bf16[1,2,64,704]{3,0,2,1:T(2,128)(2,1)S(1)} %collective-permute-done.2, s32[]{:T(128)S(6)} %select_n.136, s32[]{:T(128)} %constant.82.clone.1, s32[]{:T(128)} %constant.82.clone.1, s32[]{:T(128)} %constant.82.clone.1) | dynamic-update-slice | bytes 360452 | tf_op jit(solution)/shard_map/dynamic_update_slice | solution.py:409
  186.8 8.1 %dynamic_update_slice.75 = bf16[8,2,64,704]{3,0,2,1:T(8,128)(2,1)S(1)} dynamic-update-slice(bf16[8,2,64,704]{3,0,2,1:T(8,128)(2,1)S(1)} %dynamic_update_slice.74, bf16[1,2,64,704]{3,0,2,1:T(2,128)(2,1)S(1)} %collective-permute-done.3, s32[]{:T(128)S(6)} %select_n.137, s32[]{:T(128)} %constant.82.clone.1, s32[]{:T(128)} %constant.82.clone.1, s32[]{:T(128)} %constant.82.clone.1) | dynamic-update-slice | bytes 360452 | tf_op jit(solution)/shard_map/dynamic_update_slice | solution.py:409
  194.9 8.1 %dynamic_update_slice.76 = bf16[8,2,64,704]{3,0,2,1:T(8,128)(2,1)S(1)} dynamic-update-slice(bf16[8,2,64,704]{3,0,2,1:T(8,128)(2,1)S(1)} %dynamic_update_slice.75, bf16[1,2,64,704]{3,0,2,1:T(2,128)(2,1)S(1)} %collective-permute-done.4, s32[]{:T(128)S(6)} %select_n.138, s32[]{:T(128)} %constant.82.clone.1, s32[]{:T(128)} %constant.82.clone.1, s32[]{:T(128)} %constant.82.clone.1) | dynamic-update-slice | bytes 360452 | tf_op jit(solution)/shard_map/dynamic_update_slice | solution.py:409
  203.0 9.0 %dynamic_update_slice.77 = bf16[8,2,64,704]{3,0,2,1:T(8,128)(2,1)S(1)} dynamic-update-slice(bf16[8,2,64,704]{3,0,2,1:T(8,128)(2,1)S(1)} %dynamic_update_slice.76, bf16[1,2,64,704]{3,0,2,1:T(2,128)(2,1)} %collective-permute-done.5, s32[]{:T(128)S(6)} %select_n.139, s32[]{:T(128)} %constant.82.clone.1, s32[]{:T(128)} %constant.82.clone.1, s32[]{:T(128)} %constant.82.clone.1) | dynamic-update-slice | bytes 360452 | tf_op jit(solution)/shard_map/dynamic_update_slice | solution.py:409
  212.0 9.0 %dynamic_update_slice.78 = bf16[8,2,64,704]{3,0,2,1:T(8,128)(2,1)S(1)} dynamic-update-slice(bf16[8,2,64,704]{3,0,2,1:T(8,128)(2,1)S(1)} %dynamic_update_slice.77, bf16[1,2,64,704]{3,0,2,1:T(2,128)(2,1)} %collective-permute-done.6, s32[]{:T(128)S(6)} %select_n.140, s32[]{:T(128)} %constant.82.clone.1, s32[]{:T(128)} %constant.82.clone.1, s32[]{:T(128)} %constant.82.clone.1) | dynamic-update-slice | bytes 360452 | tf_op jit(solution)/shard_map/dynamic_update_slice | solution.py:409
  221.1 9.0 %dynamic_update_slice.79 = bf16[8,2,64,704]{3,0,2,1:T(8,128)(2,1)S(1)} dynamic-update-slice(bf16[8,2,64,704]{3,0,2,1:T(8,128)(2,1)S(1)} %dynamic_update_slice.78, bf16[1,2,64,704]{3,0,2,1:T(2,128)(2,1)} %collective-permute-done.7, s32[]{:T(128)S(6)} %select_n.141, s32[]{:T(128)} %constant.82.clone.1, s32[]{:T(128)} %constant.82.clone.1, s32[]{:T(128)} %constant.82.clone.1) | dynamic-update-slice | bytes 360452 | tf_op jit(solution)/shard_map/dynamic_update_slice | solution.py:409
  240.9 11.1 %collective-permute-done.8 = bf16[8,64,704]{2,0,1:T(8,128)(2,1)S(1)} collective-permute-done((bf16[8,64,704]{2,0,1:T(8,128)(2,1)}, bf16[8,64,704]{2,0,1:T(8,128)(2,1)S(1)}, u32[]{:S(2)}, u32[]{:S(2)}) %collective-permute-start.8) | collective-permute-done | bytes 720928 | tf_op jit(solution)/shard_map/ppermute | solution.py:55
  255.1 13.7 %collective-permute-done.9 = bf16[8,64,704]{2,0,1:T(8,128)(2,1)S(1)} collective-permute-done((bf16[8,64,704]{2,0,1:T(8,128)(2,1)}, bf16[8,64,704]{2,0,1:T(8,128)(2,1)S(1)}, u32[]{:S(2)}, u32[]{:S(2)}) %collective-permute-start.9) | collective-permute-done | bytes 720928 | tf_op jit(solution)/shard_map/ppermute | solution.py:55
  272.0 14.5 %collective-permute-done.12 = bf16[8,64,704]{2,0,1:T(8,128)(2,1)S(1)} collective-permute-done((bf16[8,64,704]{2,0,1:T(8,128)(2,1)S(1)}, bf16[8,64,704]{2,0,1:T(8,128)(2,1)S(1)}, u32[]{:S(2)}, u32[]{:S(2)}) %collective-permute-start.12) | collective-permute-done | bytes 720928 | tf_op jit(solution)/shard_map/ppermute | solution.py:55
  288.6 25.4 %shard_map.206 = (bf16[1024,704]{1,0:T(8,128)(2,1)}, bf16[1024,704]{1,0:T(8,128)(2,1)}, bf16[1024,704]{1,0:T(8,128)(2,1)}, bf16[1024,2048]{1,0:T(8,128)(2,1)}) custom-call(bf16[1024,2048]{1,0:T(8,128)(2,1)} %all-gather.9.cloned.1.call-done.x_ref, bf16[1024,2048]{1,0:T(8,128)(2,1)} %all-gather.11.cloned.1.call-done.cot_ref, ...), custom_call_target="tpu_custom_call" | custom-call | tf_op jit(solution)/shard_map/pallas_call | solution.py:477
  314.3 55.5 %reduce-scatter.7.cloned.1.call-done.grad_ref = bf16[128,2048]{1,0:T(8,128)(2,1)} async-done(((bf16[1024,2048]{1,0:T(8,128)(2,1)}), bf16[128,2048]{1,0:T(8,128)(2,1)}) %reduce-scatter.7.cloned.1.call-update) | async-done | bytes 524304 | tf_op jit(solution)/shard_map/reduce_scatter | solution.py:484
  374.7 27.1 %all_to_all.37 = bf16[4,128,2048]{2,1,0:T(8,128)(2,1)S(1)} all-to-all(bf16[4,128,2048]{2,1,0:T(8,128)(2,1)S(1)} %broadcast_in_dim.70), channel_id=1, replica_groups=mesh['rep'=4,'shard'=8] {'rep'}, dimensions={0} | all-to-all | bytes 4194304 | tf_op jit(solution)/shard_map/all_to_all | solution.py:43
  403.4 10.2 %all_to_all.38 = bf16[4,512,128]{2,1,0:T(8,128)(2,1)} all-to-all(bf16[4,512,128]{2,1,0:T(8,128)(2,1)S(1)} %bitcast.122), channel_id=1, replica_groups=mesh['rep'=4,'shard'=8] {'rep'}, dimensions={0} | all-to-all | bytes 1048576 | tf_op jit(solution)/shard_map/all_to_all | solution.py:47
  413.6 8.2 %shard_map.208 = (bf16[4,128,512]{2,1,0:T(8,128)(2,1)}, f32[4,192,128]{2,1,0:T(8,128)}) custom-call(bf16[4,4,128,128]{3,2,1,0:T(8,128)(2,1)} %bitcast.116, f32[4,8,128,192]{3,2,1,0:T(8,128)} %get-tuple-element.39.probs_ref, bf16[4,128,512]{2,1,0:T(8,128)(2,1)} %get-tuple-element.30.q_ref, bf16[4,128,128]{2,1,0:T(8,128)(2,1)} %get-tuple-element.31.own_ref, ...), custom_call_target="tpu_custom_call" | custom-call | tf_op jit(solution)/shard_map/pallas_call | solution.py:533
  426.7 13.0 %shard_map.209 = (bf16[4,128,2048]{2,1,0:T(8,128)(2,1)}, bf16[2048,768]{1,0:T(8,128)(2,1)}) custom-call(bf16[4,128,512]{2,1,0:T(8,128)(2,1)} %get-tuple-element.40.dq_ref, f32[4,192,128]{2,1,0:T(8,128)} %get-tuple-element.41.dkv_ref, f32[4,64,128]{2,1,0:T(8,128)} %copy-done.23, f32[4,128,128]{2,1,0:T(8,128)} %get-tuple-element.80.cos_ref, ...), custom_call_target="tpu_custom_call" | custom-call | tf_op jit(solution)/shard_map/pallas_call | solution.py:552
  445.4 6.5 convolution_convert_fusion
  453.3 7.0 convolution_convert_fusion.3
  466.8 7.0 convolution_convert_fusion.2
  473.8 5.0 copy.80
  482.6 5.4 convolution_convert_fusion.1
  491.7 6.1 collective-permute-done.25
  499.0 22.7 %collective-permute-done.44 = bf16[80,2048]{1,0:T(8,128)(2,1)S(1)} collective-permute-done((bf16[80,2048]{1,0:T(8,128)(2,1)S(1)}, bf16[80,2048]{1,0:T(8,128)(2,1)S(1)}, u32[]{:S(2)}, u32[]{:S(2)}) %collective-permute-start.44) | collective-permute-done | bytes 327712 | tf_op jit(solution)/shard_map/ppermute | solution.py:55
  522.8 15.7 %collective-permute-done.23 = bf16[8,64,704]{2,1,0:T(8,128)(2,1)S(1)} collective-permute-done((bf16[8,64,704]{2,1,0:T(8,128)(2,1)S(1)}, bf16[8,64,704]{2,1,0:T(8,128)(2,1)S(1)}, u32[]{:S(2)}, u32[]{:S(2)}) %collective-permute-start.23) | collective-permute-done | bytes 720928 | tf_op jit(solution)/shard_map/ppermute | solution.py:55
  542.2 6.3 collective-permute-start.27
  561.8 5.1 collective-permute-done.28
  566.9 8.9 %collective-permute-done.29 = bf16[1,2,64,704]{3,2,0,1:T(8,128)(2,1)} collective-permute-done((bf16[1,2,64,704]{3,2,0,1:T(8,128)(2,1)S(1)}, bf16[1,2,64,704]{3,2,0,1:T(8,128)(2,1)}, u32[]{:S(2)}, u32[]{:S(2)}) %collective-permute-start.29) | collective-permute-done | bytes 180256 | tf_op jit(solution)/shard_map/ppermute | solution.py:55
  582.5 8.3 %dynamic_update_slice.88 = bf16[8,2,64,704]{3,0,2,1:T(8,128)(2,1)} dynamic-update-slice(bf16[8,2,64,704]{3,0,2,1:T(8,128)(2,1)} %broadcast.46, bf16[1,2,64,704]{3,0,2,1:T(2,128)(2,1)S(1)} %copy.83, s32[]{:T(128)S(6)} %select_n.134, s32[]{:T(128)} %constant.82.clone.1, s32[]{:T(128)} %constant.82.clone.1, s32[]{:T(128)} %constant.82.clone.1) | dynamic-update-slice | bytes 360452 | tf_op jit(solution)/shard_map/dynamic_update_slice | solution.py:409
  592.0 8.3 %dynamic_update_slice.89 = bf16[8,2,64,704]{3,0,2,1:T(8,128)(2,1)} dynamic-update-slice(bf16[8,2,64,704]{3,0,2,1:T(8,128)(2,1)} %dynamic_update_slice.88, bf16[1,2,64,704]{3,0,2,1:T(2,128)(2,1)S(1)} %copy.84, s32[]{:T(128)S(6)} %select_n.135, s32[]{:T(128)} %constant.82.clone.1, s32[]{:T(128)} %constant.82.clone.1, s32[]{:T(128)} %constant.82.clone.1) | dynamic-update-slice | bytes 360452 | tf_op jit(solution)/shard_map/dynamic_update_slice | solution.py:409
  601.5 8.3 %dynamic_update_slice.90 = bf16[8,2,64,704]{3,0,2,1:T(8,128)(2,1)} dynamic-update-slice(bf16[8,2,64,704]{3,0,2,1:T(8,128)(2,1)} %dynamic_update_slice.89, bf16[1,2,64,704]{3,0,2,1:T(2,128)(2,1)S(1)} %copy.85, s32[]{:T(128)S(6)} %select_n.136, s32[]{:T(128)} %constant.82.clone.1, s32[]{:T(128)} %constant.82.clone.1, s32[]{:T(128)} %constant.82.clone.1) | dynamic-update-slice | bytes 360452 | tf_op jit(solution)/shard_map/dynamic_update_slice | solution.py:409
  611.1 8.3 %dynamic_update_slice.91 = bf16[8,2,64,704]{3,0,2,1:T(8,128)(2,1)} dynamic-update-slice(bf16[8,2,64,704]{3,0,2,1:T(8,128)(2,1)} %dynamic_update_slice.90, bf16[1,2,64,704]{3,0,2,1:T(2,128)(2,1)S(1)} %copy.86, s32[]{:T(128)S(6)} %select_n.137, s32[]{:T(128)} %constant.82.clone.1, s32[]{:T(128)} %constant.82.clone.1, s32[]{:T(128)} %constant.82.clone.1) | dynamic-update-slice | bytes 360452 | tf_op jit(solution)/shard_map/dynamic_update_slice | solution.py:409
  620.6 8.3 %dynamic_update_slice.92 = bf16[8,2,64,704]{3,0,2,1:T(8,128)(2,1)} dynamic-update-slice(bf16[8,2,64,704]{3,0,2,1:T(8,128)(2,1)} %dynamic_update_slice.91, bf16[1,2,64,704]{3,0,2,1:T(2,128)(2,1)S(1)} %copy.87, s32[]{:T(128)S(6)} %select_n.138, s32[]{:T(128)} %constant.82.clone.1, s32[]{:T(128)} %constant.82.clone.1, s32[]{:T(128)} %constant.82.clone.1) | dynamic-update-slice | bytes 360452 | tf_op jit(solution)/shard_map/dynamic_update_slice | solution.py:409
  631.1 8.3 %dynamic_update_slice.93 = bf16[8,2,64,704]{3,0,2,1:T(8,128)(2,1)} dynamic-update-slice(bf16[8,2,64,704]{3,0,2,1:T(8,128)(2,1)} %dynamic_update_slice.92, bf16[1,2,64,704]{3,0,2,1:T(2,128)(2,1)S(1)} %copy.88, s32[]{:T(128)S(6)} %select_n.139, s32[]{:T(128)} %constant.82.clone.1, s32[]{:T(128)} %constant.82.clone.1, s32[]{:T(128)} %constant.82.clone.1) | dynamic-update-slice | bytes 360452 | tf_op jit(solution)/shard_map/dynamic_update_slice | solution.py:409
  640.6 8.3 %dynamic_update_slice.94 = bf16[8,2,64,704]{3,0,2,1:T(8,128)(2,1)} dynamic-update-slice(bf16[8,2,64,704]{3,0,2,1:T(8,128)(2,1)} %dynamic_update_slice.93, bf16[1,2,64,704]{3,0,2,1:T(2,128)(2,1)S(1)} %copy.89, s32[]{:T(128)S(6)} %select_n.140, s32[]{:T(128)} %constant.82.clone.1, s32[]{:T(128)} %constant.82.clone.1, s32[]{:T(128)} %constant.82.clone.1) | dynamic-update-slice | bytes 360452 | tf_op jit(solution)/shard_map/dynamic_update_slice | solution.py:409
  649.2 8.3 %dynamic_update_slice.95 = bf16[8,2,64,704]{3,0,2,1:T(8,128)(2,1)} dynamic-update-slice(bf16[8,2,64,704]{3,0,2,1:T(8,128)(2,1)} %dynamic_update_slice.94, bf16[1,2,64,704]{3,0,2,1:T(2,128)(2,1)S(1)} %copy.90, s32[]{:T(128)S(6)} %select_n.141, s32[]{:T(128)} %constant.82.clone.1, s32[]{:T(128)} %constant.82.clone.1, s32[]{:T(128)} %constant.82.clone.1) | dynamic-update-slice | bytes 360452 | tf_op jit(solution)/shard_map/dynamic_update_slice | solution.py:409
  670.8 20.6 %collective-permute-done.49.refs_5_ = bf16[80,2048]{1,0:T(8,128)(2,1)} collective-permute-done((bf16[80,2048]{1,0:T(8,128)(2,1)S(1)}, bf16[80,2048]{1,0:T(8,128)(2,1)}, u32[]{:S(2)}, u32[]{:S(2)}) %collective-permute-start.49) | collective-permute-done | bytes 327712 | tf_op jit(solution)/shard_map/ppermute | solution.py:55
  694.5 5.3 collective-permute-done.48.refs_4_
  712.5 42.0 %collective-permute-done.50.refs_6_ = bf16[96,2048]{1,0:T(8,128)(2,1)S(1)} collective-permute-done((bf16[96,2048]{1,0:T(8,128)(2,1)S(1)}, bf16[96,2048]{1,0:T(8,128)(2,1)S(1)}, u32[]{:S(2)}, u32[]{:S(2)}) %collective-permute-start.50) | collective-permute-done | bytes 393248 | tf_op jit(solution)/shard_map/ppermute | solution.py:55
  766.0 4.8 shard_map.213
  (277 shorter events, 187.2 us)
Async XLA Ops:
  7.2 40.8 %all-gather.5.cloned.1.call-start = ((), (), s32[]{:S(2)}) async-start(), calls=%async_computation.11 | async-start | bytes 2949120 | tf_op jit(solution)/shard_map/all_gather | solution.py:394
  10.3 67.1 %all-gather.7.cloned.1.call-start = ((), (), s32[]{:S(2)}) async-start(), calls=%async_computation.12 | async-start | bytes 2359296 | tf_op jit(solution)/shard_map/all_gather | solution.py:395
  12.0 276.6 %all-gather.11.cloned.1.call-start = ((), (), s32[]{:S(2)}) async-start(), calls=%async_computation.14 | async-start | bytes 4718592 | tf_op jit(solution)/shard_map/all_gather | solution.py:426
  14.8 31.6 %all-to-all-start = ((bf16[4,128,2176]{2,1,0:T(8,128)(2,1)}), bf16[4,128,2176]{2,1,0:T(8,128)(2,1)S(1)}, u32[]{:S(2)}, u32[]{:S(2)}) async-start(bf16[4,128,2176]{2,1,0:T(8,128)(2,1)} %broadcast_in_dim.34), calls=%async_computation | async-start | bytes 4456448 | tf_op jit(solution)/shard_map/all_to_all | solution.py:43
  20.1 268.5 %all-gather.9.cloned.1.call-start = ((), (), s32[]{:S(2)}) async-start(), calls=%async_computation.13 | async-start | bytes 4718592 | tf_op jit(solution)/shard_map/all_gather | solution.py:472
  113.6 256.3 %reduce-scatter.7.cloned.1.call-start = ((), (), s32[]{:S(2)}) async-start(), calls=%async_computation.16 | async-start | bytes 4718592 | tf_op jit(solution)/shard_map/reduce_scatter | solution.py:484
  120.9 41.3 %collective-permute-start.2 = (bf16[1,2,64,704]{3,0,2,1:T(2,128)(2,1)}, bf16[1,2,64,704]{3,0,2,1:T(2,128)(2,1)S(1)}, u32[]{:S(2)}, u32[]{:S(2)}) collective-permute-start(bf16[1,2,64,704]{3,0,2,1:T(2,128)(2,1)} %get-tuple-element.100), channel_id=1, source_target_pairs={{0,2},{1,3},{2,0},{3,1},{4,6},{5,7},{6,4},{7,5},{8,10},{9,11},{10,... | collective-permute-start | bytes 540680 | tf_op jit(solution)/shard_map/ppermute | solution.py:55
  125.5 61.3 %collective-permute-start.3 = (bf16[1,2,64,704]{3,0,2,1:T(2,128)(2,1)}, bf16[1,2,64,704]{3,0,2,1:T(2,128)(2,1)S(1)}, u32[]{:S(2)}, u32[]{:S(2)}) collective-permute-start(bf16[1,2,64,704]{3,0,2,1:T(2,128)(2,1)} %get-tuple-element.101), channel_id=1, source_target_pairs={{0,3},{1,2},{2,1},{3,0},{4,7},{5,6},{6,5},{7,4},{8,11},{9,10},{10,... | collective-permute-start | bytes 540680 | tf_op jit(solution)/shard_map/ppermute | solution.py:55
  125.6 69.3 %collective-permute-start.4 = (bf16[1,2,64,704]{3,0,2,1:T(2,128)(2,1)}, bf16[1,2,64,704]{3,0,2,1:T(2,128)(2,1)S(1)}, u32[]{:S(2)}, u32[]{:S(2)}) collective-permute-start(bf16[1,2,64,704]{3,0,2,1:T(2,128)(2,1)} %get-tuple-element.102), channel_id=1, source_target_pairs={{0,4},{1,5},{2,6},{3,7},{4,0},{5,1},{6,2},{7,3},{8,12},{9,13},{10,... | collective-permute-start | bytes 540680 | tf_op jit(solution)/shard_map/ppermute | solution.py:55
  128.2 74.7 %collective-permute-start.5 = (bf16[1,2,64,704]{3,0,2,1:T(2,128)(2,1)}, bf16[1,2,64,704]{3,0,2,1:T(2,128)(2,1)}, u32[]{:S(2)}, u32[]{:S(2)}) collective-permute-start(bf16[1,2,64,704]{3,0,2,1:T(2,128)(2,1)} %get-tuple-element.104), channel_id=1, source_target_pairs={{0,5},{1,4},{2,7},{3,6},{4,1},{5,0},{6,3},{7,2},{8,13},{9,12},{10,... | collective-permute-start | bytes 540680 | tf_op jit(solution)/shard_map/ppermute | solution.py:55
  129.7 82.3 %collective-permute-start.6 = (bf16[1,2,64,704]{3,0,2,1:T(2,128)(2,1)}, bf16[1,2,64,704]{3,0,2,1:T(2,128)(2,1)}, u32[]{:S(2)}, u32[]{:S(2)}) collective-permute-start(bf16[1,2,64,704]{3,0,2,1:T(2,128)(2,1)} %get-tuple-element.103), channel_id=1, source_target_pairs={{0,6},{1,7},{2,4},{3,5},{4,2},{5,3},{6,0},{7,1},{8,14},{9,15},{10,... | collective-permute-start | bytes 540680 | tf_op jit(solution)/shard_map/ppermute | solution.py:55
  162.2 58.9 %collective-permute-start.7 = (bf16[1,2,64,704]{3,0,2,1:T(2,128)(2,1)}, bf16[1,2,64,704]{3,0,2,1:T(2,128)(2,1)}, u32[]{:S(2)}, u32[]{:S(2)}) collective-permute-start(bf16[1,2,64,704]{3,0,2,1:T(2,128)(2,1)} %get-tuple-element.97), channel_id=1, source_target_pairs={{0,7},{1,6},{2,5},{3,4},{4,3},{5,2},{6,1},{7,0},{8,15},{9,14},{10,... | collective-permute-start | bytes 540680 | tf_op jit(solution)/shard_map/ppermute | solution.py:55
  231.5 20.6 %collective-permute-start.8 = (bf16[8,64,704]{2,0,1:T(8,128)(2,1)}, bf16[8,64,704]{2,0,1:T(8,128)(2,1)S(1)}, u32[]{:S(2)}, u32[]{:S(2)}) collective-permute-start(bf16[8,64,704]{2,0,1:T(8,128)(2,1)} %get-tuple-element.94), channel_id=1, source_target_pairs={{0,8},{8,0},{16,24},{24,16},{1,9},{9,1},{17,25},{25,17},{2,10},{10... | collective-permute-start | bytes 2162696 | tf_op jit(solution)/shard_map/ppermute | solution.py:55
  232.4 20.6 %collective-permute-start.11 = (bf16[8,64,704]{2,0,1:T(8,128)(2,1)}, bf16[8,64,704]{2,0,1:T(8,128)(2,1)S(1)}, u32[]{:S(2)}, u32[]{:S(2)}) collective-permute-start(bf16[8,64,704]{2,0,1:T(8,128)(2,1)} %get-tuple-element.93), channel_id=1, source_target_pairs={{0,16},{8,24},{16,0},{24,8},{1,17},{9,25},{17,1},{25,9},{2,18},{10... | collective-permute-start | bytes 2162696 | tf_op jit(solution)/shard_map/ppermute | solution.py:55
  232.4 36.5 %collective-permute-start.9 = (bf16[8,64,704]{2,0,1:T(8,128)(2,1)}, bf16[8,64,704]{2,0,1:T(8,128)(2,1)S(1)}, u32[]{:S(2)}, u32[]{:S(2)}) collective-permute-start(bf16[8,64,704]{2,0,1:T(8,128)(2,1)} %get-tuple-element.93), channel_id=1, source_target_pairs={{0,8},{8,0},{16,24},{24,16},{1,9},{9,1},{17,25},{25,17},{2,10},{10... | collective-permute-start | bytes 2162696 | tf_op jit(solution)/shard_map/ppermute | solution.py:55
  234.4 35.5 %collective-permute-start.10 = (bf16[8,64,704]{2,0,1:T(8,128)(2,1)}, bf16[8,64,704]{2,0,1:T(8,128)(2,1)S(1)}, u32[]{:S(2)}, u32[]{:S(2)}) collective-permute-start(bf16[8,64,704]{2,0,1:T(8,128)(2,1)} %get-tuple-element.94), channel_id=1, source_target_pairs={{0,16},{8,24},{16,0},{24,8},{1,17},{9,25},{17,1},{25,9},{2,18},{10... | collective-permute-start | bytes 2162696 | tf_op jit(solution)/shard_map/ppermute | solution.py:55
  252.0 34.5 %collective-permute-start.12 = (bf16[8,64,704]{2,0,1:T(8,128)(2,1)S(1)}, bf16[8,64,704]{2,0,1:T(8,128)(2,1)S(1)}, u32[]{:S(2)}, u32[]{:S(2)}) collective-permute-start(bf16[8,64,704]{2,0,1:T(8,128)(2,1)S(1)} %collective-permute-done.8), channel_id=1, source_target_pairs={{0,16},{8,24},{16,0},{24,8},{1,17},{9,25},{17,1},{25,9},{2,18},{10... | collective-permute-start | bytes 2162696 | tf_op jit(solution)/shard_map/ppermute | solution.py:55
  253.0 34.5 %collective-permute-start.13 = (bf16[8,64,704]{2,0,1:T(8,128)(2,1)S(1)}, bf16[8,64,704]{2,0,1:T(8,128)(2,1)S(1)}, u32[]{:S(2)}, u32[]{:S(2)}) collective-permute-start(bf16[8,64,704]{2,0,1:T(8,128)(2,1)S(1)} %collective-permute-done.11), channel_id=1, source_target_pairs={{0,8},{8,0},{16,24},{24,16},{1,9},{9,1},{17,25},{25,17},{2,10},{10... | collective-permute-start | bytes 2162696 | tf_op jit(solution)/shard_map/ppermute | solution.py:55
  314.0 388.5 %reduce-scatter.9.cloned.1.call-start = ((), (), s32[]{:S(2)}) async-start(), calls=%async_computation.17 | async-start | bytes 3538944 | tf_op jit(solution)/shard_map/reduce_scatter | solution.py:572
  439.7 271.7 %reduce-scatter.11.cloned.1.call-start = ((), (), s32[]{:S(2)}) async-start(), calls=%async_computation.18 | async-start | bytes 2359296 | tf_op jit(solution)/shard_map/reduce_scatter | solution.py:530
  445.1 329.7 %reduce-scatter.5.cloned.1.call-start = ((), (), s32[]{:S(2)}) async-start(), calls=%async_computation.15 | async-start | bytes 4718592 | tf_op jit(solution)/shard_map/reduce_scatter | solution.py:487
  464.8 25.1 %collective-permute-start.22 = (bf16[8,64,704]{2,1,0:T(8,128)(2,1)}, bf16[8,64,704]{2,1,0:T(8,128)(2,1)}, u32[]{:S(2)}, u32[]{:S(2)}) collective-permute-start(bf16[8,64,704]{2,1,0:T(8,128)(2,1)} %get-tuple-element.74), channel_id=1, source_target_pairs={{0,8},{8,0},{16,24},{24,16},{1,9},{9,1},{17,25},{25,17},{2,10},{10... | collective-permute-start | bytes 2162696 | tf_op jit(solution)/shard_map/ppermute | solution.py:55
  465.7 57.0 %collective-permute-start.21 = (bf16[8,64,704]{2,1,0:T(8,128)(2,1)}, bf16[8,64,704]{2,1,0:T(8,128)(2,1)}, u32[]{:S(2)}, u32[]{:S(2)}) collective-permute-start(bf16[8,64,704]{2,1,0:T(8,128)(2,1)} %get-tuple-element.73), channel_id=1, source_target_pairs={{0,8},{8,0},{16,24},{24,16},{1,9},{9,1},{17,25},{25,17},{2,10},{10... | collective-permute-start | bytes 2162696 | tf_op jit(solution)/shard_map/ppermute | solution.py:55
  481.5 59.4 %collective-permute-start.24 = (bf16[8,64,704]{2,1,0:T(8,128)(2,1)S(1)}, bf16[8,64,704]{2,1,0:T(8,128)(2,1)S(1)}, u32[]{:S(2)}, u32[]{:S(2)}) collective-permute-start(bf16[8,64,704]{2,1,0:T(8,128)(2,1)S(1)} %get-tuple-element.71), channel_id=1, source_target_pairs={{0,16},{8,24},{16,0},{24,8},{1,17},{9,25},{17,1},{25,9},{2,18},{10... | collective-permute-start | bytes 2162696 | tf_op jit(solution)/shard_map/ppermute | solution.py:55
  488.9 63.8 %collective-permute-start.41 = (bf16[96,2048]{1,0:T(8,128)(2,1)S(1)}, bf16[96,2048]{1,0:T(8,128)(2,1)S(1)}, u32[]{:S(2)}, u32[]{:S(2)}) collective-permute-start(bf16[96,2048]{1,0:T(8,128)(2,1)S(1)} %get-tuple-element.78), channel_id=1, source_target_pairs={{0,8},{8,0},{16,24},{24,16},{1,9},{9,1},{17,25},{25,17},{2,10},{10... | collective-permute-start | bytes 1179656 | tf_op jit(solution)/shard_map/ppermute | solution.py:55
  489.9 31.8 %collective-permute-start.44 = (bf16[80,2048]{1,0:T(8,128)(2,1)S(1)}, bf16[80,2048]{1,0:T(8,128)(2,1)S(1)}, u32[]{:S(2)}, u32[]{:S(2)}) collective-permute-start(bf16[80,2048]{1,0:T(8,128)(2,1)S(1)} %get-tuple-element.76), channel_id=1, source_target_pairs={{0,16},{8,24},{16,0},{24,8},{1,17},{9,25},{17,1},{25,9},{2,18},{10... | collective-permute-start | bytes 983048 | tf_op jit(solution)/shard_map/ppermute | solution.py:55
  497.8 40.7 %collective-permute-start.23 = (bf16[8,64,704]{2,1,0:T(8,128)(2,1)S(1)}, bf16[8,64,704]{2,1,0:T(8,128)(2,1)S(1)}, u32[]{:S(2)}, u32[]{:S(2)}) collective-permute-start(bf16[8,64,704]{2,1,0:T(8,128)(2,1)S(1)} %fusion.3), channel_id=1, source_target_pairs={{0,16},{8,24},{16,0},{24,8},{1,17},{9,25},{17,1},{25,9},{2,18},{10... | collective-permute-start | bytes 2162696 | tf_op jit(solution)/shard_map/ppermute | solution.py:55
  522.7 27.2 %collective-permute-start.43 = (bf16[80,2048]{1,0:T(8,128)(2,1)S(1)}, bf16[80,2048]{1,0:T(8,128)(2,1)S(1)}, u32[]{:S(2)}, u32[]{:S(2)}) collective-permute-start(bf16[80,2048]{1,0:T(8,128)(2,1)S(1)} %get-tuple-element.75), channel_id=1, source_target_pairs={{0,16},{8,24},{16,0},{24,8},{1,17},{9,25},{17,1},{25,9},{2,18},{10... | collective-permute-start | bytes 983048 | tf_op jit(solution)/shard_map/ppermute | solution.py:55
  549.9 25.9 %collective-permute-start.29 = (bf16[1,2,64,704]{3,2,0,1:T(8,128)(2,1)S(1)}, bf16[1,2,64,704]{3,2,0,1:T(8,128)(2,1)}, u32[]{:S(2)}, u32[]{:S(2)}) collective-permute-start(bf16[1,2,64,704]{3,2,0,1:T(8,128)(2,1)S(1)} %get-tuple-element.87), channel_id=1, source_target_pairs={{0,3},{1,2},{2,1},{3,0},{4,7},{5,6},{6,5},{7,4},{8,11},{9,10},{10,... | collective-permute-start | bytes 540680 | tf_op jit(solution)/shard_map/ppermute | solution.py:55
  552.7 25.7 %collective-permute-start.30 = (bf16[1,2,64,704]{3,2,0,1:T(8,128)(2,1)S(1)}, bf16[1,2,64,704]{3,2,0,1:T(8,128)(2,1)}, u32[]{:S(2)}, u32[]{:S(2)}) collective-permute-start(bf16[1,2,64,704]{3,2,0,1:T(8,128)(2,1)S(1)} %get-tuple-element.88), channel_id=1, source_target_pairs={{0,4},{1,5},{2,6},{3,7},{4,0},{5,1},{6,2},{7,3},{8,12},{9,13},{10,... | collective-permute-start | bytes 540680 | tf_op jit(solution)/shard_map/ppermute | solution.py:55
  554.3 149.4 %all-to-all-start.5 = ((bf16[4,128,2048]{2,1,0:T(8,128)(2,1)}), bf16[4,128,2048]{2,1,0:T(8,128)(2,1)S(1)}, u32[]{:S(2)}, u32[]{:S(2)}) async-start(bf16[4,128,2048]{2,1,0:T(8,128)(2,1)} %get-tuple-element.44), calls=%async_computation.7 | async-start | bytes 4194304 | tf_op jit(solution)/shard_map/all_to_all | solution.py:47
  558.3 107.7 %collective-permute-start.40 = (bf16[96,2048]{1,0:T(8,128)(2,1)}, bf16[96,2048]{1,0:T(8,128)(2,1)}, u32[]{:S(2)}, u32[]{:S(2)}) collective-permute-start(bf16[96,2048]{1,0:T(8,128)(2,1)} %get-tuple-element.77), channel_id=1, source_target_pairs={{0,8},{8,0},{16,24},{24,16},{1,9},{9,1},{17,25},{25,17},{2,10},{10... | collective-permute-start | bytes 1179656 | tf_op jit(solution)/shard_map/ppermute | solution.py:55
  560.3 105.7 %collective-permute-start.42 = (bf16[96,2048]{1,0:T(8,128)(2,1)}, bf16[96,2048]{1,0:T(8,128)(2,1)}, u32[]{:S(2)}, u32[]{:S(2)}) collective-permute-start(bf16[96,2048]{1,0:T(8,128)(2,1)} %add_convert_fusion.2), channel_id=1, source_target_pairs={{0,16},{8,24},{16,0},{24,8},{1,17},{9,25},{17,1},{25,9},{2,18},{10... | collective-permute-start | bytes 1179656 | tf_op jit(solution)/shard_map/ppermute | solution.py:55
  566.9 62.0 %collective-permute-start.31 = (bf16[1,2,64,704]{3,2,0,1:T(8,128)(2,1)}, bf16[1,2,64,704]{3,2,0,1:T(8,128)(2,1)}, u32[]{:S(2)}, u32[]{:S(2)}) collective-permute-start(bf16[1,2,64,704]{3,2,0,1:T(8,128)(2,1)} %get-tuple-element.90), channel_id=1, source_target_pairs={{0,5},{1,4},{2,7},{3,6},{4,1},{5,0},{6,3},{7,2},{8,13},{9,12},{10,... | collective-permute-start | bytes 540680 | tf_op jit(solution)/shard_map/ppermute | solution.py:55
  575.8 63.6 %collective-permute-start.32 = (bf16[1,2,64,704]{3,2,0,1:T(8,128)(2,1)}, bf16[1,2,64,704]{3,2,0,1:T(8,128)(2,1)}, u32[]{:S(2)}, u32[]{:S(2)}) collective-permute-start(bf16[1,2,64,704]{3,2,0,1:T(8,128)(2,1)} %get-tuple-element.89), channel_id=1, source_target_pairs={{0,6},{1,7},{2,4},{3,5},{4,2},{5,3},{6,0},{7,1},{8,14},{9,15},{10,... | collective-permute-start | bytes 540680 | tf_op jit(solution)/shard_map/ppermute | solution.py:55
  578.3 70.6 %collective-permute-start.33 = (bf16[1,2,64,704]{3,2,0,1:T(8,128)(2,1)}, bf16[1,2,64,704]{3,2,0,1:T(8,128)(2,1)S(1)}, u32[]{:S(2)}, u32[]{:S(2)}) collective-permute-start(bf16[1,2,64,704]{3,2,0,1:T(8,128)(2,1)} %get-tuple-element.83), channel_id=1, source_target_pairs={{0,7},{1,6},{2,5},{3,4},{4,3},{5,2},{6,1},{7,0},{8,15},{9,14},{10,... | collective-permute-start | bytes 540680 | tf_op jit(solution)/shard_map/ppermute | solution.py:55
  628.9 40.7 %collective-permute-start.47 = (bf16[80,2048]{1,0:T(8,128)(2,1)S(1)}, bf16[80,2048]{1,0:T(8,128)(2,1)}, u32[]{:S(2)}, u32[]{:S(2)}) collective-permute-start(bf16[80,2048]{1,0:T(8,128)(2,1)S(1)} %add_convert_fusion.3.refs_1_), channel_id=1, source_target_pairs={{0,8},{8,0},{16,24},{24,16},{1,9},{9,1},{17,25},{25,17},{2,10},{10... | collective-permute-start | bytes 983048 | tf_op jit(solution)/shard_map/ppermute | solution.py:55
  662.4 31.3 %collective-permute-start.34 = (bf16[64,5632]{1,0:T(8,128)(2,1)}, bf16[64,5632]{1,0:T(8,128)(2,1)}, u32[]{:S(2)}, u32[]{:S(2)}) collective-permute-start(bf16[64,5632]{1,0:T(8,128)(2,1)} %squeeze.45.refs_0_), channel_id=1, source_target_pairs={{0,8},{8,0},{16,24},{24,16},{1,9},{9,1},{17,25},{25,17},{2,10},{10... | collective-permute-start | bytes 2162696 | tf_op jit(solution)/shard_map/ppermute | solution.py:55
  665.1 36.4 %collective-permute-start.38 = (bf16[64,5632]{1,0:T(8,128)(2,1)}, bf16[64,5632]{1,0:T(8,128)(2,1)}, u32[]{:S(2)}, u32[]{:S(2)}) collective-permute-start(bf16[64,5632]{1,0:T(8,128)(2,1)} %squeeze.46.refs_0_), channel_id=1, source_target_pairs={{0,16},{8,24},{16,0},{24,8},{1,17},{9,25},{17,1},{25,9},{2,18},{10... | collective-permute-start | bytes 2162696 | tf_op jit(solution)/shard_map/ppermute | solution.py:55
  667.4 25.0 %collective-permute-start.46 = (bf16[96,2048]{1,0:T(8,128)(2,1)S(1)}, bf16[96,2048]{1,0:T(8,128)(2,1)S(1)}, u32[]{:S(2)}, u32[]{:S(2)}) collective-permute-start(bf16[96,2048]{1,0:T(8,128)(2,1)S(1)} %add_convert_fusion.1.refs_0_), channel_id=1, source_target_pairs={{0,8},{8,0},{16,24},{24,16},{1,9},{9,1},{17,25},{25,17},{2,10},{10... | collective-permute-start | bytes 1179656 | tf_op jit(solution)/shard_map/ppermute | solution.py:55
  668.8 22.7 %collective-permute-start.49 = (bf16[80,2048]{1,0:T(8,128)(2,1)S(1)}, bf16[80,2048]{1,0:T(8,128)(2,1)}, u32[]{:S(2)}, u32[]{:S(2)}) collective-permute-start(bf16[80,2048]{1,0:T(8,128)(2,1)S(1)} %add_convert_fusion.3.refs_1_), channel_id=1, source_target_pairs={{0,16},{8,24},{16,0},{24,8},{1,17},{9,25},{17,1},{25,9},{2,18},{10... | collective-permute-start | bytes 983048 | tf_op jit(solution)/shard_map/ppermute | solution.py:55
  669.6 30.2 %collective-permute-start.48 = (bf16[96,2048]{1,0:T(8,128)(2,1)S(1)}, bf16[96,2048]{1,0:T(8,128)(2,1)S(1)}, u32[]{:S(2)}, u32[]{:S(2)}) collective-permute-start(bf16[96,2048]{1,0:T(8,128)(2,1)S(1)} %add_convert_fusion.1.refs_0_), channel_id=1, source_target_pairs={{0,16},{8,24},{16,0},{24,8},{1,17},{9,25},{17,1},{25,9},{2,18},{10... | collective-permute-start | bytes 1179656 | tf_op jit(solution)/shard_map/ppermute | solution.py:55
  692.4 63.3 %collective-permute-start.35 = (bf16[64,5632]{1,0:T(8,128)(2,1)}, bf16[64,5632]{1,0:T(8,128)(2,1)}, u32[]{:S(2)}, u32[]{:S(2)}) collective-permute-start(bf16[64,5632]{1,0:T(8,128)(2,1)} %squeeze.45.refs_0_), channel_id=1, source_target_pairs={{0,16},{8,24},{16,0},{24,8},{1,17},{9,25},{17,1},{25,9},{2,18},{10... | collective-permute-start | bytes 2162696 | tf_op jit(solution)/shard_map/ppermute | solution.py:55
  693.7 67.6 %collective-permute-start.36 = (bf16[64,5632]{1,0:T(8,128)(2,1)}, bf16[64,5632]{1,0:T(8,128)(2,1)}, u32[]{:S(2)}, u32[]{:S(2)}) collective-permute-start(bf16[64,5632]{1,0:T(8,128)(2,1)} %collective-permute-done.34.refs_1_), channel_id=1, source_target_pairs={{0,16},{8,24},{16,0},{24,8},{1,17},{9,25},{17,1},{25,9},{2,18},{10... | collective-permute-start | bytes 2162696 | tf_op jit(solution)/shard_map/ppermute | solution.py:55
  700.5 65.5 %collective-permute-start.37 = (bf16[64,5632]{1,0:T(8,128)(2,1)}, bf16[64,5632]{1,0:T(8,128)(2,1)}, u32[]{:S(2)}, u32[]{:S(2)}) collective-permute-start(bf16[64,5632]{1,0:T(8,128)(2,1)} %squeeze.46.refs_0_), channel_id=1, source_target_pairs={{0,8},{8,0},{16,24},{24,16},{1,9},{9,1},{17,25},{25,17},{2,10},{10... | collective-permute-start | bytes 2162696 | tf_op jit(solution)/shard_map/ppermute | solution.py:55
  701.5 64.5 %collective-permute-start.39 = (bf16[64,5632]{1,0:T(8,128)(2,1)}, bf16[64,5632]{1,0:T(8,128)(2,1)}, u32[]{:S(2)}, u32[]{:S(2)}) collective-permute-start(bf16[64,5632]{1,0:T(8,128)(2,1)} %collective-permute-done.38.refs_2_), channel_id=1, source_target_pairs={{0,8},{8,0},{16,24},{24,16},{1,9},{9,1},{17,25},{25,17},{2,10},{10... | collective-permute-start | bytes 2162696 | tf_op jit(solution)/shard_map/ppermute | solution.py:55
  705.6 78.8 %all-to-all-start.6 = ((bf16[4,256,768]{1,2,0:T(8,128)(2,1)}), bf16[4,256,768]{1,2,0:T(8,128)(2,1)S(1)}, u32[]{:S(2)}, u32[]{:S(2)}) async-start(bf16[4,256,768]{1,2,0:T(8,128)(2,1)} %broadcast_in_dim.71), calls=%async_computation.9 | async-start | bytes 3145728 | tf_op jit(solution)/shard_map/all_to_all | solution.py:43
  709.4 45.1 %collective-permute-start.50 = (bf16[96,2048]{1,0:T(8,128)(2,1)S(1)}, bf16[96,2048]{1,0:T(8,128)(2,1)S(1)}, u32[]{:S(2)}, u32[]{:S(2)}) collective-permute-start(bf16[96,2048]{1,0:T(8,128)(2,1)S(1)} %copy-done.17), channel_id=1, source_target_pairs={{0,16},{8,24},{16,0},{24,8},{1,17},{9,25},{17,1},{25,9},{2,18},{10... | collective-permute-start | bytes 1179656 | tf_op jit(solution)/shard_map/ppermute | solution.py:55
  (51 other events, 666.9 us)
Sparse Core Ops, SparseCore 0:
  10.4 36.4 all-gather.4
  49.1 28.2 all-gather.6
  79.0 46.9 all-gather.10
  128.0 96.3 all-gather.8
  314.2 55.6 reduce-scatter.6
  439.9 42.2 reduce-scatter.8
  484.5 35.3 reduce-scatter.10
  522.2 64.5 reduce-scatter.4
where the time goes:
time: 809 us; the launch traced here: 799 us
  waiting for transfers between devices  272 us (34%)
  local copies, waits for them, and re-layouts  202 us (25%)
  blocking collectives  90.2 us (11%)
  Pallas kernels  87 us (11%)
  starting transfers between devices  77.4 us (10%)
  matrix products  34.4 us (4%)
  other arithmetic  20.4 us (3%)
  between operations  15.2 us (2%)
    ppermute x50, waiting for transfers between devices, send(): return lax.ppermute(value, axis, pairs(count, step))  197 us
    dynamic_update_slice x16, local copies, waits for them, and re-layouts, exchange_shard(): total = lax.dynamic_update_slice_in_dim(total, piece, s ^ k, 0)  134 us
    ppermute x50, starting transfers between devices, send(): return lax.ppermute(value, axis, pairs(count, step))  61.1 us
    reduce_scatter x1, waiting for transfers between devices, body(): lax.psum_scatter(two_grad_part, 'shard', scatter_dimension=0, tiled=True)  55.5 us
    all_to_all x3, blocking collectives, swap(): return lax.all_to_all(value, axis, split_axis=0, concat_axis=0, tiled=True)  50.8 us
    dot_general x7, matrix products, dot(): lax.dot_general(left, right, (contract, ((), ())), preferred_element_type...  34.4 us
    all_to_all x1, blocking collectives, spread(): return lax.all_to_all(wide, axis, split_axis=0, concat_axis=0, tiled=True)  27.1 us
    pallas_call x1, Pallas kernels, body(): call(forward_back_kernel, (shape((group, hidden), BF),) * 3 + (shape((gro...  25.4 us
  transfers between devices with their start and end apart: 63, of which 18 were waited for; matrix products, arithmetic and copies ran while one was open for 30% of the time, Pallas kernels for 5%

commit v1 on v0

--- a/solution.py
+++ b/solution.py
@@ -55,26 +55,21 @@
     return lax.ppermute(value, axis, pairs(count, step))
 
 
-def sum_rep(chunks, count):
-    wide = lambda value: value.astype(F32)
+def parts_rep(chunks, count):
     go = lambda value, step: send(value, "rep", count, step)
     if count != 4:
-        return tuple(
-            sum([wide(go(chunks[k][h], k)) for k in range(1, count)], wide(chunks[0][h]))
+        return [
+            [chunks[0][h]] + [go(chunks[k][h], k) for k in range(1, count)]
             for h in range(2)
-        )
+        ]
+    add = lambda left, right: (left.astype(F32) + right.astype(F32)).astype(BF)
     first_one = go(chunks[1][0], 1)
     first_two = go(chunks[3][0], 1)
     second_one = go(chunks[2][1], 2)
     second_two = go(chunks[3][1], 2)
-    joint_one = (wide(chunks[2][0]) + wide(first_two)).astype(BF)
-    joint_two = (wide(chunks[1][1]) + wide(second_two)).astype(BF)
-    last_one = go(joint_one, 2)
-    last_two = go(joint_two, 1)
-    return (
-        wide(chunks[0][0]) + wide(first_one) + wide(last_one),
-        wide(chunks[0][1]) + wide(second_one) + wide(last_two),
-    )
+    last_one = go(add(chunks[2][0], first_two), 2)
+    last_two = go(add(chunks[1][1], second_two), 1)
+    return [[chunks[0][0], first_one, last_one], [chunks[0][1], second_one, last_two]]
 
 
 def gather_rep(halves, count):
@@ -120,6 +115,89 @@
         grid_spec=grid,
         compiler_params=pltpu.CompilerParams(vmem_limit_bytes=56 * 1024 * 1024),
     )(me.astype(jnp.int32).reshape(1), *flat).reshape(count * rows, width)
+
+
+def split_kernel(id_ref, gate_ref, up_ref, *refs):
+    outs, both = refs[:-1], refs[-1]
+    hidden = both.shape[3]
+    for h, ref in enumerate((gate_ref, up_ref)):
+        value = ref[...]
+        for at in range(len(outs)):
+            both[at, h] = value[:, at * hidden : (at + 1) * hidden]
+    for k, out in enumerate(outs):
+        out[...] = both[jnp.bitwise_xor(id_ref[1], k)]
+
+
+def split_pair(ids, gate, up, fine, count):
+    hidden = gate.shape[1] // count
+    rows = pl.BlockSpec((fine, gate.shape[1]), lambda g, ids: (ids[0], 0))
+    piece = (2, fine, hidden)
+    return pl.pallas_call(
+        split_kernel,
+        out_shape=(shape(piece, BF),) * count,
+        grid_spec=pltpu.PrefetchScalarGridSpec(
+            num_scalar_prefetch=1,
+            grid=(1,),
+            in_specs=[rows, rows],
+            out_specs=(pl.BlockSpec(piece, lambda g, ids: (0, 0, 0)),) * count,
+            scratch_shapes=[pltpu.VMEM((count,) + piece, BF)],
+        ),
+        name="split_pair",
+    )(ids, gate, up)
+
+
+def flat_call(kernel, ids, out_shape, values, scratch=()):
+    specs = [pl.BlockSpec(memory_space=pltpu.SMEM)]
+    specs += [pl.BlockSpec(memory_space=pltpu.VMEM)] * len(values)
+    return pl.pallas_call(
+        kernel,
+        out_shape=out_shape,
+        in_specs=specs,
+        scratch_shapes=list(scratch),
+        compiler_params=pltpu.CompilerParams(vmem_limit_bytes=56 * 1024 * 1024),
+    )(ids, *values)
+
+
+def order_kernel(id_ref, *refs):
+    pieces, (gate_ref, up_ref) = refs[:-2], refs[-2:]
+    for k, piece in enumerate(pieces):
+        at = jnp.bitwise_xor(id_ref[1], k)
+        gate_ref[at] = piece[0]
+        up_ref[at] = piece[1]
+
+
+def join_kernel(id_ref, *refs):
+    out_ref = refs[-1]
+    for k in range(len(refs) // 2):
+        at = jnp.bitwise_xor(id_ref[0], k)
+        for h in range(2):
+            value = refs[2 * k + h]
+            for row in range(value.shape[0]):
+                out_ref[h, row, at] = value[row]
+
+
+def sum_kernel(id_ref, *refs):
+    count = refs[0].shape[0]
+    outs = refs[len(refs) - count :]
+    parts = refs[: len(refs) - count]
+    half = len(parts) // 2
+    for k, out in enumerate(outs):
+        at = jnp.bitwise_xor(id_ref[1], k)
+        for h in range(2):
+            total = parts[h * half][at].astype(F32)
+            for part in parts[h * half + 1 : (h + 1) * half]:
+                total += part[at].astype(F32)
+            out[h] = total.astype(BF)
+
+
+def widen_kernel(id_ref, *refs):
+    pieces, (gate_ref, up_ref, both) = refs[:-3], refs[-3:]
+    hidden = both.shape[3]
+    for k, piece in enumerate(pieces):
+        both[jnp.bitwise_xor(id_ref[1], k)] = piece[...]
+    for h, ref in enumerate((gate_ref, up_ref)):
+        for at in range(len(pieces)):
+            ref[:, at * hidden : (at + 1) * hidden] = both[at, h]
 
 
 def norm_scale(value):
@@ -400,29 +478,23 @@
     gain_one = gains[0:1].astype(F32)
     gain_two = gains[1:2].astype(F32)
 
-    def exchange_shard(value):
-        total = jnp.zeros_like(value)
-        for k in range(n_shard):
-            piece = lax.dynamic_slice_in_dim(value, s ^ k, 1, 0)
-            if k:
-                piece = send(piece, "shard", n_shard, k)
-            total = lax.dynamic_update_slice_in_dim(total, piece, s ^ k, 0)
-        return total
-
-    def quarter(weight):
-        part = lax.dynamic_slice_in_dim(weight, r * fine, fine, 0)
-        return part.reshape(fine, n_shard, hidden).transpose(1, 0, 2)
-
-    w_pair = jnp.stack([quarter(gate_weight), quarter(up_weight)], axis=1)
-    w_pair = exchange_shard(w_pair).transpose(1, 0, 2, 3)
-    w_pair = gather_rep((w_pair[0], w_pair[1]), n_rep)
-    grown = jnp.zeros((2, n_shard, n_rep, fine, hidden), BF)
-    for k, piece in enumerate(w_pair):
-        for h in range(2):
-            grown = lax.dynamic_update_slice(
-                grown, piece[h][None, :, None], (h, 0, r ^ k, 0, 0)
-            )
-    w_pair = grown.reshape(2, width, hidden)
+    def exchange_shard(pieces):
+        rest = [send(pieces[k], "shard", n_shard, k) for k in range(1, n_shard)]
+        return [pieces[0]] + rest
+
+    block = (n_shard, fine, hidden)
+    ids = jnp.stack([r, s]).astype(jnp.int32)
+    gate_tied, up_tied, _ = lax.optimization_barrier((gate_weight, up_weight, gains))
+    w_pair = split_pair(ids, gate_tied, up_tied, fine, n_shard)
+    w_pair = exchange_shard(w_pair)
+    w_pair = flat_call(order_kernel, ids, (shape(block, BF),) * 2, w_pair)
+    w_pair = gather_rep(w_pair, n_rep)
+    w_pair = flat_call(
+        join_kernel,
+        ids,
+        shape((2, n_shard, n_rep, fine, hidden), BF),
+        [half for piece in w_pair for half in piece],
+    ).reshape(2, width, hidden)
     cot_all = lax.all_gather(cotangent, "shard", axis=0, tiled=True)
 
     half = HD // 2
@@ -504,8 +576,10 @@
                 lax.dynamic_slice_in_dim(w_down_grad, at + cut, part_rows - cut, 0),
             )
         )
-    low = lambda values: tuple(value.astype(BF) for value in values)
-    w_down_grad = low(sum_rep(chunks, n_rep))
+    w_down_grad = parts_rep(chunks, n_rep)
+    w_down_grad = tuple(
+        sum(part.astype(F32) for part in parts).astype(BF) for parts in w_down_grad
+    )
     down_out = place(gather_rep(w_down_grad, n_rep), r)
     halves = [
         rows_rows(two_all, part).astype(BF).reshape(n_shard, n_rep, fine, hidden)
@@ -515,15 +589,28 @@
         tuple(lax.dynamic_index_in_dim(half, r ^ k, 1, False) for half in halves)
         for k in range(n_rep)
     ]
-    w_pair_grad = low(sum_rep(chunks, n_rep))
-    w_pair_grad = exchange_shard(jnp.stack(w_pair_grad, axis=1))
-    w_pair_grad = w_pair_grad.transpose(1, 2, 0, 3).reshape(2, fine, n_shard * hidden)
-    w_pair_grad = gather_rep((w_pair_grad[0], w_pair_grad[1]), n_rep)
+    w_pair_grad = parts_rep(chunks, n_rep)
+    w_pair_grad = flat_call(
+        sum_kernel,
+        ids,
+        (shape((2, fine, hidden), BF),) * n_shard,
+        w_pair_grad[0] + w_pair_grad[1],
+    )
+    w_pair_grad = exchange_shard(w_pair_grad)
+    w_pair_grad = flat_call(
+        widen_kernel,
+        ids,
+        (shape((fine, n_shard * hidden), BF),) * 2,
+        w_pair_grad,
+        [pltpu.VMEM((n_shard, 2, fine, hidden), BF)],
+    )
+    w_pair_grad = gather_rep(w_pair_grad, n_rep)
     gate_out = place([piece[:1] for piece in w_pair_grad], r)
     up_out = place([piece[1:] for piece in w_pair_grad], r)
 
     branch_all = spread(branch, "rep", n_rep).reshape(all_rows, width)
     in_grad = cols_cols(branch_all, w_o).astype(BF)
+    branch_all, in_grad = lax.optimization_barrier((branch_all, in_grad))
     in_grad = in_grad.reshape(all_rows, n_rep, pair * fine).transpose(1, 0, 2)
     in_grad = swap(in_grad, "rep").reshape(n_rep, n_rep, rows, pair * fine)
     w_o_grad = rows_rows(out_in, branch_all).astype(BF)

time: 809 us -> 705 us (0.87)
  local copies, waits for them, and re-layouts: 202 us -> 43.4 us
  waiting for transfers between devices: 272 us -> 308 us
  Pallas kernels: 87 us -> 106 us
    dynamic_update_slice x24 -> x0, local copies, waits for them, and re-layouts: 142 us -> none  [the longest x16 134 us: exchange_shard(): total = lax.dynamic_update_slice_in_dim(total, piece, s ^ k, 0)]
    reduce_scatter x1, waiting for transfers between devices: 55.5 us -> 80.4 us  [body(): lax.psum_scatter(two_grad_part, 'shard', scatter_dimension=0, tiled=True)]
    pallas_call x0 -> x5, Pallas kernels: none -> 18.8 us  [the longest x4 15.3 us: flat_call(): pl.pallas_call(kernel, out_shape=out_shape, in_specs=specs, scratch_shape...]
    ppermute x50, waiting for transfers between devices: 197 us -> 210 us  [send(): return lax.ppermute(value, axis, pairs(count, step))]
    ppermute x1, starting transfers between devices: 1.29 us -> 11.7 us  [body(): lax.ppermute(kv_grad[:, :HALO], 'shard', [(i + 1, i) for i in range(n_sha...]
    another operation x7 -> x2, other arithmetic: 9.87 us -> 0.8 us  [the longest x1 0.59 us: body(): ids = jnp.stack([r, s]).astype(jnp.int32)]
  transfers between devices with their start and end apart: 63 -> 63, of which waited for: 18 -> 25; matrix products, arithmetic and copies ran while one was open for 30% -> 10% of each run, Pallas kernels for 5% -> 8%
where the time goes in v1:
time: 705 us; the launch traced here: 693 us
  waiting for transfers between devices  308 us (44%)
  Pallas kernels  106 us (15%)
  blocking collectives  90.2 us (13%)
  starting transfers between devices  82 us (12%)
  local copies, waits for them, and re-layouts  43.4 us (6%)
  matrix products  32.7 us (5%)
  other arithmetic  15.3 us (2%)
  between operations  15.1 us (2%)
    ppermute x50, waiting for transfers between devices, send(): return lax.ppermute(value, axis, pairs(count, step))  210 us
    reduce_scatter x1, waiting for transfers between devices, body(): lax.psum_scatter(two_grad_part, 'shard', scatter_dimension=0, tiled=True)  80.4 us
    ppermute x50, starting transfers between devices, send(): return lax.ppermute(value, axis, pairs(count, step))  55.6 us
    all_to_all x3, blocking collectives, swap(): return lax.all_to_all(value, axis, split_axis=0, concat_axis=0, tiled=True)  50.7 us
    dot_general x7, matrix products, dot(): lax.dot_general(left, right, (contract, ((), ())), preferred_element_type...  32.7 us
    all_to_all x1, blocking collectives, spread(): return lax.all_to_all(wide, axis, split_axis=0, concat_axis=0, tiled=True)  27.1 us
    pallas_call x1, Pallas kernels, body(): call(forward_back_kernel, (shape((group, hidden), BF),) * 3 + (shape((gro...  25.4 us
    pallas_call x4, Pallas kernels, place(): pl.pallas_call(partial(place_kernel, count), out_shape=shape((count, rows...  17.2 us
  transfers between devices with their start and end apart: 63, of which 25 were waited for; matrix products, arithmetic and copies ran while one was open for 10% of the time, Pallas kernels for 8%

profile of v1, /device:TPU:0, one launch (start us, length us, event | category | flops | bytes accessed | tf_op | source)
XLA Modules:
  0.0 692.6 jit_solution(8376746619745315543)
XLA Ops:
  14.8 5.3 all-to-all-start
  20.1 12.3 %all_gather.15 = bf16[2,2048]{1,0:T(2,128)(2,1)S(1)} all-gather(bf16[2,256]{1,0:T(2,128)(2,1)S(1)} %pad_maximum_fusion.2), channel_id=1, replica_groups=mesh['rep'=4,'shard'=8] {'shard'}, dimensions={1}, use_global_device_ids=true | all-gather | bytes 9216 | tf_op jit(solution)/shard_map/all_gather | solution.py:477
  33.1 13.3 %all-to-all-done.x_ref.pos_ref = bf16[4,128,2176]{2,1,0:T(8,128)(2,1)S(1)} async-done(((bf16[4,128,2176]{2,1,0:T(8,128)(2,1)}), bf16[4,128,2176]{2,1,0:T(8,128)(2,1)S(1)}, u32[]{:S(2)}, u32[]{:S(2)}) %all-to-all-start) | async-done | bytes 2228256 | tf_op jit(solution)/shard_map/all_to_all | solution.py:43
  48.1 6.2 shard_map.203
  57.9 6.4 shard_map.204
  64.3 10.6 %all_to_all.35 = bf16[4,4,128,128]{3,2,1,0:T(8,128)(2,1)S(1)} all-to-all(bf16[4,4,128,128]{3,2,1,0:T(8,128)(2,1)} %get-tuple-element.56), channel_id=1, replica_groups=mesh['rep'=4,'shard'=8] {'rep'}, dimensions={0} | all-to-all | bytes 1048576 | tf_op jit(solution)/shard_map/all_to_all | solution.py:47
  80.3 29.9 %all_to_all.36.part_ref = bf16[4,128,2048]{2,1,0:T(8,128)(2,1)} all-to-all(bf16[4,128,2048]{2,1,0:T(8,128)(2,1)S(1)} %bitcast.85), channel_id=1, replica_groups=mesh['rep'=4,'shard'=8] {'rep'}, dimensions={0} | all-to-all | bytes 4194304 | tf_op jit(solution)/shard_map/all_to_all | solution.py:47
  110.2 3.3 shard_map.205
  114.5 3.4 split_pair.1
  118.0 4.4 collective-permute-start.2
  126.7 9.3 %collective-permute-done.2.refs_2_ = bf16[2,64,704]{2,1,0:T(8,128)(2,1)S(1)} collective-permute-done((bf16[2,64,704]{2,1,0:T(8,128)(2,1)}, bf16[2,64,704]{2,1,0:T(8,128)(2,1)S(1)}, u32[]{:S(2)}, u32[]{:S(2)}) %collective-permute-start.2) | collective-permute-done | bytes 180256 | tf_op jit(solution)/shard_map/ppermute | solution.py:55
  140.0 12.4 %collective-permute-done.5.refs_5_ = bf16[2,64,704]{2,1,0:T(8,128)(2,1)S(1)} collective-permute-done((bf16[2,64,704]{2,1,0:T(8,128)(2,1)}, bf16[2,64,704]{2,1,0:T(8,128)(2,1)S(1)}, u32[]{:S(2)}, u32[]{:S(2)}) %collective-permute-start.5) | collective-permute-done | bytes 180256 | tf_op jit(solution)/shard_map/ppermute | solution.py:55
  161.1 12.0 %collective-permute-done.8.refs_2_ = bf16[8,64,704]{2,1,0:T(8,128)(2,1)S(1)} collective-permute-done((bf16[8,64,704]{2,1,0:T(8,128)(2,1)}, bf16[8,64,704]{2,1,0:T(8,128)(2,1)S(1)}, u32[]{:S(2)}, u32[]{:S(2)}) %collective-permute-start.8) | collective-permute-done | bytes 720928 | tf_op jit(solution)/shard_map/ppermute | solution.py:55
  176.1 13.9 %collective-permute-done.9.refs_3_ = bf16[8,64,704]{2,1,0:T(8,128)(2,1)S(1)} collective-permute-done((bf16[8,64,704]{2,1,0:T(8,128)(2,1)}, bf16[8,64,704]{2,1,0:T(8,128)(2,1)S(1)}, u32[]{:S(2)}, u32[]{:S(2)}) %collective-permute-start.9) | collective-permute-done | bytes 720928 | tf_op jit(solution)/shard_map/ppermute | solution.py:55
  190.9 16.7 %collective-permute-done.12.refs_6_ = bf16[8,64,704]{2,1,0:T(8,128)(2,1)S(1)} collective-permute-done((bf16[8,64,704]{2,1,0:T(8,128)(2,1)S(1)}, bf16[8,64,704]{2,1,0:T(8,128)(2,1)S(1)}, u32[]{:S(2)}, u32[]{:S(2)}) %collective-permute-start.12) | collective-permute-done | bytes 720928 | tf_op jit(solution)/shard_map/ppermute | solution.py:55
  209.6 5.8 shard_map.207
  215.4 25.4 %shard_map.208 = (bf16[1024,704]{1,0:T(8,128)(2,1)}, bf16[1024,704]{1,0:T(8,128)(2,1)}, bf16[1024,704]{1,0:T(8,128)(2,1)}, bf16[1024,2048]{1,0:T(8,128)(2,1)}) custom-call(bf16[1024,2048]{1,0:T(8,128)(2,1)} %all-gather.9.cloned.1.call-done.x_ref, bf16[1024,2048]{1,0:T(8,128)(2,1)} %all-gather.11.cloned.1.call-done.cot_ref, bf16[2,2048,704]{2,1,0:T(8,128)(2,1)} %bitcast.72, ...), custom_call_target="tpu_custom_call" | custom-call | tf_op jit(solution)/shard_map/pallas_call | solution.py:549
  240.9 80.4 %reduce-scatter.7.cloned.1.call-done.grad_ref = bf16[128,2048]{1,0:T(8,128)(2,1)} async-done(((bf16[1024,2048]{1,0:T(8,128)(2,1)}), bf16[128,2048]{1,0:T(8,128)(2,1)}) %reduce-scatter.7.cloned.1.call-update) | async-done | bytes 524304 | tf_op jit(solution)/shard_map/reduce_scatter | solution.py:556
  321.3 3.6 shard_map.209
  326.2 27.1 %all_to_all.37 = bf16[4,128,2048]{2,1,0:T(8,128)(2,1)S(1)} all-to-all(bf16[4,128,2048]{2,1,0:T(8,128)(2,1)S(1)} %broadcast_in_dim.21), channel_id=1, replica_groups=mesh['rep'=4,'shard'=8] {'rep'}, dimensions={0} | all-to-all | bytes 4194304 | tf_op jit(solution)/shard_map/all_to_all | solution.py:43
  354.7 10.2 %all_to_all.38 = bf16[4,512,128]{2,1,0:T(8,128)(2,1)} all-to-all(bf16[4,512,128]{2,1,0:T(8,128)(2,1)S(1)} %bitcast_bitcast_fusion), channel_id=1, replica_groups=mesh['rep'=4,'shard'=8] {'rep'}, dimensions={0} | all-to-all | bytes 1048576 | tf_op jit(solution)/shard_map/all_to_all | solution.py:47
  364.9 8.2 %shard_map.210 = (bf16[4,128,512]{2,1,0:T(8,128)(2,1)}, f32[4,192,128]{2,1,0:T(8,128)}) custom-call(bf16[4,4,128,128]{3,2,1,0:T(8,128)(2,1)} %bitcast.81, f32[4,8,128,192]{3,2,1,0:T(8,128)} %get-tuple-element.76.probs_ref, bf16[4,128,512]{2,1,0:T(8,128)(2,1)} %get-tuple-element.54.q_ref, bf16[4,128,128]{2,1,0:T(8,128)(2,1)} %get-tuple-element.55.own_ref, ...), custom_call_target="tpu_custom_call" | custom-call | tf_op jit(solution)/shard_map/pallas_call | solution.py:620
  374.1 11.7 %collective-permute-start.14 = (f32[4,64,128]{2,1,0:T(8,128)S(1)}, f32[4,64,128]{2,1,0:T(8,128)S(1)}, u32[]{:S(2)}, u32[]{:S(2)}) collective-permute-start(f32[4,64,128]{2,1,0:T(8,128)S(1)} %slice.43), channel_id=1, source_target_pairs={{1,0},{2,1},{3,2},{4,3},{5,4},{6,5},{7,6},{9,8},{10,9},{11,10},{12... | collective-permute-start | bytes 393224 | tf_op jit(solution)/shard_map/ppermute | solution.py:635
  386.5 13.0 %shard_map.211 = (bf16[4,128,2048]{2,1,0:T(8,128)(2,1)}, bf16[2048,768]{1,0:T(8,128)(2,1)}) custom-call(bf16[4,128,512]{2,1,0:T(8,128)(2,1)} %get-tuple-element.77.dq_ref, f32[4,192,128]{2,1,0:T(8,128)} %get-tuple-element.78.dkv_ref, f32[4,64,128]{2,1,0:T(8,128)} %copy-done.42, f32[4,128,128]{2,1,0:T(8,128)} %get-tuple-element.130.cos_ref, ...), custom_call_target="tpu_custom_call" | custom-call | tf_op jit(solution)/shard_map/pallas_call | solution.py:639
  399.6 4.4 convolution_convert_fusion.4
  404.0 6.4 convolution_convert_fusion
  411.9 7.0 %convolution_convert_fusion.3 = bf16[2048,704]{0,1:T(8,128)(2,1)} fusion(bf16[1024,2048]{1,0:T(8,128)(2,1)} %all-gather.9.cloned.1.call-done.x_ref, bf16[1024,704]{1,0:T(8,128)(2,1)S(1)} %copy-done.49), kind=kOutput, calls=%fused_computation.3 | convolution fusion | flops 2954231808 | bytes 8519680 | tf_op jit(solution)/shard_map/dot_general | solution.py:26
  425.7 6.0 convolution_convert_fusion.2
  431.6 4.6 copy.39
  441.3 4.8 convolution_convert_fusion.1
  448.1 12.9 %collective-permute-done.22 = bf16[8,64,704]{2,1,0:T(8,128)(2,1)} collective-permute-done((bf16[8,64,704]{2,1,0:T(8,128)(2,1)}, bf16[8,64,704]{2,1,0:T(8,128)(2,1)}, u32[]{:S(2)}, u32[]{:S(2)}) %collective-permute-start.22) | collective-permute-done | bytes 720928 | tf_op jit(solution)/shard_map/ppermute | solution.py:55
  464.2 12.6 %collective-permute-done.25 = bf16[8,64,704]{2,1,0:T(8,128)(2,1)S(1)} collective-permute-done((bf16[8,64,704]{2,1,0:T(8,128)(2,1)S(1)}, bf16[8,64,704]{2,1,0:T(8,128)(2,1)S(1)}, u32[]{:S(2)}, u32[]{:S(2)}) %collective-permute-start.25) | collective-permute-done | bytes 720928 | tf_op jit(solution)/shard_map/ppermute | solution.py:55
  480.3 3.5 collective-permute-done.44
  489.4 11.3 %collective-permute-done.23.refs_2_ = bf16[8,64,704]{2,1,0:T(8,128)(2,1)S(1)} collective-permute-done((bf16[8,64,704]{2,1,0:T(8,128)(2,1)}, bf16[8,64,704]{2,1,0:T(8,128)(2,1)S(1)}, u32[]{:S(2)}, u32[]{:S(2)}) %collective-permute-start.23) | collective-permute-done | bytes 720928 | tf_op jit(solution)/shard_map/ppermute | solution.py:55
  501.8 3.9 shard_map.214
  505.7 4.1 collective-permute-start.28
  509.8 3.8 all-to-all-start.5
  520.1 5.8 collective-permute-done.28.refs_2_
  525.9 11.1 %collective-permute-done.29.refs_3_ = bf16[2,64,704]{2,1,0:T(8,128)(2,1)S(1)} collective-permute-done((bf16[2,64,704]{2,1,0:T(8,128)(2,1)}, bf16[2,64,704]{2,1,0:T(8,128)(2,1)S(1)}, u32[]{:S(2)}, u32[]{:S(2)}) %collective-permute-start.29) | collective-permute-done | bytes 180256 | tf_op jit(solution)/shard_map/ppermute | solution.py:55
  541.8 12.7 %collective-permute-done.31.refs_5_ = bf16[2,64,704]{2,1,0:T(8,128)(2,1)S(1)} collective-permute-done((bf16[2,64,704]{2,1,0:T(8,128)(2,1)}, bf16[2,64,704]{2,1,0:T(8,128)(2,1)S(1)}, u32[]{:S(2)}, u32[]{:S(2)}) %collective-permute-start.31) | collective-permute-done | bytes 180256 | tf_op jit(solution)/shard_map/ppermute | solution.py:55
  565.0 21.5 %collective-permute-done.49.refs_5_ = bf16[80,2048]{1,0:T(8,128)(2,1)} collective-permute-done((bf16[80,2048]{1,0:T(8,128)(2,1)S(1)}, bf16[80,2048]{1,0:T(8,128)(2,1)}, u32[]{:S(2)}, u32[]{:S(2)}) %collective-permute-start.49) | collective-permute-done | bytes 327712 | tf_op jit(solution)/shard_map/ppermute | solution.py:55
  590.9 3.9 collective-permute-done.48.refs_4_
  600.6 3.6 all-to-all-start.6
  607.2 42.3 %collective-permute-done.50.refs_6_ = bf16[96,2048]{1,0:T(8,128)(2,1)S(1)} collective-permute-done((bf16[96,2048]{1,0:T(8,128)(2,1)}, bf16[96,2048]{1,0:T(8,128)(2,1)S(1)}, u32[]{:S(2)}, u32[]{:S(2)}) %collective-permute-start.50) | collective-permute-done | bytes 393248 | tf_op jit(solution)/shard_map/ppermute | solution.py:55
  650.8 4.6 shard_map.218
  655.4 4.7 shard_map.216
  660.1 4.8 shard_map.217
  670.9 3.7 shard_map.212
  (269 shorter events, 128.7 us)
Async XLA Ops:
  7.2 40.8 %all-gather.5.cloned.1.call-start = ((), (), s32[]{:S(2)}) async-start(), calls=%async_computation.11 | async-start | bytes 2949120 | tf_op jit(solution)/shard_map/all_gather | solution.py:472
  10.3 67.1 %all-gather.7.cloned.1.call-start = ((), (), s32[]{:S(2)}) async-start(), calls=%async_computation.12 | async-start | bytes 2359296 | tf_op jit(solution)/shard_map/all_gather | solution.py:473
  12.0 203.4 %all-gather.11.cloned.1.call-start = ((), (), s32[]{:S(2)}) async-start(), calls=%async_computation.14 | async-start | bytes 4718592 | tf_op jit(solution)/shard_map/all_gather | solution.py:498
  14.8 31.6 %all-to-all-start = ((bf16[4,128,2176]{2,1,0:T(8,128)(2,1)}), bf16[4,128,2176]{2,1,0:T(8,128)(2,1)S(1)}, u32[]{:S(2)}, u32[]{:S(2)}) async-start(bf16[4,128,2176]{2,1,0:T(8,128)(2,1)} %broadcast_in_dim.20), calls=%async_computation | async-start | bytes 4456448 | tf_op jit(solution)/shard_map/all_to_all | solution.py:43
  20.1 195.3 %all-gather.9.cloned.1.call-start = ((), (), s32[]{:S(2)}) async-start(), calls=%async_computation.13 | async-start | bytes 4718592 | tf_op jit(solution)/shard_map/all_gather | solution.py:544
  113.5 207.8 %reduce-scatter.7.cloned.1.call-start = ((), (), s32[]{:S(2)}) async-start(), calls=%async_computation.16 | async-start | bytes 4718592 | tf_op jit(solution)/shard_map/reduce_scatter | solution.py:556
  118.0 18.0 %collective-permute-start.2 = (bf16[2,64,704]{2,1,0:T(8,128)(2,1)}, bf16[2,64,704]{2,1,0:T(8,128)(2,1)S(1)}, u32[]{:S(2)}, u32[]{:S(2)}) collective-permute-start(bf16[2,64,704]{2,1,0:T(8,128)(2,1)} %get-tuple-element.63), channel_id=1, source_target_pairs={{0,2},{1,3},{2,0},{3,1},{4,6},{5,7},{6,4},{7,5},{8,10},{9,11},{10,... | collective-permute-start | bytes 540680 | tf_op jit(solution)/shard_map/ppermute | solution.py:55
  123.5 28.9 %collective-permute-start.5 = (bf16[2,64,704]{2,1,0:T(8,128)(2,1)}, bf16[2,64,704]{2,1,0:T(8,128)(2,1)S(1)}, u32[]{:S(2)}, u32[]{:S(2)}) collective-permute-start(bf16[2,64,704]{2,1,0:T(8,128)(2,1)} %get-tuple-element.66), channel_id=1, source_target_pairs={{0,5},{1,4},{2,7},{3,6},{4,1},{5,0},{6,3},{7,2},{8,13},{9,12},{10,... | collective-permute-start | bytes 540680 | tf_op jit(solution)/shard_map/ppermute | solution.py:55
  124.9 27.5 %collective-permute-start.6 = (bf16[2,64,704]{2,1,0:T(8,128)(2,1)}, bf16[2,64,704]{2,1,0:T(8,128)(2,1)S(1)}, u32[]{:S(2)}, u32[]{:S(2)}) collective-permute-start(bf16[2,64,704]{2,1,0:T(8,128)(2,1)} %get-tuple-element.67), channel_id=1, source_target_pairs={{0,6},{1,7},{2,4},{3,5},{4,2},{5,3},{6,0},{7,1},{8,14},{9,15},{10,... | collective-permute-start | bytes 540680 | tf_op jit(solution)/shard_map/ppermute | solution.py:55
  136.0 17.7 %collective-permute-start.7 = (bf16[2,64,704]{2,1,0:T(8,128)(2,1)}, bf16[2,64,704]{2,1,0:T(8,128)(2,1)S(1)}, u32[]{:S(2)}, u32[]{:S(2)}) collective-permute-start(bf16[2,64,704]{2,1,0:T(8,128)(2,1)} %get-tuple-element.68), channel_id=1, source_target_pairs={{0,7},{1,6},{2,5},{3,4},{4,3},{5,2},{6,1},{7,0},{8,15},{9,14},{10,... | collective-permute-start | bytes 540680 | tf_op jit(solution)/shard_map/ppermute | solution.py:55
  158.9 31.1 %collective-permute-start.9 = (bf16[8,64,704]{2,1,0:T(8,128)(2,1)}, bf16[8,64,704]{2,1,0:T(8,128)(2,1)S(1)}, u32[]{:S(2)}, u32[]{:S(2)}) collective-permute-start(bf16[8,64,704]{2,1,0:T(8,128)(2,1)} %get-tuple-element.70.refs_1_), channel_id=1, source_target_pairs={{0,8},{8,0},{16,24},{24,16},{1,9},{9,1},{17,25},{25,17},{2,10},{10... | collective-permute-start | bytes 2162696 | tf_op jit(solution)/shard_map/ppermute | solution.py:55
  159.5 31.4 %collective-permute-start.10 = (bf16[8,64,704]{2,1,0:T(8,128)(2,1)}, bf16[8,64,704]{2,1,0:T(8,128)(2,1)S(1)}, u32[]{:S(2)}, u32[]{:S(2)}) collective-permute-start(bf16[8,64,704]{2,1,0:T(8,128)(2,1)} %get-tuple-element.69.refs_0_), channel_id=1, source_target_pairs={{0,16},{8,24},{16,0},{24,8},{1,17},{9,25},{17,1},{25,9},{2,18},{10... | collective-permute-start | bytes 2162696 | tf_op jit(solution)/shard_map/ppermute | solution.py:55
  173.1 34.5 %collective-permute-start.12 = (bf16[8,64,704]{2,1,0:T(8,128)(2,1)S(1)}, bf16[8,64,704]{2,1,0:T(8,128)(2,1)S(1)}, u32[]{:S(2)}, u32[]{:S(2)}) collective-permute-start(bf16[8,64,704]{2,1,0:T(8,128)(2,1)S(1)} %collective-permute-done.8.refs_2_), channel_id=1, source_target_pairs={{0,16},{8,24},{16,0},{24,8},{1,17},{9,25},{17,1},{25,9},{2,18},{10... | collective-permute-start | bytes 2162696 | tf_op jit(solution)/shard_map/ppermute | solution.py:55
  174.0 33.6 %collective-permute-start.13 = (bf16[8,64,704]{2,1,0:T(8,128)(2,1)S(1)}, bf16[8,64,704]{2,1,0:T(8,128)(2,1)S(1)}, u32[]{:S(2)}, u32[]{:S(2)}) collective-permute-start(bf16[8,64,704]{2,1,0:T(8,128)(2,1)S(1)} %collective-permute-done.11.refs_5_), channel_id=1, source_target_pairs={{0,8},{8,0},{16,24},{24,16},{1,9},{9,1},{17,25},{25,17},{2,10},{10... | collective-permute-start | bytes 2162696 | tf_op jit(solution)/shard_map/ppermute | solution.py:55
  240.9 356.7 %reduce-scatter.9.cloned.1.call-start = ((), (), s32[]{:S(2)}) async-start(), calls=%async_computation.17 | async-start | bytes 3538944 | tf_op jit(solution)/shard_map/reduce_scatter | solution.py:659
  399.5 206.6 %reduce-scatter.11.cloned.1.call-start = ((), (), s32[]{:S(2)}) async-start(), calls=%async_computation.18 | async-start | bytes 2359296 | tf_op jit(solution)/shard_map/reduce_scatter | solution.py:617
  404.0 264.9 %reduce-scatter.5.cloned.1.call-start = ((), (), s32[]{:S(2)}) async-start(), calls=%async_computation.15 | async-start | bytes 4718592 | tf_op jit(solution)/shard_map/reduce_scatter | solution.py:559
  423.6 61.8 %collective-permute-start.21 = (bf16[8,64,704]{2,1,0:T(8,128)(2,1)}, bf16[8,64,704]{2,1,0:T(8,128)(2,1)}, u32[]{:S(2)}, u32[]{:S(2)}) collective-permute-start(bf16[8,64,704]{2,1,0:T(8,128)(2,1)} %get-tuple-element.123), channel_id=1, source_target_pairs={{0,8},{8,0},{16,24},{24,16},{1,9},{9,1},{17,25},{25,17},{2,10},{10... | collective-permute-start | bytes 2162696 | tf_op jit(solution)/shard_map/ppermute | solution.py:55
  424.5 36.5 %collective-permute-start.22 = (bf16[8,64,704]{2,1,0:T(8,128)(2,1)}, bf16[8,64,704]{2,1,0:T(8,128)(2,1)}, u32[]{:S(2)}, u32[]{:S(2)}) collective-permute-start(bf16[8,64,704]{2,1,0:T(8,128)(2,1)} %get-tuple-element.122), channel_id=1, source_target_pairs={{0,8},{8,0},{16,24},{24,16},{1,9},{9,1},{17,25},{25,17},{2,10},{10... | collective-permute-start | bytes 2162696 | tf_op jit(solution)/shard_map/ppermute | solution.py:55
  439.3 48.4 %collective-permute-start.24 = (bf16[8,64,704]{2,1,0:T(8,128)(2,1)}, bf16[8,64,704]{2,1,0:T(8,128)(2,1)}, u32[]{:S(2)}, u32[]{:S(2)}) collective-permute-start(bf16[8,64,704]{2,1,0:T(8,128)(2,1)} %get-tuple-element.120), channel_id=1, source_target_pairs={{0,16},{8,24},{16,0},{24,8},{1,17},{9,25},{17,1},{25,9},{2,18},{10... | collective-permute-start | bytes 2162696 | tf_op jit(solution)/shard_map/ppermute | solution.py:55
  440.3 36.5 %collective-permute-start.25 = (bf16[8,64,704]{2,1,0:T(8,128)(2,1)S(1)}, bf16[8,64,704]{2,1,0:T(8,128)(2,1)S(1)}, u32[]{:S(2)}, u32[]{:S(2)}) collective-permute-start(bf16[8,64,704]{2,1,0:T(8,128)(2,1)S(1)} %get-tuple-element.119), channel_id=1, source_target_pairs={{0,16},{8,24},{16,0},{24,8},{1,17},{9,25},{17,1},{25,9},{2,18},{10... | collective-permute-start | bytes 2162696 | tf_op jit(solution)/shard_map/ppermute | solution.py:55
  447.2 36.6 %collective-permute-start.44 = (bf16[80,2048]{1,0:T(8,128)(2,1)}, bf16[80,2048]{1,0:T(8,128)(2,1)S(1)}, u32[]{:S(2)}, u32[]{:S(2)}) collective-permute-start(bf16[80,2048]{1,0:T(8,128)(2,1)} %get-tuple-element.126), channel_id=1, source_target_pairs={{0,16},{8,24},{16,0},{24,8},{1,17},{9,25},{17,1},{25,9},{2,18},{10... | collective-permute-start | bytes 983048 | tf_op jit(solution)/shard_map/ppermute | solution.py:55
  463.2 37.4 %collective-permute-start.23 = (bf16[8,64,704]{2,1,0:T(8,128)(2,1)}, bf16[8,64,704]{2,1,0:T(8,128)(2,1)S(1)}, u32[]{:S(2)}, u32[]{:S(2)}) collective-permute-start(bf16[8,64,704]{2,1,0:T(8,128)(2,1)} %fusion.1), channel_id=1, source_target_pairs={{0,16},{8,24},{16,0},{24,8},{1,17},{9,25},{17,1},{25,9},{2,18},{10... | collective-permute-start | bytes 2162696 | tf_op jit(solution)/shard_map/ppermute | solution.py:55
  478.1 22.5 %collective-permute-start.26 = (bf16[8,64,704]{2,1,0:T(8,128)(2,1)S(1)}, bf16[8,64,704]{2,1,0:T(8,128)(2,1)S(1)}, u32[]{:S(2)}, u32[]{:S(2)}) collective-permute-start(bf16[8,64,704]{2,1,0:T(8,128)(2,1)S(1)} %fusion), channel_id=1, source_target_pairs={{0,8},{8,0},{16,24},{24,16},{1,9},{9,1},{17,25},{25,17},{2,10},{10... | collective-permute-start | bytes 2162696 | tf_op jit(solution)/shard_map/ppermute | solution.py:55
  484.5 29.2 %collective-permute-start.41 = (bf16[96,2048]{1,0:T(8,128)(2,1)S(1)}, bf16[96,2048]{1,0:T(8,128)(2,1)S(1)}, u32[]{:S(2)}, u32[]{:S(2)}) collective-permute-start(bf16[96,2048]{1,0:T(8,128)(2,1)S(1)} %get-tuple-element.128), channel_id=1, source_target_pairs={{0,8},{8,0},{16,24},{24,16},{1,9},{9,1},{17,25},{25,17},{2,10},{10... | collective-permute-start | bytes 1179656 | tf_op jit(solution)/shard_map/ppermute | solution.py:55
  485.5 28.1 %collective-permute-start.43 = (bf16[80,2048]{1,0:T(8,128)(2,1)}, bf16[80,2048]{1,0:T(8,128)(2,1)}, u32[]{:S(2)}, u32[]{:S(2)}) collective-permute-start(bf16[80,2048]{1,0:T(8,128)(2,1)} %get-tuple-element.125), channel_id=1, source_target_pairs={{0,16},{8,24},{16,0},{24,8},{1,17},{9,25},{17,1},{25,9},{2,18},{10... | collective-permute-start | bytes 983048 | tf_op jit(solution)/shard_map/ppermute | solution.py:55
  487.7 29.4 %collective-permute-start.45 = (bf16[80,2048]{1,0:T(8,128)(2,1)}, bf16[80,2048]{1,0:T(8,128)(2,1)}, u32[]{:S(2)}, u32[]{:S(2)}) collective-permute-start(bf16[80,2048]{1,0:T(8,128)(2,1)} %add_convert_fusion.4), channel_id=1, source_target_pairs={{0,8},{8,0},{16,24},{24,16},{1,9},{9,1},{17,25},{25,17},{2,10},{10... | collective-permute-start | bytes 983048 | tf_op jit(solution)/shard_map/ppermute | solution.py:55
  505.7 20.2 %collective-permute-start.28 = (bf16[2,64,704]{2,1,0:T(8,128)(2,1)}, bf16[2,64,704]{2,1,0:T(8,128)(2,1)}, u32[]{:S(2)}, u32[]{:S(2)}) collective-permute-start(bf16[2,64,704]{2,1,0:T(8,128)(2,1)} %get-tuple-element.89), channel_id=1, source_target_pairs={{0,2},{1,3},{2,0},{3,1},{4,6},{5,7},{6,4},{7,5},{8,10},{9,11},{10,... | collective-permute-start | bytes 540680 | tf_op jit(solution)/shard_map/ppermute | solution.py:55
  509.8 88.9 %all-to-all-start.5 = ((bf16[4,128,2048]{2,1,0:T(8,128)(2,1)}), bf16[4,128,2048]{2,1,0:T(8,128)(2,1)S(1)}, u32[]{:S(2)}, u32[]{:S(2)}) async-start(bf16[4,128,2048]{2,1,0:T(8,128)(2,1)} %get-tuple-element.81), calls=%async_computation.7 | async-start | bytes 4194304 | tf_op jit(solution)/shard_map/all_to_all | solution.py:47
  513.6 23.3 %collective-permute-start.29 = (bf16[2,64,704]{2,1,0:T(8,128)(2,1)}, bf16[2,64,704]{2,1,0:T(8,128)(2,1)S(1)}, u32[]{:S(2)}, u32[]{:S(2)}) collective-permute-start(bf16[2,64,704]{2,1,0:T(8,128)(2,1)} %get-tuple-element.90), channel_id=1, source_target_pairs={{0,3},{1,2},{2,1},{3,0},{4,7},{5,6},{6,5},{7,4},{8,11},{9,10},{10,... | collective-permute-start | bytes 540680 | tf_op jit(solution)/shard_map/ppermute | solution.py:55
  513.7 24.8 %collective-permute-start.30 = (bf16[2,64,704]{2,1,0:T(8,128)(2,1)}, bf16[2,64,704]{2,1,0:T(8,128)(2,1)S(1)}, u32[]{:S(2)}, u32[]{:S(2)}) collective-permute-start(bf16[2,64,704]{2,1,0:T(8,128)(2,1)} %get-tuple-element.91), channel_id=1, source_target_pairs={{0,4},{1,5},{2,6},{3,7},{4,0},{5,1},{6,2},{7,3},{8,12},{9,13},{10,... | collective-permute-start | bytes 540680 | tf_op jit(solution)/shard_map/ppermute | solution.py:55
  517.1 43.4 %collective-permute-start.40 = (bf16[96,2048]{1,0:T(8,128)(2,1)S(1)}, bf16[96,2048]{1,0:T(8,128)(2,1)S(1)}, u32[]{:S(2)}, u32[]{:S(2)}) collective-permute-start(bf16[96,2048]{1,0:T(8,128)(2,1)S(1)} %get-tuple-element.127), channel_id=1, source_target_pairs={{0,8},{8,0},{16,24},{24,16},{1,9},{9,1},{17,25},{25,17},{2,10},{10... | collective-permute-start | bytes 1179656 | tf_op jit(solution)/shard_map/ppermute | solution.py:55
  518.6 41.9 %collective-permute-start.42 = (bf16[96,2048]{1,0:T(8,128)(2,1)S(1)}, bf16[96,2048]{1,0:T(8,128)(2,1)S(1)}, u32[]{:S(2)}, u32[]{:S(2)}) collective-permute-start(bf16[96,2048]{1,0:T(8,128)(2,1)S(1)} %add_convert_fusion.2), channel_id=1, source_target_pairs={{0,16},{8,24},{16,0},{24,8},{1,17},{9,25},{17,1},{25,9},{2,18},{10... | collective-permute-start | bytes 1179656 | tf_op jit(solution)/shard_map/ppermute | solution.py:55
  525.9 28.5 %collective-permute-start.31 = (bf16[2,64,704]{2,1,0:T(8,128)(2,1)}, bf16[2,64,704]{2,1,0:T(8,128)(2,1)S(1)}, u32[]{:S(2)}, u32[]{:S(2)}) collective-permute-start(bf16[2,64,704]{2,1,0:T(8,128)(2,1)} %get-tuple-element.92), channel_id=1, source_target_pairs={{0,5},{1,4},{2,7},{3,6},{4,1},{5,0},{6,3},{7,2},{8,13},{9,12},{10,... | collective-permute-start | bytes 540680 | tf_op jit(solution)/shard_map/ppermute | solution.py:55
  558.1 30.7 %collective-permute-start.34 = (bf16[64,5632]{1,0:T(8,128)(2,1)}, bf16[64,5632]{1,0:T(8,128)(2,1)}, u32[]{:S(2)}, u32[]{:S(2)}) collective-permute-start(bf16[64,5632]{1,0:T(8,128)(2,1)} %get-tuple-element.95.refs_0_), channel_id=1, source_target_pairs={{0,8},{8,0},{16,24},{24,16},{1,9},{9,1},{17,25},{25,17},{2,10},{10... | collective-permute-start | bytes 2162696 | tf_op jit(solution)/shard_map/ppermute | solution.py:55
  560.1 35.5 %collective-permute-start.38 = (bf16[64,5632]{1,0:T(8,128)(2,1)}, bf16[64,5632]{1,0:T(8,128)(2,1)}, u32[]{:S(2)}, u32[]{:S(2)}) collective-permute-start(bf16[64,5632]{1,0:T(8,128)(2,1)} %get-tuple-element.96.refs_0_), channel_id=1, source_target_pairs={{0,16},{8,24},{16,0},{24,8},{1,17},{9,25},{17,1},{25,9},{2,18},{10... | collective-permute-start | bytes 2162696 | tf_op jit(solution)/shard_map/ppermute | solution.py:55
  561.6 27.2 %collective-permute-start.46 = (bf16[96,2048]{1,0:T(8,128)(2,1)S(1)}, bf16[96,2048]{1,0:T(8,128)(2,1)S(1)}, u32[]{:S(2)}, u32[]{:S(2)}) collective-permute-start(bf16[96,2048]{1,0:T(8,128)(2,1)S(1)} %add_convert_fusion.1.refs_0_), channel_id=1, source_target_pairs={{0,8},{8,0},{16,24},{24,16},{1,9},{9,1},{17,25},{25,17},{2,10},{10... | collective-permute-start | bytes 1179656 | tf_op jit(solution)/shard_map/ppermute | solution.py:55
  562.3 24.2 %collective-permute-start.49 = (bf16[80,2048]{1,0:T(8,128)(2,1)S(1)}, bf16[80,2048]{1,0:T(8,128)(2,1)}, u32[]{:S(2)}, u32[]{:S(2)}) collective-permute-start(bf16[80,2048]{1,0:T(8,128)(2,1)S(1)} %add_convert_fusion.3.refs_1_), channel_id=1, source_target_pairs={{0,16},{8,24},{16,0},{24,8},{1,17},{9,25},{17,1},{25,9},{2,18},{10... | collective-permute-start | bytes 983048 | tf_op jit(solution)/shard_map/ppermute | solution.py:55
  565.0 29.8 %collective-permute-start.48 = (bf16[96,2048]{1,0:T(8,128)(2,1)S(1)}, bf16[96,2048]{1,0:T(8,128)(2,1)S(1)}, u32[]{:S(2)}, u32[]{:S(2)}) collective-permute-start(bf16[96,2048]{1,0:T(8,128)(2,1)S(1)} %add_convert_fusion.1.refs_0_), channel_id=1, source_target_pairs={{0,16},{8,24},{16,0},{24,8},{1,17},{9,25},{17,1},{25,9},{2,18},{10... | collective-permute-start | bytes 1179656 | tf_op jit(solution)/shard_map/ppermute | solution.py:55
  586.5 17.7 %collective-permute-start.51 = (bf16[80,2048]{1,0:T(8,128)(2,1)}, bf16[80,2048]{1,0:T(8,128)(2,1)}, u32[]{:S(2)}, u32[]{:S(2)}) collective-permute-start(bf16[80,2048]{1,0:T(8,128)(2,1)} %collective-permute-done.49.refs_5_), channel_id=1, source_target_pairs={{0,8},{8,0},{16,24},{24,16},{1,9},{9,1},{17,25},{25,17},{2,10},{10... | collective-permute-start | bytes 983048 | tf_op jit(solution)/shard_map/ppermute | solution.py:55
  588.9 60.9 %collective-permute-start.35 = (bf16[64,5632]{1,0:T(8,128)(2,1)}, bf16[64,5632]{1,0:T(8,128)(2,1)}, u32[]{:S(2)}, u32[]{:S(2)}) collective-permute-start(bf16[64,5632]{1,0:T(8,128)(2,1)} %get-tuple-element.95.refs_0_), channel_id=1, source_target_pairs={{0,16},{8,24},{16,0},{24,8},{1,17},{9,25},{17,1},{25,9},{2,18},{10... | collective-permute-start | bytes 2162696 | tf_op jit(solution)/shard_map/ppermute | solution.py:55
  588.9 66.5 %collective-permute-start.36 = (bf16[64,5632]{1,0:T(8,128)(2,1)}, bf16[64,5632]{1,0:T(8,128)(2,1)}, u32[]{:S(2)}, u32[]{:S(2)}) collective-permute-start(bf16[64,5632]{1,0:T(8,128)(2,1)} %collective-permute-done.34.refs_1_), channel_id=1, source_target_pairs={{0,16},{8,24},{16,0},{24,8},{1,17},{9,25},{17,1},{25,9},{2,18},{10... | collective-permute-start | bytes 2162696 | tf_op jit(solution)/shard_map/ppermute | solution.py:55
  595.5 64.5 %collective-permute-start.37 = (bf16[64,5632]{1,0:T(8,128)(2,1)}, bf16[64,5632]{1,0:T(8,128)(2,1)}, u32[]{:S(2)}, u32[]{:S(2)}) collective-permute-start(bf16[64,5632]{1,0:T(8,128)(2,1)} %get-tuple-element.96.refs_0_), channel_id=1, source_target_pairs={{0,8},{8,0},{16,24},{24,16},{1,9},{9,1},{17,25},{25,17},{2,10},{10... | collective-permute-start | bytes 2162696 | tf_op jit(solution)/shard_map/ppermute | solution.py:55
  595.6 64.5 %collective-permute-start.39 = (bf16[64,5632]{1,0:T(8,128)(2,1)}, bf16[64,5632]{1,0:T(8,128)(2,1)}, u32[]{:S(2)}, u32[]{:S(2)}) collective-permute-start(bf16[64,5632]{1,0:T(8,128)(2,1)} %collective-permute-done.38.refs_2_), channel_id=1, source_target_pairs={{0,8},{8,0},{16,24},{24,16},{1,9},{9,1},{17,25},{25,17},{2,10},{10... | collective-permute-start | bytes 2162696 | tf_op jit(solution)/shard_map/ppermute | solution.py:55
  600.6 77.8 %all-to-all-start.6 = ((bf16[4,256,768]{1,2,0:T(8,128)(2,1)}), bf16[4,256,768]{1,2,0:T(8,128)(2,1)S(1)}, u32[]{:S(2)}, u32[]{:S(2)}) async-start(bf16[4,256,768]{1,2,0:T(8,128)(2,1)} %broadcast_in_dim.22), calls=%async_computation.9 | async-start | bytes 3145728 | tf_op jit(solution)/shard_map/all_to_all | solution.py:43
  604.2 45.3 %collective-permute-start.50 = (bf16[96,2048]{1,0:T(8,128)(2,1)}, bf16[96,2048]{1,0:T(8,128)(2,1)S(1)}, u32[]{:S(2)}, u32[]{:S(2)}) collective-permute-start(bf16[96,2048]{1,0:T(8,128)(2,1)} %copy-done.23), channel_id=1, source_target_pairs={{0,16},{8,24},{16,0},{24,8},{1,17},{9,25},{17,1},{25,9},{2,18},{10... | collective-permute-start | bytes 1179656 | tf_op jit(solution)/shard_map/ppermute | solution.py:55
  649.5 18.1 %collective-permute-start.15 = (bf16[32,2048]{1,0:T(8,128)(2,1)S(1)}, bf16[32,2048]{1,0:T(8,128)(2,1)S(1)}, u32[]{:S(2)}, u32[]{:S(2)}) collective-permute-start(bf16[32,2048]{1,0:T(8,128)(2,1)S(1)} %get-tuple-element.134.refs_0_), channel_id=1, source_target_pairs={{0,8},{8,0},{16,24},{24,16},{1,9},{9,1},{17,25},{25,17},{2,10},{10... | collective-permute-start | bytes 393224 | tf_op jit(solution)/shard_map/ppermute | solution.py:55
  649.8 18.5 %collective-permute-start.18 = (bf16[32,2048]{1,0:T(8,128)(2,1)S(1)}, bf16[32,2048]{1,0:T(8,128)(2,1)S(1)}, u32[]{:S(2)}, u32[]{:S(2)}) collective-permute-start(bf16[32,2048]{1,0:T(8,128)(2,1)S(1)} %get-tuple-element.133.refs_1_), channel_id=1, source_target_pairs={{0,16},{8,24},{16,0},{24,8},{1,17},{9,25},{17,1},{25,9},{2,18},{10... | collective-permute-start | bytes 393224 | tf_op jit(solution)/shard_map/ppermute | solution.py:55
  (68 other events, 819.9 us)
Sparse Core Ops, SparseCore 0:
  10.4 36.4 all-gather.4
  49.1 28.2 all-gather.6
  79.0 47.0 all-gather.10
  128.1 67.2 all-gather.8
  241.0 80.3 reduce-scatter.6
  399.7 41.2 reduce-scatter.8
  443.2 35.3 reduce-scatter.10
  481.0 63.6 reduce-scatter.4

commit v2 on v1

--- a/solution.py
+++ b/solution.py
@@ -198,6 +198,64 @@
     for h, ref in enumerate((gate_ref, up_ref)):
         for at in range(len(pieces)):
             ref[:, at * hidden : (at + 1) * hidden] = both[at, h]
+
+
+def qkv_kernel(share, id_ref, *refs):
+    pieces = refs[:-6]
+    q_ref, k_ref, v_ref, gain_ref, k_all, v_all = refs[-6:]
+    count = k_all.shape[0]
+    q_cols = q_ref.shape[1] // count
+    row = 0
+    for h in range(2):
+        rows = slice(row, row + pieces[h].shape[0])
+        total = 0.0
+        for k in range(count):
+            at = jnp.bitwise_xor(id_ref[0], k)
+            value = pieces[2 * k + h][...].astype(F32)
+            q_ref[rows, pl.ds(pl.multiple_of(at * q_cols, LANES), q_cols)] = value[:, :q_cols]
+            k_all[at, rows] = value[:, q_cols : q_cols + HD]
+            v_all[at, rows] = value[:, q_cols + HD : q_cols + 2 * HD]
+            total += value[:, q_cols + 2 * HD :]
+        gain_ref[rows] = total
+        row = rows.stop
+    for ref, both in ((k_ref, k_all), (v_ref, v_all)):
+        for head in range(count // share):
+            total = both[head * share]
+            for other in range(head * share + 1, (head + 1) * share):
+                total += both[other]
+            ref[:, head * HD : (head + 1) * HD] = total
+
+
+def pair_grad_kernel(fine, id_ref, x_ref, grad_ref, *refs):
+    outs, total_ref = refs[:-1], refs[-1]
+    total_ref[...] = rows_rows(x_ref[...], grad_ref[...])
+    own = fine * len(outs)
+    for k, out in enumerate(outs):
+        row = jnp.bitwise_xor(id_ref[0], k) * fine
+        for block in range(out.shape[0]):
+            at = pl.multiple_of(block * own + row, fine)
+            out[block] = total_ref[pl.ds(at, fine)].astype(BF)
+
+
+def pair_grad(ids, x, grad, fine, count, blocks):
+    width, hidden = x.shape[1], grad.shape[1]
+    tile = 2 * fine * count
+    out = (2, fine, hidden)
+    return pl.pallas_call(
+        partial(pair_grad_kernel, fine),
+        out_shape=(shape((blocks, fine, hidden), BF),) * count,
+        grid_spec=pltpu.PrefetchScalarGridSpec(
+            num_scalar_prefetch=1,
+            grid=(width // tile,),
+            in_specs=[
+                pl.BlockSpec((x.shape[0], tile), lambda g, ids: (0, g)),
+                pl.BlockSpec(grad.shape, lambda g, ids: (0, 0), pipeline_mode=pl.Buffered(1)),
+            ],
+            out_specs=(pl.BlockSpec(out, lambda g, ids: (g, 0, 0)),) * count,
+            scratch_shapes=[pltpu.VMEM((tile, hidden), F32)],
+        ),
+        compiler_params=pltpu.CompilerParams(vmem_limit_bytes=56 * 1024 * 1024),
+    )(ids, x, grad)
 
 
 def norm_scale(value):
@@ -554,19 +612,23 @@
         (hidden_block,) * 3 + (token_block,),
     )(two_all, cot_all, w_pair, down_weight)
     two_grad = lax.psum_scatter(two_grad_part, "shard", scatter_dimension=0, tiled=True)
-    mixed, two_grad_part = lax.optimization_barrier((mixed, two_grad_part))
-    down_part = rows_cols(mixed, down_weight).astype(BF)
-    down_rows = lax.psum_scatter(down_part, "shard", scatter_dimension=0, tiled=True)
-    layer_out = (x_mid + down_rows.astype(F32)).astype(BF)
-
     mid_grad, branch, gain_two_rows = call(
         middle_back_kernel,
         (shape((rows, width), F32), shape((rows, width), BF), shape((rows, width), BF)),
     )(two_grad, x_mid, gain_two, cotangent)
 
+    gate_chunks = pair_grad(ids, two_all, gate_grad, fine, n_rep, n_shard)
+    up_grad, _ = lax.optimization_barrier((up_grad, gate_chunks[0]))
+    up_chunks = pair_grad(ids, two_all, up_grad, fine, n_rep, n_shard)
+    pair_chunks = list(zip(gate_chunks, up_chunks))
+    mixed, _ = lax.optimization_barrier((mixed, up_chunks[0]))
     part_rows = hidden // n_rep
     cut = (part_rows // 2 + 15) // 16 * 16
     w_down_grad = rows_rows(mixed, cot_all).astype(BF)
+    mixed, w_down_grad = lax.optimization_barrier((mixed, w_down_grad))
+    down_part = rows_cols(mixed, down_weight).astype(BF)
+    down_rows = lax.psum_scatter(down_part, "shard", scatter_dimension=0, tiled=True)
+    layer_out = (x_mid + down_rows.astype(F32)).astype(BF)
     chunks = []
     for k in range(n_rep):
         at = (r ^ k) * part_rows
@@ -581,15 +643,7 @@
         sum(part.astype(F32) for part in parts).astype(BF) for parts in w_down_grad
     )
     down_out = place(gather_rep(w_down_grad, n_rep), r)
-    halves = [
-        rows_rows(two_all, part).astype(BF).reshape(n_shard, n_rep, fine, hidden)
-        for part in (gate_grad, up_grad)
-    ]
-    chunks = [
-        tuple(lax.dynamic_index_in_dim(half, r ^ k, 1, False) for half in halves)
-        for k in range(n_rep)
-    ]
-    w_pair_grad = parts_rep(chunks, n_rep)
+    w_pair_grad = parts_rep(pair_chunks, n_rep)
     w_pair_grad = flat_call(
         sum_kernel,
         ids,
@@ -660,18 +714,19 @@
     input_grad = call(last_kernel, shape((rows, width), BF))(
         swap(one_grad_part, "rep"), tokens, gain_one, mid_grad
     )
-    w_qkv_grad = spread(w_qkv_grad, "rep", n_rep).astype(F32)
-
-    def columns(part):
-        return part.transpose(1, 0, 2).reshape(own, -1)
-
-    def kv_columns(part):
-        return columns(jnp.sum(part.reshape(-1, share, own, HD), axis=1))
-
-    q_out = columns(w_qkv_grad[..., :q_cols])
-    k_out = kv_columns(w_qkv_grad[..., q_cols : q_cols + HD])
-    v_out = kv_columns(w_qkv_grad[..., q_cols + HD : qkv_cols])
-    gain_sums = jnp.sum(w_qkv_grad[..., qkv_cols:], axis=0)
+    w_qkv_grad = (w_qkv_grad[: own // 2], w_qkv_grad[own // 2 :])
+    q_out, k_out, v_out, gain_sums = flat_call(
+        partial(qkv_kernel, share),
+        ids,
+        (
+            shape((own, width), F32),
+            shape((own, KVH * HD), F32),
+            shape((own, KVH * HD), F32),
+            shape((own, LANES), F32),
+        ),
+        [half for piece in gather_rep(w_qkv_grad, n_rep) for half in piece],
+        [pltpu.VMEM((n_rep, own, HD), F32)] * 2,
+    )
     return (
         layer_out,
         input_grad,

time: 705 us -> 688 us (0.976)
  Pallas kernels: 106 us -> 126 us
  local copies, waits for them, and re-layouts: 43.4 us -> 24.2 us
  matrix products: 32.7 us -> 16.3 us
    ppermute x50 -> x56, starting transfers between devices: 55.6 us -> 72.7 us  [send(): return lax.ppermute(value, axis, pairs(count, step))]
    pallas_call x0 -> x2, Pallas kernels: none -> 16.8 us  [pair_grad(): pl.pallas_call(partial(pair_grad_kernel, fine), out_shape=(shape((blocks,...]
    dot_general x7 -> x5, matrix products: 32.7 us -> 16.3 us  [dot(): lax.dot_general(left, right, (contract, ((), ())), preferred_element_type...]
    ppermute x1, starting transfers between devices: 11.7 us -> 1.51 us  [body(): lax.ppermute(kv_grad[:, :HALO], 'shard', [(i + 1, i) for i in range(n_sha...]
    convert_element_type x2 -> x0, local copies, waits for them, and re-layouts: 7.74 us -> none  [body(): rows_rows(two_all, part).astype(BF).reshape(n_shard, n_rep, fine, hidden)]
    unnamed x109 -> x102, local copies, waits for them, and re-layouts: 15.6 us -> 8.91 us
    pallas_call x4 -> x5, Pallas kernels: 15.3 us -> 18.6 us  [flat_call(): pl.pallas_call(kernel, out_shape=out_shape, in_specs=specs, scratch_shape...]
    ppermute x50 -> x56, waiting for transfers between devices: 210 us -> 210 us  [send(): return lax.ppermute(value, axis, pairs(count, step))]
  transfers between devices with their start and end apart: 63 -> 68, of which waited for: 25 -> 26; matrix products, arithmetic and copies ran while one was open for 10% -> 6% of each run, Pallas kernels for 8% -> 14%
where the time goes in v2:
time: 688 us; the launch traced here: 681 us
  waiting for transfers between devices  309 us (45%)
  Pallas kernels  126 us (18%)
  blocking collectives  90.2 us (13%)
  starting transfers between devices  85.2 us (12%)
  local copies, waits for them, and re-layouts  24.2 us (4%)
  matrix products  16.3 us (2%)
  other arithmetic  15 us (2%)
  between operations  14.7 us (2%)
    ppermute x56, waiting for transfers between devices, send(): return lax.ppermute(value, axis, pairs(count, step))  210 us
    reduce_scatter x1, waiting for transfers between devices, body(): lax.psum_scatter(two_grad_part, 'shard', scatter_dimension=0, tiled=True)  80.5 us
    ppermute x56, starting transfers between devices, send(): return lax.ppermute(value, axis, pairs(count, step))  72.7 us
    all_to_all x3, blocking collectives, swap(): return lax.all_to_all(value, axis, split_axis=0, concat_axis=0, tiled=True)  50.7 us
    all_to_all x1, blocking collectives, spread(): return lax.all_to_all(wide, axis, split_axis=0, concat_axis=0, tiled=True)  27.1 us
    pallas_call x1, Pallas kernels, body(): call(forward_back_kernel, (shape((group, hidden), BF),) * 3 + (shape((gro...  25.4 us
    pallas_call x5, Pallas kernels, flat_call(): pl.pallas_call(kernel, out_shape=out_shape, in_specs=specs, scratch_shape...  18.6 us
    pallas_call x4, Pallas kernels, place(): pl.pallas_call(partial(place_kernel, count), out_shape=shape((count, rows...  17.2 us
  transfers between devices with their start and end apart: 68, of which 26 were waited for; matrix products, arithmetic and copies ran while one was open for 6% of the time, Pallas kernels for 14%

profile of v2, /device:TPU:0, one launch (start us, length us, event | category | flops | bytes accessed | tf_op | source)
XLA Modules:
  0.0 680.7 jit_solution(7681911254433033500)
XLA Ops:
  14.8 5.3 all-to-all-start
  20.1 12.3 %all_gather.15 = bf16[2,2048]{1,0:T(2,128)(2,1)S(1)} all-gather(bf16[2,256]{1,0:T(2,128)(2,1)S(1)} %pad_maximum_fusion.2), channel_id=1, replica_groups=mesh['rep'=4,'shard'=8] {'shard'}, dimensions={1}, use_global_device_ids=true | all-gather | bytes 9216 | tf_op jit(solution)/shard_map/all_gather | solution.py:535
  33.1 13.3 %all-to-all-done.x_ref.pos_ref = bf16[4,128,2176]{2,1,0:T(8,128)(2,1)S(1)} async-done(((bf16[4,128,2176]{2,1,0:T(8,128)(2,1)}), bf16[4,128,2176]{2,1,0:T(8,128)(2,1)S(1)}, u32[]{:S(2)}, u32[]{:S(2)}) %all-to-all-start) | async-done | bytes 2228256 | tf_op jit(solution)/shard_map/all_to_all | solution.py:43
  48.1 6.2 shard_map.203
  57.9 6.4 shard_map.204
  64.3 10.6 %all_to_all.30 = bf16[4,4,128,128]{3,2,1,0:T(8,128)(2,1)S(1)} all-to-all(bf16[4,4,128,128]{3,2,1,0:T(8,128)(2,1)} %get-tuple-element.71), channel_id=1, replica_groups=mesh['rep'=4,'shard'=8] {'rep'}, dimensions={0} | all-to-all | bytes 1048576 | tf_op jit(solution)/shard_map/all_to_all | solution.py:47
  77.4 2.9 convolution_convert_fusion.3
  80.3 29.9 %all_to_all.31.part_ref = bf16[4,128,2048]{2,1,0:T(8,128)(2,1)} all-to-all(bf16[4,128,2048]{2,1,0:T(8,128)(2,1)S(1)} %bitcast.41), channel_id=1, replica_groups=mesh['rep'=4,'shard'=8] {'rep'}, dimensions={0} | all-to-all | bytes 4194304 | tf_op jit(solution)/shard_map/all_to_all | solution.py:47
  110.2 3.3 shard_map.205
  114.4 3.4 split_pair.1
  117.8 4.4 collective-permute-start.2
  126.6 9.5 %collective-permute-done.2.refs_2_ = bf16[2,64,704]{2,1,0:T(8,128)(2,1)S(1)} collective-permute-done((bf16[2,64,704]{2,1,0:T(8,128)(2,1)}, bf16[2,64,704]{2,1,0:T(8,128)(2,1)S(1)}, u32[]{:S(2)}, u32[]{:S(2)}) %collective-permute-start.2) | collective-permute-done | bytes 180256 | tf_op jit(solution)/shard_map/ppermute | solution.py:55
  140.1 12.0 %collective-permute-done.5.refs_5_ = bf16[2,64,704]{2,1,0:T(8,128)(2,1)S(1)} collective-permute-done((bf16[2,64,704]{2,1,0:T(8,128)(2,1)}, bf16[2,64,704]{2,1,0:T(8,128)(2,1)S(1)}, u32[]{:S(2)}, u32[]{:S(2)}) %collective-permute-start.5) | collective-permute-done | bytes 180256 | tf_op jit(solution)/shard_map/ppermute | solution.py:55
  153.8 2.7 shard_map.206
  160.6 11.7 %collective-permute-done.8.refs_2_ = bf16[8,64,704]{2,1,0:T(8,128)(2,1)S(1)} collective-permute-done((bf16[8,64,704]{2,1,0:T(8,128)(2,1)}, bf16[8,64,704]{2,1,0:T(8,128)(2,1)S(1)}, u32[]{:S(2)}, u32[]{:S(2)}) %collective-permute-start.8) | collective-permute-done | bytes 720928 | tf_op jit(solution)/shard_map/ppermute | solution.py:55
  177.3 11.8 %collective-permute-done.9.refs_3_ = bf16[8,64,704]{2,1,0:T(8,128)(2,1)S(1)} collective-permute-done((bf16[8,64,704]{2,1,0:T(8,128)(2,1)}, bf16[8,64,704]{2,1,0:T(8,128)(2,1)S(1)}, u32[]{:S(2)}, u32[]{:S(2)}) %collective-permute-start.9) | collective-permute-done | bytes 720928 | tf_op jit(solution)/shard_map/ppermute | solution.py:55
  190.8 16.7 %collective-permute-done.12.refs_6_ = bf16[8,64,704]{2,1,0:T(8,128)(2,1)S(1)} collective-permute-done((bf16[8,64,704]{2,1,0:T(8,128)(2,1)S(1)}, bf16[8,64,704]{2,1,0:T(8,128)(2,1)S(1)}, u32[]{:S(2)}, u32[]{:S(2)}) %collective-permute-start.12) | collective-permute-done | bytes 720928 | tf_op jit(solution)/shard_map/ppermute | solution.py:55
  209.5 5.8 shard_map.207
  215.3 25.4 %shard_map.208 = (bf16[1024,704]{1,0:T(8,128)(2,1)}, bf16[1024,704]{1,0:T(8,128)(2,1)}, bf16[1024,704]{1,0:T(8,128)(2,1)}, bf16[1024,2048]{1,0:T(8,128)(2,1)}) custom-call(bf16[1024,2048]{1,0:T(8,128)(2,1)} %all-gather.9.cloned.1.call-done.x_ref, bf16[1024,2048]{1,0:T(8,128)(2,1)} %all-gather.11.cloned.1.call-done.cot_ref, bf16[2,2048,704]{2,1,0:T(8,128)(2,1)} %bitcast.33, ...), custom_call_target="tpu_custom_call" | custom-call | tf_op jit(solution)/shard_map/pallas_call | solution.py:607
  240.8 80.5 %reduce-scatter.7.cloned.1.call-done.grad_ref = bf16[128,2048]{1,0:T(8,128)(2,1)} async-done(((bf16[1024,2048]{1,0:T(8,128)(2,1)}), bf16[128,2048]{1,0:T(8,128)(2,1)}) %reduce-scatter.7.cloned.1.call-update) | async-done | bytes 524304 | tf_op jit(solution)/shard_map/reduce_scatter | solution.py:614
  321.4 3.6 shard_map.211
  326.2 27.1 %all_to_all.32 = bf16[4,128,2048]{2,1,0:T(8,128)(2,1)S(1)} all-to-all(bf16[4,128,2048]{2,1,0:T(8,128)(2,1)S(1)} %broadcast_in_dim.19), channel_id=1, replica_groups=mesh['rep'=4,'shard'=8] {'rep'}, dimensions={0} | all-to-all | bytes 4194304 | tf_op jit(solution)/shard_map/all_to_all | solution.py:43
  357.4 10.2 %all_to_all.33 = bf16[4,512,128]{2,1,0:T(8,128)(2,1)} all-to-all(bf16[4,512,128]{2,1,0:T(8,128)(2,1)S(1)} %bitcast_bitcast_fusion), channel_id=1, replica_groups=mesh['rep'=4,'shard'=8] {'rep'}, dimensions={0} | all-to-all | bytes 1048576 | tf_op jit(solution)/shard_map/all_to_all | solution.py:47
  367.6 8.3 %shard_map.212 = (bf16[4,128,512]{2,1,0:T(8,128)(2,1)}, f32[4,192,128]{2,1,0:T(8,128)}) custom-call(bf16[4,4,128,128]{3,2,1,0:T(8,128)(2,1)} %bitcast.37, f32[4,8,128,192]{3,2,1,0:T(8,128)} %get-tuple-element.97.probs_ref, bf16[4,128,512]{2,1,0:T(8,128)(2,1)} %get-tuple-element.69.q_ref, bf16[4,128,128]{2,1,0:T(8,128)(2,1)} %get-tuple-element.70.own_ref, ...), custom_call_target="tpu_custom_call" | custom-call | tf_op jit(solution)/shard_map/pallas_call | solution.py:674
  380.7 13.0 %shard_map.213 = (bf16[4,128,2048]{2,1,0:T(8,128)(2,1)}, bf16[2048,768]{1,0:T(8,128)(2,1)}) custom-call(bf16[4,128,512]{2,1,0:T(8,128)(2,1)} %get-tuple-element.98.dq_ref, f32[4,192,128]{2,1,0:T(8,128)} %get-tuple-element.99.dkv_ref, f32[4,64,128]{2,1,0:T(8,128)} %copy-done.42, f32[4,128,128]{2,1,0:T(8,128)} %get-tuple-element.134.cos_ref, ...), custom_call_target="tpu_custom_call" | custom-call | tf_op jit(solution)/shard_map/pallas_call | solution.py:693
  393.8 8.1 %shard_map.209 = (bf16[8,64,704]{2,1,0:T(8,128)(2,1)}, bf16[8,64,704]{2,1,0:T(8,128)(2,1)}, bf16[8,64,704]{2,1,0:T(8,128)(2,1)}, bf16[8,64,704]{2,1,0:T(8,128)(2,1)}) custom-call(s32[2]{0:T(128)} %pad_add_fusion.id_ref, bf16[1024,2048]{1,0:T(8,128)(2,1)} %all-gather.9.cloned.1.call-done.x_ref, bf16[1024,704]{1,0:T(8,128)(2,1)} %get-tuple-element.88.grad_ref), custom_call_target="tpu_custom_call" | custom-call | tf_op jit(solution)/shard_map/pallas_call | solution.py:244
  402.0 8.7 %shard_map.210 = (bf16[8,64,704]{2,1,0:T(8,128)(2,1)}, bf16[8,64,704]{2,1,0:T(8,128)(2,1)}, bf16[8,64,704]{2,1,0:T(8,128)(2,1)}, bf16[8,64,704]{2,1,0:T(8,128)(2,1)}) custom-call(s32[2]{0:T(128)} %pad_add_fusion.id_ref, bf16[1024,2048]{1,0:T(8,128)(2,1)} %all-gather.9.cloned.1.call-done.x_ref, bf16[1024,704]{1,0:T(8,128)(2,1)} %get-tuple-element.90.grad_ref), custom_call_target="tpu_custom_call" | custom-call | tf_op jit(solution)/shard_map/pallas_call | solution.py:244
  410.6 4.5 convolution_convert_fusion.1
  415.2 5.0 convolution_convert_fusion
  427.2 6.7 collective-permute-done.28
  440.5 18.4 %collective-permute-done.50 = bf16[80,2048]{1,0:T(8,128)(2,1)} collective-permute-done((bf16[80,2048]{1,0:T(8,128)(2,1)}, bf16[80,2048]{1,0:T(8,128)(2,1)}, u32[]{:S(2)}, u32[]{:S(2)}) %collective-permute-start.50) | collective-permute-done | bytes 327712 | tf_op jit(solution)/shard_map/ppermute | solution.py:55
  462.4 13.2 %collective-permute-done.29.refs_2_ = bf16[8,64,704]{2,1,0:T(8,128)(2,1)S(1)} collective-permute-done((bf16[8,64,704]{2,1,0:T(8,128)(2,1)}, bf16[8,64,704]{2,1,0:T(8,128)(2,1)S(1)}, u32[]{:S(2)}, u32[]{:S(2)}) %collective-permute-start.29) | collective-permute-done | bytes 720928 | tf_op jit(solution)/shard_map/ppermute | solution.py:55
  477.4 3.9 shard_map.217
  481.3 10.7 %collective-permute-start.33 = (bf16[2,64,704]{2,1,0:T(8,128)(2,1)}, bf16[2,64,704]{2,1,0:T(8,128)(2,1)S(1)}, u32[]{:S(2)}, u32[]{:S(2)}) collective-permute-start(bf16[2,64,704]{2,1,0:T(8,128)(2,1)} %get-tuple-element.117), channel_id=1, source_target_pairs={{0,1},{1,0},{2,3},{3,2},{4,5},{5,4},{6,7},{7,6},{8,9},{9,8},{10,11... | collective-permute-start | bytes 540680 | tf_op jit(solution)/shard_map/ppermute | solution.py:55
  492.0 4.6 collective-permute-start.34
  501.3 5.5 collective-permute-done.34.refs_2_
  506.8 3.0 collective-permute-done.35.refs_3_
  514.8 13.8 %collective-permute-done.37.refs_5_ = bf16[2,64,704]{2,1,0:T(8,128)(2,1)S(1)} collective-permute-done((bf16[2,64,704]{2,1,0:T(8,128)(2,1)}, bf16[2,64,704]{2,1,0:T(8,128)(2,1)S(1)}, u32[]{:S(2)}, u32[]{:S(2)}) %collective-permute-start.37) | collective-permute-done | bytes 180256 | tf_op jit(solution)/shard_map/ppermute | solution.py:55
  529.9 2.9 shard_map.218
  539.9 20.8 %collective-permute-done.55.refs_5_ = bf16[80,2048]{1,0:T(8,128)(2,1)} collective-permute-done((bf16[80,2048]{1,0:T(8,128)(2,1)S(1)}, bf16[80,2048]{1,0:T(8,128)(2,1)}, u32[]{:S(2)}, u32[]{:S(2)}) %collective-permute-start.55) | collective-permute-done | bytes 327712 | tf_op jit(solution)/shard_map/ppermute | solution.py:55
  563.8 3.9 all-to-all-start.5
  574.9 54.4 %collective-permute-done.56.refs_6_ = bf16[96,2048]{1,0:T(8,128)(2,1)} collective-permute-done((bf16[96,2048]{1,0:T(8,128)(2,1)S(1)}, bf16[96,2048]{1,0:T(8,128)(2,1)}, u32[]{:S(2)}, u32[]{:S(2)}) %collective-permute-start.56) | collective-permute-done | bytes 393248 | tf_op jit(solution)/shard_map/ppermute | solution.py:55
  639.0 4.6 shard_map.221
  643.7 4.7 shard_map.219
  648.4 4.7 shard_map.220
  661.9 3.8 shard_map.214
  665.7 3.2 shard_map.216
  668.9 3.2 shard_map.215
  (264 shorter events, 117.4 us)
Async XLA Ops:
  7.2 40.8 %all-gather.5.cloned.1.call-start = ((), (), s32[]{:S(2)}) async-start(), calls=%async_computation.10 | async-start | bytes 2949120 | tf_op jit(solution)/shard_map/all_gather | solution.py:530
  10.3 67.1 %all-gather.7.cloned.1.call-start = ((), (), s32[]{:S(2)}) async-start(), calls=%async_computation.11 | async-start | bytes 2359296 | tf_op jit(solution)/shard_map/all_gather | solution.py:531
  12.0 203.3 %all-gather.11.cloned.1.call-start = ((), (), s32[]{:S(2)}) async-start(), calls=%async_computation.13 | async-start | bytes 4718592 | tf_op jit(solution)/shard_map/all_gather | solution.py:556
  14.8 31.6 %all-to-all-start = ((bf16[4,128,2176]{2,1,0:T(8,128)(2,1)}), bf16[4,128,2176]{2,1,0:T(8,128)(2,1)S(1)}, u32[]{:S(2)}, u32[]{:S(2)}) async-start(bf16[4,128,2176]{2,1,0:T(8,128)(2,1)} %broadcast_in_dim.18), calls=%async_computation | async-start | bytes 4456448 | tf_op jit(solution)/shard_map/all_to_all | solution.py:43
  20.1 195.3 %all-gather.9.cloned.1.call-start = ((), (), s32[]{:S(2)}) async-start(), calls=%async_computation.12 | async-start | bytes 4718592 | tf_op jit(solution)/shard_map/all_gather | solution.py:602
  113.5 207.9 %reduce-scatter.7.cloned.1.call-start = ((), (), s32[]{:S(2)}) async-start(), calls=%async_computation.15 | async-start | bytes 4718592 | tf_op jit(solution)/shard_map/reduce_scatter | solution.py:614
  117.8 18.2 %collective-permute-start.2 = (bf16[2,64,704]{2,1,0:T(8,128)(2,1)}, bf16[2,64,704]{2,1,0:T(8,128)(2,1)S(1)}, u32[]{:S(2)}, u32[]{:S(2)}) collective-permute-start(bf16[2,64,704]{2,1,0:T(8,128)(2,1)} %get-tuple-element.78), channel_id=1, source_target_pairs={{0,2},{1,3},{2,0},{3,1},{4,6},{5,7},{6,4},{7,5},{8,10},{9,11},{10,... | collective-permute-start | bytes 540680 | tf_op jit(solution)/shard_map/ppermute | solution.py:55
  122.3 17.8 %collective-permute-start.3 = (bf16[2,64,704]{2,1,0:T(8,128)(2,1)}, bf16[2,64,704]{2,1,0:T(8,128)(2,1)S(1)}, u32[]{:S(2)}, u32[]{:S(2)}) collective-permute-start(bf16[2,64,704]{2,1,0:T(8,128)(2,1)} %get-tuple-element.79), channel_id=1, source_target_pairs={{0,3},{1,2},{2,1},{3,0},{4,7},{5,6},{6,5},{7,4},{8,11},{9,10},{10,... | collective-permute-start | bytes 540680 | tf_op jit(solution)/shard_map/ppermute | solution.py:55
  122.4 17.7 %collective-permute-start.4 = (bf16[2,64,704]{2,1,0:T(8,128)(2,1)}, bf16[2,64,704]{2,1,0:T(8,128)(2,1)S(1)}, u32[]{:S(2)}, u32[]{:S(2)}) collective-permute-start(bf16[2,64,704]{2,1,0:T(8,128)(2,1)} %get-tuple-element.80), channel_id=1, source_target_pairs={{0,4},{1,5},{2,6},{3,7},{4,0},{5,1},{6,2},{7,3},{8,12},{9,13},{10,... | collective-permute-start | bytes 540680 | tf_op jit(solution)/shard_map/ppermute | solution.py:55
  123.3 28.7 %collective-permute-start.5 = (bf16[2,64,704]{2,1,0:T(8,128)(2,1)}, bf16[2,64,704]{2,1,0:T(8,128)(2,1)S(1)}, u32[]{:S(2)}, u32[]{:S(2)}) collective-permute-start(bf16[2,64,704]{2,1,0:T(8,128)(2,1)} %get-tuple-element.81), channel_id=1, source_target_pairs={{0,5},{1,4},{2,7},{3,6},{4,1},{5,0},{6,3},{7,2},{8,13},{9,12},{10,... | collective-permute-start | bytes 540680 | tf_op jit(solution)/shard_map/ppermute | solution.py:55
  124.8 27.3 %collective-permute-start.6 = (bf16[2,64,704]{2,1,0:T(8,128)(2,1)}, bf16[2,64,704]{2,1,0:T(8,128)(2,1)S(1)}, u32[]{:S(2)}, u32[]{:S(2)}) collective-permute-start(bf16[2,64,704]{2,1,0:T(8,128)(2,1)} %get-tuple-element.82), channel_id=1, source_target_pairs={{0,6},{1,7},{2,4},{3,5},{4,2},{5,3},{6,0},{7,1},{8,14},{9,15},{10,... | collective-permute-start | bytes 540680 | tf_op jit(solution)/shard_map/ppermute | solution.py:55
  157.2 17.8 %collective-permute-start.11 = (bf16[8,64,704]{2,1,0:T(8,128)(2,1)}, bf16[8,64,704]{2,1,0:T(8,128)(2,1)S(1)}, u32[]{:S(2)}, u32[]{:S(2)}) collective-permute-start(bf16[8,64,704]{2,1,0:T(8,128)(2,1)} %get-tuple-element.85.refs_1_), channel_id=1, source_target_pairs={{0,16},{8,24},{16,0},{24,8},{1,17},{9,25},{17,1},{25,9},{2,18},{10... | collective-permute-start | bytes 2162696 | tf_op jit(solution)/shard_map/ppermute | solution.py:55
  158.7 30.5 %collective-permute-start.9 = (bf16[8,64,704]{2,1,0:T(8,128)(2,1)}, bf16[8,64,704]{2,1,0:T(8,128)(2,1)S(1)}, u32[]{:S(2)}, u32[]{:S(2)}) collective-permute-start(bf16[8,64,704]{2,1,0:T(8,128)(2,1)} %get-tuple-element.85.refs_1_), channel_id=1, source_target_pairs={{0,8},{8,0},{16,24},{24,16},{1,9},{9,1},{17,25},{25,17},{2,10},{10... | collective-permute-start | bytes 2162696 | tf_op jit(solution)/shard_map/ppermute | solution.py:55
  159.2 31.6 %collective-permute-start.10 = (bf16[8,64,704]{2,1,0:T(8,128)(2,1)}, bf16[8,64,704]{2,1,0:T(8,128)(2,1)S(1)}, u32[]{:S(2)}, u32[]{:S(2)}) collective-permute-start(bf16[8,64,704]{2,1,0:T(8,128)(2,1)} %get-tuple-element.84.refs_0_), channel_id=1, source_target_pairs={{0,16},{8,24},{16,0},{24,8},{1,17},{9,25},{17,1},{25,9},{2,18},{10... | collective-permute-start | bytes 2162696 | tf_op jit(solution)/shard_map/ppermute | solution.py:55
  172.3 35.3 %collective-permute-start.12 = (bf16[8,64,704]{2,1,0:T(8,128)(2,1)S(1)}, bf16[8,64,704]{2,1,0:T(8,128)(2,1)S(1)}, u32[]{:S(2)}, u32[]{:S(2)}) collective-permute-start(bf16[8,64,704]{2,1,0:T(8,128)(2,1)S(1)} %collective-permute-done.8.refs_2_), channel_id=1, source_target_pairs={{0,16},{8,24},{16,0},{24,8},{1,17},{9,25},{17,1},{25,9},{2,18},{10... | collective-permute-start | bytes 2162696 | tf_op jit(solution)/shard_map/ppermute | solution.py:55
  175.0 32.6 %collective-permute-start.13 = (bf16[8,64,704]{2,1,0:T(8,128)(2,1)S(1)}, bf16[8,64,704]{2,1,0:T(8,128)(2,1)S(1)}, u32[]{:S(2)}, u32[]{:S(2)}) collective-permute-start(bf16[8,64,704]{2,1,0:T(8,128)(2,1)S(1)} %collective-permute-done.11.refs_5_), channel_id=1, source_target_pairs={{0,8},{8,0},{16,24},{24,16},{1,9},{9,1},{17,25},{25,17},{2,10},{10... | collective-permute-start | bytes 2162696 | tf_op jit(solution)/shard_map/ppermute | solution.py:55
  240.8 332.4 %reduce-scatter.11.cloned.1.call-start = ((), (), s32[]{:S(2)}) async-start(), calls=%async_computation.17 | async-start | bytes 2359296 | tf_op jit(solution)/shard_map/reduce_scatter | solution.py:671
  357.3 274.1 %reduce-scatter.9.cloned.1.call-start = ((), (), s32[]{:S(2)}) async-start(), calls=%async_computation.16 | async-start | bytes 3538944 | tf_op jit(solution)/shard_map/reduce_scatter | solution.py:713
  393.8 264.9 %reduce-scatter.5.cloned.1.call-start = ((), (), s32[]{:S(2)}) async-start(), calls=%async_computation.14 | async-start | bytes 4718592 | tf_op jit(solution)/shard_map/reduce_scatter | solution.py:630
  421.6 38.6 %collective-permute-start.27 = (bf16[8,64,704]{2,1,0:T(8,128)(2,1)}, bf16[8,64,704]{2,1,0:T(8,128)(2,1)S(1)}, u32[]{:S(2)}, u32[]{:S(2)}) collective-permute-start(bf16[8,64,704]{2,1,0:T(8,128)(2,1)} %get-tuple-element.110), channel_id=1, source_target_pairs={{0,8},{8,0},{16,24},{24,16},{1,9},{9,1},{17,25},{25,17},{2,10},{10... | collective-permute-start | bytes 2162696 | tf_op jit(solution)/shard_map/ppermute | solution.py:55
  423.2 38.9 %collective-permute-start.30 = (bf16[8,64,704]{2,1,0:T(8,128)(2,1)}, bf16[8,64,704]{2,1,0:T(8,128)(2,1)S(1)}, u32[]{:S(2)}, u32[]{:S(2)}) collective-permute-start(bf16[8,64,704]{2,1,0:T(8,128)(2,1)} %get-tuple-element.113), channel_id=1, source_target_pairs={{0,16},{8,24},{16,0},{24,8},{1,17},{9,25},{17,1},{25,9},{2,18},{10... | collective-permute-start | bytes 2162696 | tf_op jit(solution)/shard_map/ppermute | solution.py:55
  426.3 32.6 %collective-permute-start.50 = (bf16[80,2048]{1,0:T(8,128)(2,1)}, bf16[80,2048]{1,0:T(8,128)(2,1)}, u32[]{:S(2)}, u32[]{:S(2)}) collective-permute-start(bf16[80,2048]{1,0:T(8,128)(2,1)} %get-tuple-element.130), channel_id=1, source_target_pairs={{0,16},{8,24},{16,0},{24,8},{1,17},{9,25},{17,1},{25,9},{2,18},{10... | collective-permute-start | bytes 983048 | tf_op jit(solution)/shard_map/ppermute | solution.py:55
  436.2 39.4 %collective-permute-start.29 = (bf16[8,64,704]{2,1,0:T(8,128)(2,1)}, bf16[8,64,704]{2,1,0:T(8,128)(2,1)S(1)}, u32[]{:S(2)}, u32[]{:S(2)}) collective-permute-start(bf16[8,64,704]{2,1,0:T(8,128)(2,1)} %add_convert_fusion.1), channel_id=1, source_target_pairs={{0,16},{8,24},{16,0},{24,8},{1,17},{9,25},{17,1},{25,9},{2,18},{10... | collective-permute-start | bytes 2162696 | tf_op jit(solution)/shard_map/ppermute | solution.py:55
  439.2 36.4 %collective-permute-start.32 = (bf16[8,64,704]{2,1,0:T(8,128)(2,1)}, bf16[8,64,704]{2,1,0:T(8,128)(2,1)S(1)}, u32[]{:S(2)}, u32[]{:S(2)}) collective-permute-start(bf16[8,64,704]{2,1,0:T(8,128)(2,1)} %add_convert_fusion), channel_id=1, source_target_pairs={{0,8},{8,0},{16,24},{24,16},{1,9},{9,1},{17,25},{25,17},{2,10},{10... | collective-permute-start | bytes 2162696 | tf_op jit(solution)/shard_map/ppermute | solution.py:55
  458.9 37.8 %collective-permute-start.47 = (bf16[96,2048]{1,0:T(8,128)(2,1)S(1)}, bf16[96,2048]{1,0:T(8,128)(2,1)S(1)}, u32[]{:S(2)}, u32[]{:S(2)}) collective-permute-start(bf16[96,2048]{1,0:T(8,128)(2,1)S(1)} %get-tuple-element.132), channel_id=1, source_target_pairs={{0,8},{8,0},{16,24},{24,16},{1,9},{9,1},{17,25},{25,17},{2,10},{10... | collective-permute-start | bytes 1179656 | tf_op jit(solution)/shard_map/ppermute | solution.py:55
  460.1 36.5 %collective-permute-start.49 = (bf16[80,2048]{1,0:T(8,128)(2,1)}, bf16[80,2048]{1,0:T(8,128)(2,1)S(1)}, u32[]{:S(2)}, u32[]{:S(2)}) collective-permute-start(bf16[80,2048]{1,0:T(8,128)(2,1)} %get-tuple-element.129), channel_id=1, source_target_pairs={{0,16},{8,24},{16,0},{24,8},{1,17},{9,25},{17,1},{25,9},{2,18},{10... | collective-permute-start | bytes 983048 | tf_op jit(solution)/shard_map/ppermute | solution.py:55
  462.2 37.1 %collective-permute-start.51 = (bf16[80,2048]{1,0:T(8,128)(2,1)S(1)}, bf16[80,2048]{1,0:T(8,128)(2,1)S(1)}, u32[]{:S(2)}, u32[]{:S(2)}) collective-permute-start(bf16[80,2048]{1,0:T(8,128)(2,1)S(1)} %add_convert_fusion.6), channel_id=1, source_target_pairs={{0,8},{8,0},{16,24},{24,16},{1,9},{9,1},{17,25},{25,17},{2,10},{10... | collective-permute-start | bytes 983048 | tf_op jit(solution)/shard_map/ppermute | solution.py:55
  481.3 18.5 %collective-permute-start.33 = (bf16[2,64,704]{2,1,0:T(8,128)(2,1)}, bf16[2,64,704]{2,1,0:T(8,128)(2,1)S(1)}, u32[]{:S(2)}, u32[]{:S(2)}) collective-permute-start(bf16[2,64,704]{2,1,0:T(8,128)(2,1)} %get-tuple-element.117), channel_id=1, source_target_pairs={{0,1},{1,0},{2,3},{3,2},{4,5},{5,4},{6,7},{7,6},{8,9},{9,8},{10,11... | collective-permute-start | bytes 540680 | tf_op jit(solution)/shard_map/ppermute | solution.py:55
  499.3 35.8 %collective-permute-start.46 = (bf16[96,2048]{1,0:T(8,128)(2,1)S(1)}, bf16[96,2048]{1,0:T(8,128)(2,1)S(1)}, u32[]{:S(2)}, u32[]{:S(2)}) collective-permute-start(bf16[96,2048]{1,0:T(8,128)(2,1)S(1)} %get-tuple-element.131), channel_id=1, source_target_pairs={{0,8},{8,0},{16,24},{24,16},{1,9},{9,1},{17,25},{25,17},{2,10},{10... | collective-permute-start | bytes 1179656 | tf_op jit(solution)/shard_map/ppermute | solution.py:55
  499.8 35.2 %collective-permute-start.48 = (bf16[96,2048]{1,0:T(8,128)(2,1)S(1)}, bf16[96,2048]{1,0:T(8,128)(2,1)S(1)}, u32[]{:S(2)}, u32[]{:S(2)}) collective-permute-start(bf16[96,2048]{1,0:T(8,128)(2,1)S(1)} %add_convert_fusion.4), channel_id=1, source_target_pairs={{0,16},{8,24},{16,0},{24,8},{1,17},{9,25},{17,1},{25,9},{2,18},{10... | collective-permute-start | bytes 1179656 | tf_op jit(solution)/shard_map/ppermute | solution.py:55
  506.8 21.8 %collective-permute-start.37 = (bf16[2,64,704]{2,1,0:T(8,128)(2,1)}, bf16[2,64,704]{2,1,0:T(8,128)(2,1)S(1)}, u32[]{:S(2)}, u32[]{:S(2)}) collective-permute-start(bf16[2,64,704]{2,1,0:T(8,128)(2,1)} %get-tuple-element.121), channel_id=1, source_target_pairs={{0,5},{1,4},{2,7},{3,6},{4,1},{5,0},{6,3},{7,2},{8,13},{9,12},{10,... | collective-permute-start | bytes 540680 | tf_op jit(solution)/shard_map/ppermute | solution.py:55
  509.8 19.4 %collective-permute-start.38 = (bf16[2,64,704]{2,1,0:T(8,128)(2,1)}, bf16[2,64,704]{2,1,0:T(8,128)(2,1)S(1)}, u32[]{:S(2)}, u32[]{:S(2)}) collective-permute-start(bf16[2,64,704]{2,1,0:T(8,128)(2,1)} %get-tuple-element.122), channel_id=1, source_target_pairs={{0,6},{1,7},{2,4},{3,5},{4,2},{5,3},{6,0},{7,1},{8,14},{9,15},{10,... | collective-permute-start | bytes 540680 | tf_op jit(solution)/shard_map/ppermute | solution.py:55
  511.7 17.4 %collective-permute-start.39 = (bf16[2,64,704]{2,1,0:T(8,128)(2,1)}, bf16[2,64,704]{2,1,0:T(8,128)(2,1)S(1)}, u32[]{:S(2)}, u32[]{:S(2)}) collective-permute-start(bf16[2,64,704]{2,1,0:T(8,128)(2,1)} %get-tuple-element.123), channel_id=1, source_target_pairs={{0,7},{1,6},{2,5},{3,4},{4,3},{5,2},{6,1},{7,0},{8,15},{9,14},{10,... | collective-permute-start | bytes 540680 | tf_op jit(solution)/shard_map/ppermute | solution.py:55
  532.8 36.8 %collective-permute-start.40 = (bf16[64,5632]{1,0:T(8,128)(2,1)}, bf16[64,5632]{1,0:T(8,128)(2,1)}, u32[]{:S(2)}, u32[]{:S(2)}) collective-permute-start(bf16[64,5632]{1,0:T(8,128)(2,1)} %get-tuple-element.124.refs_0_), channel_id=1, source_target_pairs={{0,8},{8,0},{16,24},{24,16},{1,9},{9,1},{17,25},{25,17},{2,10},{10... | collective-permute-start | bytes 2162696 | tf_op jit(solution)/shard_map/ppermute | solution.py:55
  534.3 37.3 %collective-permute-start.44 = (bf16[64,5632]{1,0:T(8,128)(2,1)}, bf16[64,5632]{1,0:T(8,128)(2,1)}, u32[]{:S(2)}, u32[]{:S(2)}) collective-permute-start(bf16[64,5632]{1,0:T(8,128)(2,1)} %get-tuple-element.125.refs_0_), channel_id=1, source_target_pairs={{0,16},{8,24},{16,0},{24,8},{1,17},{9,25},{17,1},{25,9},{2,18},{10... | collective-permute-start | bytes 2162696 | tf_op jit(solution)/shard_map/ppermute | solution.py:55
  536.2 26.9 %collective-permute-start.52 = (bf16[96,2048]{1,0:T(8,128)(2,1)S(1)}, bf16[96,2048]{1,0:T(8,128)(2,1)S(1)}, u32[]{:S(2)}, u32[]{:S(2)}) collective-permute-start(bf16[96,2048]{1,0:T(8,128)(2,1)S(1)} %add_convert_fusion.3.refs_0_), channel_id=1, source_target_pairs={{0,8},{8,0},{16,24},{24,16},{1,9},{9,1},{17,25},{25,17},{2,10},{10... | collective-permute-start | bytes 1179656 | tf_op jit(solution)/shard_map/ppermute | solution.py:55
  537.5 23.1 %collective-permute-start.55 = (bf16[80,2048]{1,0:T(8,128)(2,1)S(1)}, bf16[80,2048]{1,0:T(8,128)(2,1)}, u32[]{:S(2)}, u32[]{:S(2)}) collective-permute-start(bf16[80,2048]{1,0:T(8,128)(2,1)S(1)} %add_convert_fusion.5.refs_1_), channel_id=1, source_target_pairs={{0,16},{8,24},{16,0},{24,8},{1,17},{9,25},{17,1},{25,9},{2,18},{10... | collective-permute-start | bytes 983048 | tf_op jit(solution)/shard_map/ppermute | solution.py:55
  539.2 29.9 %collective-permute-start.54 = (bf16[96,2048]{1,0:T(8,128)(2,1)S(1)}, bf16[96,2048]{1,0:T(8,128)(2,1)}, u32[]{:S(2)}, u32[]{:S(2)}) collective-permute-start(bf16[96,2048]{1,0:T(8,128)(2,1)S(1)} %add_convert_fusion.3.refs_0_), channel_id=1, source_target_pairs={{0,16},{8,24},{16,0},{24,8},{1,17},{9,25},{17,1},{25,9},{2,18},{10... | collective-permute-start | bytes 1179656 | tf_op jit(solution)/shard_map/ppermute | solution.py:55
  563.1 66.7 %collective-permute-start.41 = (bf16[64,5632]{1,0:T(8,128)(2,1)}, bf16[64,5632]{1,0:T(8,128)(2,1)}, u32[]{:S(2)}, u32[]{:S(2)}) collective-permute-start(bf16[64,5632]{1,0:T(8,128)(2,1)} %get-tuple-element.124.refs_0_), channel_id=1, source_target_pairs={{0,16},{8,24},{16,0},{24,8},{1,17},{9,25},{17,1},{25,9},{2,18},{10... | collective-permute-start | bytes 2162696 | tf_op jit(solution)/shard_map/ppermute | solution.py:55
  563.8 96.8 %all-to-all-start.5 = ((bf16[4,128,2048]{2,1,0:T(8,128)(2,1)}), bf16[4,128,2048]{2,1,0:T(8,128)(2,1)S(1)}, u32[]{:S(2)}, u32[]{:S(2)}) async-start(bf16[4,128,2048]{2,1,0:T(8,128)(2,1)} %get-tuple-element.102), calls=%async_computation.7 | async-start | bytes 4194304 | tf_op jit(solution)/shard_map/all_to_all | solution.py:47
  569.1 63.3 %collective-permute-start.43 = (bf16[64,5632]{1,0:T(8,128)(2,1)}, bf16[64,5632]{1,0:T(8,128)(2,1)S(1)}, u32[]{:S(2)}, u32[]{:S(2)}) collective-permute-start(bf16[64,5632]{1,0:T(8,128)(2,1)} %get-tuple-element.125.refs_0_), channel_id=1, source_target_pairs={{0,8},{8,0},{16,24},{24,16},{1,9},{9,1},{17,25},{25,17},{2,10},{10... | collective-permute-start | bytes 2162696 | tf_op jit(solution)/shard_map/ppermute | solution.py:55
  569.6 63.4 %collective-permute-start.42 = (bf16[64,5632]{1,0:T(8,128)(2,1)}, bf16[64,5632]{1,0:T(8,128)(2,1)}, u32[]{:S(2)}, u32[]{:S(2)}) collective-permute-start(bf16[64,5632]{1,0:T(8,128)(2,1)} %collective-permute-done.40.refs_1_), channel_id=1, source_target_pairs={{0,16},{8,24},{16,0},{24,8},{1,17},{9,25},{17,1},{25,9},{2,18},{10... | collective-permute-start | bytes 2162696 | tf_op jit(solution)/shard_map/ppermute | solution.py:55
  571.1 58.2 %collective-permute-start.56 = (bf16[96,2048]{1,0:T(8,128)(2,1)S(1)}, bf16[96,2048]{1,0:T(8,128)(2,1)}, u32[]{:S(2)}, u32[]{:S(2)}) collective-permute-start(bf16[96,2048]{1,0:T(8,128)(2,1)S(1)} %collective-permute-done.52.refs_2_), channel_id=1, source_target_pairs={{0,16},{8,24},{16,0},{24,8},{1,17},{9,25},{17,1},{25,9},{2,18},{10... | collective-permute-start | bytes 1179656 | tf_op jit(solution)/shard_map/ppermute | solution.py:55
  571.6 62.8 %collective-permute-start.45 = (bf16[64,5632]{1,0:T(8,128)(2,1)}, bf16[64,5632]{1,0:T(8,128)(2,1)}, u32[]{:S(2)}, u32[]{:S(2)}) collective-permute-start(bf16[64,5632]{1,0:T(8,128)(2,1)} %collective-permute-done.44.refs_2_), channel_id=1, source_target_pairs={{0,8},{8,0},{16,24},{24,16},{1,9},{9,1},{17,25},{25,17},{2,10},{10... | collective-permute-start | bytes 2162696 | tf_op jit(solution)/shard_map/ppermute | solution.py:55
  632.4 24.2 %collective-permute-start.15 = (bf16[128,768]{1,0:T(8,128)(2,1)S(1)}, bf16[128,768]{1,0:T(8,128)(2,1)}, u32[]{:S(2)}, u32[]{:S(2)}) collective-permute-start(bf16[128,768]{1,0:T(8,128)(2,1)S(1)} %get-tuple-element.136.refs_0_), channel_id=1, source_target_pairs={{0,8},{8,0},{16,24},{24,16},{1,9},{9,1},{17,25},{25,17},{2,10},{10... | collective-permute-start | bytes 589832 | tf_op jit(solution)/shard_map/ppermute | solution.py:55
  633.0 24.3 %collective-permute-start.18 = (bf16[128,768]{1,0:T(8,128)(2,1)S(1)}, bf16[128,768]{1,0:T(8,128)(2,1)}, u32[]{:S(2)}, u32[]{:S(2)}) collective-permute-start(bf16[128,768]{1,0:T(8,128)(2,1)S(1)} %get-tuple-element.135.refs_1_), channel_id=1, source_target_pairs={{0,16},{8,24},{16,0},{24,8},{1,17},{9,25},{17,1},{25,9},{2,18},{10... | collective-permute-start | bytes 589832 | tf_op jit(solution)/shard_map/ppermute | solution.py:55
  634.5 18.6 %collective-permute-start.24 = (bf16[32,2048]{1,0:T(8,128)(2,1)}, bf16[32,2048]{1,0:T(8,128)(2,1)}, u32[]{:S(2)}, u32[]{:S(2)}) collective-permute-start(bf16[32,2048]{1,0:T(8,128)(2,1)} %get-tuple-element.137.refs_1_), channel_id=1, source_target_pairs={{0,16},{8,24},{16,0},{24,8},{1,17},{9,25},{17,1},{25,9},{2,18},{10... | collective-permute-start | bytes 393224 | tf_op jit(solution)/shard_map/ppermute | solution.py:55
  636.0 18.4 %collective-permute-start.23 = (bf16[32,2048]{1,0:T(8,128)(2,1)}, bf16[32,2048]{1,0:T(8,128)(2,1)S(1)}, u32[]{:S(2)}, u32[]{:S(2)}) collective-permute-start(bf16[32,2048]{1,0:T(8,128)(2,1)} %get-tuple-element.138.refs_0_), channel_id=1, source_target_pairs={{0,16},{8,24},{16,0},{24,8},{1,17},{9,25},{17,1},{25,9},{2,18},{10... | collective-permute-start | bytes 393224 | tf_op jit(solution)/shard_map/ppermute | solution.py:55
  (71 other events, 841.5 us)
Sparse Core Ops, SparseCore 0:
  10.4 36.4 all-gather.4
  49.1 28.2 all-gather.6
  79.0 47.0 all-gather.10
  128.1 67.0 all-gather.8
  240.9 80.4 reduce-scatter.6
  357.4 35.2 reduce-scatter.10
  395.5 44.3 reduce-scatter.8
  442.2 49.2 reduce-scatter.4

commit v3 on v2

--- a/solution.py
+++ b/solution.py
@@ -70,6 +70,10 @@
     last_one = go(add(chunks[2][0], first_two), 2)
     last_two = go(add(chunks[1][1], second_two), 1)
     return [[chunks[0][0], first_one, last_one], [chunks[0][1], second_one, last_two]]
+
+
+def gather_direct(value, count):
+    return [value] + [send(value, "rep", count, k) for k in range(1, count)]
 
 
 def gather_rep(halves, count):
@@ -205,19 +209,15 @@
     q_ref, k_ref, v_ref, gain_ref, k_all, v_all = refs[-6:]
     count = k_all.shape[0]
     q_cols = q_ref.shape[1] // count
-    row = 0
-    for h in range(2):
-        rows = slice(row, row + pieces[h].shape[0])
-        total = 0.0
-        for k in range(count):
-            at = jnp.bitwise_xor(id_ref[0], k)
-            value = pieces[2 * k + h][...].astype(F32)
-            q_ref[rows, pl.ds(pl.multiple_of(at * q_cols, LANES), q_cols)] = value[:, :q_cols]
-            k_all[at, rows] = value[:, q_cols : q_cols + HD]
-            v_all[at, rows] = value[:, q_cols + HD : q_cols + 2 * HD]
-            total += value[:, q_cols + 2 * HD :]
-        gain_ref[rows] = total
-        row = rows.stop
+    total = 0.0
+    for k, piece in enumerate(pieces):
+        at = jnp.bitwise_xor(id_ref[0], k)
+        value = piece[...].astype(F32)
+        q_ref[:, pl.ds(pl.multiple_of(at * q_cols, LANES), q_cols)] = value[:, :q_cols]
+        k_all[at] = value[:, q_cols : q_cols + HD]
+        v_all[at] = value[:, q_cols + HD : q_cols + 2 * HD]
+        total += value[:, q_cols + 2 * HD :]
+    gain_ref[...] = total
     for ref, both in ((k_ref, k_all), (v_ref, v_all)):
         for head in range(count // share):
             total = both[head * share]
@@ -669,8 +669,7 @@
     in_grad = swap(in_grad, "rep").reshape(n_rep, n_rep, rows, pair * fine)
     w_o_grad = rows_rows(out_in, branch_all).astype(BF)
     w_o_grad = lax.psum_scatter(w_o_grad, "shard", scatter_dimension=0, tiled=True)
-    w_o_grad = (w_o_grad[: fine // 2], w_o_grad[fine // 2 :])
-    o_out = place(gather_rep(w_o_grad, n_rep), r)
+    o_out = place([(v,) for v in gather_direct(w_o_grad, n_rep)], r)
     query_grad, kv_grad = call(
         partial(attend_back_kernel, fine),
         (shape((n_rep, rows, q_cols), BF), shape((n_rep, span, LANES), F32)),
@@ -714,7 +713,6 @@
     input_grad = call(last_kernel, shape((rows, width), BF))(
         swap(one_grad_part, "rep"), tokens, gain_one, mid_grad
     )
-    w_qkv_grad = (w_qkv_grad[: own // 2], w_qkv_grad[own // 2 :])
     q_out, k_out, v_out, gain_sums = flat_call(
         partial(qkv_kernel, share),
         ids,
@@ -724,7 +722,7 @@
             shape((own, KVH * HD), F32),
             shape((own, LANES), F32),
         ),
-        [half for piece in gather_rep(w_qkv_grad, n_rep) for half in piece],
+        gather_direct(w_qkv_grad, n_rep),
         [pltpu.VMEM((n_rep, own, HD), F32)] * 2,
     )
     return (

time: 688 us -> 685 us (level)
  waiting for transfers between devices: 309 us -> 316 us
    ppermute x56 -> x50, waiting for transfers between devices: 210 us -> 217 us  [send(): return lax.ppermute(value, axis, pairs(count, step))]
    ppermute x56 -> x50, starting transfers between devices: 72.7 us -> 69 us  [send(): return lax.ppermute(value, axis, pairs(count, step))]
  transfers between devices with their start and end apart: 68 -> 62, of which waited for: 26 -> 27; matrix products, arithmetic and copies ran while one was open for 6% -> 5% of each run, Pallas kernels for 14% -> 14%
where the time goes in v3:
time: 685 us; the launch traced here: 681 us
  waiting for transfers between devices  316 us (46%)
  Pallas kernels  126 us (18%)
  blocking collectives  90.2 us (13%)
  starting transfers between devices  81.4 us (12%)
  local copies, waits for them, and re-layouts  21.6 us (3%)
  matrix products  16.2 us (2%)
  other arithmetic  15 us (2%)
  between operations  14.6 us (2%)
    ppermute x50, waiting for transfers between devices, send(): return lax.ppermute(value, axis, pairs(count, step))  217 us
    reduce_scatter x1, waiting for transfers between devices, body(): lax.psum_scatter(two_grad_part, 'shard', scatter_dimension=0, tiled=True)  80.5 us
    ppermute x50, starting transfers between devices, send(): return lax.ppermute(value, axis, pairs(count, step))  69 us
    all_to_all x3, blocking collectives, swap(): return lax.all_to_all(value, axis, split_axis=0, concat_axis=0, tiled=True)  50.7 us
    all_to_all x1, blocking collectives, spread(): return lax.all_to_all(wide, axis, split_axis=0, concat_axis=0, tiled=True)  27.1 us
    pallas_call x1, Pallas kernels, body(): call(forward_back_kernel, (shape((group, hidden), BF),) * 3 + (shape((gro...  25.4 us
    pallas_call x5, Pallas kernels, flat_call(): pl.pallas_call(kernel, out_shape=out_shape, in_specs=specs, scratch_shape...  18.4 us
    pallas_call x4, Pallas kernels, place(): pl.pallas_call(partial(place_kernel, count), out_shape=shape((count, rows...  17.2 us
  transfers between devices with their start and end apart: 62, of which 27 were waited for; matrix products, arithmetic and copies ran while one was open for 5% of the time, Pallas kernels for 14%

profile of v3, /device:TPU:0, one launch (start us, length us, event | category | flops | bytes accessed | tf_op | source)
XLA Modules:
  0.0 680.8 jit_solution(3427267743925017805)
XLA Ops:
  14.8 5.3 all-to-all-start
  20.1 12.3 %all_gather.15 = bf16[2,2048]{1,0:T(2,128)(2,1)S(1)} all-gather(bf16[2,256]{1,0:T(2,128)(2,1)S(1)} %pad_maximum_fusion.2), channel_id=1, replica_groups=mesh['rep'=4,'shard'=8] {'shard'}, dimensions={1}, use_global_device_ids=true | all-gather | bytes 9216 | tf_op jit(solution)/shard_map/all_gather | solution.py:535
  33.1 13.2 %all-to-all-done.x_ref.pos_ref = bf16[4,128,2176]{2,1,0:T(8,128)(2,1)S(1)} async-done(((bf16[4,128,2176]{2,1,0:T(8,128)(2,1)}), bf16[4,128,2176]{2,1,0:T(8,128)(2,1)S(1)}, u32[]{:S(2)}, u32[]{:S(2)}) %all-to-all-start) | async-done | bytes 2228256 | tf_op jit(solution)/shard_map/all_to_all | solution.py:43
  48.1 6.2 shard_map.203
  58.0 6.4 shard_map.204
  64.3 10.6 %all_to_all.30 = bf16[4,4,128,128]{3,2,1,0:T(8,128)(2,1)S(1)} all-to-all(bf16[4,4,128,128]{3,2,1,0:T(8,128)(2,1)} %get-tuple-element.71), channel_id=1, replica_groups=mesh['rep'=4,'shard'=8] {'rep'}, dimensions={0} | all-to-all | bytes 1048576 | tf_op jit(solution)/shard_map/all_to_all | solution.py:47
  80.3 30.0 %all_to_all.31.part_ref = bf16[4,128,2048]{2,1,0:T(8,128)(2,1)} all-to-all(bf16[4,128,2048]{2,1,0:T(8,128)(2,1)S(1)} %bitcast.41), channel_id=1, replica_groups=mesh['rep'=4,'shard'=8] {'rep'}, dimensions={0} | all-to-all | bytes 4194304 | tf_op jit(solution)/shard_map/all_to_all | solution.py:47
  110.2 3.3 shard_map.205
  114.4 3.4 split_pair.1
  117.9 4.4 collective-permute-start.2
  126.6 9.4 %collective-permute-done.2.refs_2_ = bf16[2,64,704]{2,1,0:T(8,128)(2,1)S(1)} collective-permute-done((bf16[2,64,704]{2,1,0:T(8,128)(2,1)}, bf16[2,64,704]{2,1,0:T(8,128)(2,1)S(1)}, u32[]{:S(2)}, u32[]{:S(2)}) %collective-permute-start.2) | collective-permute-done | bytes 180256 | tf_op jit(solution)/shard_map/ppermute | solution.py:55
  140.1 12.0 %collective-permute-done.5.refs_5_ = bf16[2,64,704]{2,1,0:T(8,128)(2,1)S(1)} collective-permute-done((bf16[2,64,704]{2,1,0:T(8,128)(2,1)}, bf16[2,64,704]{2,1,0:T(8,128)(2,1)S(1)}, u32[]{:S(2)}, u32[]{:S(2)}) %collective-permute-start.5) | collective-permute-done | bytes 180256 | tf_op jit(solution)/shard_map/ppermute | solution.py:55
  160.6 11.7 %collective-permute-done.8.refs_2_ = bf16[8,64,704]{2,1,0:T(8,128)(2,1)S(1)} collective-permute-done((bf16[8,64,704]{2,1,0:T(8,128)(2,1)}, bf16[8,64,704]{2,1,0:T(8,128)(2,1)S(1)}, u32[]{:S(2)}, u32[]{:S(2)}) %collective-permute-start.8) | collective-permute-done | bytes 720928 | tf_op jit(solution)/shard_map/ppermute | solution.py:55
  177.3 11.9 %collective-permute-done.9.refs_3_ = bf16[8,64,704]{2,1,0:T(8,128)(2,1)S(1)} collective-permute-done((bf16[8,64,704]{2,1,0:T(8,128)(2,1)}, bf16[8,64,704]{2,1,0:T(8,128)(2,1)S(1)}, u32[]{:S(2)}, u32[]{:S(2)}) %collective-permute-start.9) | collective-permute-done | bytes 720928 | tf_op jit(solution)/shard_map/ppermute | solution.py:55
  190.8 16.7 %collective-permute-done.12.refs_6_ = bf16[8,64,704]{2,1,0:T(8,128)(2,1)S(1)} collective-permute-done((bf16[8,64,704]{2,1,0:T(8,128)(2,1)S(1)}, bf16[8,64,704]{2,1,0:T(8,128)(2,1)S(1)}, u32[]{:S(2)}, u32[]{:S(2)}) %collective-permute-start.12) | collective-permute-done | bytes 720928 | tf_op jit(solution)/shard_map/ppermute | solution.py:55
  209.5 5.8 shard_map.207
  215.3 25.4 %shard_map.208 = (bf16[1024,704]{1,0:T(8,128)(2,1)}, bf16[1024,704]{1,0:T(8,128)(2,1)}, bf16[1024,704]{1,0:T(8,128)(2,1)}, bf16[1024,2048]{1,0:T(8,128)(2,1)}) custom-call(bf16[1024,2048]{1,0:T(8,128)(2,1)} %all-gather.9.cloned.1.call-done.x_ref, bf16[1024,2048]{1,0:T(8,128)(2,1)} %all-gather.11.cloned.1.call-done.cot_ref, bf16[2,2048,704]{2,1,0:T(8,128)(2,1)} %bitcast.33, ...), custom_call_target="tpu_custom_call" | custom-call | tf_op jit(solution)/shard_map/pallas_call | solution.py:607
  240.9 80.5 %reduce-scatter.7.cloned.1.call-done.grad_ref = bf16[128,2048]{1,0:T(8,128)(2,1)} async-done(((bf16[1024,2048]{1,0:T(8,128)(2,1)}), bf16[128,2048]{1,0:T(8,128)(2,1)}) %reduce-scatter.7.cloned.1.call-update) | async-done | bytes 524304 | tf_op jit(solution)/shard_map/reduce_scatter | solution.py:614
  321.4 3.6 shard_map.211
  326.2 27.1 %all_to_all.32 = bf16[4,128,2048]{2,1,0:T(8,128)(2,1)S(1)} all-to-all(bf16[4,128,2048]{2,1,0:T(8,128)(2,1)S(1)} %broadcast_in_dim.19), channel_id=1, replica_groups=mesh['rep'=4,'shard'=8] {'rep'}, dimensions={0} | all-to-all | bytes 4194304 | tf_op jit(solution)/shard_map/all_to_all | solution.py:43
  357.4 10.2 %all_to_all.33 = bf16[4,512,128]{2,1,0:T(8,128)(2,1)} all-to-all(bf16[4,512,128]{2,1,0:T(8,128)(2,1)S(1)} %bitcast_bitcast_fusion), channel_id=1, replica_groups=mesh['rep'=4,'shard'=8] {'rep'}, dimensions={0} | all-to-all | bytes 1048576 | tf_op jit(solution)/shard_map/all_to_all | solution.py:47
  367.6 8.3 %shard_map.212 = (bf16[4,128,512]{2,1,0:T(8,128)(2,1)}, f32[4,192,128]{2,1,0:T(8,128)}) custom-call(bf16[4,4,128,128]{3,2,1,0:T(8,128)(2,1)} %bitcast.37, f32[4,8,128,192]{3,2,1,0:T(8,128)} %get-tuple-element.97.probs_ref, bf16[4,128,512]{2,1,0:T(8,128)(2,1)} %get-tuple-element.69.q_ref, bf16[4,128,128]{2,1,0:T(8,128)(2,1)} %get-tuple-element.70.own_ref, ...), custom_call_target="tpu_custom_call" | custom-call | tf_op jit(solution)/shard_map/pallas_call | solution.py:673
  380.7 13.0 %shard_map.213 = (bf16[4,128,2048]{2,1,0:T(8,128)(2,1)}, bf16[2048,768]{1,0:T(8,128)(2,1)}) custom-call(bf16[4,128,512]{2,1,0:T(8,128)(2,1)} %get-tuple-element.98.dq_ref, f32[4,192,128]{2,1,0:T(8,128)} %get-tuple-element.99.dkv_ref, f32[4,64,128]{2,1,0:T(8,128)} %copy-done.42, f32[4,128,128]{2,1,0:T(8,128)} %get-tuple-element.134.cos_ref, ...), custom_call_target="tpu_custom_call" | custom-call | tf_op jit(solution)/shard_map/pallas_call | solution.py:692
  393.8 8.1 %shard_map.209 = (bf16[8,64,704]{2,1,0:T(8,128)(2,1)}, bf16[8,64,704]{2,1,0:T(8,128)(2,1)}, bf16[8,64,704]{2,1,0:T(8,128)(2,1)}, bf16[8,64,704]{2,1,0:T(8,128)(2,1)}) custom-call(s32[2]{0:T(128)} %pad_add_fusion.id_ref, bf16[1024,2048]{1,0:T(8,128)(2,1)} %all-gather.9.cloned.1.call-done.x_ref, bf16[1024,704]{1,0:T(8,128)(2,1)} %get-tuple-element.88.grad_ref), custom_call_target="tpu_custom_call" | custom-call | tf_op jit(solution)/shard_map/pallas_call | solution.py:244
  401.9 8.7 %shard_map.210 = (bf16[8,64,704]{2,1,0:T(8,128)(2,1)}, bf16[8,64,704]{2,1,0:T(8,128)(2,1)}, bf16[8,64,704]{2,1,0:T(8,128)(2,1)}, bf16[8,64,704]{2,1,0:T(8,128)(2,1)}) custom-call(s32[2]{0:T(128)} %pad_add_fusion.id_ref, bf16[1024,2048]{1,0:T(8,128)(2,1)} %all-gather.9.cloned.1.call-done.x_ref, bf16[1024,704]{1,0:T(8,128)(2,1)} %get-tuple-element.90.grad_ref), custom_call_target="tpu_custom_call" | custom-call | tf_op jit(solution)/shard_map/pallas_call | solution.py:244
  410.6 4.5 convolution_convert_fusion.1
  415.1 5.0 convolution_convert_fusion
  427.1 6.7 collective-permute-done.22
  440.4 18.5 %collective-permute-done.44 = bf16[80,2048]{1,0:T(8,128)(2,1)} collective-permute-done((bf16[80,2048]{1,0:T(8,128)(2,1)}, bf16[80,2048]{1,0:T(8,128)(2,1)}, u32[]{:S(2)}, u32[]{:S(2)}) %collective-permute-start.44) | collective-permute-done | bytes 327712 | tf_op jit(solution)/shard_map/ppermute | solution.py:55
  462.5 13.2 %collective-permute-done.23.refs_2_ = bf16[8,64,704]{2,1,0:T(8,128)(2,1)S(1)} collective-permute-done((bf16[8,64,704]{2,1,0:T(8,128)(2,1)}, bf16[8,64,704]{2,1,0:T(8,128)(2,1)S(1)}, u32[]{:S(2)}, u32[]{:S(2)}) %collective-permute-start.23) | collective-permute-done | bytes 720928 | tf_op jit(solution)/shard_map/ppermute | solution.py:55
  477.4 3.9 shard_map.217
  481.3 10.5 %collective-permute-start.27 = (bf16[2,64,704]{2,1,0:T(8,128)(2,1)}, bf16[2,64,704]{2,1,0:T(8,128)(2,1)S(1)}, u32[]{:S(2)}, u32[]{:S(2)}) collective-permute-start(bf16[2,64,704]{2,1,0:T(8,128)(2,1)} %get-tuple-element.117), channel_id=1, source_target_pairs={{0,1},{1,0},{2,3},{3,2},{4,5},{5,4},{6,7},{7,6},{8,9},{9,8},{10,11... | collective-permute-start | bytes 540680 | tf_op jit(solution)/shard_map/ppermute | solution.py:55
  491.9 4.4 collective-permute-start.28
  501.2 5.2 collective-permute-done.28.refs_2_
  506.5 3.0 collective-permute-done.29.refs_3_
  514.5 14.0 %collective-permute-done.31.refs_5_ = bf16[2,64,704]{2,1,0:T(8,128)(2,1)S(1)} collective-permute-done((bf16[2,64,704]{2,1,0:T(8,128)(2,1)}, bf16[2,64,704]{2,1,0:T(8,128)(2,1)S(1)}, u32[]{:S(2)}, u32[]{:S(2)}) %collective-permute-start.31) | collective-permute-done | bytes 180256 | tf_op jit(solution)/shard_map/ppermute | solution.py:55
  539.8 3.9 all-to-all-start.5
  545.4 17.5 %collective-permute-done.46.refs_2_ = bf16[96,2048]{1,0:T(8,128)(2,1)S(1)} collective-permute-done((bf16[96,2048]{1,0:T(8,128)(2,1)S(1)}, bf16[96,2048]{1,0:T(8,128)(2,1)S(1)}, u32[]{:S(2)}, u32[]{:S(2)}) %collective-permute-start.46) | collective-permute-done | bytes 393248 | tf_op jit(solution)/shard_map/ppermute | solution.py:55
  565.0 10.0 %collective-permute-done.48.refs_4_ = bf16[96,2048]{1,0:T(8,128)(2,1)} collective-permute-done((bf16[96,2048]{1,0:T(8,128)(2,1)S(1)}, bf16[96,2048]{1,0:T(8,128)(2,1)}, u32[]{:S(2)}, u32[]{:S(2)}) %collective-permute-start.48) | collective-permute-done | bytes 393248 | tf_op jit(solution)/shard_map/ppermute | solution.py:55
  577.0 15.5 %collective-permute-done.51.refs_7_ = bf16[80,2048]{1,0:T(8,128)(2,1)S(1)} collective-permute-done((bf16[80,2048]{1,0:T(8,128)(2,1)}, bf16[80,2048]{1,0:T(8,128)(2,1)S(1)}, u32[]{:S(2)}, u32[]{:S(2)}) %collective-permute-start.51) | collective-permute-done | bytes 327712 | tf_op jit(solution)/shard_map/ppermute | solution.py:55
  593.0 31.1 %collective-permute-done.50.refs_6_ = bf16[96,2048]{1,0:T(8,128)(2,1)S(1)} collective-permute-done((bf16[96,2048]{1,0:T(8,128)(2,1)S(1)}, bf16[96,2048]{1,0:T(8,128)(2,1)S(1)}, u32[]{:S(2)}, u32[]{:S(2)}) %collective-permute-start.50) | collective-permute-done | bytes 393248 | tf_op jit(solution)/shard_map/ppermute | solution.py:55
  625.5 4.7 shard_map.221
  630.1 4.7 shard_map.219
  634.8 4.8 shard_map.220
  648.5 3.8 shard_map.214
  654.0 3.0 shard_map.216
  658.9 10.2 %collective-permute-done.16.refs_2_ = bf16[256,768]{1,0:T(8,128)(2,1)} collective-permute-done((bf16[256,768]{1,0:T(8,128)(2,1)}, bf16[256,768]{1,0:T(8,128)(2,1)}, u32[]{:S(2)}, u32[]{:S(2)}) %collective-permute-start.16) | collective-permute-done | bytes 393248 | tf_op jit(solution)/shard_map/ppermute | solution.py:55
  669.1 3.1 shard_map.215
  (244 shorter events, 117.2 us)
Async XLA Ops:
  7.2 40.8 %all-gather.5.cloned.1.call-start = ((), (), s32[]{:S(2)}) async-start(), calls=%async_computation.10 | async-start | bytes 2949120 | tf_op jit(solution)/shard_map/all_gather | solution.py:530
  10.3 67.1 %all-gather.7.cloned.1.call-start = ((), (), s32[]{:S(2)}) async-start(), calls=%async_computation.11 | async-start | bytes 2359296 | tf_op jit(solution)/shard_map/all_gather | solution.py:531
  12.0 203.3 %all-gather.11.cloned.1.call-start = ((), (), s32[]{:S(2)}) async-start(), calls=%async_computation.13 | async-start | bytes 4718592 | tf_op jit(solution)/shard_map/all_gather | solution.py:556
  14.8 31.6 %all-to-all-start = ((bf16[4,128,2176]{2,1,0:T(8,128)(2,1)}), bf16[4,128,2176]{2,1,0:T(8,128)(2,1)S(1)}, u32[]{:S(2)}, u32[]{:S(2)}) async-start(bf16[4,128,2176]{2,1,0:T(8,128)(2,1)} %broadcast_in_dim.18), calls=%async_computation | async-start | bytes 4456448 | tf_op jit(solution)/shard_map/all_to_all | solution.py:43
  20.1 195.3 %all-gather.9.cloned.1.call-start = ((), (), s32[]{:S(2)}) async-start(), calls=%async_computation.12 | async-start | bytes 4718592 | tf_op jit(solution)/shard_map/all_gather | solution.py:602
  113.5 207.8 %reduce-scatter.7.cloned.1.call-start = ((), (), s32[]{:S(2)}) async-start(), calls=%async_computation.15 | async-start | bytes 4718592 | tf_op jit(solution)/shard_map/reduce_scatter | solution.py:614
  117.9 18.2 %collective-permute-start.2 = (bf16[2,64,704]{2,1,0:T(8,128)(2,1)}, bf16[2,64,704]{2,1,0:T(8,128)(2,1)S(1)}, u32[]{:S(2)}, u32[]{:S(2)}) collective-permute-start(bf16[2,64,704]{2,1,0:T(8,128)(2,1)} %get-tuple-element.78), channel_id=1, source_target_pairs={{0,2},{1,3},{2,0},{3,1},{4,6},{5,7},{6,4},{7,5},{8,10},{9,11},{10,... | collective-permute-start | bytes 540680 | tf_op jit(solution)/shard_map/ppermute | solution.py:55
  122.3 17.8 %collective-permute-start.3 = (bf16[2,64,704]{2,1,0:T(8,128)(2,1)}, bf16[2,64,704]{2,1,0:T(8,128)(2,1)S(1)}, u32[]{:S(2)}, u32[]{:S(2)}) collective-permute-start(bf16[2,64,704]{2,1,0:T(8,128)(2,1)} %get-tuple-element.79), channel_id=1, source_target_pairs={{0,3},{1,2},{2,1},{3,0},{4,7},{5,6},{6,5},{7,4},{8,11},{9,10},{10,... | collective-permute-start | bytes 540680 | tf_op jit(solution)/shard_map/ppermute | solution.py:55
  122.4 17.6 %collective-permute-start.4 = (bf16[2,64,704]{2,1,0:T(8,128)(2,1)}, bf16[2,64,704]{2,1,0:T(8,128)(2,1)S(1)}, u32[]{:S(2)}, u32[]{:S(2)}) collective-permute-start(bf16[2,64,704]{2,1,0:T(8,128)(2,1)} %get-tuple-element.80), channel_id=1, source_target_pairs={{0,4},{1,5},{2,6},{3,7},{4,0},{5,1},{6,2},{7,3},{8,12},{9,13},{10,... | collective-permute-start | bytes 540680 | tf_op jit(solution)/shard_map/ppermute | solution.py:55
  123.3 28.8 %collective-permute-start.5 = (bf16[2,64,704]{2,1,0:T(8,128)(2,1)}, bf16[2,64,704]{2,1,0:T(8,128)(2,1)S(1)}, u32[]{:S(2)}, u32[]{:S(2)}) collective-permute-start(bf16[2,64,704]{2,1,0:T(8,128)(2,1)} %get-tuple-element.81), channel_id=1, source_target_pairs={{0,5},{1,4},{2,7},{3,6},{4,1},{5,0},{6,3},{7,2},{8,13},{9,12},{10,... | collective-permute-start | bytes 540680 | tf_op jit(solution)/shard_map/ppermute | solution.py:55
  124.8 27.3 %collective-permute-start.6 = (bf16[2,64,704]{2,1,0:T(8,128)(2,1)}, bf16[2,64,704]{2,1,0:T(8,128)(2,1)S(1)}, u32[]{:S(2)}, u32[]{:S(2)}) collective-permute-start(bf16[2,64,704]{2,1,0:T(8,128)(2,1)} %get-tuple-element.82), channel_id=1, source_target_pairs={{0,6},{1,7},{2,4},{3,5},{4,2},{5,3},{6,0},{7,1},{8,14},{9,15},{10,... | collective-permute-start | bytes 540680 | tf_op jit(solution)/shard_map/ppermute | solution.py:55
  136.0 17.2 %collective-permute-start.7 = (bf16[2,64,704]{2,1,0:T(8,128)(2,1)}, bf16[2,64,704]{2,1,0:T(8,128)(2,1)S(1)}, u32[]{:S(2)}, u32[]{:S(2)}) collective-permute-start(bf16[2,64,704]{2,1,0:T(8,128)(2,1)} %get-tuple-element.83), channel_id=1, source_target_pairs={{0,7},{1,6},{2,5},{3,4},{4,3},{5,2},{6,1},{7,0},{8,15},{9,14},{10,... | collective-permute-start | bytes 540680 | tf_op jit(solution)/shard_map/ppermute | solution.py:55
  157.2 17.7 %collective-permute-start.11 = (bf16[8,64,704]{2,1,0:T(8,128)(2,1)}, bf16[8,64,704]{2,1,0:T(8,128)(2,1)S(1)}, u32[]{:S(2)}, u32[]{:S(2)}) collective-permute-start(bf16[8,64,704]{2,1,0:T(8,128)(2,1)} %get-tuple-element.85.refs_1_), channel_id=1, source_target_pairs={{0,16},{8,24},{16,0},{24,8},{1,17},{9,25},{17,1},{25,9},{2,18},{10... | collective-permute-start | bytes 2162696 | tf_op jit(solution)/shard_map/ppermute | solution.py:55
  158.7 30.5 %collective-permute-start.9 = (bf16[8,64,704]{2,1,0:T(8,128)(2,1)}, bf16[8,64,704]{2,1,0:T(8,128)(2,1)S(1)}, u32[]{:S(2)}, u32[]{:S(2)}) collective-permute-start(bf16[8,64,704]{2,1,0:T(8,128)(2,1)} %get-tuple-element.85.refs_1_), channel_id=1, source_target_pairs={{0,8},{8,0},{16,24},{24,16},{1,9},{9,1},{17,25},{25,17},{2,10},{10... | collective-permute-start | bytes 2162696 | tf_op jit(solution)/shard_map/ppermute | solution.py:55
  159.3 31.6 %collective-permute-start.10 = (bf16[8,64,704]{2,1,0:T(8,128)(2,1)}, bf16[8,64,704]{2,1,0:T(8,128)(2,1)S(1)}, u32[]{:S(2)}, u32[]{:S(2)}) collective-permute-start(bf16[8,64,704]{2,1,0:T(8,128)(2,1)} %get-tuple-element.84.refs_0_), channel_id=1, source_target_pairs={{0,16},{8,24},{16,0},{24,8},{1,17},{9,25},{17,1},{25,9},{2,18},{10... | collective-permute-start | bytes 2162696 | tf_op jit(solution)/shard_map/ppermute | solution.py:55
  172.4 35.2 %collective-permute-start.12 = (bf16[8,64,704]{2,1,0:T(8,128)(2,1)S(1)}, bf16[8,64,704]{2,1,0:T(8,128)(2,1)S(1)}, u32[]{:S(2)}, u32[]{:S(2)}) collective-permute-start(bf16[8,64,704]{2,1,0:T(8,128)(2,1)S(1)} %collective-permute-done.8.refs_2_), channel_id=1, source_target_pairs={{0,16},{8,24},{16,0},{24,8},{1,17},{9,25},{17,1},{25,9},{2,18},{10... | collective-permute-start | bytes 2162696 | tf_op jit(solution)/shard_map/ppermute | solution.py:55
  174.9 32.6 %collective-permute-start.13 = (bf16[8,64,704]{2,1,0:T(8,128)(2,1)S(1)}, bf16[8,64,704]{2,1,0:T(8,128)(2,1)S(1)}, u32[]{:S(2)}, u32[]{:S(2)}) collective-permute-start(bf16[8,64,704]{2,1,0:T(8,128)(2,1)S(1)} %collective-permute-done.11.refs_5_), channel_id=1, source_target_pairs={{0,8},{8,0},{16,24},{24,16},{1,9},{9,1},{17,25},{25,17},{2,10},{10... | collective-permute-start | bytes 2162696 | tf_op jit(solution)/shard_map/ppermute | solution.py:55
  240.8 383.3 %reduce-scatter.11.cloned.1.call-start = ((), (), s32[]{:S(2)}) async-start(), calls=%async_computation.17 | async-start | bytes 2359296 | tf_op jit(solution)/shard_map/reduce_scatter | solution.py:671
  357.2 284.5 %reduce-scatter.9.cloned.1.call-start = ((), (), s32[]{:S(2)}) async-start(), calls=%async_computation.16 | async-start | bytes 3538944 | tf_op jit(solution)/shard_map/reduce_scatter | solution.py:712
  393.7 251.5 %reduce-scatter.5.cloned.1.call-start = ((), (), s32[]{:S(2)}) async-start(), calls=%async_computation.14 | async-start | bytes 4718592 | tf_op jit(solution)/shard_map/reduce_scatter | solution.py:630
  421.5 38.5 %collective-permute-start.21 = (bf16[8,64,704]{2,1,0:T(8,128)(2,1)}, bf16[8,64,704]{2,1,0:T(8,128)(2,1)S(1)}, u32[]{:S(2)}, u32[]{:S(2)}) collective-permute-start(bf16[8,64,704]{2,1,0:T(8,128)(2,1)} %get-tuple-element.110), channel_id=1, source_target_pairs={{0,8},{8,0},{16,24},{24,16},{1,9},{9,1},{17,25},{25,17},{2,10},{10... | collective-permute-start | bytes 2162696 | tf_op jit(solution)/shard_map/ppermute | solution.py:55
  423.1 38.9 %collective-permute-start.24 = (bf16[8,64,704]{2,1,0:T(8,128)(2,1)}, bf16[8,64,704]{2,1,0:T(8,128)(2,1)S(1)}, u32[]{:S(2)}, u32[]{:S(2)}) collective-permute-start(bf16[8,64,704]{2,1,0:T(8,128)(2,1)} %get-tuple-element.113), channel_id=1, source_target_pairs={{0,16},{8,24},{16,0},{24,8},{1,17},{9,25},{17,1},{25,9},{2,18},{10... | collective-permute-start | bytes 2162696 | tf_op jit(solution)/shard_map/ppermute | solution.py:55
  426.2 32.7 %collective-permute-start.44 = (bf16[80,2048]{1,0:T(8,128)(2,1)}, bf16[80,2048]{1,0:T(8,128)(2,1)}, u32[]{:S(2)}, u32[]{:S(2)}) collective-permute-start(bf16[80,2048]{1,0:T(8,128)(2,1)} %get-tuple-element.130), channel_id=1, source_target_pairs={{0,16},{8,24},{16,0},{24,8},{1,17},{9,25},{17,1},{25,9},{2,18},{10... | collective-permute-start | bytes 983048 | tf_op jit(solution)/shard_map/ppermute | solution.py:55
  436.0 39.7 %collective-permute-start.23 = (bf16[8,64,704]{2,1,0:T(8,128)(2,1)}, bf16[8,64,704]{2,1,0:T(8,128)(2,1)S(1)}, u32[]{:S(2)}, u32[]{:S(2)}) collective-permute-start(bf16[8,64,704]{2,1,0:T(8,128)(2,1)} %add_convert_fusion.1), channel_id=1, source_target_pairs={{0,16},{8,24},{16,0},{24,8},{1,17},{9,25},{17,1},{25,9},{2,18},{10... | collective-permute-start | bytes 2162696 | tf_op jit(solution)/shard_map/ppermute | solution.py:55
  439.1 36.6 %collective-permute-start.26 = (bf16[8,64,704]{2,1,0:T(8,128)(2,1)}, bf16[8,64,704]{2,1,0:T(8,128)(2,1)S(1)}, u32[]{:S(2)}, u32[]{:S(2)}) collective-permute-start(bf16[8,64,704]{2,1,0:T(8,128)(2,1)} %add_convert_fusion), channel_id=1, source_target_pairs={{0,8},{8,0},{16,24},{24,16},{1,9},{9,1},{17,25},{25,17},{2,10},{10... | collective-permute-start | bytes 2162696 | tf_op jit(solution)/shard_map/ppermute | solution.py:55
  458.9 37.4 %collective-permute-start.41 = (bf16[96,2048]{1,0:T(8,128)(2,1)S(1)}, bf16[96,2048]{1,0:T(8,128)(2,1)S(1)}, u32[]{:S(2)}, u32[]{:S(2)}) collective-permute-start(bf16[96,2048]{1,0:T(8,128)(2,1)S(1)} %get-tuple-element.132), channel_id=1, source_target_pairs={{0,8},{8,0},{16,24},{24,16},{1,9},{9,1},{17,25},{25,17},{2,10},{10... | collective-permute-start | bytes 1179656 | tf_op jit(solution)/shard_map/ppermute | solution.py:55
  460.0 36.3 %collective-permute-start.43 = (bf16[80,2048]{1,0:T(8,128)(2,1)}, bf16[80,2048]{1,0:T(8,128)(2,1)S(1)}, u32[]{:S(2)}, u32[]{:S(2)}) collective-permute-start(bf16[80,2048]{1,0:T(8,128)(2,1)} %get-tuple-element.129), channel_id=1, source_target_pairs={{0,16},{8,24},{16,0},{24,8},{1,17},{9,25},{17,1},{25,9},{2,18},{10... | collective-permute-start | bytes 983048 | tf_op jit(solution)/shard_map/ppermute | solution.py:55
  462.1 37.0 %collective-permute-start.45 = (bf16[80,2048]{1,0:T(8,128)(2,1)S(1)}, bf16[80,2048]{1,0:T(8,128)(2,1)S(1)}, u32[]{:S(2)}, u32[]{:S(2)}) collective-permute-start(bf16[80,2048]{1,0:T(8,128)(2,1)S(1)} %add_convert_fusion.6), channel_id=1, source_target_pairs={{0,8},{8,0},{16,24},{24,16},{1,9},{9,1},{17,25},{25,17},{2,10},{10... | collective-permute-start | bytes 983048 | tf_op jit(solution)/shard_map/ppermute | solution.py:55
  481.3 18.6 %collective-permute-start.27 = (bf16[2,64,704]{2,1,0:T(8,128)(2,1)}, bf16[2,64,704]{2,1,0:T(8,128)(2,1)S(1)}, u32[]{:S(2)}, u32[]{:S(2)}) collective-permute-start(bf16[2,64,704]{2,1,0:T(8,128)(2,1)} %get-tuple-element.117), channel_id=1, source_target_pairs={{0,1},{1,0},{2,3},{3,2},{4,5},{5,4},{6,7},{7,6},{8,9},{9,8},{10,11... | collective-permute-start | bytes 540680 | tf_op jit(solution)/shard_map/ppermute | solution.py:55
  499.1 35.5 %collective-permute-start.40 = (bf16[96,2048]{1,0:T(8,128)(2,1)S(1)}, bf16[96,2048]{1,0:T(8,128)(2,1)S(1)}, u32[]{:S(2)}, u32[]{:S(2)}) collective-permute-start(bf16[96,2048]{1,0:T(8,128)(2,1)S(1)} %get-tuple-element.131), channel_id=1, source_target_pairs={{0,8},{8,0},{16,24},{24,16},{1,9},{9,1},{17,25},{25,17},{2,10},{10... | collective-permute-start | bytes 1179656 | tf_op jit(solution)/shard_map/ppermute | solution.py:55
  499.9 36.2 %collective-permute-start.42 = (bf16[96,2048]{1,0:T(8,128)(2,1)S(1)}, bf16[96,2048]{1,0:T(8,128)(2,1)S(1)}, u32[]{:S(2)}, u32[]{:S(2)}) collective-permute-start(bf16[96,2048]{1,0:T(8,128)(2,1)S(1)} %add_convert_fusion.4), channel_id=1, source_target_pairs={{0,16},{8,24},{16,0},{24,8},{1,17},{9,25},{17,1},{25,9},{2,18},{10... | collective-permute-start | bytes 1179656 | tf_op jit(solution)/shard_map/ppermute | solution.py:55
  506.5 22.0 %collective-permute-start.31 = (bf16[2,64,704]{2,1,0:T(8,128)(2,1)}, bf16[2,64,704]{2,1,0:T(8,128)(2,1)S(1)}, u32[]{:S(2)}, u32[]{:S(2)}) collective-permute-start(bf16[2,64,704]{2,1,0:T(8,128)(2,1)} %get-tuple-element.121), channel_id=1, source_target_pairs={{0,5},{1,4},{2,7},{3,6},{4,1},{5,0},{6,3},{7,2},{8,13},{9,12},{10,... | collective-permute-start | bytes 540680 | tf_op jit(solution)/shard_map/ppermute | solution.py:55
  509.4 19.8 %collective-permute-start.32 = (bf16[2,64,704]{2,1,0:T(8,128)(2,1)}, bf16[2,64,704]{2,1,0:T(8,128)(2,1)S(1)}, u32[]{:S(2)}, u32[]{:S(2)}) collective-permute-start(bf16[2,64,704]{2,1,0:T(8,128)(2,1)} %get-tuple-element.122), channel_id=1, source_target_pairs={{0,6},{1,7},{2,4},{3,5},{4,2},{5,3},{6,0},{7,1},{8,14},{9,15},{10,... | collective-permute-start | bytes 540680 | tf_op jit(solution)/shard_map/ppermute | solution.py:55
  511.6 18.9 %collective-permute-start.33 = (bf16[2,64,704]{2,1,0:T(8,128)(2,1)}, bf16[2,64,704]{2,1,0:T(8,128)(2,1)S(1)}, u32[]{:S(2)}, u32[]{:S(2)}) collective-permute-start(bf16[2,64,704]{2,1,0:T(8,128)(2,1)} %get-tuple-element.123), channel_id=1, source_target_pairs={{0,7},{1,6},{2,5},{3,4},{4,3},{5,2},{6,1},{7,0},{8,15},{9,14},{10,... | collective-permute-start | bytes 540680 | tf_op jit(solution)/shard_map/ppermute | solution.py:55
  534.1 29.4 %collective-permute-start.34 = (bf16[64,5632]{1,0:T(8,128)(2,1)}, bf16[64,5632]{1,0:T(8,128)(2,1)}, u32[]{:S(2)}, u32[]{:S(2)}) collective-permute-start(bf16[64,5632]{1,0:T(8,128)(2,1)} %get-tuple-element.124.refs_0_), channel_id=1, source_target_pairs={{0,8},{8,0},{16,24},{24,16},{1,9},{9,1},{17,25},{25,17},{2,10},{10... | collective-permute-start | bytes 2162696 | tf_op jit(solution)/shard_map/ppermute | solution.py:55
  534.6 40.4 %collective-permute-start.38 = (bf16[64,5632]{1,0:T(8,128)(2,1)}, bf16[64,5632]{1,0:T(8,128)(2,1)}, u32[]{:S(2)}, u32[]{:S(2)}) collective-permute-start(bf16[64,5632]{1,0:T(8,128)(2,1)} %get-tuple-element.125.refs_0_), channel_id=1, source_target_pairs={{0,16},{8,24},{16,0},{24,8},{1,17},{9,25},{17,1},{25,9},{2,18},{10... | collective-permute-start | bytes 2162696 | tf_op jit(solution)/shard_map/ppermute | solution.py:55
  537.3 25.6 %collective-permute-start.46 = (bf16[96,2048]{1,0:T(8,128)(2,1)S(1)}, bf16[96,2048]{1,0:T(8,128)(2,1)S(1)}, u32[]{:S(2)}, u32[]{:S(2)}) collective-permute-start(bf16[96,2048]{1,0:T(8,128)(2,1)S(1)} %add_convert_fusion.3.refs_0_), channel_id=1, source_target_pairs={{0,8},{8,0},{16,24},{24,16},{1,9},{9,1},{17,25},{25,17},{2,10},{10... | collective-permute-start | bytes 1179656 | tf_op jit(solution)/shard_map/ppermute | solution.py:55
  539.1 35.9 %collective-permute-start.48 = (bf16[96,2048]{1,0:T(8,128)(2,1)S(1)}, bf16[96,2048]{1,0:T(8,128)(2,1)}, u32[]{:S(2)}, u32[]{:S(2)}) collective-permute-start(bf16[96,2048]{1,0:T(8,128)(2,1)S(1)} %add_convert_fusion.3.refs_0_), channel_id=1, source_target_pairs={{0,16},{8,24},{16,0},{24,8},{1,17},{9,25},{17,1},{25,9},{2,18},{10... | collective-permute-start | bytes 1179656 | tf_op jit(solution)/shard_map/ppermute | solution.py:55
  539.8 107.4 %all-to-all-start.5 = ((bf16[4,128,2048]{2,1,0:T(8,128)(2,1)}), bf16[4,128,2048]{2,1,0:T(8,128)(2,1)S(1)}, u32[]{:S(2)}, u32[]{:S(2)}) async-start(bf16[4,128,2048]{2,1,0:T(8,128)(2,1)} %get-tuple-element.102), calls=%async_computation.7 | async-start | bytes 4194304 | tf_op jit(solution)/shard_map/all_to_all | solution.py:47
  543.7 48.8 %collective-permute-start.51 = (bf16[80,2048]{1,0:T(8,128)(2,1)}, bf16[80,2048]{1,0:T(8,128)(2,1)S(1)}, u32[]{:S(2)}, u32[]{:S(2)}) collective-permute-start(bf16[80,2048]{1,0:T(8,128)(2,1)} %collective-permute-done.49.refs_5_), channel_id=1, source_target_pairs={{0,8},{8,0},{16,24},{24,16},{1,9},{9,1},{17,25},{25,17},{2,10},{10... | collective-permute-start | bytes 983048 | tf_op jit(solution)/shard_map/ppermute | solution.py:55
  562.9 67.2 %collective-permute-start.35 = (bf16[64,5632]{1,0:T(8,128)(2,1)}, bf16[64,5632]{1,0:T(8,128)(2,1)}, u32[]{:S(2)}, u32[]{:S(2)}) collective-permute-start(bf16[64,5632]{1,0:T(8,128)(2,1)} %get-tuple-element.124.refs_0_), channel_id=1, source_target_pairs={{0,16},{8,24},{16,0},{24,8},{1,17},{9,25},{17,1},{25,9},{2,18},{10... | collective-permute-start | bytes 2162696 | tf_op jit(solution)/shard_map/ppermute | solution.py:55
  563.5 66.7 %collective-permute-start.36 = (bf16[64,5632]{1,0:T(8,128)(2,1)}, bf16[64,5632]{1,0:T(8,128)(2,1)}, u32[]{:S(2)}, u32[]{:S(2)}) collective-permute-start(bf16[64,5632]{1,0:T(8,128)(2,1)} %collective-permute-done.34.refs_1_), channel_id=1, source_target_pairs={{0,16},{8,24},{16,0},{24,8},{1,17},{9,25},{17,1},{25,9},{2,18},{10... | collective-permute-start | bytes 2162696 | tf_op jit(solution)/shard_map/ppermute | solution.py:55
  575.0 59.8 %collective-permute-start.37 = (bf16[64,5632]{1,0:T(8,128)(2,1)}, bf16[64,5632]{1,0:T(8,128)(2,1)}, u32[]{:S(2)}, u32[]{:S(2)}) collective-permute-start(bf16[64,5632]{1,0:T(8,128)(2,1)} %get-tuple-element.125.refs_0_), channel_id=1, source_target_pairs={{0,8},{8,0},{16,24},{24,16},{1,9},{9,1},{17,25},{25,17},{2,10},{10... | collective-permute-start | bytes 2162696 | tf_op jit(solution)/shard_map/ppermute | solution.py:55
  575.0 59.8 %collective-permute-start.39 = (bf16[64,5632]{1,0:T(8,128)(2,1)}, bf16[64,5632]{1,0:T(8,128)(2,1)}, u32[]{:S(2)}, u32[]{:S(2)}) collective-permute-start(bf16[64,5632]{1,0:T(8,128)(2,1)} %collective-permute-done.38.refs_2_), channel_id=1, source_target_pairs={{0,8},{8,0},{16,24},{24,16},{1,9},{9,1},{17,25},{25,17},{2,10},{10... | collective-permute-start | bytes 2162696 | tf_op jit(solution)/shard_map/ppermute | solution.py:55
  592.5 31.6 %collective-permute-start.50 = (bf16[96,2048]{1,0:T(8,128)(2,1)S(1)}, bf16[96,2048]{1,0:T(8,128)(2,1)S(1)}, u32[]{:S(2)}, u32[]{:S(2)}) collective-permute-start(bf16[96,2048]{1,0:T(8,128)(2,1)S(1)} %collective-permute-done.46.refs_2_), channel_id=1, source_target_pairs={{0,16},{8,24},{16,0},{24,8},{1,17},{9,25},{17,1},{25,9},{2,18},{10... | collective-permute-start | bytes 1179656 | tf_op jit(solution)/shard_map/ppermute | solution.py:55
  624.1 19.7 %collective-permute-start.18 = (bf16[64,2048]{1,0:T(8,128)(2,1)}, bf16[64,2048]{1,0:T(8,128)(2,1)}, u32[]{:S(2)}, u32[]{:S(2)}) collective-permute-start(bf16[64,2048]{1,0:T(8,128)(2,1)} %reduce-scatter.11.cloned.1.call-done.refs_0_), channel_id=1, source_target_pairs={{0,8},{8,0},{16,24},{24,16},{1,9},{9,1},{17,25},{25,17},{2,10},{10... | collective-permute-start | bytes 786440 | tf_op jit(solution)/shard_map/ppermute | solution.py:55
  643.1 26.0 %collective-permute-start.16 = (bf16[256,768]{1,0:T(8,128)(2,1)}, bf16[256,768]{1,0:T(8,128)(2,1)}, u32[]{:S(2)}, u32[]{:S(2)}) collective-permute-start(bf16[256,768]{1,0:T(8,128)(2,1)} %reduce-scatter.9.cloned.1.call-done.refs_0_), channel_id=1, source_target_pairs={{0,16},{8,24},{16,0},{24,8},{1,17},{9,25},{17,1},{25,9},{2,18},{10... | collective-permute-start | bytes 1179656 | tf_op jit(solution)/shard_map/ppermute | solution.py:55
  643.8 25.3 %collective-permute-start.17 = (bf16[256,768]{1,0:T(8,128)(2,1)}, bf16[256,768]{1,0:T(8,128)(2,1)}, u32[]{:S(2)}, u32[]{:S(2)}) collective-permute-start(bf16[256,768]{1,0:T(8,128)(2,1)} %reduce-scatter.9.cloned.1.call-done.refs_0_), channel_id=1, source_target_pairs={{0,24},{8,16},{16,8},{24,0},{1,25},{9,17},{17,9},{25,1},{2,26},{10... | collective-permute-start | bytes 1179656 | tf_op jit(solution)/shard_map/ppermute | solution.py:55
  (62 other events, 759.0 us)
Sparse Core Ops, SparseCore 0:
  10.4 36.4 all-gather.4
  49.1 28.2 all-gather.6
  79.0 47.0 all-gather.10
  128.1 67.1 all-gather.8
  240.9 80.3 reduce-scatter.6
  357.3 35.3 reduce-scatter.10
  395.0 44.2 reduce-scatter.8
  441.6 49.1 reduce-scatter.4

commit v4 on v3

--- a/solution.py
+++ b/solution.py
@@ -277,9 +277,17 @@
     return jnp.where(lane < HD, turn(tile, cosine, sine), tile)
 
 
-def in_kernel(x_ref, gain_ref, w_ref, cos_ref, sin_ref, normed_ref, q_ref, kv_ref):
+def in_kernel(
+    x_ref, w_ref, lane_ref, cos_ref, sin_ref, normed_ref, q_ref, kv_ref, gain_ref
+):
+    @pl.when(pl.program_id(0) == 0)
+    def _():
+        row = lax.broadcasted_iota(jnp.int32, (gain_ref.shape[0], LANES), 0)
+        lane = lax.broadcasted_iota(jnp.int32, (gain_ref.shape[0], LANES), 1)
+        gain_ref[...] = cols_cols((lane == row * HD).astype(BF), lane_ref[...])
+
     x = x_ref[0].astype(F32)
-    normed = (x * norm_scale(x) * gain_ref[...]).astype(BF)
+    normed = (x * norm_scale(x) * gain_ref[0:1]).astype(BF)
     normed_ref[0] = normed
     qkv = rows_cols(normed, w_ref[...])
     cosine, sine = cos_ref[0], sin_ref[0]
@@ -287,6 +295,41 @@
     for at in range(0, q_cols, LANES):
         q_ref[0, :, at : at + LANES] = turn(qkv[:, at : at + LANES], cosine, sine).astype(BF)
     kv_ref[0] = turn_first(qkv[:, q_cols:], cosine, sine).astype(BF)
+
+
+def out_kernel(heads_ref, w_ref, part_ref, joined_ref):
+    cols = part_ref.shape[2]
+
+    @pl.when(pl.program_id(0) == 0)
+    def _():
+        joined_ref[...] = jnp.concatenate(
+            [heads_ref[source] for source in range(heads_ref.shape[0])], axis=1
+        )
+
+    w = w_ref[:, 0].reshape(joined_ref.shape[1], w_ref.shape[3])[:, :cols]
+    part = rows_cols(joined_ref[...], w).astype(BF)
+    part_ref[...] = part.reshape(part_ref.shape)
+
+
+def out_back_kernel(grad_ref, w_ref, heads_ref, total_ref):
+    at = pl.program_id(0)
+    cols = grad_ref.shape[1]
+    w = w_ref[:, 0].reshape(total_ref.shape[1], w_ref.shape[3])[:, :cols]
+    part = cols_cols(grad_ref[...], w)
+
+    @pl.when(at == 0)
+    def _():
+        total_ref[...] = part
+
+    @pl.when(at > 0)
+    def _():
+        total_ref[...] += part
+
+    @pl.when(at == pl.num_programs(0) - 1)
+    def _():
+        size = heads_ref.shape[2]
+        for source in range(heads_ref.shape[0]):
+            heads_ref[source] = total_ref[:, source * size : (source + 1) * size].astype(BF)
 
 
 def stack_heads(value):
@@ -403,7 +446,7 @@
     for at in range(part_ref.shape[0]):
         mid += part_ref[at].astype(F32)
     mid_ref[...] = mid
-    normed_ref[...] = (mid * norm_scale(mid) * gain_ref[...]).astype(BF)
+    normed_ref[...] = (mid * norm_scale(mid) * gain_ref[1:2]).astype(BF)
 
 
 def middle_back_kernel(grad_ref, mid_ref, gain_ref, cot_ref, out_ref, low_ref, gain_out_ref):
@@ -411,7 +454,7 @@
     scale = norm_scale(mid)
     grad = grad_ref[...].astype(F32)
     gain_out_ref[...] = (grad * mid * scale).astype(BF)
-    scaled = grad * gain_ref[...]
+    scaled = grad * gain_ref[1:2]
     out = (
         cot_ref[...].astype(F32)
         + scale * scaled
@@ -427,7 +470,7 @@
     grad = part_ref[0].astype(F32)
     for at in range(1, part_ref.shape[0]):
         grad += part_ref[at].astype(F32)
-    scaled = grad * gain_ref[...]
+    scaled = grad * gain_ref[0:1]
     out = (
         mid_ref[...]
         + scale * scaled
@@ -519,22 +562,20 @@
     )
     offset = jnp.broadcast_to((places[:, None] - first).astype(BF), (rows, LANES))
 
-    w_qkv_own = jnp.concatenate(
+    w_o_own = lax.dynamic_slice_in_dim(o_weight, r * fine, fine, 0)
+    w_own = jnp.concatenate(
         [
             lax.dynamic_slice_in_dim(q_weight, r * q_cols, q_cols, 1),
             lax.dynamic_slice_in_dim(k_weight, kv_at * HD, HD, 1),
             lax.dynamic_slice_in_dim(v_weight, kv_at * HD, HD, 1),
+            w_o_own.reshape(fine, n_rep, q_cols).transpose(1, 0, 2).reshape(own, q_cols),
+            jnp.broadcast_to(attn_gain[:, None], (own, HD)),
+            jnp.broadcast_to(mlp_gain[:, None], (own, LANES - HD)),
         ],
         axis=1,
     )
-    w_qkv = lax.all_gather(w_qkv_own, "shard", axis=0, tiled=True)
-    w_o = lax.all_gather(
-        lax.dynamic_slice_in_dim(o_weight, r * fine, fine, 0), "shard", axis=0, tiled=True
-    )
+    w_attn = lax.all_gather(w_own, "shard", axis=0, tiled=True)
     x_all = spread(jnp.concatenate([tokens, offset], axis=1), "rep", n_rep)
-    gains = lax.all_gather(jnp.stack([attn_gain, mlp_gain]), "shard", axis=1, tiled=True)
-    gain_one = gains[0:1].astype(F32)
-    gain_two = gains[1:2].astype(F32)
 
     def exchange_shard(pieces):
         rest = [send(pieces[k], "shard", n_shard, k) for k in range(1, n_shard)]
@@ -542,8 +583,7 @@
 
     block = (n_shard, fine, hidden)
     ids = jnp.stack([r, s]).astype(jnp.int32)
-    gate_tied, up_tied, _ = lax.optimization_barrier((gate_weight, up_weight, gains))
-    w_pair = split_pair(ids, gate_tied, up_tied, fine, n_shard)
+    w_pair = split_pair(ids, gate_weight, up_weight, fine, n_shard)
     w_pair = exchange_shard(w_pair)
     w_pair = flat_call(order_kernel, ids, (shape(block, BF),) * 2, w_pair)
     w_pair = gather_rep(w_pair, n_rep)
@@ -561,17 +601,25 @@
     cosine, sine = jnp.cos(angles), jnp.sin(angles)
     x_block = by_block((rows, width))
     table = by_block((rows, LANES))
-    normed_one, queries, kv_own = call(
+    w_qkv_block = whole((width, qkv_cols))
+    normed_one, queries, kv_own, gains = call(
         in_kernel,
         (
             shape((n_rep, rows, width), BF),
             shape((n_rep, rows, q_cols), BF),
             shape((n_rep, rows, LANES), BF),
+            shape((8, width), F32),
         ),
         (n_rep,),
-        [x_block, whole((1, width)), whole((width, qkv_cols)), table, table],
-        (x_block, by_block((rows, q_cols)), table),
-    )(x_all, gain_one, w_qkv, cosine, sine)
+        [
+            x_block,
+            w_qkv_block,
+            pl.BlockSpec((width, LANES), lambda g: (0, 2 * qkv_cols // LANES - 1)),
+            table,
+            table,
+        ],
+        (x_block, by_block((rows, q_cols)), table, pl.BlockSpec((8, width), lambda g: (0, 0))),
+    )(x_all, w_attn, w_attn, cosine, sine)
     kv_halo = lax.ppermute(
         kv_own[:, rows - HALO :], "shard", [(i, i + 1) for i in range(n_shard - 1)]
     )
@@ -593,11 +641,22 @@
         (probs_block, head_block),
     )(queries, kv_own, kv_halo, x_all)
     out_in = swap(out_in, "rep").reshape(n_rep, all_rows, pair * fine)
-    out_in = out_in.transpose(1, 0, 2).reshape(all_rows, q_cols)
-    mid_part = rows_cols(out_in, w_o).astype(BF).reshape(n_rep, rows, width)
+    w_out = w_attn.reshape(n_shard, n_rep, fine, 2 * qkv_cols)
+    w_out_block = pl.BlockSpec((n_shard, 1, fine, qkv_cols), lambda g: (0, g, 0, 1))
+    heads_block = whole((n_rep, all_rows, pair * fine))
+    mid_part, out_in = call(
+        out_kernel,
+        (shape((n_rep, rows, width), BF), shape((all_rows, q_cols), BF)),
+        (n_rep,),
+        [heads_block, w_out_block],
+        (
+            pl.BlockSpec((n_rep, rows, q_cols), lambda g: (0, 0, g)),
+            pl.BlockSpec((all_rows, q_cols), lambda g: (0, 0)),
+        ),
+    )(out_in, w_out)
     x_mid, normed_two = call(
         middle_kernel, (shape((rows, width), F32), shape((rows, width), BF))
-    )(swap(mid_part, "rep"), tokens, gain_two)
+    )(swap(mid_part, "rep"), tokens, gains)
 
     two_all = lax.all_gather(normed_two, "shard", axis=0, tiled=True)
     step = 256
@@ -615,7 +674,7 @@
     mid_grad, branch, gain_two_rows = call(
         middle_back_kernel,
         (shape((rows, width), F32), shape((rows, width), BF), shape((rows, width), BF)),
-    )(two_grad, x_mid, gain_two, cotangent)
+    )(two_grad, x_mid, gains, cotangent)
 
     gate_chunks = pair_grad(ids, two_all, gate_grad, fine, n_rep, n_shard)
     up_grad, _ = lax.optimization_barrier((up_grad, gate_chunks[0]))
@@ -663,9 +722,15 @@
     up_out = place([piece[1:] for piece in w_pair_grad], r)
 
     branch_all = spread(branch, "rep", n_rep).reshape(all_rows, width)
-    in_grad = cols_cols(branch_all, w_o).astype(BF)
+    in_grad = call(
+        out_back_kernel,
+        shape((n_rep, all_rows, pair * fine), BF),
+        (n_rep,),
+        [pl.BlockSpec((all_rows, q_cols), lambda g: (0, g)), w_out_block],
+        pl.BlockSpec((n_rep, all_rows, pair * fine), lambda g: (0, 0, 0)),
+        [pltpu.VMEM((all_rows, q_cols), F32)],
+    )(branch_all, w_out)
     branch_all, in_grad = lax.optimization_barrier((branch_all, in_grad))
-    in_grad = in_grad.reshape(all_rows, n_rep, pair * fine).transpose(1, 0, 2)
     in_grad = swap(in_grad, "rep").reshape(n_rep, n_rep, rows, pair * fine)
     w_o_grad = rows_rows(out_in, branch_all).astype(BF)
     w_o_grad = lax.psum_scatter(w_o_grad, "shard", scatter_dimension=0, tiled=True)
@@ -702,16 +767,16 @@
             x_block,
             x_block,
             whole((rows, width)),
-            whole((width, qkv_cols)),
+            w_qkv_block,
         ],
         (x_block, pl.BlockSpec((width, grad_cols), lambda g: (0, 0))),
         [pltpu.VMEM((width, grad_cols), F32)],
     )(
-        query_grad, kv_grad, kv_back, cosine, sine, normed_one, x_all, gain_two_rows, w_qkv
+        query_grad, kv_grad, kv_back, cosine, sine, normed_one, x_all, gain_two_rows, w_attn
     )
     w_qkv_grad = lax.psum_scatter(w_qkv_grad, "shard", scatter_dimension=0, tiled=True)
     input_grad = call(last_kernel, shape((rows, width), BF))(
-        swap(one_grad_part, "rep"), tokens, gain_one, mid_grad
+        swap(one_grad_part, "rep"), tokens, gains, mid_grad
     )
     q_out, k_out, v_out, gain_sums = flat_call(
         partial(qkv_kernel, share),

time: 685 us -> 724 us (1.057)
  waiting for transfers between devices: 316 us -> 364 us
  Pallas kernels: 126 us -> 137 us
  blocking collectives: 90.2 us -> 81.2 us
    ppermute x50, waiting for transfers between devices: 217 us -> 244 us  [send(): return lax.ppermute(value, axis, pairs(count, step))]
    all_gather x2 -> x1, waiting for transfers between devices: 2.3 us -> 23 us  [body(): w_attn = lax.all_gather(w_own, 'shard', axis=0, tiled=True)]
    reduce_scatter x1, waiting for transfers between devices: 80.5 us -> 66.8 us  [body(): lax.psum_scatter(two_grad_part, 'shard', scatter_dimension=0, tiled=True)]
    all_to_all x1, waiting for transfers between devices: 13.2 us -> 26.3 us  [spread(): return lax.all_to_all(wide, axis, split_axis=0, concat_axis=0, tiled=True)]
    all_gather x1 -> x0, blocking collectives: 12.3 us -> none  [body(): lax.all_gather(jnp.stack([attn_gain, mlp_gain]), 'shard', axis=1, tiled=T...]
    pallas_call x0 -> x2, Pallas kernels: none -> 10.3 us  [the longest x1 5.31 us: body(): call(out_back_kernel, shape((n_rep, all_rows, pair * fine), BF), (n_rep,)...]
    ppermute x50, starting transfers between devices: 69 us -> 61.3 us  [send(): return lax.ppermute(value, axis, pairs(count, step))]
    dot_general x5 -> x3, matrix products: 16.2 us -> 12.1 us  [dot(): lax.dot_general(left, right, (contract, ((), ())), preferred_element_type...]
  transfers between devices with their start and end apart: 62 -> 61, of which waited for: 27 -> 27; matrix products, arithmetic and copies ran while one was open for 5% -> 4% of each run, Pallas kernels for 14% -> 14%
where the time goes in v4:
time: 724 us; the launch traced here: 719 us
  waiting for transfers between devices  364 us (50%)
  Pallas kernels  137 us (19%)
  blocking collectives  81.2 us (11%)
  starting transfers between devices  74.4 us (10%)
  local copies, waits for them, and re-layouts  22.8 us (3%)
  between operations  14.6 us (2%)
  other arithmetic  13.8 us (2%)
  matrix products  12.1 us (2%)
    ppermute x50, waiting for transfers between devices, send(): return lax.ppermute(value, axis, pairs(count, step))  244 us
    reduce_scatter x1, waiting for transfers between devices, body(): lax.psum_scatter(two_grad_part, 'shard', scatter_dimension=0, tiled=True)  66.8 us
    ppermute x50, starting transfers between devices, send(): return lax.ppermute(value, axis, pairs(count, step))  61.3 us
    all_to_all x3, blocking collectives, swap(): return lax.all_to_all(value, axis, split_axis=0, concat_axis=0, tiled=True)  54.1 us
    all_to_all x1, blocking collectives, spread(): return lax.all_to_all(wide, axis, split_axis=0, concat_axis=0, tiled=True)  27 us
    all_to_all x1, waiting for transfers between devices, spread(): return lax.all_to_all(wide, axis, split_axis=0, concat_axis=0, tiled=True)  26.3 us
    pallas_call x1, Pallas kernels, body(): call(forward_back_kernel, (shape((group, hidden), BF),) * 3 + (shape((gro...  25.4 us
    all_gather x1, waiting for transfers between devices, body(): w_attn = lax.all_gather(w_own, 'shard', axis=0, tiled=True)  23 us
  transfers between devices with their start and end apart: 61, of which 27 were waited for; matrix products, arithmetic and copies ran while one was open for 4% of the time, Pallas kernels for 14%

profile of v4, /device:TPU:0, one launch (start us, length us, event | category | flops | bytes accessed | tf_op | source)
XLA Modules:
  0.0 719.2 jit_solution(14965712369637555443)
XLA Ops:
  14.7 5.2 all-to-all-start
  19.9 26.3 %all-to-all-done.x_ref.pos_ref = bf16[4,128,2176]{2,1,0:T(8,128)(2,1)S(1)} async-done(((bf16[4,128,2176]{2,1,0:T(8,128)(2,1)}), bf16[4,128,2176]{2,1,0:T(8,128)(2,1)S(1)}, u32[]{:S(2)}, u32[]{:S(2)}) %all-to-all-start) | async-done | bytes 2228256 | tf_op jit(solution)/shard_map/all_to_all | solution.py:43
  47.8 23.0 %all-gather.4.cloned.1.call-done.w_ref.lane_ref = bf16[2048,1280]{1,0:T(8,128)(2,1)} async-done(((bf16[256,1280]{1,0:T(8,128)(2,1)}), bf16[2048,1280]{1,0:T(8,128)(2,1)}) %all-gather.4.cloned.1.call-update) | async-done | bytes 5242896 | tf_op jit(solution)/shard_map/all_gather | solution.py:577
  70.8 6.5 shard_map.203
  81.8 6.4 shard_map.204
  88.2 13.2 %all_to_all.30 = bf16[4,4,128,128]{3,2,1,0:T(8,128)(2,1)} all-to-all(bf16[4,4,128,128]{3,2,1,0:T(8,128)(2,1)} %get-tuple-element.72), channel_id=1, replica_groups=mesh['rep'=4,'shard'=8] {'rep'}, dimensions={0} | all-to-all | bytes 1048576 | tf_op jit(solution)/shard_map/all_to_all | solution.py:47
  101.4 4.9 shard_map.205
  106.3 30.7 %all_to_all.31.part_ref = bf16[4,128,2048]{2,1,0:T(8,128)(2,1)} all-to-all(bf16[4,128,2048]{2,1,0:T(8,128)(2,1)} %get-tuple-element.73), channel_id=1, replica_groups=mesh['rep'=4,'shard'=8] {'rep'}, dimensions={0} | all-to-all | bytes 4194304 | tf_op jit(solution)/shard_map/all_to_all | solution.py:47
  137.0 3.3 shard_map.206
  141.1 3.4 split_pair.1
  150.1 17.2 %collective-permute-done.2.refs_2_ = bf16[2,64,704]{2,1,0:T(8,128)(2,1)S(1)} collective-permute-done((bf16[2,64,704]{2,1,0:T(8,128)(2,1)}, bf16[2,64,704]{2,1,0:T(8,128)(2,1)S(1)}, u32[]{:S(2)}, u32[]{:S(2)}) %collective-permute-start.2) | collective-permute-done | bytes 180256 | tf_op jit(solution)/shard_map/ppermute | solution.py:55
  167.3 8.0 %collective-permute-done.3.refs_3_ = bf16[2,64,704]{2,1,0:T(8,128)(2,1)S(1)} collective-permute-done((bf16[2,64,704]{2,1,0:T(8,128)(2,1)}, bf16[2,64,704]{2,1,0:T(8,128)(2,1)S(1)}, u32[]{:S(2)}, u32[]{:S(2)}) %collective-permute-start.3) | collective-permute-done | bytes 180256 | tf_op jit(solution)/shard_map/ppermute | solution.py:55
  175.3 19.4 %collective-permute-done.5.refs_5_ = bf16[2,64,704]{2,1,0:T(8,128)(2,1)S(1)} collective-permute-done((bf16[2,64,704]{2,1,0:T(8,128)(2,1)}, bf16[2,64,704]{2,1,0:T(8,128)(2,1)S(1)}, u32[]{:S(2)}, u32[]{:S(2)}) %collective-permute-start.5) | collective-permute-done | bytes 180256 | tf_op jit(solution)/shard_map/ppermute | solution.py:55
  204.8 16.6 %collective-permute-done.8.refs_2_ = bf16[8,64,704]{2,1,0:T(8,128)(2,1)S(1)} collective-permute-done((bf16[8,64,704]{2,1,0:T(8,128)(2,1)}, bf16[8,64,704]{2,1,0:T(8,128)(2,1)S(1)}, u32[]{:S(2)}, u32[]{:S(2)}) %collective-permute-start.8) | collective-permute-done | bytes 720928 | tf_op jit(solution)/shard_map/ppermute | solution.py:55
  223.4 14.8 %collective-permute-done.9.refs_3_ = bf16[8,64,704]{2,1,0:T(8,128)(2,1)S(1)} collective-permute-done((bf16[8,64,704]{2,1,0:T(8,128)(2,1)}, bf16[8,64,704]{2,1,0:T(8,128)(2,1)S(1)}, u32[]{:S(2)}, u32[]{:S(2)}) %collective-permute-start.9) | collective-permute-done | bytes 720928 | tf_op jit(solution)/shard_map/ppermute | solution.py:55
  239.0 16.2 %collective-permute-done.12.refs_6_ = bf16[8,64,704]{2,1,0:T(8,128)(2,1)S(1)} collective-permute-done((bf16[8,64,704]{2,1,0:T(8,128)(2,1)S(1)}, bf16[8,64,704]{2,1,0:T(8,128)(2,1)S(1)}, u32[]{:S(2)}, u32[]{:S(2)}) %collective-permute-start.12) | collective-permute-done | bytes 720928 | tf_op jit(solution)/shard_map/ppermute | solution.py:55
  257.1 5.8 shard_map.208
  262.9 25.4 %shard_map.209 = (bf16[1024,704]{1,0:T(8,128)(2,1)}, bf16[1024,704]{1,0:T(8,128)(2,1)}, bf16[1024,704]{1,0:T(8,128)(2,1)}, bf16[1024,2048]{1,0:T(8,128)(2,1)}) custom-call(bf16[1024,2048]{1,0:T(8,128)(2,1)} %all-gather.6.cloned.1.call-done.x_ref, bf16[1024,2048]{1,0:T(8,128)(2,1)} %all-gather.8.cloned.1.call-done.cot_ref, bf16[2,2048,704]{2,1,0:T(8,128)(2,1)} %bitcast.23, ...), custom_call_target="tpu_custom_call" | custom-call | tf_op jit(solution)/shard_map/pallas_call | solution.py:666
  288.6 66.8 %reduce-scatter.7.cloned.1.call-done.grad_ref = bf16[128,2048]{1,0:T(8,128)(2,1)} async-done(((bf16[1024,2048]{1,0:T(8,128)(2,1)}), bf16[128,2048]{1,0:T(8,128)(2,1)}) %reduce-scatter.7.cloned.1.call-update) | async-done | bytes 524304 | tf_op jit(solution)/shard_map/reduce_scatter | solution.py:673
  355.3 3.6 shard_map.212
  360.2 27.0 %all_to_all.32 = bf16[4,128,2048]{2,1,0:T(8,128)(2,1)} all-to-all(bf16[4,128,2048]{2,1,0:T(8,128)(2,1)S(1)} %broadcast_in_dim.25), channel_id=1, replica_groups=mesh['rep'=4,'shard'=8] {'rep'}, dimensions={0} | all-to-all | bytes 4194304 | tf_op jit(solution)/shard_map/all_to_all | solution.py:43
  387.2 5.3 shard_map.213
  396.2 10.2 %all_to_all.33 = bf16[4,512,128]{2,1,0:T(8,128)(2,1)} all-to-all(bf16[4,512,128]{2,1,0:T(8,128)(2,1)S(1)} %copy-done.9), channel_id=1, replica_groups=mesh['rep'=4,'shard'=8] {'rep'}, dimensions={0} | all-to-all | bytes 1048576 | tf_op jit(solution)/shard_map/all_to_all | solution.py:47
  406.4 8.3 %shard_map.214 = (bf16[4,128,512]{2,1,0:T(8,128)(2,1)}, f32[4,192,128]{2,1,0:T(8,128)}) custom-call(bf16[4,4,128,128]{3,2,1,0:T(8,128)(2,1)} %bitcast.29, f32[4,8,128,192]{3,2,1,0:T(8,128)} %get-tuple-element.98.probs_ref, bf16[4,128,512]{2,1,0:T(8,128)(2,1)} %get-tuple-element.70.q_ref, bf16[4,128,128]{2,1,0:T(8,128)(2,1)} %get-tuple-element.71.own_ref, ...), custom_call_target="tpu_custom_call" | custom-call | tf_op jit(solution)/shard_map/pallas_call | solution.py:738
  419.5 13.1 %shard_map.215 = (bf16[4,128,2048]{2,1,0:T(8,128)(2,1)}, bf16[2048,768]{1,0:T(8,128)(2,1)}) custom-call(bf16[4,128,512]{2,1,0:T(8,128)(2,1)} %get-tuple-element.99.dq_ref, f32[4,192,128]{2,1,0:T(8,128)} %get-tuple-element.100.dkv_ref, f32[4,64,128]{2,1,0:T(8,128)} %copy-done.43, f32[4,128,128]{2,1,0:T(8,128)} %get-tuple-element.136.cos_ref, ...), custom_call_target="tpu_custom_call" | custom-call | tf_op jit(solution)/shard_map/pallas_call | solution.py:757
  432.8 8.1 %shard_map.210 = (bf16[8,64,704]{2,1,0:T(8,128)(2,1)}, bf16[8,64,704]{2,1,0:T(8,128)(2,1)}, bf16[8,64,704]{2,1,0:T(8,128)(2,1)}, bf16[8,64,704]{2,1,0:T(8,128)(2,1)}) custom-call(s32[2]{0:T(128)} %pad_add_fusion.id_ref, bf16[1024,2048]{1,0:T(8,128)(2,1)} %all-gather.6.cloned.1.call-done.x_ref, bf16[1024,704]{1,0:T(8,128)(2,1)} %get-tuple-element.89.grad_ref), custom_call_target="tpu_custom_call" | custom-call | tf_op jit(solution)/shard_map/pallas_call | solution.py:244
  441.0 8.8 %shard_map.211 = (bf16[8,64,704]{2,1,0:T(8,128)(2,1)}, bf16[8,64,704]{2,1,0:T(8,128)(2,1)}, bf16[8,64,704]{2,1,0:T(8,128)(2,1)}, bf16[8,64,704]{2,1,0:T(8,128)(2,1)}) custom-call(s32[2]{0:T(128)} %pad_add_fusion.id_ref, bf16[1024,2048]{1,0:T(8,128)(2,1)} %all-gather.6.cloned.1.call-done.x_ref, bf16[1024,704]{1,0:T(8,128)(2,1)} %get-tuple-element.91.grad_ref), custom_call_target="tpu_custom_call" | custom-call | tf_op jit(solution)/shard_map/pallas_call | solution.py:244
  449.8 4.5 convolution_convert_fusion.1
  454.3 5.0 convolution_convert_fusion
  466.2 7.5 %collective-permute-done.22 = bf16[8,64,704]{2,1,0:T(8,128)(2,1)} collective-permute-done((bf16[8,64,704]{2,1,0:T(8,128)(2,1)}, bf16[8,64,704]{2,1,0:T(8,128)(2,1)}, u32[]{:S(2)}, u32[]{:S(2)}) %collective-permute-start.22) | collective-permute-done | bytes 720928 | tf_op jit(solution)/shard_map/ppermute | solution.py:55
  479.7 18.2 %collective-permute-done.44 = bf16[80,2048]{1,0:T(8,128)(2,1)} collective-permute-done((bf16[80,2048]{1,0:T(8,128)(2,1)}, bf16[80,2048]{1,0:T(8,128)(2,1)}, u32[]{:S(2)}, u32[]{:S(2)}) %collective-permute-start.44) | collective-permute-done | bytes 327712 | tf_op jit(solution)/shard_map/ppermute | solution.py:55
  501.5 13.2 %collective-permute-done.23.refs_2_ = bf16[8,64,704]{2,1,0:T(8,128)(2,1)S(1)} collective-permute-done((bf16[8,64,704]{2,1,0:T(8,128)(2,1)}, bf16[8,64,704]{2,1,0:T(8,128)(2,1)S(1)}, u32[]{:S(2)}, u32[]{:S(2)}) %collective-permute-start.23) | collective-permute-done | bytes 720928 | tf_op jit(solution)/shard_map/ppermute | solution.py:55
  516.5 3.9 shard_map.219
  520.4 10.6 %collective-permute-start.27 = (bf16[2,64,704]{2,1,0:T(8,128)(2,1)}, bf16[2,64,704]{2,1,0:T(8,128)(2,1)S(1)}, u32[]{:S(2)}, u32[]{:S(2)}) collective-permute-start(bf16[2,64,704]{2,1,0:T(8,128)(2,1)} %get-tuple-element.119), channel_id=1, source_target_pairs={{0,1},{1,0},{2,3},{3,2},{4,5},{5,4},{6,7},{7,6},{8,9},{9,8},{10,11... | collective-permute-start | bytes 540680 | tf_op jit(solution)/shard_map/ppermute | solution.py:55
  531.0 3.5 collective-permute-start.28
  539.9 4.8 collective-permute-done.28.refs_2_
  544.7 3.2 collective-permute-done.29.refs_3_
  552.8 14.2 %collective-permute-done.31.refs_5_ = bf16[2,64,704]{2,1,0:T(8,128)(2,1)S(1)} collective-permute-done((bf16[2,64,704]{2,1,0:T(8,128)(2,1)}, bf16[2,64,704]{2,1,0:T(8,128)(2,1)S(1)}, u32[]{:S(2)}, u32[]{:S(2)}) %collective-permute-start.31) | collective-permute-done | bytes 180256 | tf_op jit(solution)/shard_map/ppermute | solution.py:55
  578.8 3.9 all-to-all-start.5
  584.4 17.0 %collective-permute-done.46.refs_2_ = bf16[96,2048]{1,0:T(8,128)(2,1)S(1)} collective-permute-done((bf16[96,2048]{1,0:T(8,128)(2,1)S(1)}, bf16[96,2048]{1,0:T(8,128)(2,1)S(1)}, u32[]{:S(2)}, u32[]{:S(2)}) %collective-permute-start.46) | collective-permute-done | bytes 393248 | tf_op jit(solution)/shard_map/ppermute | solution.py:55
  603.5 10.1 %collective-permute-done.48.refs_4_ = bf16[96,2048]{1,0:T(8,128)(2,1)} collective-permute-done((bf16[96,2048]{1,0:T(8,128)(2,1)S(1)}, bf16[96,2048]{1,0:T(8,128)(2,1)}, u32[]{:S(2)}, u32[]{:S(2)}) %collective-permute-start.48) | collective-permute-done | bytes 393248 | tf_op jit(solution)/shard_map/ppermute | solution.py:55
  615.7 15.4 %collective-permute-done.51.refs_7_ = bf16[80,2048]{1,0:T(8,128)(2,1)} collective-permute-done((bf16[80,2048]{1,0:T(8,128)(2,1)}, bf16[80,2048]{1,0:T(8,128)(2,1)}, u32[]{:S(2)}, u32[]{:S(2)}) %collective-permute-start.51) | collective-permute-done | bytes 327712 | tf_op jit(solution)/shard_map/ppermute | solution.py:55
  632.3 30.4 %collective-permute-done.50.refs_6_ = bf16[96,2048]{1,0:T(8,128)(2,1)S(1)} collective-permute-done((bf16[96,2048]{1,0:T(8,128)(2,1)S(1)}, bf16[96,2048]{1,0:T(8,128)(2,1)S(1)}, u32[]{:S(2)}, u32[]{:S(2)}) %collective-permute-start.50) | collective-permute-done | bytes 393248 | tf_op jit(solution)/shard_map/ppermute | solution.py:55
  663.9 4.7 shard_map.223
  668.6 4.7 shard_map.221
  673.3 4.8 shard_map.222
  687.2 3.8 shard_map.216
  697.3 10.2 %collective-permute-done.16.refs_2_ = bf16[256,768]{1,0:T(8,128)(2,1)} collective-permute-done((bf16[256,768]{1,0:T(8,128)(2,1)}, bf16[256,768]{1,0:T(8,128)(2,1)}, u32[]{:S(2)}, u32[]{:S(2)}) %collective-permute-start.16) | collective-permute-done | bytes 393248 | tf_op jit(solution)/shard_map/ppermute | solution.py:55
  (240 shorter events, 113.6 us)
Async XLA Ops:
  7.2 63.6 %all-gather.4.cloned.1.call-start = ((), (), s32[]{:S(2)}) async-start(), calls=%async_computation.10 | async-start | bytes 5898240 | tf_op jit(solution)/shard_map/all_gather | solution.py:577
  11.9 250.9 %all-gather.8.cloned.1.call-start = ((), (), s32[]{:S(2)}) async-start(), calls=%async_computation.12 | async-start | bytes 4718592 | tf_op jit(solution)/shard_map/all_gather | solution.py:596
  14.7 31.5 %all-to-all-start = ((bf16[4,128,2176]{2,1,0:T(8,128)(2,1)}), bf16[4,128,2176]{2,1,0:T(8,128)(2,1)S(1)}, u32[]{:S(2)}, u32[]{:S(2)}) async-start(bf16[4,128,2176]{2,1,0:T(8,128)(2,1)} %broadcast_in_dim.22), calls=%async_computation | async-start | bytes 4456448 | tf_op jit(solution)/shard_map/all_to_all | solution.py:43
  19.9 243.0 %all-gather.6.cloned.1.call-start = ((), (), s32[]{:S(2)}) async-start(), calls=%async_computation.11 | async-start | bytes 4718592 | tf_op jit(solution)/shard_map/all_gather | solution.py:661
  140.4 214.9 %reduce-scatter.7.cloned.1.call-start = ((), (), s32[]{:S(2)}) async-start(), calls=%async_computation.14 | async-start | bytes 4718592 | tf_op jit(solution)/shard_map/reduce_scatter | solution.py:673
  144.7 22.6 %collective-permute-start.2 = (bf16[2,64,704]{2,1,0:T(8,128)(2,1)}, bf16[2,64,704]{2,1,0:T(8,128)(2,1)S(1)}, u32[]{:S(2)}, u32[]{:S(2)}) collective-permute-start(bf16[2,64,704]{2,1,0:T(8,128)(2,1)} %get-tuple-element.79), channel_id=1, source_target_pairs={{0,2},{1,3},{2,0},{3,1},{4,6},{5,7},{6,4},{7,5},{8,10},{9,11},{10,... | collective-permute-start | bytes 540680 | tf_op jit(solution)/shard_map/ppermute | solution.py:55
  145.8 29.5 %collective-permute-start.3 = (bf16[2,64,704]{2,1,0:T(8,128)(2,1)}, bf16[2,64,704]{2,1,0:T(8,128)(2,1)S(1)}, u32[]{:S(2)}, u32[]{:S(2)}) collective-permute-start(bf16[2,64,704]{2,1,0:T(8,128)(2,1)} %get-tuple-element.80), channel_id=1, source_target_pairs={{0,3},{1,2},{2,1},{3,0},{4,7},{5,6},{6,5},{7,4},{8,11},{9,10},{10,... | collective-permute-start | bytes 540680 | tf_op jit(solution)/shard_map/ppermute | solution.py:55
  146.4 28.9 %collective-permute-start.4 = (bf16[2,64,704]{2,1,0:T(8,128)(2,1)}, bf16[2,64,704]{2,1,0:T(8,128)(2,1)S(1)}, u32[]{:S(2)}, u32[]{:S(2)}) collective-permute-start(bf16[2,64,704]{2,1,0:T(8,128)(2,1)} %get-tuple-element.81), channel_id=1, source_target_pairs={{0,4},{1,5},{2,6},{3,7},{4,0},{5,1},{6,2},{7,3},{8,12},{9,13},{10,... | collective-permute-start | bytes 540680 | tf_op jit(solution)/shard_map/ppermute | solution.py:55
  146.6 48.1 %collective-permute-start.5 = (bf16[2,64,704]{2,1,0:T(8,128)(2,1)}, bf16[2,64,704]{2,1,0:T(8,128)(2,1)S(1)}, u32[]{:S(2)}, u32[]{:S(2)}) collective-permute-start(bf16[2,64,704]{2,1,0:T(8,128)(2,1)} %get-tuple-element.82), channel_id=1, source_target_pairs={{0,5},{1,4},{2,7},{3,6},{4,1},{5,0},{6,3},{7,2},{8,13},{9,12},{10,... | collective-permute-start | bytes 540680 | tf_op jit(solution)/shard_map/ppermute | solution.py:55
  149.1 45.6 %collective-permute-start.6 = (bf16[2,64,704]{2,1,0:T(8,128)(2,1)}, bf16[2,64,704]{2,1,0:T(8,128)(2,1)S(1)}, u32[]{:S(2)}, u32[]{:S(2)}) collective-permute-start(bf16[2,64,704]{2,1,0:T(8,128)(2,1)} %get-tuple-element.83), channel_id=1, source_target_pairs={{0,6},{1,7},{2,4},{3,5},{4,2},{5,3},{6,0},{7,1},{8,14},{9,15},{10,... | collective-permute-start | bytes 540680 | tf_op jit(solution)/shard_map/ppermute | solution.py:55
  167.3 30.1 %collective-permute-start.7 = (bf16[2,64,704]{2,1,0:T(8,128)(2,1)}, bf16[2,64,704]{2,1,0:T(8,128)(2,1)S(1)}, u32[]{:S(2)}, u32[]{:S(2)}) collective-permute-start(bf16[2,64,704]{2,1,0:T(8,128)(2,1)} %get-tuple-element.84), channel_id=1, source_target_pairs={{0,7},{1,6},{2,5},{3,4},{4,3},{5,2},{6,1},{7,0},{8,15},{9,14},{10,... | collective-permute-start | bytes 540680 | tf_op jit(solution)/shard_map/ppermute | solution.py:55
  200.8 20.6 %collective-permute-start.8 = (bf16[8,64,704]{2,1,0:T(8,128)(2,1)}, bf16[8,64,704]{2,1,0:T(8,128)(2,1)S(1)}, u32[]{:S(2)}, u32[]{:S(2)}) collective-permute-start(bf16[8,64,704]{2,1,0:T(8,128)(2,1)} %get-tuple-element.85.refs_0_), channel_id=1, source_target_pairs={{0,8},{8,0},{16,24},{24,16},{1,9},{9,1},{17,25},{25,17},{2,10},{10... | collective-permute-start | bytes 2162696 | tf_op jit(solution)/shard_map/ppermute | solution.py:55
  201.5 20.6 %collective-permute-start.11 = (bf16[8,64,704]{2,1,0:T(8,128)(2,1)}, bf16[8,64,704]{2,1,0:T(8,128)(2,1)S(1)}, u32[]{:S(2)}, u32[]{:S(2)}) collective-permute-start(bf16[8,64,704]{2,1,0:T(8,128)(2,1)} %get-tuple-element.86.refs_1_), channel_id=1, source_target_pairs={{0,16},{8,24},{16,0},{24,8},{1,17},{9,25},{17,1},{25,9},{2,18},{10... | collective-permute-start | bytes 2162696 | tf_op jit(solution)/shard_map/ppermute | solution.py:55
  201.5 36.7 %collective-permute-start.9 = (bf16[8,64,704]{2,1,0:T(8,128)(2,1)}, bf16[8,64,704]{2,1,0:T(8,128)(2,1)S(1)}, u32[]{:S(2)}, u32[]{:S(2)}) collective-permute-start(bf16[8,64,704]{2,1,0:T(8,128)(2,1)} %get-tuple-element.86.refs_1_), channel_id=1, source_target_pairs={{0,8},{8,0},{16,24},{24,16},{1,9},{9,1},{17,25},{25,17},{2,10},{10... | collective-permute-start | bytes 2162696 | tf_op jit(solution)/shard_map/ppermute | solution.py:55
  203.5 35.4 %collective-permute-start.10 = (bf16[8,64,704]{2,1,0:T(8,128)(2,1)}, bf16[8,64,704]{2,1,0:T(8,128)(2,1)S(1)}, u32[]{:S(2)}, u32[]{:S(2)}) collective-permute-start(bf16[8,64,704]{2,1,0:T(8,128)(2,1)} %get-tuple-element.85.refs_0_), channel_id=1, source_target_pairs={{0,16},{8,24},{16,0},{24,8},{1,17},{9,25},{17,1},{25,9},{2,18},{10... | collective-permute-start | bytes 2162696 | tf_op jit(solution)/shard_map/ppermute | solution.py:55
  221.4 33.8 %collective-permute-start.12 = (bf16[8,64,704]{2,1,0:T(8,128)(2,1)S(1)}, bf16[8,64,704]{2,1,0:T(8,128)(2,1)S(1)}, u32[]{:S(2)}, u32[]{:S(2)}) collective-permute-start(bf16[8,64,704]{2,1,0:T(8,128)(2,1)S(1)} %collective-permute-done.8.refs_2_), channel_id=1, source_target_pairs={{0,16},{8,24},{16,0},{24,8},{1,17},{9,25},{17,1},{25,9},{2,18},{10... | collective-permute-start | bytes 2162696 | tf_op jit(solution)/shard_map/ppermute | solution.py:55
  222.1 33.0 %collective-permute-start.13 = (bf16[8,64,704]{2,1,0:T(8,128)(2,1)S(1)}, bf16[8,64,704]{2,1,0:T(8,128)(2,1)S(1)}, u32[]{:S(2)}, u32[]{:S(2)}) collective-permute-start(bf16[8,64,704]{2,1,0:T(8,128)(2,1)S(1)} %collective-permute-done.11.refs_5_), channel_id=1, source_target_pairs={{0,8},{8,0},{16,24},{24,16},{1,9},{9,1},{17,25},{25,17},{2,10},{10... | collective-permute-start | bytes 2162696 | tf_op jit(solution)/shard_map/ppermute | solution.py:55
  288.3 374.5 %reduce-scatter.11.cloned.1.call-start = ((), (), s32[]{:S(2)}) async-start(), calls=%async_computation.16 | async-start | bytes 2359296 | tf_op jit(solution)/shard_map/reduce_scatter | solution.py:736
  395.2 285.2 %reduce-scatter.9.cloned.1.call-start = ((), (), s32[]{:S(2)}) async-start(), calls=%async_computation.15 | async-start | bytes 3538944 | tf_op jit(solution)/shard_map/reduce_scatter | solution.py:777
  432.6 251.3 %reduce-scatter.5.cloned.1.call-start = ((), (), s32[]{:S(2)}) async-start(), calls=%async_computation.13 | async-start | bytes 4718592 | tf_op jit(solution)/shard_map/reduce_scatter | solution.py:689
  460.6 39.3 %collective-permute-start.21 = (bf16[8,64,704]{2,1,0:T(8,128)(2,1)}, bf16[8,64,704]{2,1,0:T(8,128)(2,1)S(1)}, u32[]{:S(2)}, u32[]{:S(2)}) collective-permute-start(bf16[8,64,704]{2,1,0:T(8,128)(2,1)} %get-tuple-element.112), channel_id=1, source_target_pairs={{0,8},{8,0},{16,24},{24,16},{1,9},{9,1},{17,25},{25,17},{2,10},{10... | collective-permute-start | bytes 2162696 | tf_op jit(solution)/shard_map/ppermute | solution.py:55
  462.2 39.2 %collective-permute-start.24 = (bf16[8,64,704]{2,1,0:T(8,128)(2,1)}, bf16[8,64,704]{2,1,0:T(8,128)(2,1)S(1)}, u32[]{:S(2)}, u32[]{:S(2)}) collective-permute-start(bf16[8,64,704]{2,1,0:T(8,128)(2,1)} %get-tuple-element.115), channel_id=1, source_target_pairs={{0,16},{8,24},{16,0},{24,8},{1,17},{9,25},{17,1},{25,9},{2,18},{10... | collective-permute-start | bytes 2162696 | tf_op jit(solution)/shard_map/ppermute | solution.py:55
  465.5 32.4 %collective-permute-start.44 = (bf16[80,2048]{1,0:T(8,128)(2,1)}, bf16[80,2048]{1,0:T(8,128)(2,1)}, u32[]{:S(2)}, u32[]{:S(2)}) collective-permute-start(bf16[80,2048]{1,0:T(8,128)(2,1)} %get-tuple-element.132), channel_id=1, source_target_pairs={{0,16},{8,24},{16,0},{24,8},{1,17},{9,25},{17,1},{25,9},{2,18},{10... | collective-permute-start | bytes 983048 | tf_op jit(solution)/shard_map/ppermute | solution.py:55
  476.0 38.6 %collective-permute-start.23 = (bf16[8,64,704]{2,1,0:T(8,128)(2,1)}, bf16[8,64,704]{2,1,0:T(8,128)(2,1)S(1)}, u32[]{:S(2)}, u32[]{:S(2)}) collective-permute-start(bf16[8,64,704]{2,1,0:T(8,128)(2,1)} %add_convert_fusion.1), channel_id=1, source_target_pairs={{0,16},{8,24},{16,0},{24,8},{1,17},{9,25},{17,1},{25,9},{2,18},{10... | collective-permute-start | bytes 2162696 | tf_op jit(solution)/shard_map/ppermute | solution.py:55
  478.2 36.4 %collective-permute-start.26 = (bf16[8,64,704]{2,1,0:T(8,128)(2,1)}, bf16[8,64,704]{2,1,0:T(8,128)(2,1)S(1)}, u32[]{:S(2)}, u32[]{:S(2)}) collective-permute-start(bf16[8,64,704]{2,1,0:T(8,128)(2,1)} %add_convert_fusion), channel_id=1, source_target_pairs={{0,8},{8,0},{16,24},{24,16},{1,9},{9,1},{17,25},{25,17},{2,10},{10... | collective-permute-start | bytes 2162696 | tf_op jit(solution)/shard_map/ppermute | solution.py:55
  497.9 37.3 %collective-permute-start.41 = (bf16[96,2048]{1,0:T(8,128)(2,1)S(1)}, bf16[96,2048]{1,0:T(8,128)(2,1)S(1)}, u32[]{:S(2)}, u32[]{:S(2)}) collective-permute-start(bf16[96,2048]{1,0:T(8,128)(2,1)S(1)} %get-tuple-element.134), channel_id=1, source_target_pairs={{0,8},{8,0},{16,24},{24,16},{1,9},{9,1},{17,25},{25,17},{2,10},{10... | collective-permute-start | bytes 1179656 | tf_op jit(solution)/shard_map/ppermute | solution.py:55
  499.9 34.6 %collective-permute-start.43 = (bf16[80,2048]{1,0:T(8,128)(2,1)}, bf16[80,2048]{1,0:T(8,128)(2,1)S(1)}, u32[]{:S(2)}, u32[]{:S(2)}) collective-permute-start(bf16[80,2048]{1,0:T(8,128)(2,1)} %get-tuple-element.131), channel_id=1, source_target_pairs={{0,16},{8,24},{16,0},{24,8},{1,17},{9,25},{17,1},{25,9},{2,18},{10... | collective-permute-start | bytes 983048 | tf_op jit(solution)/shard_map/ppermute | solution.py:55
  501.4 36.3 %collective-permute-start.45 = (bf16[80,2048]{1,0:T(8,128)(2,1)S(1)}, bf16[80,2048]{1,0:T(8,128)(2,1)S(1)}, u32[]{:S(2)}, u32[]{:S(2)}) collective-permute-start(bf16[80,2048]{1,0:T(8,128)(2,1)S(1)} %add_convert_fusion.6), channel_id=1, source_target_pairs={{0,8},{8,0},{16,24},{24,16},{1,9},{9,1},{17,25},{25,17},{2,10},{10... | collective-permute-start | bytes 983048 | tf_op jit(solution)/shard_map/ppermute | solution.py:55
  520.4 18.1 %collective-permute-start.27 = (bf16[2,64,704]{2,1,0:T(8,128)(2,1)}, bf16[2,64,704]{2,1,0:T(8,128)(2,1)S(1)}, u32[]{:S(2)}, u32[]{:S(2)}) collective-permute-start(bf16[2,64,704]{2,1,0:T(8,128)(2,1)} %get-tuple-element.119), channel_id=1, source_target_pairs={{0,1},{1,0},{2,3},{3,2},{4,5},{5,4},{6,7},{7,6},{8,9},{9,8},{10,11... | collective-permute-start | bytes 540680 | tf_op jit(solution)/shard_map/ppermute | solution.py:55
  537.6 36.3 %collective-permute-start.40 = (bf16[96,2048]{1,0:T(8,128)(2,1)S(1)}, bf16[96,2048]{1,0:T(8,128)(2,1)S(1)}, u32[]{:S(2)}, u32[]{:S(2)}) collective-permute-start(bf16[96,2048]{1,0:T(8,128)(2,1)S(1)} %get-tuple-element.133), channel_id=1, source_target_pairs={{0,8},{8,0},{16,24},{24,16},{1,9},{9,1},{17,25},{25,17},{2,10},{10... | collective-permute-start | bytes 1179656 | tf_op jit(solution)/shard_map/ppermute | solution.py:55
  538.6 36.2 %collective-permute-start.42 = (bf16[96,2048]{1,0:T(8,128)(2,1)S(1)}, bf16[96,2048]{1,0:T(8,128)(2,1)S(1)}, u32[]{:S(2)}, u32[]{:S(2)}) collective-permute-start(bf16[96,2048]{1,0:T(8,128)(2,1)S(1)} %add_convert_fusion.4), channel_id=1, source_target_pairs={{0,16},{8,24},{16,0},{24,8},{1,17},{9,25},{17,1},{25,9},{2,18},{10... | collective-permute-start | bytes 1179656 | tf_op jit(solution)/shard_map/ppermute | solution.py:55
  544.7 22.3 %collective-permute-start.31 = (bf16[2,64,704]{2,1,0:T(8,128)(2,1)}, bf16[2,64,704]{2,1,0:T(8,128)(2,1)S(1)}, u32[]{:S(2)}, u32[]{:S(2)}) collective-permute-start(bf16[2,64,704]{2,1,0:T(8,128)(2,1)} %get-tuple-element.123), channel_id=1, source_target_pairs={{0,5},{1,4},{2,7},{3,6},{4,1},{5,0},{6,3},{7,2},{8,13},{9,12},{10,... | collective-permute-start | bytes 540680 | tf_op jit(solution)/shard_map/ppermute | solution.py:55
  547.9 20.0 %collective-permute-start.32 = (bf16[2,64,704]{2,1,0:T(8,128)(2,1)}, bf16[2,64,704]{2,1,0:T(8,128)(2,1)S(1)}, u32[]{:S(2)}, u32[]{:S(2)}) collective-permute-start(bf16[2,64,704]{2,1,0:T(8,128)(2,1)} %get-tuple-element.124), channel_id=1, source_target_pairs={{0,6},{1,7},{2,4},{3,5},{4,2},{5,3},{6,0},{7,1},{8,14},{9,15},{10,... | collective-permute-start | bytes 540680 | tf_op jit(solution)/shard_map/ppermute | solution.py:55
  550.1 19.1 %collective-permute-start.33 = (bf16[2,64,704]{2,1,0:T(8,128)(2,1)}, bf16[2,64,704]{2,1,0:T(8,128)(2,1)S(1)}, u32[]{:S(2)}, u32[]{:S(2)}) collective-permute-start(bf16[2,64,704]{2,1,0:T(8,128)(2,1)} %get-tuple-element.125), channel_id=1, source_target_pairs={{0,7},{1,6},{2,5},{3,4},{4,3},{5,2},{6,1},{7,0},{8,15},{9,14},{10,... | collective-permute-start | bytes 540680 | tf_op jit(solution)/shard_map/ppermute | solution.py:55
  572.8 29.9 %collective-permute-start.34 = (bf16[64,5632]{1,0:T(8,128)(2,1)}, bf16[64,5632]{1,0:T(8,128)(2,1)}, u32[]{:S(2)}, u32[]{:S(2)}) collective-permute-start(bf16[64,5632]{1,0:T(8,128)(2,1)} %get-tuple-element.126.refs_0_), channel_id=1, source_target_pairs={{0,8},{8,0},{16,24},{24,16},{1,9},{9,1},{17,25},{25,17},{2,10},{10... | collective-permute-start | bytes 2162696 | tf_op jit(solution)/shard_map/ppermute | solution.py:55
  573.9 39.7 %collective-permute-start.38 = (bf16[64,5632]{1,0:T(8,128)(2,1)}, bf16[64,5632]{1,0:T(8,128)(2,1)}, u32[]{:S(2)}, u32[]{:S(2)}) collective-permute-start(bf16[64,5632]{1,0:T(8,128)(2,1)} %get-tuple-element.127.refs_0_), channel_id=1, source_target_pairs={{0,16},{8,24},{16,0},{24,8},{1,17},{9,25},{17,1},{25,9},{2,18},{10... | collective-permute-start | bytes 2162696 | tf_op jit(solution)/shard_map/ppermute | solution.py:55
  575.9 25.6 %collective-permute-start.46 = (bf16[96,2048]{1,0:T(8,128)(2,1)S(1)}, bf16[96,2048]{1,0:T(8,128)(2,1)S(1)}, u32[]{:S(2)}, u32[]{:S(2)}) collective-permute-start(bf16[96,2048]{1,0:T(8,128)(2,1)S(1)} %add_convert_fusion.3.refs_0_), channel_id=1, source_target_pairs={{0,8},{8,0},{16,24},{24,16},{1,9},{9,1},{17,25},{25,17},{2,10},{10... | collective-permute-start | bytes 1179656 | tf_op jit(solution)/shard_map/ppermute | solution.py:55
  577.6 36.0 %collective-permute-start.48 = (bf16[96,2048]{1,0:T(8,128)(2,1)S(1)}, bf16[96,2048]{1,0:T(8,128)(2,1)}, u32[]{:S(2)}, u32[]{:S(2)}) collective-permute-start(bf16[96,2048]{1,0:T(8,128)(2,1)S(1)} %add_convert_fusion.3.refs_0_), channel_id=1, source_target_pairs={{0,16},{8,24},{16,0},{24,8},{1,17},{9,25},{17,1},{25,9},{2,18},{10... | collective-permute-start | bytes 1179656 | tf_op jit(solution)/shard_map/ppermute | solution.py:55
  578.8 107.0 %all-to-all-start.5 = ((bf16[4,128,2048]{2,1,0:T(8,128)(2,1)}), bf16[4,128,2048]{2,1,0:T(8,128)(2,1)S(1)}, u32[]{:S(2)}, u32[]{:S(2)}) async-start(bf16[4,128,2048]{2,1,0:T(8,128)(2,1)} %get-tuple-element.103), calls=%async_computation.7 | async-start | bytes 4194304 | tf_op jit(solution)/shard_map/all_to_all | solution.py:47
  582.7 48.4 %collective-permute-start.51 = (bf16[80,2048]{1,0:T(8,128)(2,1)}, bf16[80,2048]{1,0:T(8,128)(2,1)}, u32[]{:S(2)}, u32[]{:S(2)}) collective-permute-start(bf16[80,2048]{1,0:T(8,128)(2,1)} %collective-permute-done.49.refs_5_), channel_id=1, source_target_pairs={{0,8},{8,0},{16,24},{24,16},{1,9},{9,1},{17,25},{25,17},{2,10},{10... | collective-permute-start | bytes 983048 | tf_op jit(solution)/shard_map/ppermute | solution.py:55
  601.5 67.1 %collective-permute-start.35 = (bf16[64,5632]{1,0:T(8,128)(2,1)}, bf16[64,5632]{1,0:T(8,128)(2,1)}, u32[]{:S(2)}, u32[]{:S(2)}) collective-permute-start(bf16[64,5632]{1,0:T(8,128)(2,1)} %get-tuple-element.126.refs_0_), channel_id=1, source_target_pairs={{0,16},{8,24},{16,0},{24,8},{1,17},{9,25},{17,1},{25,9},{2,18},{10... | collective-permute-start | bytes 2162696 | tf_op jit(solution)/shard_map/ppermute | solution.py:55
  602.7 65.9 %collective-permute-start.36 = (bf16[64,5632]{1,0:T(8,128)(2,1)}, bf16[64,5632]{1,0:T(8,128)(2,1)}, u32[]{:S(2)}, u32[]{:S(2)}) collective-permute-start(bf16[64,5632]{1,0:T(8,128)(2,1)} %collective-permute-done.34.refs_1_), channel_id=1, source_target_pairs={{0,16},{8,24},{16,0},{24,8},{1,17},{9,25},{17,1},{25,9},{2,18},{10... | collective-permute-start | bytes 2162696 | tf_op jit(solution)/shard_map/ppermute | solution.py:55
  613.6 59.6 %collective-permute-start.37 = (bf16[64,5632]{1,0:T(8,128)(2,1)}, bf16[64,5632]{1,0:T(8,128)(2,1)}, u32[]{:S(2)}, u32[]{:S(2)}) collective-permute-start(bf16[64,5632]{1,0:T(8,128)(2,1)} %get-tuple-element.127.refs_0_), channel_id=1, source_target_pairs={{0,8},{8,0},{16,24},{24,16},{1,9},{9,1},{17,25},{25,17},{2,10},{10... | collective-permute-start | bytes 2162696 | tf_op jit(solution)/shard_map/ppermute | solution.py:55
  613.6 59.6 %collective-permute-start.39 = (bf16[64,5632]{1,0:T(8,128)(2,1)}, bf16[64,5632]{1,0:T(8,128)(2,1)}, u32[]{:S(2)}, u32[]{:S(2)}) collective-permute-start(bf16[64,5632]{1,0:T(8,128)(2,1)} %collective-permute-done.38.refs_2_), channel_id=1, source_target_pairs={{0,8},{8,0},{16,24},{24,16},{1,9},{9,1},{17,25},{25,17},{2,10},{10... | collective-permute-start | bytes 2162696 | tf_op jit(solution)/shard_map/ppermute | solution.py:55
  631.1 31.7 %collective-permute-start.50 = (bf16[96,2048]{1,0:T(8,128)(2,1)S(1)}, bf16[96,2048]{1,0:T(8,128)(2,1)S(1)}, u32[]{:S(2)}, u32[]{:S(2)}) collective-permute-start(bf16[96,2048]{1,0:T(8,128)(2,1)S(1)} %collective-permute-done.46.refs_2_), channel_id=1, source_target_pairs={{0,16},{8,24},{16,0},{24,8},{1,17},{9,25},{17,1},{25,9},{2,18},{10... | collective-permute-start | bytes 1179656 | tf_op jit(solution)/shard_map/ppermute | solution.py:55
  662.8 20.1 %collective-permute-start.18 = (bf16[64,2048]{1,0:T(8,128)(2,1)}, bf16[64,2048]{1,0:T(8,128)(2,1)}, u32[]{:S(2)}, u32[]{:S(2)}) collective-permute-start(bf16[64,2048]{1,0:T(8,128)(2,1)} %reduce-scatter.11.cloned.1.call-done.refs_0_), channel_id=1, source_target_pairs={{0,8},{8,0},{16,24},{24,16},{1,9},{9,1},{17,25},{25,17},{2,10},{10... | collective-permute-start | bytes 786440 | tf_op jit(solution)/shard_map/ppermute | solution.py:55
  681.5 25.9 %collective-permute-start.16 = (bf16[256,768]{1,0:T(8,128)(2,1)}, bf16[256,768]{1,0:T(8,128)(2,1)}, u32[]{:S(2)}, u32[]{:S(2)}) collective-permute-start(bf16[256,768]{1,0:T(8,128)(2,1)} %reduce-scatter.9.cloned.1.call-done.refs_0_), channel_id=1, source_target_pairs={{0,16},{8,24},{16,0},{24,8},{1,17},{9,25},{17,1},{25,9},{2,18},{10... | collective-permute-start | bytes 1179656 | tf_op jit(solution)/shard_map/ppermute | solution.py:55
  682.8 24.6 %collective-permute-start.17 = (bf16[256,768]{1,0:T(8,128)(2,1)}, bf16[256,768]{1,0:T(8,128)(2,1)}, u32[]{:S(2)}, u32[]{:S(2)}) collective-permute-start(bf16[256,768]{1,0:T(8,128)(2,1)} %reduce-scatter.9.cloned.1.call-done.refs_0_), channel_id=1, source_target_pairs={{0,24},{8,16},{16,8},{24,0},{1,25},{9,17},{17,9},{25,1},{2,26},{10... | collective-permute-start | bytes 1179656 | tf_op jit(solution)/shard_map/ppermute | solution.py:55
  (62 other events, 884.9 us)
Sparse Core Ops, SparseCore 0:
  12.1 58.6 all-gather.3
  72.4 45.6 all-gather.7
  140.5 77.3 all-gather.5
  288.4 66.8 reduce-scatter.6
  395.3 35.1 reduce-scatter.10
  432.7 45.3 reduce-scatter.8
  480.4 49.2 reduce-scatter.4

commit v5 on v3

--- a/solution.py
+++ b/solution.py
@@ -58,10 +58,7 @@
 def parts_rep(chunks, count):
     go = lambda value, step: send(value, "rep", count, step)
     if count != 4:
-        return [
-            [chunks[0][h]] + [go(chunks[k][h], k) for k in range(1, count)]
-            for h in range(2)
-        ]
+        return [[chunks[0][h]] + [go(chunks[k][h], k) for k in range(1, count)] for h in range(2)]
     add = lambda left, right: (left.astype(F32) + right.astype(F32)).astype(BF)
     first_one = go(chunks[1][0], 1)
     first_two = go(chunks[3][0], 1)
@@ -256,6 +253,42 @@
         ),
         compiler_params=pltpu.CompilerParams(vmem_limit_bytes=56 * 1024 * 1024),
     )(ids, x, grad)
+
+
+def down_grad_kernel(id_ref, mixed_ref, cot_ref, *refs):
+    outs, total_ref = refs[:-1], refs[-1]
+    total_ref[...] = rows_rows(mixed_ref[...], cot_ref[...])
+    rows = total_ref.shape[0] // (len(outs) // 2)
+    for k in range(len(outs) // 2):
+        at = jnp.bitwise_xor(id_ref[0], k) * rows
+        for h in range(2):
+            out = outs[2 * k + h]
+            start = at + h * outs[0].shape[0]
+            out[...] = total_ref[pl.ds(pl.multiple_of(start, 16), out.shape[0])].astype(BF)
+
+
+def down_grad(ids, mixed, cot, cut, count):
+    hidden, width = mixed.shape[1], cot.shape[1]
+    rest = hidden // count - cut
+    tile = width // 2
+    heights = (cut, rest) * count
+    outs = pl.pallas_call(
+        down_grad_kernel,
+        out_shape=tuple(shape((rows, width), BF) for rows in heights),
+        grid_spec=pltpu.PrefetchScalarGridSpec(
+            num_scalar_prefetch=1,
+            grid=(width // tile,),
+            in_specs=[
+                pl.BlockSpec(mixed.shape, lambda g, ids: (0, 0), pipeline_mode=pl.Buffered(1)),
+                pl.BlockSpec((cot.shape[0], tile), lambda g, ids: (0, g)),
+            ],
+            out_specs=tuple(pl.BlockSpec((rows, tile), lambda g, ids: (0, g)) for rows in heights),
+            scratch_shapes=[pltpu.VMEM((hidden, tile), F32)],
+        ),
+        name="down_grad",
+        compiler_params=pltpu.CompilerParams(vmem_limit_bytes=56 * 1024 * 1024),
+    )(ids, mixed, cot)
+    return list(zip(outs[0::2], outs[1::2]))
 
 
 def norm_scale(value):
@@ -436,22 +469,21 @@
     out_ref[...] = out.astype(BF)
 
 
-def forward_back_kernel(
-    x_ref, cot_ref, pair_ref, down_ref, mixed_ref, gate_out, up_out, part_ref
-):
+def forward_kernel(x_ref, back_ref, pair_ref, mixed_ref, gate_out, up_out):
     x = x_ref[...]
     gate = rows_cols(x, pair_ref[0])
     up = rows_cols(x, pair_ref[1])
-    mixed_grad = cols_cols(cot_ref[...], down_ref[...])
+    mixed_grad = back_ref[...]
     sigma = jax.nn.sigmoid(gate)
     silu = gate * sigma
     mixed_ref[...] = (silu * up).astype(BF)
-    gate_grad = (mixed_grad * up * sigma * (1.0 + gate * (1.0 - sigma))).astype(BF)
-    up_grad = (mixed_grad * silu).astype(BF)
-    gate_out[...] = gate_grad
-    up_out[...] = up_grad
+    gate_out[...] = (mixed_grad * up * sigma * (1.0 + gate * (1.0 - sigma))).astype(BF)
+    up_out[...] = (mixed_grad * silu).astype(BF)
+
+
+def back_kernel(gate_ref, up_ref, pair_ref, part_ref):
     part_ref[...] = (
-        cols_cols(gate_grad, pair_ref[0]) + cols_cols(up_grad, pair_ref[1])
+        cols_cols(gate_ref[...], pair_ref[0]) + cols_cols(up_ref[...], pair_ref[1])
     ).astype(BF)
 
 
@@ -600,17 +632,37 @@
     )(swap(mid_part, "rep"), tokens, gain_two)
 
     two_all = lax.all_gather(normed_two, "shard", axis=0, tiled=True)
+    mixed_grad = cols_cols(cot_all, down_weight)
     step = 256
     group = two_all.shape[0]
     token_block = pl.BlockSpec((step, width), lambda g: (g, 0))
     hidden_block = pl.BlockSpec((step, hidden), lambda g: (g, 0))
-    mixed, gate_grad, up_grad, two_grad_part = call(
-        forward_back_kernel,
-        (shape((group, hidden), BF),) * 3 + (shape((group, width), BF),),
+    mixed, gate_grad, up_grad = call(
+        forward_kernel,
+        (shape((group, hidden), BF),) * 3,
         (group // step,),
-        [token_block, token_block, whole((2, width, hidden)), whole((hidden, width))],
-        (hidden_block,) * 3 + (token_block,),
-    )(two_all, cot_all, w_pair, down_weight)
+        [token_block, hidden_block, whole((2, width, hidden))],
+        (hidden_block,) * 3,
+    )(two_all, mixed_grad, w_pair)
+    part_rows = hidden // n_rep
+    cut = (part_rows // 2 + 15) // 16 * 16
+    if part_rows % 16:
+        whole_grad = rows_rows(mixed, cot_all).astype(BF)
+        down_chunks = []
+        for k in range(n_rep):
+            part = lax.dynamic_slice_in_dim(whole_grad, (r ^ k) * part_rows, part_rows, 0)
+            down_chunks.append((part[:cut], part[cut:]))
+    else:
+        down_chunks = down_grad(ids, mixed, cot_all, cut, n_rep)
+    gate_tied, _ = lax.optimization_barrier((gate_grad, down_chunks[0][0]))
+    two_grad_part = call(
+        back_kernel,
+        shape((group, width), BF),
+        (group // step,),
+        [hidden_block, hidden_block, whole((2, width, hidden))],
+        token_block,
+    )(gate_tied, up_grad, w_pair)
+    gate_grad, _ = lax.optimization_barrier((gate_grad, two_grad_part))
     two_grad = lax.psum_scatter(two_grad_part, "shard", scatter_dimension=0, tiled=True)
     mid_grad, branch, gain_two_rows = call(
         middle_back_kernel,
@@ -622,33 +674,17 @@
     up_chunks = pair_grad(ids, two_all, up_grad, fine, n_rep, n_shard)
     pair_chunks = list(zip(gate_chunks, up_chunks))
     mixed, _ = lax.optimization_barrier((mixed, up_chunks[0]))
-    part_rows = hidden // n_rep
-    cut = (part_rows // 2 + 15) // 16 * 16
-    w_down_grad = rows_rows(mixed, cot_all).astype(BF)
-    mixed, w_down_grad = lax.optimization_barrier((mixed, w_down_grad))
     down_part = rows_cols(mixed, down_weight).astype(BF)
     down_rows = lax.psum_scatter(down_part, "shard", scatter_dimension=0, tiled=True)
     layer_out = (x_mid + down_rows.astype(F32)).astype(BF)
-    chunks = []
-    for k in range(n_rep):
-        at = (r ^ k) * part_rows
-        chunks.append(
-            (
-                lax.dynamic_slice_in_dim(w_down_grad, at, cut, 0),
-                lax.dynamic_slice_in_dim(w_down_grad, at + cut, part_rows - cut, 0),
-            )
-        )
-    w_down_grad = parts_rep(chunks, n_rep)
+    w_down_grad = parts_rep(down_chunks, n_rep)
     w_down_grad = tuple(
         sum(part.astype(F32) for part in parts).astype(BF) for parts in w_down_grad
     )
     down_out = place(gather_rep(w_down_grad, n_rep), r)
     w_pair_grad = parts_rep(pair_chunks, n_rep)
     w_pair_grad = flat_call(
-        sum_kernel,
-        ids,
-        (shape((2, fine, hidden), BF),) * n_shard,
-        w_pair_grad[0] + w_pair_grad[1],
+        sum_kernel, ids, (shape((2, fine, hidden), BF),) * n_shard, w_pair_grad[0] + w_pair_grad[1]
     )
     w_pair_grad = exchange_shard(w_pair_grad)
     w_pair_grad = flat_call(

time: 685 us -> 689 us (level)
    ppermute x50, waiting for transfers between devices: 217 us -> 237 us  [send(): return lax.ppermute(value, axis, pairs(count, step))]
    reduce_scatter x1, waiting for transfers between devices: 80.5 us -> 65.8 us  [body(): lax.psum_scatter(two_grad_part, 'shard', scatter_dimension=0, tiled=True)]
    pallas_call x1 -> x3, Pallas kernels: 25.4 us -> 30.9 us  [the longest x1 12.1 us: body(): call(forward_kernel, (shape((group, hidden), BF),) * 3, (group // step,),...]
  transfers between devices with their start and end apart: 62 -> 62, of which waited for: 27 -> 28; matrix products, arithmetic and copies ran while one was open for 5% -> 4% of each run, Pallas kernels for 14% -> 14%
where the time goes in v5:
time: 689 us; the launch traced here: 684 us
  waiting for transfers between devices  320 us (46%)
  Pallas kernels  131 us (19%)
  blocking collectives  88.9 us (13%)
  starting transfers between devices  83 us (12%)
  matrix products  19.2 us (3%)
  local copies, waits for them, and re-layouts  17.4 us (3%)
  between operations  14.6 us (2%)
  other arithmetic  9.95 us (1%)
    ppermute x50, waiting for transfers between devices, send(): return lax.ppermute(value, axis, pairs(count, step))  237 us
    ppermute x50, starting transfers between devices, send(): return lax.ppermute(value, axis, pairs(count, step))  69.9 us
    reduce_scatter x1, waiting for transfers between devices, body(): lax.psum_scatter(two_grad_part, 'shard', scatter_dimension=0, tiled=True)  65.8 us
    all_to_all x3, blocking collectives, swap(): return lax.all_to_all(value, axis, split_axis=0, concat_axis=0, tiled=True)  48.6 us
    all_to_all x1, blocking collectives, spread(): return lax.all_to_all(wide, axis, split_axis=0, concat_axis=0, tiled=True)  27.1 us
    dot_general x5, matrix products, dot(): lax.dot_general(left, right, (contract, ((), ())), preferred_element_type...  19.2 us
    pallas_call x5, Pallas kernels, flat_call(): pl.pallas_call(kernel, out_shape=out_shape, in_specs=specs, scratch_shape...  18.4 us
    pallas_call x4, Pallas kernels, place(): pl.pallas_call(partial(place_kernel, count), out_shape=shape((count, rows...  17.1 us
  transfers between devices with their start and end apart: 62, of which 28 were waited for; matrix products, arithmetic and copies ran while one was open for 4% of the time, Pallas kernels for 14%

profile of v5, /device:TPU:0, one launch (start us, length us, event | category | flops | bytes accessed | tf_op | source)
XLA Modules:
  0.0 683.9 jit_solution(8178900368395866935)
XLA Ops:
  14.7 5.3 all-to-all-start
  20.1 13.2 %all_gather.15 = bf16[2,2048]{1,0:T(2,128)(2,1)S(1)} all-gather(bf16[2,256]{1,0:T(2,128)(2,1)S(1)} %pad_maximum_fusion.2), channel_id=1, replica_groups=mesh['rep'=4,'shard'=8] {'shard'}, dimensions={1}, use_global_device_ids=true | all-gather | bytes 9216 | tf_op jit(solution)/shard_map/all_gather | solution.py:567
  34.0 13.2 %all-to-all-done.x_ref.pos_ref = bf16[4,128,2176]{2,1,0:T(8,128)(2,1)} async-done(((bf16[4,128,2176]{2,1,0:T(8,128)(2,1)}), bf16[4,128,2176]{2,1,0:T(8,128)(2,1)}, u32[]{:S(2)}, u32[]{:S(2)}) %all-to-all-start) | async-done | bytes 2228256 | tf_op jit(solution)/shard_map/all_to_all | solution.py:43
  49.7 6.2 shard_map.203
  59.6 6.4 shard_map.204
  66.0 10.6 %all_to_all.30 = bf16[4,4,128,128]{3,2,1,0:T(8,128)(2,1)S(1)} all-to-all(bf16[4,4,128,128]{3,2,1,0:T(8,128)(2,1)} %get-tuple-element.78), channel_id=1, replica_groups=mesh['rep'=4,'shard'=8] {'rep'}, dimensions={0} | all-to-all | bytes 1048576 | tf_op jit(solution)/shard_map/all_to_all | solution.py:47
  80.6 27.8 %all_to_all.31.part_ref = bf16[4,128,2048]{2,1,0:T(8,128)(2,1)} all-to-all(bf16[4,128,2048]{2,1,0:T(8,128)(2,1)S(1)} %bitcast.42), channel_id=1, replica_groups=mesh['rep'=4,'shard'=8] {'rep'}, dimensions={0} | all-to-all | bytes 4194304 | tf_op jit(solution)/shard_map/all_to_all | solution.py:47
  118.6 5.6 collective-permute-start.2
  128.8 10.3 %collective-permute-done.2.refs_2_ = bf16[2,64,704]{2,1,0:T(8,128)(2,1)S(1)} collective-permute-done((bf16[2,64,704]{2,1,0:T(8,128)(2,1)}, bf16[2,64,704]{2,1,0:T(8,128)(2,1)S(1)}, u32[]{:S(2)}, u32[]{:S(2)}) %collective-permute-start.2) | collective-permute-done | bytes 180256 | tf_op jit(solution)/shard_map/ppermute | solution.py:55
  139.7 8.7 %collective-permute-done.3.refs_3_ = bf16[2,64,704]{2,1,0:T(8,128)(2,1)S(1)} collective-permute-done((bf16[2,64,704]{2,1,0:T(8,128)(2,1)}, bf16[2,64,704]{2,1,0:T(8,128)(2,1)S(1)}, u32[]{:S(2)}, u32[]{:S(2)}) %collective-permute-start.3) | collective-permute-done | bytes 180256 | tf_op jit(solution)/shard_map/ppermute | solution.py:55
  150.4 9.4 %collective-permute-done.6.refs_6_ = bf16[2,64,704]{2,1,0:T(8,128)(2,1)S(1)} collective-permute-done((bf16[2,64,704]{2,1,0:T(8,128)(2,1)}, bf16[2,64,704]{2,1,0:T(8,128)(2,1)S(1)}, u32[]{:S(2)}, u32[]{:S(2)}) %collective-permute-start.6) | collective-permute-done | bytes 180256 | tf_op jit(solution)/shard_map/ppermute | solution.py:55
  159.8 7.0 %collective-permute-done.7.refs_7_ = bf16[2,64,704]{2,1,0:T(8,128)(2,1)S(1)} collective-permute-done((bf16[2,64,704]{2,1,0:T(8,128)(2,1)}, bf16[2,64,704]{2,1,0:T(8,128)(2,1)S(1)}, u32[]{:S(2)}, u32[]{:S(2)}) %collective-permute-start.7) | collective-permute-done | bytes 180256 | tf_op jit(solution)/shard_map/ppermute | solution.py:55
  174.2 16.6 %collective-permute-done.8.refs_2_ = bf16[8,64,704]{2,1,0:T(8,128)(2,1)S(1)} collective-permute-done((bf16[8,64,704]{2,1,0:T(8,128)(2,1)}, bf16[8,64,704]{2,1,0:T(8,128)(2,1)S(1)}, u32[]{:S(2)}, u32[]{:S(2)}) %collective-permute-start.8) | collective-permute-done | bytes 720928 | tf_op jit(solution)/shard_map/ppermute | solution.py:55
  192.8 15.0 %collective-permute-done.10.refs_4_ = bf16[8,64,704]{2,1,0:T(8,128)(2,1)S(1)} collective-permute-done((bf16[8,64,704]{2,1,0:T(8,128)(2,1)}, bf16[8,64,704]{2,1,0:T(8,128)(2,1)S(1)}, u32[]{:S(2)}, u32[]{:S(2)}) %collective-permute-start.10) | collective-permute-done | bytes 720928 | tf_op jit(solution)/shard_map/ppermute | solution.py:55
  207.8 16.7 %collective-permute-done.12.refs_6_ = bf16[8,64,704]{2,1,0:T(8,128)(2,1)S(1)} collective-permute-done((bf16[8,64,704]{2,1,0:T(8,128)(2,1)S(1)}, bf16[8,64,704]{2,1,0:T(8,128)(2,1)S(1)}, u32[]{:S(2)}, u32[]{:S(2)}) %collective-permute-start.12) | collective-permute-done | bytes 720928 | tf_op jit(solution)/shard_map/ppermute | solution.py:55
  226.2 5.8 shard_map.207
  232.0 7.3 %fusion.5.back_ref = f32[1024,704]{1,0:T(8,128)} fusion(bf16[1024,2048]{1,0:T(8,128)(2,1)} %all-gather.11.cloned.1.call-done.cot_ref, bf16[704,2048]{1,0:T(8,128)(2,1)S(1)} %copy-done), kind=kOutput, calls=%fused_computation.35 | convolution fusion | flops 2952790016 | bytes 9961472 | tf_op jit(solution)/shard_map/dot_general | solution.py:26
  239.3 12.1 %shard_map.208 = (bf16[1024,704]{1,0:T(8,128)(2,1)}, bf16[1024,704]{1,0:T(8,128)(2,1)}, bf16[1024,704]{1,0:T(8,128)(2,1)}) custom-call(bf16[1024,2048]{1,0:T(8,128)(2,1)} %all-gather.9.cloned.1.call-done.x_ref, f32[1024,704]{1,0:T(8,128)} %fusion.5.back_ref, bf16[2,2048,704]{2,1,0:T(8,128)(2,1)} %bitcast.33), custom_call_target="tpu_custom_call" | custom-call | tf_op jit(solution)/shard_map/pallas_call | solution.py:640
  251.4 7.4 %down_grad.1 = (bf16[96,2048]{1,0:T(8,128)(2,1)}, bf16[80,2048]{1,0:T(8,128)(2,1)}, bf16[96,2048]{1,0:T(8,128)(2,1)}, bf16[80,2048]{1,0:T(8,128)(2,1)}, bf16[96,...) custom-call(s32[2]{0:T(128)} %pad_add_fusion.id_ref, ...), custom_call_target="tpu_custom_call" | custom-call | tf_op jit(solution)/shard_map/down_grad/pallas_call | solution.py:275
  258.9 11.4 %shard_map.209 = bf16[1024,2048]{1,0:T(8,128)(2,1)} custom-call(bf16[1024,704]{1,0:T(8,128)(2,1)} %get-tuple-element.98.gate_ref.grad_ref, bf16[1024,704]{1,0:T(8,128)(2,1)} %get-tuple-element.100.up_ref.grad_ref, bf16[2,2048,704]{2,1,0:T(8,128)(2,1)} %bitcast.34), custom_call_target="tpu_custom_call" | custom-call | tf_op jit(solution)/shard_map/pallas_call | solution.py:658
  270.3 65.8 %reduce-scatter.7.cloned.1.call-done.grad_ref = bf16[128,2048]{1,0:T(8,128)(2,1)} async-done(((bf16[1024,2048]{1,0:T(8,128)(2,1)}), bf16[128,2048]{1,0:T(8,128)(2,1)}) %reduce-scatter.7.cloned.1.call-update) | async-done | bytes 524304 | tf_op jit(solution)/shard_map/reduce_scatter | solution.py:666
  341.0 27.1 %all_to_all.32 = bf16[4,128,2048]{2,1,0:T(8,128)(2,1)S(1)} all-to-all(bf16[4,128,2048]{2,1,0:T(8,128)(2,1)S(1)} %broadcast_in_dim.19), channel_id=1, replica_groups=mesh['rep'=4,'shard'=8] {'rep'}, dimensions={0} | all-to-all | bytes 4194304 | tf_op jit(solution)/shard_map/all_to_all | solution.py:43
  372.1 10.2 %all_to_all.33 = bf16[4,512,128]{2,1,0:T(8,128)(2,1)} all-to-all(bf16[4,512,128]{2,1,0:T(8,128)(2,1)S(1)} %bitcast_bitcast_fusion), channel_id=1, replica_groups=mesh['rep'=4,'shard'=8] {'rep'}, dimensions={0} | all-to-all | bytes 1048576 | tf_op jit(solution)/shard_map/all_to_all | solution.py:47
  382.4 8.3 %shard_map.213 = (bf16[4,128,512]{2,1,0:T(8,128)(2,1)}, f32[4,192,128]{2,1,0:T(8,128)}) custom-call(bf16[4,4,128,128]{3,2,1,0:T(8,128)(2,1)} %bitcast.38, f32[4,8,128,192]{3,2,1,0:T(8,128)} %get-tuple-element.105.probs_ref, bf16[4,128,512]{2,1,0:T(8,128)(2,1)} %get-tuple-element.76.q_ref, bf16[4,128,128]{2,1,0:T(8,128)(2,1)} %get-tuple-element.77.own_ref, ...), custom_call_target="tpu_custom_call" | custom-call | tf_op jit(solution)/shard_map/pallas_call | solution.py:709
  395.5 13.0 %shard_map.214 = (bf16[4,128,2048]{2,1,0:T(8,128)(2,1)}, bf16[2048,768]{1,0:T(8,128)(2,1)}) custom-call(bf16[4,128,512]{2,1,0:T(8,128)(2,1)} %get-tuple-element.106.dq_ref, f32[4,192,128]{2,1,0:T(8,128)} %get-tuple-element.107.dkv_ref, f32[4,64,128]{2,1,0:T(8,128)} %copy-done.39, f32[4,128,128]{2,1,0:T(8,128)} %get-tuple-element.144.cos_ref, ...), custom_call_target="tpu_custom_call" | custom-call | tf_op jit(solution)/shard_map/pallas_call | solution.py:728
  408.9 8.1 %shard_map.210 = (bf16[8,64,704]{2,1,0:T(8,128)(2,1)}, bf16[8,64,704]{2,1,0:T(8,128)(2,1)}, bf16[8,64,704]{2,1,0:T(8,128)(2,1)}, bf16[8,64,704]{2,1,0:T(8,128)(2,1)}) custom-call(s32[2]{0:T(128)} %pad_add_fusion.id_ref, bf16[1024,2048]{1,0:T(8,128)(2,1)} %all-gather.9.cloned.1.call-done.x_ref, bf16[1024,704]{1,0:T(8,128)(2,1)} %get-tuple-element.98.gate_ref.grad_ref), custom_call_target="tpu_custom_call" | custom-call | tf_op jit(solution)/shard_map/pallas_call | solution.py:241
  417.0 8.3 %shard_map.211 = (bf16[8,64,704]{2,1,0:T(8,128)(2,1)}, bf16[8,64,704]{2,1,0:T(8,128)(2,1)}, bf16[8,64,704]{2,1,0:T(8,128)(2,1)}, bf16[8,64,704]{2,1,0:T(8,128)(2,1)}) custom-call(s32[2]{0:T(128)} %pad_add_fusion.id_ref, bf16[1024,2048]{1,0:T(8,128)(2,1)} %all-gather.9.cloned.1.call-done.x_ref, bf16[1024,704]{1,0:T(8,128)(2,1)} %get-tuple-element.100.up_ref.grad_ref), custom_call_target="tpu_custom_call" | custom-call | tf_op jit(solution)/shard_map/pallas_call | solution.py:241
  425.3 5.0 convolution_convert_fusion
  435.3 8.7 %collective-permute-done.25 = bf16[8,64,704]{2,1,0:T(8,128)(2,1)S(1)} collective-permute-done((bf16[8,64,704]{2,1,0:T(8,128)(2,1)}, bf16[8,64,704]{2,1,0:T(8,128)(2,1)S(1)}, u32[]{:S(2)}, u32[]{:S(2)}) %collective-permute-start.25) | collective-permute-done | bytes 720928 | tf_op jit(solution)/shard_map/ppermute | solution.py:55
  446.6 4.5 collective-permute-done.44
  451.7 16.2 %collective-permute-done.24.refs_4_ = bf16[8,64,704]{2,1,0:T(8,128)(2,1)S(1)} collective-permute-done((bf16[8,64,704]{2,1,0:T(8,128)(2,1)}, bf16[8,64,704]{2,1,0:T(8,128)(2,1)S(1)}, u32[]{:S(2)}, u32[]{:S(2)}) %collective-permute-start.24) | collective-permute-done | bytes 720928 | tf_op jit(solution)/shard_map/ppermute | solution.py:55
  470.2 8.5 %collective-permute-done.26.refs_5_ = bf16[8,64,704]{2,1,0:T(8,128)(2,1)S(1)} collective-permute-done((bf16[8,64,704]{2,1,0:T(8,128)(2,1)S(1)}, bf16[8,64,704]{2,1,0:T(8,128)(2,1)S(1)}, u32[]{:S(2)}, u32[]{:S(2)}) %collective-permute-start.26) | collective-permute-done | bytes 720928 | tf_op jit(solution)/shard_map/ppermute | solution.py:55
  478.7 6.1 collective-permute-done.23.refs_2_
  485.7 3.9 shard_map.218
  489.6 10.7 %collective-permute-start.27 = (bf16[2,64,704]{2,1,0:T(8,128)(2,1)}, bf16[2,64,704]{2,1,0:T(8,128)(2,1)S(1)}, u32[]{:S(2)}, u32[]{:S(2)}) collective-permute-start(bf16[2,64,704]{2,1,0:T(8,128)(2,1)} %get-tuple-element.125), channel_id=1, source_target_pairs={{0,1},{1,0},{2,3},{3,2},{4,5},{5,4},{6,7},{7,6},{8,9},{9,8},{10,11... | collective-permute-start | bytes 540680 | tf_op jit(solution)/shard_map/ppermute | solution.py:55
  500.3 4.7 collective-permute-start.28
  508.3 6.9 %collective-permute-done.28.refs_2_ = bf16[2,64,704]{2,1,0:T(8,128)(2,1)S(1)} collective-permute-done((bf16[2,64,704]{2,1,0:T(8,128)(2,1)}, bf16[2,64,704]{2,1,0:T(8,128)(2,1)S(1)}, u32[]{:S(2)}, u32[]{:S(2)}) %collective-permute-start.28) | collective-permute-done | bytes 180256 | tf_op jit(solution)/shard_map/ppermute | solution.py:55
  522.6 13.9 %collective-permute-done.31.refs_5_ = bf16[2,64,704]{2,1,0:T(8,128)(2,1)S(1)} collective-permute-done((bf16[2,64,704]{2,1,0:T(8,128)(2,1)}, bf16[2,64,704]{2,1,0:T(8,128)(2,1)S(1)}, u32[]{:S(2)}, u32[]{:S(2)}) %collective-permute-start.31) | collective-permute-done | bytes 180256 | tf_op jit(solution)/shard_map/ppermute | solution.py:55
  548.1 4.5 all-to-all-start.5
  554.6 17.8 %collective-permute-done.48.refs_4_ = bf16[96,2048]{1,0:T(8,128)(2,1)} collective-permute-done((bf16[96,2048]{1,0:T(8,128)(2,1)S(1)}, bf16[96,2048]{1,0:T(8,128)(2,1)}, u32[]{:S(2)}, u32[]{:S(2)}) %collective-permute-start.48) | collective-permute-done | bytes 393248 | tf_op jit(solution)/shard_map/ppermute | solution.py:55
  576.5 25.4 %collective-permute-done.51.refs_7_ = bf16[80,2048]{1,0:T(8,128)(2,1)S(1)} collective-permute-done((bf16[80,2048]{1,0:T(8,128)(2,1)}, bf16[80,2048]{1,0:T(8,128)(2,1)S(1)}, u32[]{:S(2)}, u32[]{:S(2)}) %collective-permute-start.51) | collective-permute-done | bytes 327712 | tf_op jit(solution)/shard_map/ppermute | solution.py:55
  603.5 28.5 %collective-permute-done.50.refs_6_ = bf16[96,2048]{1,0:T(8,128)(2,1)S(1)} collective-permute-done((bf16[96,2048]{1,0:T(8,128)(2,1)}, bf16[96,2048]{1,0:T(8,128)(2,1)S(1)}, u32[]{:S(2)}, u32[]{:S(2)}) %collective-permute-start.50) | collective-permute-done | bytes 393248 | tf_op jit(solution)/shard_map/ppermute | solution.py:55
  633.4 4.6 shard_map.222
  638.1 4.7 shard_map.221
  642.8 4.7 shard_map.220
  655.2 3.7 shard_map.215
  658.9 4.8 collective-permute-done.19.refs_2_
  666.7 4.8 collective-permute-done.16.refs_2_
  (238 shorter events, 119.9 us)
Async XLA Ops:
  7.2 42.5 %all-gather.5.cloned.1.call-start = ((), (), s32[]{:S(2)}) async-start(), calls=%async_computation.10 | async-start | bytes 2949120 | tf_op jit(solution)/shard_map/all_gather | solution.py:562
  10.2 67.3 %all-gather.7.cloned.1.call-start = ((), (), s32[]{:S(2)}) async-start(), calls=%async_computation.11 | async-start | bytes 2359296 | tf_op jit(solution)/shard_map/all_gather | solution.py:563
  12.0 220.0 %all-gather.11.cloned.1.call-start = ((), (), s32[]{:S(2)}) async-start(), calls=%async_computation.13 | async-start | bytes 4718592 | tf_op jit(solution)/shard_map/all_gather | solution.py:588
  14.7 32.5 %all-to-all-start = ((bf16[4,128,2176]{2,1,0:T(8,128)(2,1)}), bf16[4,128,2176]{2,1,0:T(8,128)(2,1)}, u32[]{:S(2)}, u32[]{:S(2)}) async-start(bf16[4,128,2176]{2,1,0:T(8,128)(2,1)} %broadcast_in_dim.18), calls=%async_computation | async-start | bytes 4456448 | tf_op jit(solution)/shard_map/all_to_all | solution.py:43
  20.1 219.3 %all-gather.9.cloned.1.call-start = ((), (), s32[]{:S(2)}) async-start(), calls=%async_computation.12 | async-start | bytes 4718592 | tf_op jit(solution)/shard_map/all_gather | solution.py:634
  111.8 224.3 %reduce-scatter.7.cloned.1.call-start = ((), (), s32[]{:S(2)}) async-start(), calls=%async_computation.15 | async-start | bytes 4718592 | tf_op jit(solution)/shard_map/reduce_scatter | solution.py:666
  118.6 20.5 %collective-permute-start.2 = (bf16[2,64,704]{2,1,0:T(8,128)(2,1)}, bf16[2,64,704]{2,1,0:T(8,128)(2,1)S(1)}, u32[]{:S(2)}, u32[]{:S(2)}) collective-permute-start(bf16[2,64,704]{2,1,0:T(8,128)(2,1)} %get-tuple-element.85), channel_id=1, source_target_pairs={{0,2},{1,3},{2,0},{3,1},{4,6},{5,7},{6,4},{7,5},{8,10},{9,11},{10,... | collective-permute-start | bytes 540680 | tf_op jit(solution)/shard_map/ppermute | solution.py:55
  124.2 24.1 %collective-permute-start.3 = (bf16[2,64,704]{2,1,0:T(8,128)(2,1)}, bf16[2,64,704]{2,1,0:T(8,128)(2,1)S(1)}, u32[]{:S(2)}, u32[]{:S(2)}) collective-permute-start(bf16[2,64,704]{2,1,0:T(8,128)(2,1)} %get-tuple-element.86), channel_id=1, source_target_pairs={{0,3},{1,2},{2,1},{3,0},{4,7},{5,6},{6,5},{7,4},{8,11},{9,10},{10,... | collective-permute-start | bytes 540680 | tf_op jit(solution)/shard_map/ppermute | solution.py:55
  124.3 24.0 %collective-permute-start.4 = (bf16[2,64,704]{2,1,0:T(8,128)(2,1)}, bf16[2,64,704]{2,1,0:T(8,128)(2,1)S(1)}, u32[]{:S(2)}, u32[]{:S(2)}) collective-permute-start(bf16[2,64,704]{2,1,0:T(8,128)(2,1)} %get-tuple-element.87), channel_id=1, source_target_pairs={{0,4},{1,5},{2,6},{3,7},{4,0},{5,1},{6,2},{7,3},{8,12},{9,13},{10,... | collective-permute-start | bytes 540680 | tf_op jit(solution)/shard_map/ppermute | solution.py:55
  126.7 23.6 %collective-permute-start.5 = (bf16[2,64,704]{2,1,0:T(8,128)(2,1)}, bf16[2,64,704]{2,1,0:T(8,128)(2,1)S(1)}, u32[]{:S(2)}, u32[]{:S(2)}) collective-permute-start(bf16[2,64,704]{2,1,0:T(8,128)(2,1)} %get-tuple-element.88), channel_id=1, source_target_pairs={{0,5},{1,4},{2,7},{3,6},{4,1},{5,0},{6,3},{7,2},{8,13},{9,12},{10,... | collective-permute-start | bytes 540680 | tf_op jit(solution)/shard_map/ppermute | solution.py:55
  126.7 33.1 %collective-permute-start.6 = (bf16[2,64,704]{2,1,0:T(8,128)(2,1)}, bf16[2,64,704]{2,1,0:T(8,128)(2,1)S(1)}, u32[]{:S(2)}, u32[]{:S(2)}) collective-permute-start(bf16[2,64,704]{2,1,0:T(8,128)(2,1)} %get-tuple-element.89), channel_id=1, source_target_pairs={{0,6},{1,7},{2,4},{3,5},{4,2},{5,3},{6,0},{7,1},{8,14},{9,15},{10,... | collective-permute-start | bytes 540680 | tf_op jit(solution)/shard_map/ppermute | solution.py:55
  139.1 27.6 %collective-permute-start.7 = (bf16[2,64,704]{2,1,0:T(8,128)(2,1)}, bf16[2,64,704]{2,1,0:T(8,128)(2,1)S(1)}, u32[]{:S(2)}, u32[]{:S(2)}) collective-permute-start(bf16[2,64,704]{2,1,0:T(8,128)(2,1)} %get-tuple-element.90), channel_id=1, source_target_pairs={{0,7},{1,6},{2,5},{3,4},{4,3},{5,2},{6,1},{7,0},{8,15},{9,14},{10,... | collective-permute-start | bytes 540680 | tf_op jit(solution)/shard_map/ppermute | solution.py:55
  170.1 20.6 %collective-permute-start.8 = (bf16[8,64,704]{2,1,0:T(8,128)(2,1)}, bf16[8,64,704]{2,1,0:T(8,128)(2,1)S(1)}, u32[]{:S(2)}, u32[]{:S(2)}) collective-permute-start(bf16[8,64,704]{2,1,0:T(8,128)(2,1)} %get-tuple-element.91.refs_0_), channel_id=1, source_target_pairs={{0,8},{8,0},{16,24},{24,16},{1,9},{9,1},{17,25},{25,17},{2,10},{10... | collective-permute-start | bytes 2162696 | tf_op jit(solution)/shard_map/ppermute | solution.py:55
  170.3 20.6 %collective-permute-start.11 = (bf16[8,64,704]{2,1,0:T(8,128)(2,1)}, bf16[8,64,704]{2,1,0:T(8,128)(2,1)S(1)}, u32[]{:S(2)}, u32[]{:S(2)}) collective-permute-start(bf16[8,64,704]{2,1,0:T(8,128)(2,1)} %get-tuple-element.92.refs_1_), channel_id=1, source_target_pairs={{0,16},{8,24},{16,0},{24,8},{1,17},{9,25},{17,1},{25,9},{2,18},{10... | collective-permute-start | bytes 2162696 | tf_op jit(solution)/shard_map/ppermute | solution.py:55
  170.3 37.5 %collective-permute-start.10 = (bf16[8,64,704]{2,1,0:T(8,128)(2,1)}, bf16[8,64,704]{2,1,0:T(8,128)(2,1)S(1)}, u32[]{:S(2)}, u32[]{:S(2)}) collective-permute-start(bf16[8,64,704]{2,1,0:T(8,128)(2,1)} %get-tuple-element.91.refs_0_), channel_id=1, source_target_pairs={{0,16},{8,24},{16,0},{24,8},{1,17},{9,25},{17,1},{25,9},{2,18},{10... | collective-permute-start | bytes 2162696 | tf_op jit(solution)/shard_map/ppermute | solution.py:55
  172.3 35.5 %collective-permute-start.9 = (bf16[8,64,704]{2,1,0:T(8,128)(2,1)}, bf16[8,64,704]{2,1,0:T(8,128)(2,1)S(1)}, u32[]{:S(2)}, u32[]{:S(2)}) collective-permute-start(bf16[8,64,704]{2,1,0:T(8,128)(2,1)} %get-tuple-element.92.refs_1_), channel_id=1, source_target_pairs={{0,8},{8,0},{16,24},{24,16},{1,9},{9,1},{17,25},{25,17},{2,10},{10... | collective-permute-start | bytes 2162696 | tf_op jit(solution)/shard_map/ppermute | solution.py:55
  190.8 33.7 %collective-permute-start.12 = (bf16[8,64,704]{2,1,0:T(8,128)(2,1)S(1)}, bf16[8,64,704]{2,1,0:T(8,128)(2,1)S(1)}, u32[]{:S(2)}, u32[]{:S(2)}) collective-permute-start(bf16[8,64,704]{2,1,0:T(8,128)(2,1)S(1)} %collective-permute-done.8.refs_2_), channel_id=1, source_target_pairs={{0,16},{8,24},{16,0},{24,8},{1,17},{9,25},{17,1},{25,9},{2,18},{10... | collective-permute-start | bytes 2162696 | tf_op jit(solution)/shard_map/ppermute | solution.py:55
  190.9 33.5 %collective-permute-start.13 = (bf16[8,64,704]{2,1,0:T(8,128)(2,1)S(1)}, bf16[8,64,704]{2,1,0:T(8,128)(2,1)S(1)}, u32[]{:S(2)}, u32[]{:S(2)}) collective-permute-start(bf16[8,64,704]{2,1,0:T(8,128)(2,1)S(1)} %collective-permute-done.11.refs_5_), channel_id=1, source_target_pairs={{0,8},{8,0},{16,24},{24,16},{1,9},{9,1},{17,25},{25,17},{2,10},{10... | collective-permute-start | bytes 2162696 | tf_op jit(solution)/shard_map/ppermute | solution.py:55
  270.3 361.7 %reduce-scatter.11.cloned.1.call-start = ((), (), s32[]{:S(2)}) async-start(), calls=%async_computation.17 | async-start | bytes 2359296 | tf_op jit(solution)/shard_map/reduce_scatter | solution.py:707
  372.0 277.5 %reduce-scatter.9.cloned.1.call-start = ((), (), s32[]{:S(2)}) async-start(), calls=%async_computation.16 | async-start | bytes 3538944 | tf_op jit(solution)/shard_map/reduce_scatter | solution.py:748
  408.6 244.4 %reduce-scatter.5.cloned.1.call-start = ((), (), s32[]{:S(2)}) async-start(), calls=%async_computation.14 | async-start | bytes 4718592 | tf_op jit(solution)/shard_map/reduce_scatter | solution.py:678
  431.7 19.4 %collective-permute-start.44 = (bf16[80,2048]{1,0:T(8,128)(2,1)S(1)}, bf16[80,2048]{1,0:T(8,128)(2,1)S(1)}, u32[]{:S(2)}, u32[]{:S(2)}) collective-permute-start(bf16[80,2048]{1,0:T(8,128)(2,1)S(1)} %copy-done.41), channel_id=1, source_target_pairs={{0,16},{8,24},{16,0},{24,8},{1,17},{9,25},{17,1},{25,9},{2,18},{10... | collective-permute-start | bytes 983048 | tf_op jit(solution)/shard_map/ppermute | solution.py:55
  433.3 34.6 %collective-permute-start.24 = (bf16[8,64,704]{2,1,0:T(8,128)(2,1)}, bf16[8,64,704]{2,1,0:T(8,128)(2,1)S(1)}, u32[]{:S(2)}, u32[]{:S(2)}) collective-permute-start(bf16[8,64,704]{2,1,0:T(8,128)(2,1)} %get-tuple-element.121), channel_id=1, source_target_pairs={{0,16},{8,24},{16,0},{24,8},{1,17},{9,25},{17,1},{25,9},{2,18},{10... | collective-permute-start | bytes 2162696 | tf_op jit(solution)/shard_map/ppermute | solution.py:55
  433.7 35.1 %collective-permute-start.21 = (bf16[8,64,704]{2,1,0:T(8,128)(2,1)}, bf16[8,64,704]{2,1,0:T(8,128)(2,1)S(1)}, u32[]{:S(2)}, u32[]{:S(2)}) collective-permute-start(bf16[8,64,704]{2,1,0:T(8,128)(2,1)} %get-tuple-element.118), channel_id=1, source_target_pairs={{0,8},{8,0},{16,24},{24,16},{1,9},{9,1},{17,25},{25,17},{2,10},{10... | collective-permute-start | bytes 2162696 | tf_op jit(solution)/shard_map/ppermute | solution.py:55
  445.4 33.3 %collective-permute-start.26 = (bf16[8,64,704]{2,1,0:T(8,128)(2,1)S(1)}, bf16[8,64,704]{2,1,0:T(8,128)(2,1)S(1)}, u32[]{:S(2)}, u32[]{:S(2)}) collective-permute-start(bf16[8,64,704]{2,1,0:T(8,128)(2,1)S(1)} %add_convert_fusion), channel_id=1, source_target_pairs={{0,8},{8,0},{16,24},{24,16},{1,9},{9,1},{17,25},{25,17},{2,10},{10... | collective-permute-start | bytes 2162696 | tf_op jit(solution)/shard_map/ppermute | solution.py:55
  446.4 38.3 %collective-permute-start.23 = (bf16[8,64,704]{2,1,0:T(8,128)(2,1)S(1)}, bf16[8,64,704]{2,1,0:T(8,128)(2,1)S(1)}, u32[]{:S(2)}, u32[]{:S(2)}) collective-permute-start(bf16[8,64,704]{2,1,0:T(8,128)(2,1)S(1)} %add_convert_fusion.1), channel_id=1, source_target_pairs={{0,16},{8,24},{16,0},{24,8},{1,17},{9,25},{17,1},{25,9},{2,18},{10... | collective-permute-start | bytes 2162696 | tf_op jit(solution)/shard_map/ppermute | solution.py:55
  451.1 53.9 %collective-permute-start.43 = (bf16[80,2048]{1,0:T(8,128)(2,1)}, bf16[80,2048]{1,0:T(8,128)(2,1)S(1)}, u32[]{:S(2)}, u32[]{:S(2)}) collective-permute-start(bf16[80,2048]{1,0:T(8,128)(2,1)} %get-tuple-element.138), channel_id=1, source_target_pairs={{0,16},{8,24},{16,0},{24,8},{1,17},{9,25},{17,1},{25,9},{2,18},{10... | collective-permute-start | bytes 983048 | tf_op jit(solution)/shard_map/ppermute | solution.py:55
  467.9 37.3 %collective-permute-start.41 = (bf16[96,2048]{1,0:T(8,128)(2,1)}, bf16[96,2048]{1,0:T(8,128)(2,1)S(1)}, u32[]{:S(2)}, u32[]{:S(2)}) collective-permute-start(bf16[96,2048]{1,0:T(8,128)(2,1)} %get-tuple-element.136), channel_id=1, source_target_pairs={{0,8},{8,0},{16,24},{24,16},{1,9},{9,1},{17,25},{25,17},{2,10},{10... | collective-permute-start | bytes 1179656 | tf_op jit(solution)/shard_map/ppermute | solution.py:55
  468.8 37.3 %collective-permute-start.45 = (bf16[80,2048]{1,0:T(8,128)(2,1)S(1)}, bf16[80,2048]{1,0:T(8,128)(2,1)S(1)}, u32[]{:S(2)}, u32[]{:S(2)}) collective-permute-start(bf16[80,2048]{1,0:T(8,128)(2,1)S(1)} %add_convert_fusion.6), channel_id=1, source_target_pairs={{0,8},{8,0},{16,24},{24,16},{1,9},{9,1},{17,25},{25,17},{2,10},{10... | collective-permute-start | bytes 983048 | tf_op jit(solution)/shard_map/ppermute | solution.py:55
  506.2 37.1 %collective-permute-start.40 = (bf16[96,2048]{1,0:T(8,128)(2,1)}, bf16[96,2048]{1,0:T(8,128)(2,1)S(1)}, u32[]{:S(2)}, u32[]{:S(2)}) collective-permute-start(bf16[96,2048]{1,0:T(8,128)(2,1)} %get-tuple-element.134), channel_id=1, source_target_pairs={{0,8},{8,0},{16,24},{24,16},{1,9},{9,1},{17,25},{25,17},{2,10},{10... | collective-permute-start | bytes 1179656 | tf_op jit(solution)/shard_map/ppermute | solution.py:55
  507.0 37.1 %collective-permute-start.42 = (bf16[96,2048]{1,0:T(8,128)(2,1)S(1)}, bf16[96,2048]{1,0:T(8,128)(2,1)S(1)}, u32[]{:S(2)}, u32[]{:S(2)}) collective-permute-start(bf16[96,2048]{1,0:T(8,128)(2,1)S(1)} %add_convert_fusion.4), channel_id=1, source_target_pairs={{0,16},{8,24},{16,0},{24,8},{1,17},{9,25},{17,1},{25,9},{2,18},{10... | collective-permute-start | bytes 1179656 | tf_op jit(solution)/shard_map/ppermute | solution.py:55
  515.2 21.4 %collective-permute-start.31 = (bf16[2,64,704]{2,1,0:T(8,128)(2,1)}, bf16[2,64,704]{2,1,0:T(8,128)(2,1)S(1)}, u32[]{:S(2)}, u32[]{:S(2)}) collective-permute-start(bf16[2,64,704]{2,1,0:T(8,128)(2,1)} %get-tuple-element.129), channel_id=1, source_target_pairs={{0,5},{1,4},{2,7},{3,6},{4,1},{5,0},{6,3},{7,2},{8,13},{9,12},{10,... | collective-permute-start | bytes 540680 | tf_op jit(solution)/shard_map/ppermute | solution.py:55
  518.1 19.6 %collective-permute-start.32 = (bf16[2,64,704]{2,1,0:T(8,128)(2,1)}, bf16[2,64,704]{2,1,0:T(8,128)(2,1)S(1)}, u32[]{:S(2)}, u32[]{:S(2)}) collective-permute-start(bf16[2,64,704]{2,1,0:T(8,128)(2,1)} %get-tuple-element.130), channel_id=1, source_target_pairs={{0,6},{1,7},{2,4},{3,5},{4,2},{5,3},{6,0},{7,1},{8,14},{9,15},{10,... | collective-permute-start | bytes 540680 | tf_op jit(solution)/shard_map/ppermute | solution.py:55
  519.6 19.0 %collective-permute-start.33 = (bf16[2,64,704]{2,1,0:T(8,128)(2,1)}, bf16[2,64,704]{2,1,0:T(8,128)(2,1)S(1)}, u32[]{:S(2)}, u32[]{:S(2)}) collective-permute-start(bf16[2,64,704]{2,1,0:T(8,128)(2,1)} %get-tuple-element.131), channel_id=1, source_target_pairs={{0,7},{1,6},{2,5},{3,4},{4,3},{5,2},{6,1},{7,0},{8,15},{9,14},{10,... | collective-permute-start | bytes 540680 | tf_op jit(solution)/shard_map/ppermute | solution.py:55
  542.1 33.5 %collective-permute-start.34 = (bf16[64,5632]{1,0:T(8,128)(2,1)}, bf16[64,5632]{1,0:T(8,128)(2,1)}, u32[]{:S(2)}, u32[]{:S(2)}) collective-permute-start(bf16[64,5632]{1,0:T(8,128)(2,1)} %get-tuple-element.132.refs_0_), channel_id=1, source_target_pairs={{0,8},{8,0},{16,24},{24,16},{1,9},{9,1},{17,25},{25,17},{2,10},{10... | collective-permute-start | bytes 2162696 | tf_op jit(solution)/shard_map/ppermute | solution.py:55
  543.3 29.1 %collective-permute-start.38 = (bf16[64,5632]{1,0:T(8,128)(2,1)}, bf16[64,5632]{1,0:T(8,128)(2,1)}, u32[]{:S(2)}, u32[]{:S(2)}) collective-permute-start(bf16[64,5632]{1,0:T(8,128)(2,1)} %get-tuple-element.133.refs_0_), channel_id=1, source_target_pairs={{0,16},{8,24},{16,0},{24,8},{1,17},{9,25},{17,1},{25,9},{2,18},{10... | collective-permute-start | bytes 2162696 | tf_op jit(solution)/shard_map/ppermute | solution.py:55
  544.3 28.1 %collective-permute-start.48 = (bf16[96,2048]{1,0:T(8,128)(2,1)S(1)}, bf16[96,2048]{1,0:T(8,128)(2,1)}, u32[]{:S(2)}, u32[]{:S(2)}) collective-permute-start(bf16[96,2048]{1,0:T(8,128)(2,1)S(1)} %add_convert_fusion.3.refs_0_), channel_id=1, source_target_pairs={{0,16},{8,24},{16,0},{24,8},{1,17},{9,25},{17,1},{25,9},{2,18},{10... | collective-permute-start | bytes 1179656 | tf_op jit(solution)/shard_map/ppermute | solution.py:55
  547.4 27.0 %collective-permute-start.46 = (bf16[96,2048]{1,0:T(8,128)(2,1)S(1)}, bf16[96,2048]{1,0:T(8,128)(2,1)}, u32[]{:S(2)}, u32[]{:S(2)}) collective-permute-start(bf16[96,2048]{1,0:T(8,128)(2,1)S(1)} %add_convert_fusion.3.refs_0_), channel_id=1, source_target_pairs={{0,8},{8,0},{16,24},{24,16},{1,9},{9,1},{17,25},{25,17},{2,10},{10... | collective-permute-start | bytes 1179656 | tf_op jit(solution)/shard_map/ppermute | solution.py:55
  548.1 107.1 %all-to-all-start.5 = ((bf16[4,128,2048]{2,1,0:T(8,128)(2,1)}), bf16[4,128,2048]{2,1,0:T(8,128)(2,1)}, u32[]{:S(2)}, u32[]{:S(2)}) async-start(bf16[4,128,2048]{2,1,0:T(8,128)(2,1)} %get-tuple-element.110), calls=%async_computation.7 | async-start | bytes 4194304 | tf_op jit(solution)/shard_map/all_to_all | solution.py:47
  552.6 49.3 %collective-permute-start.51 = (bf16[80,2048]{1,0:T(8,128)(2,1)}, bf16[80,2048]{1,0:T(8,128)(2,1)S(1)}, u32[]{:S(2)}, u32[]{:S(2)}) collective-permute-start(bf16[80,2048]{1,0:T(8,128)(2,1)} %collective-permute-done.49.refs_5_), channel_id=1, source_target_pairs={{0,8},{8,0},{16,24},{24,16},{1,9},{9,1},{17,25},{25,17},{2,10},{10... | collective-permute-start | bytes 983048 | tf_op jit(solution)/shard_map/ppermute | solution.py:55
  572.4 65.7 %collective-permute-start.37 = (bf16[64,5632]{1,0:T(8,128)(2,1)}, bf16[64,5632]{1,0:T(8,128)(2,1)}, u32[]{:S(2)}, u32[]{:S(2)}) collective-permute-start(bf16[64,5632]{1,0:T(8,128)(2,1)} %get-tuple-element.133.refs_0_), channel_id=1, source_target_pairs={{0,8},{8,0},{16,24},{24,16},{1,9},{9,1},{17,25},{25,17},{2,10},{10... | collective-permute-start | bytes 2162696 | tf_op jit(solution)/shard_map/ppermute | solution.py:55
  572.4 65.7 %collective-permute-start.39 = (bf16[64,5632]{1,0:T(8,128)(2,1)}, bf16[64,5632]{1,0:T(8,128)(2,1)}, u32[]{:S(2)}, u32[]{:S(2)}) collective-permute-start(bf16[64,5632]{1,0:T(8,128)(2,1)} %collective-permute-done.38.refs_2_), channel_id=1, source_target_pairs={{0,8},{8,0},{16,24},{24,16},{1,9},{9,1},{17,25},{25,17},{2,10},{10... | collective-permute-start | bytes 2162696 | tf_op jit(solution)/shard_map/ppermute | solution.py:55
  574.5 68.3 %collective-permute-start.35 = (bf16[64,5632]{1,0:T(8,128)(2,1)}, bf16[64,5632]{1,0:T(8,128)(2,1)}, u32[]{:S(2)}, u32[]{:S(2)}) collective-permute-start(bf16[64,5632]{1,0:T(8,128)(2,1)} %get-tuple-element.132.refs_0_), channel_id=1, source_target_pairs={{0,16},{8,24},{16,0},{24,8},{1,17},{9,25},{17,1},{25,9},{2,18},{10... | collective-permute-start | bytes 2162696 | tf_op jit(solution)/shard_map/ppermute | solution.py:55
  575.6 67.1 %collective-permute-start.36 = (bf16[64,5632]{1,0:T(8,128)(2,1)}, bf16[64,5632]{1,0:T(8,128)(2,1)}, u32[]{:S(2)}, u32[]{:S(2)}) collective-permute-start(bf16[64,5632]{1,0:T(8,128)(2,1)} %collective-permute-done.34.refs_1_), channel_id=1, source_target_pairs={{0,16},{8,24},{16,0},{24,8},{1,17},{9,25},{17,1},{25,9},{2,18},{10... | collective-permute-start | bytes 2162696 | tf_op jit(solution)/shard_map/ppermute | solution.py:55
  602.7 29.3 %collective-permute-start.50 = (bf16[96,2048]{1,0:T(8,128)(2,1)}, bf16[96,2048]{1,0:T(8,128)(2,1)S(1)}, u32[]{:S(2)}, u32[]{:S(2)}) collective-permute-start(bf16[96,2048]{1,0:T(8,128)(2,1)} %collective-permute-done.46.refs_2_), channel_id=1, source_target_pairs={{0,16},{8,24},{16,0},{24,8},{1,17},{9,25},{17,1},{25,9},{2,18},{10... | collective-permute-start | bytes 1179656 | tf_op jit(solution)/shard_map/ppermute | solution.py:55
  632.0 19.8 %collective-permute-start.20 = (bf16[64,2048]{1,0:T(8,128)(2,1)}, bf16[64,2048]{1,0:T(8,128)(2,1)}, u32[]{:S(2)}, u32[]{:S(2)}) collective-permute-start(bf16[64,2048]{1,0:T(8,128)(2,1)} %reduce-scatter.11.cloned.1.call-done.refs_0_), channel_id=1, source_target_pairs={{0,24},{8,16},{16,8},{24,0},{1,25},{9,17},{17,9},{25,1},{2,26},{10... | collective-permute-start | bytes 786440 | tf_op jit(solution)/shard_map/ppermute | solution.py:55
  651.0 20.6 %collective-permute-start.16 = (bf16[256,768]{1,0:T(8,128)(2,1)}, bf16[256,768]{1,0:T(8,128)(2,1)}, u32[]{:S(2)}, u32[]{:S(2)}) collective-permute-start(bf16[256,768]{1,0:T(8,128)(2,1)} %reduce-scatter.9.cloned.1.call-done.refs_0_), channel_id=1, source_target_pairs={{0,16},{8,24},{16,0},{24,8},{1,17},{9,25},{17,1},{25,9},{2,18},{10... | collective-permute-start | bytes 1179656 | tf_op jit(solution)/shard_map/ppermute | solution.py:55
  651.7 20.4 %collective-permute-start.15 = (bf16[256,768]{1,0:T(8,128)(2,1)}, bf16[256,768]{1,0:T(8,128)(2,1)}, u32[]{:S(2)}, u32[]{:S(2)}) collective-permute-start(bf16[256,768]{1,0:T(8,128)(2,1)} %reduce-scatter.9.cloned.1.call-done.refs_0_), channel_id=1, source_target_pairs={{0,8},{8,0},{16,24},{24,16},{1,9},{9,1},{17,25},{25,17},{2,10},{10... | collective-permute-start | bytes 1179656 | tf_op jit(solution)/shard_map/ppermute | solution.py:55
  (59 other events, 1036.1 us)
Sparse Core Ops, SparseCore 0:
  10.4 36.4 all-gather.4
  49.1 28.2 all-gather.6
  79.0 46.9 all-gather.10
  127.4 69.6 all-gather.8
  270.4 65.6 reduce-scatter.6
  372.1 35.2 reduce-scatter.10
  409.8 44.9 reduce-scatter.8
  457.0 49.1 reduce-scatter.4

commit v6 on v3

--- a/solution.py
+++ b/solution.py
@@ -436,22 +436,21 @@
     out_ref[...] = out.astype(BF)
 
 
-def forward_back_kernel(
-    x_ref, cot_ref, pair_ref, down_ref, mixed_ref, gate_out, up_out, part_ref
-):
+def forward_kernel(x_ref, back_ref, pair_ref, mixed_ref, gate_out, up_out):
     x = x_ref[...]
     gate = rows_cols(x, pair_ref[0])
     up = rows_cols(x, pair_ref[1])
-    mixed_grad = cols_cols(cot_ref[...], down_ref[...])
+    mixed_grad = back_ref[...]
     sigma = jax.nn.sigmoid(gate)
     silu = gate * sigma
     mixed_ref[...] = (silu * up).astype(BF)
-    gate_grad = (mixed_grad * up * sigma * (1.0 + gate * (1.0 - sigma))).astype(BF)
-    up_grad = (mixed_grad * silu).astype(BF)
-    gate_out[...] = gate_grad
-    up_out[...] = up_grad
+    gate_out[...] = (mixed_grad * up * sigma * (1.0 + gate * (1.0 - sigma))).astype(BF)
+    up_out[...] = (mixed_grad * silu).astype(BF)
+
+
+def back_kernel(gate_ref, up_ref, pair_ref, part_ref):
     part_ref[...] = (
-        cols_cols(gate_grad, pair_ref[0]) + cols_cols(up_grad, pair_ref[1])
+        cols_cols(gate_ref[...], pair_ref[0]) + cols_cols(up_ref[...], pair_ref[1])
     ).astype(BF)
 
 
@@ -600,45 +599,53 @@
     )(swap(mid_part, "rep"), tokens, gain_two)
 
     two_all = lax.all_gather(normed_two, "shard", axis=0, tiled=True)
+    mixed_grad = cols_cols(cot_all, down_weight)
     step = 256
     group = two_all.shape[0]
     token_block = pl.BlockSpec((step, width), lambda g: (g, 0))
     hidden_block = pl.BlockSpec((step, hidden), lambda g: (g, 0))
-    mixed, gate_grad, up_grad, two_grad_part = call(
-        forward_back_kernel,
-        (shape((group, hidden), BF),) * 3 + (shape((group, width), BF),),
+    mixed, gate_grad, up_grad = call(
+        forward_kernel,
+        (shape((group, hidden), BF),) * 3,
         (group // step,),
-        [token_block, token_block, whole((2, width, hidden)), whole((hidden, width))],
-        (hidden_block,) * 3 + (token_block,),
-    )(two_all, cot_all, w_pair, down_weight)
+        [token_block, hidden_block, whole((2, width, hidden))],
+        (hidden_block,) * 3,
+    )(two_all, mixed_grad, w_pair)
+    gate_chunks = pair_grad(ids, two_all, gate_grad, fine, n_rep, n_shard)
+    gate_tied, _ = lax.optimization_barrier((gate_grad, gate_chunks[0]))
+    two_grad_part = call(
+        back_kernel,
+        shape((group, width), BF),
+        (group // step,),
+        [hidden_block, hidden_block, whole((2, width, hidden))],
+        token_block,
+    )(gate_tied, up_grad, w_pair)
+    up_grad, _ = lax.optimization_barrier((up_grad, two_grad_part))
     two_grad = lax.psum_scatter(two_grad_part, "shard", scatter_dimension=0, tiled=True)
     mid_grad, branch, gain_two_rows = call(
         middle_back_kernel,
         (shape((rows, width), F32), shape((rows, width), BF), shape((rows, width), BF)),
     )(two_grad, x_mid, gain_two, cotangent)
 
-    gate_chunks = pair_grad(ids, two_all, gate_grad, fine, n_rep, n_shard)
-    up_grad, _ = lax.optimization_barrier((up_grad, gate_chunks[0]))
     up_chunks = pair_grad(ids, two_all, up_grad, fine, n_rep, n_shard)
     pair_chunks = list(zip(gate_chunks, up_chunks))
     mixed, _ = lax.optimization_barrier((mixed, up_chunks[0]))
     part_rows = hidden // n_rep
     cut = (part_rows // 2 + 15) // 16 * 16
-    w_down_grad = rows_rows(mixed, cot_all).astype(BF)
-    mixed, w_down_grad = lax.optimization_barrier((mixed, w_down_grad))
+    down_grad = rows_rows(mixed, cot_all).astype(BF)
+    down_chunks = []
+    for k in range(n_rep):
+        at = (r ^ k) * part_rows
+        down_chunks.append(
+            (
+                lax.dynamic_slice_in_dim(down_grad, at, cut, 0),
+                lax.dynamic_slice_in_dim(down_grad, at + cut, part_rows - cut, 0),
+            )
+        )
     down_part = rows_cols(mixed, down_weight).astype(BF)
     down_rows = lax.psum_scatter(down_part, "shard", scatter_dimension=0, tiled=True)
     layer_out = (x_mid + down_rows.astype(F32)).astype(BF)
-    chunks = []
-    for k in range(n_rep):
-        at = (r ^ k) * part_rows
-        chunks.append(
-            (
-                lax.dynamic_slice_in_dim(w_down_grad, at, cut, 0),
-                lax.dynamic_slice_in_dim(w_down_grad, at + cut, part_rows - cut, 0),
-            )
-        )
-    w_down_grad = parts_rep(chunks, n_rep)
+    w_down_grad = parts_rep(down_chunks, n_rep)
     w_down_grad = tuple(
         sum(part.astype(F32) for part in parts).astype(BF) for parts in w_down_grad
     )

time: 685 us -> 698 us (1.019)
  matrix products: 16.2 us -> 25.2 us
    ppermute x50, waiting for transfers between devices: 217 us -> 237 us  [send(): return lax.ppermute(value, axis, pairs(count, step))]
    reduce_scatter x1, waiting for transfers between devices: 80.5 us -> 65.7 us  [body(): lax.psum_scatter(two_grad_part, 'shard', scatter_dimension=0, tiled=True)]
    dot_general x5 -> x6, matrix products: 16.2 us -> 25.2 us  [dot(): lax.dot_general(left, right, (contract, ((), ())), preferred_element_type...]
    pallas_call x1 -> x2, Pallas kernels: 25.4 us -> 23.5 us  [the longest x1 12.1 us: body(): call(forward_kernel, (shape((group, hidden), BF),) * 3, (group // step,),...]
  transfers between devices with their start and end apart: 62 -> 62, of which waited for: 27 -> 29; matrix products, arithmetic and copies ran while one was open for 5% -> 6% of each run, Pallas kernels for 14% -> 12%
where the time goes in v6:
time: 698 us; the launch traced here: 689 us
  waiting for transfers between devices  319 us (46%)
  Pallas kernels  123 us (18%)
  blocking collectives  89.5 us (13%)
  starting transfers between devices  85.2 us (12%)
  matrix products  25.2 us (4%)
  local copies, waits for them, and re-layouts  17.7 us (3%)
  between operations  14.9 us (2%)
  other arithmetic  14.4 us (2%)
    ppermute x50, waiting for transfers between devices, send(): return lax.ppermute(value, axis, pairs(count, step))  237 us
    ppermute x50, starting transfers between devices, send(): return lax.ppermute(value, axis, pairs(count, step))  71.9 us
    reduce_scatter x1, waiting for transfers between devices, body(): lax.psum_scatter(two_grad_part, 'shard', scatter_dimension=0, tiled=True)  65.7 us
    all_to_all x3, blocking collectives, swap(): return lax.all_to_all(value, axis, split_axis=0, concat_axis=0, tiled=True)  48.6 us
    all_to_all x1, blocking collectives, spread(): return lax.all_to_all(wide, axis, split_axis=0, concat_axis=0, tiled=True)  27.6 us
    dot_general x6, matrix products, dot(): lax.dot_general(left, right, (contract, ((), ())), preferred_element_type...  25.2 us
    pallas_call x5, Pallas kernels, flat_call(): pl.pallas_call(kernel, out_shape=out_shape, in_specs=specs, scratch_shape...  18.4 us
    pallas_call x4, Pallas kernels, place(): pl.pallas_call(partial(place_kernel, count), out_shape=shape((count, rows...  17.1 us
  transfers between devices with their start and end apart: 62, of which 29 were waited for; matrix products, arithmetic and copies ran while one was open for 6% of the time, Pallas kernels for 12%

profile of v6, /device:TPU:0, one launch (start us, length us, event | category | flops | bytes accessed | tf_op | source)
XLA Modules:
  0.0 689.3 jit_solution(9941141670096125977)
XLA Ops:
  14.7 5.3 all-to-all-start
  20.1 13.3 %all_gather.15 = bf16[2,2048]{1,0:T(2,128)(2,1)S(1)} all-gather(bf16[2,256]{1,0:T(2,128)(2,1)S(1)} %pad_maximum_fusion.2), channel_id=1, replica_groups=mesh['rep'=4,'shard'=8] {'shard'}, dimensions={1}, use_global_device_ids=true | all-gather | bytes 9216 | tf_op jit(solution)/shard_map/all_gather | solution.py:534
  34.1 13.2 %all-to-all-done.x_ref.pos_ref = bf16[4,128,2176]{2,1,0:T(8,128)(2,1)} async-done(((bf16[4,128,2176]{2,1,0:T(8,128)(2,1)}), bf16[4,128,2176]{2,1,0:T(8,128)(2,1)}, u32[]{:S(2)}, u32[]{:S(2)}) %all-to-all-start) | async-done | bytes 2228256 | tf_op jit(solution)/shard_map/all_to_all | solution.py:43
  49.7 6.2 shard_map.203
  59.6 6.4 shard_map.204
  66.0 10.6 %all_to_all.30 = bf16[4,4,128,128]{3,2,1,0:T(8,128)(2,1)S(1)} all-to-all(bf16[4,4,128,128]{3,2,1,0:T(8,128)(2,1)} %get-tuple-element.69), channel_id=1, replica_groups=mesh['rep'=4,'shard'=8] {'rep'}, dimensions={0} | all-to-all | bytes 1048576 | tf_op jit(solution)/shard_map/all_to_all | solution.py:47
  80.6 27.8 %all_to_all.31.part_ref = bf16[4,128,2048]{2,1,0:T(8,128)(2,1)} all-to-all(bf16[4,128,2048]{2,1,0:T(8,128)(2,1)S(1)} %bitcast.44), channel_id=1, replica_groups=mesh['rep'=4,'shard'=8] {'rep'}, dimensions={0} | all-to-all | bytes 4194304 | tf_op jit(solution)/shard_map/all_to_all | solution.py:47
  118.6 5.6 collective-permute-start.2
  128.8 10.3 %collective-permute-done.2.refs_2_ = bf16[2,64,704]{2,1,0:T(8,128)(2,1)S(1)} collective-permute-done((bf16[2,64,704]{2,1,0:T(8,128)(2,1)}, bf16[2,64,704]{2,1,0:T(8,128)(2,1)S(1)}, u32[]{:S(2)}, u32[]{:S(2)}) %collective-permute-start.2) | collective-permute-done | bytes 180256 | tf_op jit(solution)/shard_map/ppermute | solution.py:55
  139.7 8.7 %collective-permute-done.3.refs_3_ = bf16[2,64,704]{2,1,0:T(8,128)(2,1)S(1)} collective-permute-done((bf16[2,64,704]{2,1,0:T(8,128)(2,1)}, bf16[2,64,704]{2,1,0:T(8,128)(2,1)S(1)}, u32[]{:S(2)}, u32[]{:S(2)}) %collective-permute-start.3) | collective-permute-done | bytes 180256 | tf_op jit(solution)/shard_map/ppermute | solution.py:55
  150.4 9.5 %collective-permute-done.6.refs_6_ = bf16[2,64,704]{2,1,0:T(8,128)(2,1)S(1)} collective-permute-done((bf16[2,64,704]{2,1,0:T(8,128)(2,1)}, bf16[2,64,704]{2,1,0:T(8,128)(2,1)S(1)}, u32[]{:S(2)}, u32[]{:S(2)}) %collective-permute-start.6) | collective-permute-done | bytes 180256 | tf_op jit(solution)/shard_map/ppermute | solution.py:55
  159.8 6.9 %collective-permute-done.7.refs_7_ = bf16[2,64,704]{2,1,0:T(8,128)(2,1)S(1)} collective-permute-done((bf16[2,64,704]{2,1,0:T(8,128)(2,1)}, bf16[2,64,704]{2,1,0:T(8,128)(2,1)S(1)}, u32[]{:S(2)}, u32[]{:S(2)}) %collective-permute-start.7) | collective-permute-done | bytes 180256 | tf_op jit(solution)/shard_map/ppermute | solution.py:55
  174.2 16.6 %collective-permute-done.8.refs_2_ = bf16[8,64,704]{2,1,0:T(8,128)(2,1)S(1)} collective-permute-done((bf16[8,64,704]{2,1,0:T(8,128)(2,1)}, bf16[8,64,704]{2,1,0:T(8,128)(2,1)S(1)}, u32[]{:S(2)}, u32[]{:S(2)}) %collective-permute-start.8) | collective-permute-done | bytes 720928 | tf_op jit(solution)/shard_map/ppermute | solution.py:55
  192.8 14.8 %collective-permute-done.9.refs_3_ = bf16[8,64,704]{2,1,0:T(8,128)(2,1)S(1)} collective-permute-done((bf16[8,64,704]{2,1,0:T(8,128)(2,1)}, bf16[8,64,704]{2,1,0:T(8,128)(2,1)S(1)}, u32[]{:S(2)}, u32[]{:S(2)}) %collective-permute-start.9) | collective-permute-done | bytes 720928 | tf_op jit(solution)/shard_map/ppermute | solution.py:55
  207.8 16.7 %collective-permute-done.12.refs_6_ = bf16[8,64,704]{2,1,0:T(8,128)(2,1)S(1)} collective-permute-done((bf16[8,64,704]{2,1,0:T(8,128)(2,1)S(1)}, bf16[8,64,704]{2,1,0:T(8,128)(2,1)S(1)}, u32[]{:S(2)}, u32[]{:S(2)}) %collective-permute-start.12) | collective-permute-done | bytes 720928 | tf_op jit(solution)/shard_map/ppermute | solution.py:55
  226.3 5.8 shard_map.207
  232.1 7.3 %fusion.5.back_ref = f32[1024,704]{1,0:T(8,128)} fusion(bf16[1024,2048]{1,0:T(8,128)(2,1)} %all-gather.11.cloned.1.call-done, bf16[704,2048]{1,0:T(8,128)(2,1)S(1)} %copy-done), kind=kOutput, calls=%fused_computation.40 | convolution fusion | flops 2952790016 | bytes 9961472 | tf_op jit(solution)/shard_map/dot_general | solution.py:26
  239.4 12.1 %shard_map.208 = (bf16[1024,704]{1,0:T(8,128)(2,1)}, bf16[1024,704]{1,0:T(8,128)(2,1)}, bf16[1024,704]{1,0:T(8,128)(2,1)}) custom-call(bf16[1024,2048]{1,0:T(8,128)(2,1)} %all-gather.9.cloned.1.call-done.x_ref, f32[1024,704]{1,0:T(8,128)} %fusion.5.back_ref, bf16[2,2048,704]{2,1,0:T(8,128)(2,1)} %bitcast.35), custom_call_target="tpu_custom_call" | custom-call | tf_op jit(solution)/shard_map/pallas_call | solution.py:607
  251.5 8.1 %shard_map.209 = (bf16[8,64,704]{2,1,0:T(8,128)(2,1)}, bf16[8,64,704]{2,1,0:T(8,128)(2,1)}, bf16[8,64,704]{2,1,0:T(8,128)(2,1)}, bf16[8,64,704]{2,1,0:T(8,128)(2,1)}) custom-call(s32[2]{0:T(128)} %pad_add_fusion.id_ref, bf16[1024,2048]{1,0:T(8,128)(2,1)} %all-gather.9.cloned.1.call-done.x_ref, bf16[1024,704]{1,0:T(8,128)(2,1)} %get-tuple-element.88.grad_ref.gate_ref), custom_call_target="tpu_custom_call" | custom-call | tf_op jit(solution)/shard_map/pallas_call | solution.py:244
  259.6 11.4 %shard_map.210 = bf16[1024,2048]{1,0:T(8,128)(2,1)} custom-call(bf16[1024,704]{1,0:T(8,128)(2,1)} %get-tuple-element.88.grad_ref.gate_ref, bf16[1024,704]{1,0:T(8,128)(2,1)} %get-tuple-element.89.up_ref.grad_ref, bf16[2,2048,704]{2,1,0:T(8,128)(2,1)} %bitcast.36), custom_call_target="tpu_custom_call" | custom-call | tf_op jit(solution)/shard_map/pallas_call | solution.py:616
  271.1 65.7 %reduce-scatter.7.cloned.1.call-done.grad_ref = bf16[128,2048]{1,0:T(8,128)(2,1)} async-done(((bf16[1024,2048]{1,0:T(8,128)(2,1)}), bf16[128,2048]{1,0:T(8,128)(2,1)}) %reduce-scatter.7.cloned.1.call-update) | async-done | bytes 524304 | tf_op jit(solution)/shard_map/reduce_scatter | solution.py:624
  336.8 3.6 shard_map.212
  341.7 27.6 %all_to_all.32 = bf16[4,128,2048]{2,1,0:T(8,128)(2,1)S(1)} all-to-all(bf16[4,128,2048]{2,1,0:T(8,128)(2,1)S(1)} %broadcast_in_dim.19), channel_id=1, replica_groups=mesh['rep'=4,'shard'=8] {'rep'}, dimensions={0} | all-to-all | bytes 4194304 | tf_op jit(solution)/shard_map/all_to_all | solution.py:43
  373.4 10.2 %all_to_all.33 = bf16[4,512,128]{2,1,0:T(8,128)(2,1)} all-to-all(bf16[4,512,128]{2,1,0:T(8,128)(2,1)S(1)} %bitcast_bitcast_fusion), channel_id=1, replica_groups=mesh['rep'=4,'shard'=8] {'rep'}, dimensions={0} | all-to-all | bytes 1048576 | tf_op jit(solution)/shard_map/all_to_all | solution.py:47
  383.6 8.3 %shard_map.213 = (bf16[4,128,512]{2,1,0:T(8,128)(2,1)}, f32[4,192,128]{2,1,0:T(8,128)}) custom-call(bf16[4,4,128,128]{3,2,1,0:T(8,128)(2,1)} %bitcast.40, f32[4,8,128,192]{3,2,1,0:T(8,128)} %get-tuple-element.94.probs_ref, bf16[4,128,512]{2,1,0:T(8,128)(2,1)} %get-tuple-element.67.q_ref, bf16[4,128,128]{2,1,0:T(8,128)(2,1)} %get-tuple-element.68.own_ref, ...), custom_call_target="tpu_custom_call" | custom-call | tf_op jit(solution)/shard_map/pallas_call | solution.py:680
  396.7 13.0 %shard_map.214 = (bf16[4,128,2048]{2,1,0:T(8,128)(2,1)}, bf16[2048,768]{1,0:T(8,128)(2,1)}) custom-call(bf16[4,128,512]{2,1,0:T(8,128)(2,1)} %get-tuple-element.95.dq_ref, f32[4,192,128]{2,1,0:T(8,128)} %get-tuple-element.96.dkv_ref, f32[4,64,128]{2,1,0:T(8,128)} %copy-done.30, f32[4,128,128]{2,1,0:T(8,128)} %get-tuple-element.130.cos_ref, ...), custom_call_target="tpu_custom_call" | custom-call | tf_op jit(solution)/shard_map/pallas_call | solution.py:699
  410.0 8.3 %shard_map.211 = (bf16[8,64,704]{2,1,0:T(8,128)(2,1)}, bf16[8,64,704]{2,1,0:T(8,128)(2,1)}, bf16[8,64,704]{2,1,0:T(8,128)(2,1)}, bf16[8,64,704]{2,1,0:T(8,128)(2,1)}) custom-call(s32[2]{0:T(128)} %pad_add_fusion.id_ref, bf16[1024,2048]{1,0:T(8,128)(2,1)} %all-gather.9.cloned.1.call-done.x_ref, bf16[1024,704]{1,0:T(8,128)(2,1)} %get-tuple-element.89.up_ref.grad_ref), custom_call_target="tpu_custom_call" | custom-call | tf_op jit(solution)/shard_map/pallas_call | solution.py:244
  418.3 5.0 convolution_convert_fusion
  427.5 5.9 convolution_convert_fusion.1
  435.1 18.9 %collective-permute-done.22 = bf16[8,64,704]{2,1,0:T(8,128)(2,1)S(1)} collective-permute-done((bf16[8,64,704]{2,1,0:T(8,128)(2,1)}, bf16[8,64,704]{2,1,0:T(8,128)(2,1)S(1)}, u32[]{:S(2)}, u32[]{:S(2)}) %collective-permute-start.22) | collective-permute-done | bytes 720928 | tf_op jit(solution)/shard_map/ppermute | solution.py:55
  459.6 4.0 collective-permute-done.44
  467.6 13.0 %collective-permute-done.23.refs_2_ = bf16[8,64,704]{2,1,0:T(8,128)(2,1)} collective-permute-done((bf16[8,64,704]{2,1,0:T(8,128)(2,1)}, bf16[8,64,704]{2,1,0:T(8,128)(2,1)}, u32[]{:S(2)}, u32[]{:S(2)}) %collective-permute-start.23) | collective-permute-done | bytes 720928 | tf_op jit(solution)/shard_map/ppermute | solution.py:55
  480.6 3.9 shard_map.218
  484.5 10.0 %collective-permute-start.27 = (bf16[2,64,704]{2,1,0:T(8,128)(2,1)}, bf16[2,64,704]{2,1,0:T(8,128)(2,1)S(1)}, u32[]{:S(2)}, u32[]{:S(2)}) collective-permute-start(bf16[2,64,704]{2,1,0:T(8,128)(2,1)} %get-tuple-element.114), channel_id=1, source_target_pairs={{0,1},{1,0},{2,3},{3,2},{4,5},{5,4},{6,7},{7,6},{8,9},{9,8},{10,11... | collective-permute-start | bytes 540680 | tf_op jit(solution)/shard_map/ppermute | solution.py:55
  494.4 3.9 collective-permute-start.28
  503.9 9.9 %collective-permute-done.28.refs_2_ = bf16[2,64,704]{2,1,0:T(8,128)(2,1)S(1)} collective-permute-done((bf16[2,64,704]{2,1,0:T(8,128)(2,1)}, bf16[2,64,704]{2,1,0:T(8,128)(2,1)S(1)}, u32[]{:S(2)}, u32[]{:S(2)}) %collective-permute-start.28) | collective-permute-done | bytes 180256 | tf_op jit(solution)/shard_map/ppermute | solution.py:55
  513.8 4.0 collective-permute-done.29.refs_3_
  523.1 13.2 %collective-permute-done.31.refs_5_ = bf16[2,64,704]{2,1,0:T(8,128)(2,1)S(1)} collective-permute-done((bf16[2,64,704]{2,1,0:T(8,128)(2,1)}, bf16[2,64,704]{2,1,0:T(8,128)(2,1)S(1)}, u32[]{:S(2)}, u32[]{:S(2)}) %collective-permute-start.31) | collective-permute-done | bytes 180256 | tf_op jit(solution)/shard_map/ppermute | solution.py:55
  548.6 4.7 all-to-all-start.5
  555.4 15.6 %collective-permute-done.46.refs_2_ = bf16[96,2048]{1,0:T(8,128)(2,1)} collective-permute-done((bf16[96,2048]{1,0:T(8,128)(2,1)S(1)}, bf16[96,2048]{1,0:T(8,128)(2,1)}, u32[]{:S(2)}, u32[]{:S(2)}) %collective-permute-start.46) | collective-permute-done | bytes 393248 | tf_op jit(solution)/shard_map/ppermute | solution.py:55
  573.0 10.7 %collective-permute-done.48.refs_4_ = bf16[96,2048]{1,0:T(8,128)(2,1)} collective-permute-done((bf16[96,2048]{1,0:T(8,128)(2,1)S(1)}, bf16[96,2048]{1,0:T(8,128)(2,1)}, u32[]{:S(2)}, u32[]{:S(2)}) %collective-permute-start.48) | collective-permute-done | bytes 393248 | tf_op jit(solution)/shard_map/ppermute | solution.py:55
  585.8 14.8 %collective-permute-done.51.refs_7_ = bf16[80,2048]{1,0:T(8,128)(2,1)} collective-permute-done((bf16[80,2048]{1,0:T(8,128)(2,1)}, bf16[80,2048]{1,0:T(8,128)(2,1)}, u32[]{:S(2)}, u32[]{:S(2)}) %collective-permute-start.51) | collective-permute-done | bytes 327712 | tf_op jit(solution)/shard_map/ppermute | solution.py:55
  602.0 31.1 %collective-permute-done.50.refs_6_ = bf16[96,2048]{1,0:T(8,128)(2,1)} collective-permute-done((bf16[96,2048]{1,0:T(8,128)(2,1)}, bf16[96,2048]{1,0:T(8,128)(2,1)}, u32[]{:S(2)}, u32[]{:S(2)}) %collective-permute-start.50) | collective-permute-done | bytes 393248 | tf_op jit(solution)/shard_map/ppermute | solution.py:55
  633.7 4.6 shard_map.222
  638.4 4.7 shard_map.220
  643.1 4.7 shard_map.221
  656.4 3.7 shard_map.215
  666.8 10.5 %collective-permute-done.16.refs_2_ = bf16[256,768]{1,0:T(8,128)(2,1)} collective-permute-done((bf16[256,768]{1,0:T(8,128)(2,1)}, bf16[256,768]{1,0:T(8,128)(2,1)}, u32[]{:S(2)}, u32[]{:S(2)}) %collective-permute-start.16) | collective-permute-done | bytes 393248 | tf_op jit(solution)/shard_map/ppermute | solution.py:55
  (222 shorter events, 124.3 us)
Async XLA Ops:
  7.2 42.5 %all-gather.5.cloned.1.call-start = ((), (), s32[]{:S(2)}) async-start(), calls=%async_computation.10 | async-start | bytes 2949120 | tf_op jit(solution)/shard_map/all_gather | solution.py:529
  10.2 67.3 %all-gather.7.cloned.1.call-start = ((), (), s32[]{:S(2)}) async-start(), calls=%async_computation.11 | async-start | bytes 2359296 | tf_op jit(solution)/shard_map/all_gather | solution.py:530
  12.0 220.1 %all-gather.11.cloned.1.call-start = ((), (), s32[]{:S(2)}) async-start(), calls=%async_computation.13 | async-start | bytes 4718592 | tf_op jit(solution)/shard_map/all_gather | solution.py:555
  14.7 32.5 %all-to-all-start = ((bf16[4,128,2176]{2,1,0:T(8,128)(2,1)}), bf16[4,128,2176]{2,1,0:T(8,128)(2,1)}, u32[]{:S(2)}, u32[]{:S(2)}) async-start(bf16[4,128,2176]{2,1,0:T(8,128)(2,1)} %broadcast_in_dim.18), calls=%async_computation | async-start | bytes 4456448 | tf_op jit(solution)/shard_map/all_to_all | solution.py:43
  20.1 219.3 %all-gather.9.cloned.1.call-start = ((), (), s32[]{:S(2)}) async-start(), calls=%async_computation.12 | async-start | bytes 4718592 | tf_op jit(solution)/shard_map/all_gather | solution.py:601
  111.7 225.1 %reduce-scatter.7.cloned.1.call-start = ((), (), s32[]{:S(2)}) async-start(), calls=%async_computation.15 | async-start | bytes 4718592 | tf_op jit(solution)/shard_map/reduce_scatter | solution.py:624
  118.6 20.5 %collective-permute-start.2 = (bf16[2,64,704]{2,1,0:T(8,128)(2,1)}, bf16[2,64,704]{2,1,0:T(8,128)(2,1)S(1)}, u32[]{:S(2)}, u32[]{:S(2)}) collective-permute-start(bf16[2,64,704]{2,1,0:T(8,128)(2,1)} %get-tuple-element.76), channel_id=1, source_target_pairs={{0,2},{1,3},{2,0},{3,1},{4,6},{5,7},{6,4},{7,5},{8,10},{9,11},{10,... | collective-permute-start | bytes 540680 | tf_op jit(solution)/shard_map/ppermute | solution.py:55
  124.2 24.2 %collective-permute-start.3 = (bf16[2,64,704]{2,1,0:T(8,128)(2,1)}, bf16[2,64,704]{2,1,0:T(8,128)(2,1)S(1)}, u32[]{:S(2)}, u32[]{:S(2)}) collective-permute-start(bf16[2,64,704]{2,1,0:T(8,128)(2,1)} %get-tuple-element.77), channel_id=1, source_target_pairs={{0,3},{1,2},{2,1},{3,0},{4,7},{5,6},{6,5},{7,4},{8,11},{9,10},{10,... | collective-permute-start | bytes 540680 | tf_op jit(solution)/shard_map/ppermute | solution.py:55
  124.3 24.1 %collective-permute-start.4 = (bf16[2,64,704]{2,1,0:T(8,128)(2,1)}, bf16[2,64,704]{2,1,0:T(8,128)(2,1)S(1)}, u32[]{:S(2)}, u32[]{:S(2)}) collective-permute-start(bf16[2,64,704]{2,1,0:T(8,128)(2,1)} %get-tuple-element.78), channel_id=1, source_target_pairs={{0,4},{1,5},{2,6},{3,7},{4,0},{5,1},{6,2},{7,3},{8,12},{9,13},{10,... | collective-permute-start | bytes 540680 | tf_op jit(solution)/shard_map/ppermute | solution.py:55
  126.7 23.6 %collective-permute-start.5 = (bf16[2,64,704]{2,1,0:T(8,128)(2,1)}, bf16[2,64,704]{2,1,0:T(8,128)(2,1)S(1)}, u32[]{:S(2)}, u32[]{:S(2)}) collective-permute-start(bf16[2,64,704]{2,1,0:T(8,128)(2,1)} %get-tuple-element.79), channel_id=1, source_target_pairs={{0,5},{1,4},{2,7},{3,6},{4,1},{5,0},{6,3},{7,2},{8,13},{9,12},{10,... | collective-permute-start | bytes 540680 | tf_op jit(solution)/shard_map/ppermute | solution.py:55
  126.7 33.1 %collective-permute-start.6 = (bf16[2,64,704]{2,1,0:T(8,128)(2,1)}, bf16[2,64,704]{2,1,0:T(8,128)(2,1)S(1)}, u32[]{:S(2)}, u32[]{:S(2)}) collective-permute-start(bf16[2,64,704]{2,1,0:T(8,128)(2,1)} %get-tuple-element.80), channel_id=1, source_target_pairs={{0,6},{1,7},{2,4},{3,5},{4,2},{5,3},{6,0},{7,1},{8,14},{9,15},{10,... | collective-permute-start | bytes 540680 | tf_op jit(solution)/shard_map/ppermute | solution.py:55
  139.2 27.6 %collective-permute-start.7 = (bf16[2,64,704]{2,1,0:T(8,128)(2,1)}, bf16[2,64,704]{2,1,0:T(8,128)(2,1)S(1)}, u32[]{:S(2)}, u32[]{:S(2)}) collective-permute-start(bf16[2,64,704]{2,1,0:T(8,128)(2,1)} %get-tuple-element.81), channel_id=1, source_target_pairs={{0,7},{1,6},{2,5},{3,4},{4,3},{5,2},{6,1},{7,0},{8,15},{9,14},{10,... | collective-permute-start | bytes 540680 | tf_op jit(solution)/shard_map/ppermute | solution.py:55
  170.1 20.6 %collective-permute-start.8 = (bf16[8,64,704]{2,1,0:T(8,128)(2,1)}, bf16[8,64,704]{2,1,0:T(8,128)(2,1)S(1)}, u32[]{:S(2)}, u32[]{:S(2)}) collective-permute-start(bf16[8,64,704]{2,1,0:T(8,128)(2,1)} %get-tuple-element.82.refs_0_), channel_id=1, source_target_pairs={{0,8},{8,0},{16,24},{24,16},{1,9},{9,1},{17,25},{25,17},{2,10},{10... | collective-permute-start | bytes 2162696 | tf_op jit(solution)/shard_map/ppermute | solution.py:55
  170.3 20.6 %collective-permute-start.11 = (bf16[8,64,704]{2,1,0:T(8,128)(2,1)}, bf16[8,64,704]{2,1,0:T(8,128)(2,1)S(1)}, u32[]{:S(2)}, u32[]{:S(2)}) collective-permute-start(bf16[8,64,704]{2,1,0:T(8,128)(2,1)} %get-tuple-element.83.refs_1_), channel_id=1, source_target_pairs={{0,16},{8,24},{16,0},{24,8},{1,17},{9,25},{17,1},{25,9},{2,18},{10... | collective-permute-start | bytes 2162696 | tf_op jit(solution)/shard_map/ppermute | solution.py:55
  170.3 37.3 %collective-permute-start.9 = (bf16[8,64,704]{2,1,0:T(8,128)(2,1)}, bf16[8,64,704]{2,1,0:T(8,128)(2,1)S(1)}, u32[]{:S(2)}, u32[]{:S(2)}) collective-permute-start(bf16[8,64,704]{2,1,0:T(8,128)(2,1)} %get-tuple-element.83.refs_1_), channel_id=1, source_target_pairs={{0,8},{8,0},{16,24},{24,16},{1,9},{9,1},{17,25},{25,17},{2,10},{10... | collective-permute-start | bytes 2162696 | tf_op jit(solution)/shard_map/ppermute | solution.py:55
  172.3 35.5 %collective-permute-start.10 = (bf16[8,64,704]{2,1,0:T(8,128)(2,1)}, bf16[8,64,704]{2,1,0:T(8,128)(2,1)S(1)}, u32[]{:S(2)}, u32[]{:S(2)}) collective-permute-start(bf16[8,64,704]{2,1,0:T(8,128)(2,1)} %get-tuple-element.82.refs_0_), channel_id=1, source_target_pairs={{0,16},{8,24},{16,0},{24,8},{1,17},{9,25},{17,1},{25,9},{2,18},{10... | collective-permute-start | bytes 2162696 | tf_op jit(solution)/shard_map/ppermute | solution.py:55
  190.7 33.7 %collective-permute-start.12 = (bf16[8,64,704]{2,1,0:T(8,128)(2,1)S(1)}, bf16[8,64,704]{2,1,0:T(8,128)(2,1)S(1)}, u32[]{:S(2)}, u32[]{:S(2)}) collective-permute-start(bf16[8,64,704]{2,1,0:T(8,128)(2,1)S(1)} %collective-permute-done.8.refs_2_), channel_id=1, source_target_pairs={{0,16},{8,24},{16,0},{24,8},{1,17},{9,25},{17,1},{25,9},{2,18},{10... | collective-permute-start | bytes 2162696 | tf_op jit(solution)/shard_map/ppermute | solution.py:55
  190.9 33.6 %collective-permute-start.13 = (bf16[8,64,704]{2,1,0:T(8,128)(2,1)S(1)}, bf16[8,64,704]{2,1,0:T(8,128)(2,1)S(1)}, u32[]{:S(2)}, u32[]{:S(2)}) collective-permute-start(bf16[8,64,704]{2,1,0:T(8,128)(2,1)S(1)} %collective-permute-done.11.refs_5_), channel_id=1, source_target_pairs={{0,8},{8,0},{16,24},{24,16},{1,9},{9,1},{17,25},{25,17},{2,10},{10... | collective-permute-start | bytes 2162696 | tf_op jit(solution)/shard_map/ppermute | solution.py:55
  271.1 362.1 %reduce-scatter.11.cloned.1.call-start = ((), (), s32[]{:S(2)}) async-start(), calls=%async_computation.17 | async-start | bytes 2359296 | tf_op jit(solution)/shard_map/reduce_scatter | solution.py:678
  373.2 277.5 %reduce-scatter.9.cloned.1.call-start = ((), (), s32[]{:S(2)}) async-start(), calls=%async_computation.16 | async-start | bytes 3538944 | tf_op jit(solution)/shard_map/reduce_scatter | solution.py:719
  409.8 244.4 %reduce-scatter.5.cloned.1.call-start = ((), (), s32[]{:S(2)}) async-start(), calls=%async_computation.14 | async-start | bytes 4718592 | tf_op jit(solution)/shard_map/reduce_scatter | solution.py:646
  423.3 41.0 %collective-permute-start.21 = (bf16[8,64,704]{2,1,0:T(8,128)(2,1)}, bf16[8,64,704]{2,1,0:T(8,128)(2,1)}, u32[]{:S(2)}, u32[]{:S(2)}) collective-permute-start(bf16[8,64,704]{2,1,0:T(8,128)(2,1)} %get-tuple-element.107), channel_id=1, source_target_pairs={{0,8},{8,0},{16,24},{24,16},{1,9},{9,1},{17,25},{25,17},{2,10},{10... | collective-permute-start | bytes 2162696 | tf_op jit(solution)/shard_map/ppermute | solution.py:55
  424.3 29.7 %collective-permute-start.22 = (bf16[8,64,704]{2,1,0:T(8,128)(2,1)}, bf16[8,64,704]{2,1,0:T(8,128)(2,1)S(1)}, u32[]{:S(2)}, u32[]{:S(2)}) collective-permute-start(bf16[8,64,704]{2,1,0:T(8,128)(2,1)} %get-tuple-element.109), channel_id=1, source_target_pairs={{0,8},{8,0},{16,24},{24,16},{1,9},{9,1},{17,25},{25,17},{2,10},{10... | collective-permute-start | bytes 2162696 | tf_op jit(solution)/shard_map/ppermute | solution.py:55
  425.4 40.1 %collective-permute-start.24 = (bf16[8,64,704]{2,1,0:T(8,128)(2,1)}, bf16[8,64,704]{2,1,0:T(8,128)(2,1)}, u32[]{:S(2)}, u32[]{:S(2)}) collective-permute-start(bf16[8,64,704]{2,1,0:T(8,128)(2,1)} %get-tuple-element.110), channel_id=1, source_target_pairs={{0,16},{8,24},{16,0},{24,8},{1,17},{9,25},{17,1},{25,9},{2,18},{10... | collective-permute-start | bytes 2162696 | tf_op jit(solution)/shard_map/ppermute | solution.py:55
  426.3 30.2 %collective-permute-start.25 = (bf16[8,64,704]{2,1,0:T(8,128)(2,1)}, bf16[8,64,704]{2,1,0:T(8,128)(2,1)S(1)}, u32[]{:S(2)}, u32[]{:S(2)}) collective-permute-start(bf16[8,64,704]{2,1,0:T(8,128)(2,1)} %get-tuple-element.112), channel_id=1, source_target_pairs={{0,16},{8,24},{16,0},{24,8},{1,17},{9,25},{17,1},{25,9},{2,18},{10... | collective-permute-start | bytes 2162696 | tf_op jit(solution)/shard_map/ppermute | solution.py:55
  434.2 29.4 %collective-permute-start.44 = (bf16[80,2048]{1,0:T(8,128)(2,1)}, bf16[80,2048]{1,0:T(8,128)(2,1)S(1)}, u32[]{:S(2)}, u32[]{:S(2)}) collective-permute-start(bf16[80,2048]{1,0:T(8,128)(2,1)} %get-tuple-element.126), channel_id=1, source_target_pairs={{0,16},{8,24},{16,0},{24,8},{1,17},{9,25},{17,1},{25,9},{2,18},{10... | collective-permute-start | bytes 983048 | tf_op jit(solution)/shard_map/ppermute | solution.py:55
  455.1 25.5 %collective-permute-start.23 = (bf16[8,64,704]{2,1,0:T(8,128)(2,1)}, bf16[8,64,704]{2,1,0:T(8,128)(2,1)}, u32[]{:S(2)}, u32[]{:S(2)}) collective-permute-start(bf16[8,64,704]{2,1,0:T(8,128)(2,1)} %add_convert_fusion.1), channel_id=1, source_target_pairs={{0,16},{8,24},{16,0},{24,8},{1,17},{9,25},{17,1},{25,9},{2,18},{10... | collective-permute-start | bytes 2162696 | tf_op jit(solution)/shard_map/ppermute | solution.py:55
  457.7 22.9 %collective-permute-start.26 = (bf16[8,64,704]{2,1,0:T(8,128)(2,1)}, bf16[8,64,704]{2,1,0:T(8,128)(2,1)}, u32[]{:S(2)}, u32[]{:S(2)}) collective-permute-start(bf16[8,64,704]{2,1,0:T(8,128)(2,1)} %add_convert_fusion), channel_id=1, source_target_pairs={{0,8},{8,0},{16,24},{24,16},{1,9},{9,1},{17,25},{25,17},{2,10},{10... | collective-permute-start | bytes 2162696 | tf_op jit(solution)/shard_map/ppermute | solution.py:55
  463.6 36.7 %collective-permute-start.41 = (bf16[96,2048]{1,0:T(8,128)(2,1)S(1)}, bf16[96,2048]{1,0:T(8,128)(2,1)S(1)}, u32[]{:S(2)}, u32[]{:S(2)}) collective-permute-start(bf16[96,2048]{1,0:T(8,128)(2,1)S(1)} %get-tuple-element.128), channel_id=1, source_target_pairs={{0,8},{8,0},{16,24},{24,16},{1,9},{9,1},{17,25},{25,17},{2,10},{10... | collective-permute-start | bytes 1179656 | tf_op jit(solution)/shard_map/ppermute | solution.py:55
  464.4 34.0 %collective-permute-start.43 = (bf16[80,2048]{1,0:T(8,128)(2,1)S(1)}, bf16[80,2048]{1,0:T(8,128)(2,1)S(1)}, u32[]{:S(2)}, u32[]{:S(2)}) collective-permute-start(bf16[80,2048]{1,0:T(8,128)(2,1)S(1)} %get-tuple-element.125), channel_id=1, source_target_pairs={{0,16},{8,24},{16,0},{24,8},{1,17},{9,25},{17,1},{25,9},{2,18},{10... | collective-permute-start | bytes 983048 | tf_op jit(solution)/shard_map/ppermute | solution.py:55
  465.5 36.1 %collective-permute-start.45 = (bf16[80,2048]{1,0:T(8,128)(2,1)S(1)}, bf16[80,2048]{1,0:T(8,128)(2,1)S(1)}, u32[]{:S(2)}, u32[]{:S(2)}) collective-permute-start(bf16[80,2048]{1,0:T(8,128)(2,1)S(1)} %add_convert_fusion.6), channel_id=1, source_target_pairs={{0,8},{8,0},{16,24},{24,16},{1,9},{9,1},{17,25},{25,17},{2,10},{10... | collective-permute-start | bytes 983048 | tf_op jit(solution)/shard_map/ppermute | solution.py:55
  501.6 41.7 %collective-permute-start.40 = (bf16[96,2048]{1,0:T(8,128)(2,1)S(1)}, bf16[96,2048]{1,0:T(8,128)(2,1)S(1)}, u32[]{:S(2)}, u32[]{:S(2)}) collective-permute-start(bf16[96,2048]{1,0:T(8,128)(2,1)S(1)} %get-tuple-element.127), channel_id=1, source_target_pairs={{0,8},{8,0},{16,24},{24,16},{1,9},{9,1},{17,25},{25,17},{2,10},{10... | collective-permute-start | bytes 1179656 | tf_op jit(solution)/shard_map/ppermute | solution.py:55
  503.1 40.8 %collective-permute-start.42 = (bf16[96,2048]{1,0:T(8,128)(2,1)S(1)}, bf16[96,2048]{1,0:T(8,128)(2,1)S(1)}, u32[]{:S(2)}, u32[]{:S(2)}) collective-permute-start(bf16[96,2048]{1,0:T(8,128)(2,1)S(1)} %add_convert_fusion.4), channel_id=1, source_target_pairs={{0,16},{8,24},{16,0},{24,8},{1,17},{9,25},{17,1},{25,9},{2,18},{10... | collective-permute-start | bytes 1179656 | tf_op jit(solution)/shard_map/ppermute | solution.py:55
  513.8 22.4 %collective-permute-start.31 = (bf16[2,64,704]{2,1,0:T(8,128)(2,1)}, bf16[2,64,704]{2,1,0:T(8,128)(2,1)S(1)}, u32[]{:S(2)}, u32[]{:S(2)}) collective-permute-start(bf16[2,64,704]{2,1,0:T(8,128)(2,1)} %get-tuple-element.118), channel_id=1, source_target_pairs={{0,5},{1,4},{2,7},{3,6},{4,1},{5,0},{6,3},{7,2},{8,13},{9,12},{10,... | collective-permute-start | bytes 540680 | tf_op jit(solution)/shard_map/ppermute | solution.py:55
  517.9 19.9 %collective-permute-start.32 = (bf16[2,64,704]{2,1,0:T(8,128)(2,1)}, bf16[2,64,704]{2,1,0:T(8,128)(2,1)S(1)}, u32[]{:S(2)}, u32[]{:S(2)}) collective-permute-start(bf16[2,64,704]{2,1,0:T(8,128)(2,1)} %get-tuple-element.119), channel_id=1, source_target_pairs={{0,6},{1,7},{2,4},{3,5},{4,2},{5,3},{6,0},{7,1},{8,14},{9,15},{10,... | collective-permute-start | bytes 540680 | tf_op jit(solution)/shard_map/ppermute | solution.py:55
  542.8 29.7 %collective-permute-start.34 = (bf16[64,5632]{1,0:T(8,128)(2,1)}, bf16[64,5632]{1,0:T(8,128)(2,1)}, u32[]{:S(2)}, u32[]{:S(2)}) collective-permute-start(bf16[64,5632]{1,0:T(8,128)(2,1)} %get-tuple-element.121.refs_0_), channel_id=1, source_target_pairs={{0,8},{8,0},{16,24},{24,16},{1,9},{9,1},{17,25},{25,17},{2,10},{10... | collective-permute-start | bytes 2162696 | tf_op jit(solution)/shard_map/ppermute | solution.py:55
  543.4 40.4 %collective-permute-start.38 = (bf16[64,5632]{1,0:T(8,128)(2,1)}, bf16[64,5632]{1,0:T(8,128)(2,1)}, u32[]{:S(2)}, u32[]{:S(2)}) collective-permute-start(bf16[64,5632]{1,0:T(8,128)(2,1)} %get-tuple-element.122.refs_0_), channel_id=1, source_target_pairs={{0,16},{8,24},{16,0},{24,8},{1,17},{9,25},{17,1},{25,9},{2,18},{10... | collective-permute-start | bytes 2162696 | tf_op jit(solution)/shard_map/ppermute | solution.py:55
  545.1 26.0 %collective-permute-start.46 = (bf16[96,2048]{1,0:T(8,128)(2,1)S(1)}, bf16[96,2048]{1,0:T(8,128)(2,1)}, u32[]{:S(2)}, u32[]{:S(2)}) collective-permute-start(bf16[96,2048]{1,0:T(8,128)(2,1)S(1)} %add_convert_fusion.3.refs_0_), channel_id=1, source_target_pairs={{0,8},{8,0},{16,24},{24,16},{1,9},{9,1},{17,25},{25,17},{2,10},{10... | collective-permute-start | bytes 1179656 | tf_op jit(solution)/shard_map/ppermute | solution.py:55
  547.1 36.6 %collective-permute-start.48 = (bf16[96,2048]{1,0:T(8,128)(2,1)S(1)}, bf16[96,2048]{1,0:T(8,128)(2,1)}, u32[]{:S(2)}, u32[]{:S(2)}) collective-permute-start(bf16[96,2048]{1,0:T(8,128)(2,1)S(1)} %add_convert_fusion.3.refs_0_), channel_id=1, source_target_pairs={{0,16},{8,24},{16,0},{24,8},{1,17},{9,25},{17,1},{25,9},{2,18},{10... | collective-permute-start | bytes 1179656 | tf_op jit(solution)/shard_map/ppermute | solution.py:55
  548.6 107.8 %all-to-all-start.5 = ((bf16[4,128,2048]{2,1,0:T(8,128)(2,1)}), bf16[4,128,2048]{2,1,0:T(8,128)(2,1)}, u32[]{:S(2)}, u32[]{:S(2)}) async-start(bf16[4,128,2048]{2,1,0:T(8,128)(2,1)} %get-tuple-element.99), calls=%async_computation.7 | async-start | bytes 4194304 | tf_op jit(solution)/shard_map/all_to_all | solution.py:47
  553.3 47.2 %collective-permute-start.51 = (bf16[80,2048]{1,0:T(8,128)(2,1)}, bf16[80,2048]{1,0:T(8,128)(2,1)}, u32[]{:S(2)}, u32[]{:S(2)}) collective-permute-start(bf16[80,2048]{1,0:T(8,128)(2,1)} %collective-permute-done.49.refs_5_), channel_id=1, source_target_pairs={{0,8},{8,0},{16,24},{24,16},{1,9},{9,1},{17,25},{25,17},{2,10},{10... | collective-permute-start | bytes 983048 | tf_op jit(solution)/shard_map/ppermute | solution.py:55
  571.0 67.3 %collective-permute-start.35 = (bf16[64,5632]{1,0:T(8,128)(2,1)}, bf16[64,5632]{1,0:T(8,128)(2,1)}, u32[]{:S(2)}, u32[]{:S(2)}) collective-permute-start(bf16[64,5632]{1,0:T(8,128)(2,1)} %get-tuple-element.121.refs_0_), channel_id=1, source_target_pairs={{0,16},{8,24},{16,0},{24,8},{1,17},{9,25},{17,1},{25,9},{2,18},{10... | collective-permute-start | bytes 2162696 | tf_op jit(solution)/shard_map/ppermute | solution.py:55
  572.5 65.9 %collective-permute-start.36 = (bf16[64,5632]{1,0:T(8,128)(2,1)}, bf16[64,5632]{1,0:T(8,128)(2,1)}, u32[]{:S(2)}, u32[]{:S(2)}) collective-permute-start(bf16[64,5632]{1,0:T(8,128)(2,1)} %collective-permute-done.34.refs_1_), channel_id=1, source_target_pairs={{0,16},{8,24},{16,0},{24,8},{1,17},{9,25},{17,1},{25,9},{2,18},{10... | collective-permute-start | bytes 2162696 | tf_op jit(solution)/shard_map/ppermute | solution.py:55
  583.7 59.3 %collective-permute-start.37 = (bf16[64,5632]{1,0:T(8,128)(2,1)}, bf16[64,5632]{1,0:T(8,128)(2,1)}, u32[]{:S(2)}, u32[]{:S(2)}) collective-permute-start(bf16[64,5632]{1,0:T(8,128)(2,1)} %get-tuple-element.122.refs_0_), channel_id=1, source_target_pairs={{0,8},{8,0},{16,24},{24,16},{1,9},{9,1},{17,25},{25,17},{2,10},{10... | collective-permute-start | bytes 2162696 | tf_op jit(solution)/shard_map/ppermute | solution.py:55
  583.7 59.3 %collective-permute-start.39 = (bf16[64,5632]{1,0:T(8,128)(2,1)}, bf16[64,5632]{1,0:T(8,128)(2,1)}, u32[]{:S(2)}, u32[]{:S(2)}) collective-permute-start(bf16[64,5632]{1,0:T(8,128)(2,1)} %collective-permute-done.38.refs_2_), channel_id=1, source_target_pairs={{0,8},{8,0},{16,24},{24,16},{1,9},{9,1},{17,25},{25,17},{2,10},{10... | collective-permute-start | bytes 2162696 | tf_op jit(solution)/shard_map/ppermute | solution.py:55
  600.6 32.6 %collective-permute-start.50 = (bf16[96,2048]{1,0:T(8,128)(2,1)}, bf16[96,2048]{1,0:T(8,128)(2,1)}, u32[]{:S(2)}, u32[]{:S(2)}) collective-permute-start(bf16[96,2048]{1,0:T(8,128)(2,1)} %collective-permute-done.46.refs_2_), channel_id=1, source_target_pairs={{0,16},{8,24},{16,0},{24,8},{1,17},{9,25},{17,1},{25,9},{2,18},{10... | collective-permute-start | bytes 1179656 | tf_op jit(solution)/shard_map/ppermute | solution.py:55
  651.3 26.1 %collective-permute-start.16 = (bf16[256,768]{1,0:T(8,128)(2,1)}, bf16[256,768]{1,0:T(8,128)(2,1)}, u32[]{:S(2)}, u32[]{:S(2)}) collective-permute-start(bf16[256,768]{1,0:T(8,128)(2,1)} %reduce-scatter.9.cloned.1.call-done.refs_0_), channel_id=1, source_target_pairs={{0,16},{8,24},{16,0},{24,8},{1,17},{9,25},{17,1},{25,9},{2,18},{10... | collective-permute-start | bytes 1179656 | tf_op jit(solution)/shard_map/ppermute | solution.py:55
  652.7 24.6 %collective-permute-start.17 = (bf16[256,768]{1,0:T(8,128)(2,1)}, bf16[256,768]{1,0:T(8,128)(2,1)}, u32[]{:S(2)}, u32[]{:S(2)}) collective-permute-start(bf16[256,768]{1,0:T(8,128)(2,1)} %reduce-scatter.9.cloned.1.call-done.refs_0_), channel_id=1, source_target_pairs={{0,24},{8,16},{16,8},{24,0},{1,25},{9,17},{17,9},{25,1},{2,26},{10... | collective-permute-start | bytes 1179656 | tf_op jit(solution)/shard_map/ppermute | solution.py:55
  (50 other events, 1005.8 us)
Sparse Core Ops, SparseCore 0:
  10.4 36.4 all-gather.4
  49.1 28.2 all-gather.6
  79.0 46.9 all-gather.10
  127.4 69.6 all-gather.8
  271.2 65.5 reduce-scatter.6
  373.3 35.2 reduce-scatter.10
  410.9 44.8 reduce-scatter.8
  458.2 54.4 reduce-scatter.4

commit v7 on v6

--- a/solution.py
+++ b/solution.py
@@ -55,7 +55,7 @@
     return lax.ppermute(value, axis, pairs(count, step))
 
 
-def parts_rep(chunks, count):
+def parts_rep(chunks, count, after=None):
     go = lambda value, step: send(value, "rep", count, step)
     if count != 4:
         return [
@@ -67,8 +67,10 @@
     first_two = go(chunks[3][0], 1)
     second_one = go(chunks[2][1], 2)
     second_two = go(chunks[3][1], 2)
-    last_one = go(add(chunks[2][0], first_two), 2)
-    last_two = go(add(chunks[1][1], second_two), 1)
+    joint_one, joint_two = add(chunks[2][0], first_two), add(chunks[1][1], second_two)
+    if after is not None:
+        joint_one, joint_two, _ = lax.optimization_barrier((joint_one, joint_two, after))
+    last_one, last_two = go(joint_one, 2), go(joint_two, 1)
     return [[chunks[0][0], first_one, last_one], [chunks[0][1], second_one, last_two]]
 
 
@@ -645,11 +647,6 @@
     down_part = rows_cols(mixed, down_weight).astype(BF)
     down_rows = lax.psum_scatter(down_part, "shard", scatter_dimension=0, tiled=True)
     layer_out = (x_mid + down_rows.astype(F32)).astype(BF)
-    w_down_grad = parts_rep(down_chunks, n_rep)
-    w_down_grad = tuple(
-        sum(part.astype(F32) for part in parts).astype(BF) for parts in w_down_grad
-    )
-    down_out = place(gather_rep(w_down_grad, n_rep), r)
     w_pair_grad = parts_rep(pair_chunks, n_rep)
     w_pair_grad = flat_call(
         sum_kernel,
@@ -671,12 +668,13 @@
 
     branch_all = spread(branch, "rep", n_rep).reshape(all_rows, width)
     in_grad = cols_cols(branch_all, w_o).astype(BF)
-    branch_all, in_grad = lax.optimization_barrier((branch_all, in_grad))
     in_grad = in_grad.reshape(all_rows, n_rep, pair * fine).transpose(1, 0, 2)
-    in_grad = swap(in_grad, "rep").reshape(n_rep, n_rep, rows, pair * fine)
-    w_o_grad = rows_rows(out_in, branch_all).astype(BF)
-    w_o_grad = lax.psum_scatter(w_o_grad, "shard", scatter_dimension=0, tiled=True)
-    o_out = place([(v,) for v in gather_direct(w_o_grad, n_rep)], r)
+    swapped = swap(in_grad, "rep").reshape(n_rep, n_rep, rows, pair * fine)
+    w_down_grad = parts_rep(down_chunks, n_rep, in_grad)
+    w_down_grad = tuple(
+        sum(part.astype(F32) for part in parts).astype(BF) for parts in w_down_grad
+    )
+    down_out = place(gather_rep(w_down_grad, n_rep), r)
     query_grad, kv_grad = call(
         partial(attend_back_kernel, fine),
         (shape((n_rep, rows, q_cols), BF), shape((n_rep, span, LANES), F32)),
@@ -691,7 +689,7 @@
             table,
         ],
         (by_block((rows, q_cols)), by_block((span, LANES))),
-    )(in_grad, probs, queries, kv_own, kv_halo, cosine, sine)
+    )(swapped, probs, queries, kv_own, kv_halo, cosine, sine)
     kv_back = lax.ppermute(
         kv_grad[:, :HALO], "shard", [(i + 1, i) for i in range(n_shard - 1)]
     )
@@ -716,7 +714,11 @@
     )(
         query_grad, kv_grad, kv_back, cosine, sine, normed_one, x_all, gain_two_rows, w_qkv
     )
+    branch_all, _ = lax.optimization_barrier((branch_all, w_qkv_grad))
     w_qkv_grad = lax.psum_scatter(w_qkv_grad, "shard", scatter_dimension=0, tiled=True)
+    w_o_grad = rows_rows(out_in, branch_all).astype(BF)
+    w_o_grad = lax.psum_scatter(w_o_grad, "shard", scatter_dimension=0, tiled=True)
+    o_out = place([(v,) for v in gather_direct(w_o_grad, n_rep)], r)
     input_grad = call(last_kernel, shape((rows, width), BF))(
         swap(one_grad_part, "rep"), tokens, gain_one, mid_grad
     )

time: 698 us -> 718 us (1.029)
  the two profiles are of different devices: /device:TPU:0 before, /device:TPU:9 now
where the time goes in v7:
time: 718 us; the launch traced here: 712 us
  waiting for transfers between devices  354 us (49%)
  Pallas kernels  123 us (17%)
  blocking collectives  96.8 us (13%)
  starting transfers between devices  56.2 us (8%)
  matrix products  27.2 us (4%)
  local copies, waits for them, and re-layouts  20.7 us (3%)
  other arithmetic  19.1 us (3%)
  between operations  14.8 us (2%)
    ppermute x50, waiting for transfers between devices, send(): return lax.ppermute(value, axis, pairs(count, step))  283 us
    all_to_all x3, blocking collectives, swap(): return lax.all_to_all(value, axis, split_axis=0, concat_axis=0, tiled=True)  58.4 us
    reduce_scatter x1, waiting for transfers between devices, body(): lax.psum_scatter(two_grad_part, 'shard', scatter_dimension=0, tiled=True)  47.2 us
    ppermute x50, starting transfers between devices, send(): return lax.ppermute(value, axis, pairs(count, step))  38.5 us
    all_to_all x1, blocking collectives, spread(): return lax.all_to_all(wide, axis, split_axis=0, concat_axis=0, tiled=True)  28.5 us
    dot_general x6, matrix products, dot(): lax.dot_general(left, right, (contract, ((), ())), preferred_element_type...  27.2 us
    pallas_call x5, Pallas kernels, flat_call(): pl.pallas_call(kernel, out_shape=out_shape, in_specs=specs, scratch_shape...  18.5 us
    pallas_call x4, Pallas kernels, place(): pl.pallas_call(partial(place_kernel, count), out_shape=shape((count, rows...  17 us
  transfers between devices with their start and end apart: 62, of which 29 were waited for; matrix products, arithmetic and copies ran while one was open for 7% of the time, Pallas kernels for 9%

profile of v7, /device:TPU:9, one launch (start us, length us, event | category | flops | bytes accessed | tf_op | source)
XLA Modules:
  0.0 712.0 jit_solution(17801181308156557051)
XLA Ops:
  14.7 4.6 all-to-all-start
  19.5 9.9 %all_gather.15 = bf16[2,2048]{1,0:T(2,128)(2,1)S(1)} all-gather(bf16[2,256]{1,0:T(2,128)(2,1)S(1)} %pad_maximum_fusion.2), channel_id=1, replica_groups=mesh['rep'=4,'shard'=8] {'shard'}, dimensions={1}, use_global_device_ids=true | all-gather | bytes 9216 | tf_op jit(solution)/shard_map/all_gather | solution.py:536
  30.0 15.2 %all-to-all-done.x_ref.pos_ref = bf16[4,128,2176]{2,1,0:T(8,128)(2,1)} async-done(((bf16[4,128,2176]{2,1,0:T(8,128)(2,1)}), bf16[4,128,2176]{2,1,0:T(8,128)(2,1)}, u32[]{:S(2)}, u32[]{:S(2)}) %all-to-all-start) | async-done | bytes 2228256 | tf_op jit(solution)/shard_map/all_to_all | solution.py:43
  47.7 6.2 shard_map.203
  54.8 4.5 collective-permute-start
  63.3 6.4 shard_map.204
  69.6 10.9 %all_to_all.30 = bf16[4,4,128,128]{3,2,1,0:T(8,128)(2,1)S(1)} all-to-all(bf16[4,4,128,128]{3,2,1,0:T(8,128)(2,1)} %get-tuple-element.70), channel_id=1, replica_groups=mesh['rep'=4,'shard'=8] {'rep'}, dimensions={0} | all-to-all | bytes 1048576 | tf_op jit(solution)/shard_map/all_to_all | solution.py:47
  84.6 26.2 %all_to_all.31.part_ref = bf16[4,128,2048]{2,1,0:T(8,128)(2,1)} all-to-all(bf16[4,128,2048]{2,1,0:T(8,128)(2,1)S(1)} %bitcast.39), channel_id=1, replica_groups=mesh['rep'=4,'shard'=8] {'rep'}, dimensions={0} | all-to-all | bytes 4194304 | tf_op jit(solution)/shard_map/all_to_all | solution.py:47
  127.3 8.3 %collective-permute-done.2.refs_2_ = bf16[2,64,704]{2,1,0:T(8,128)(2,1)S(1)} collective-permute-done((bf16[2,64,704]{2,1,0:T(8,128)(2,1)}, bf16[2,64,704]{2,1,0:T(8,128)(2,1)S(1)}, u32[]{:S(2)}, u32[]{:S(2)}) %collective-permute-start.2) | collective-permute-done | bytes 180256 | tf_op jit(solution)/shard_map/ppermute | solution.py:55
  136.9 7.9 %collective-permute-done.3.refs_3_ = bf16[2,64,704]{2,1,0:T(8,128)(2,1)S(1)} collective-permute-done((bf16[2,64,704]{2,1,0:T(8,128)(2,1)}, bf16[2,64,704]{2,1,0:T(8,128)(2,1)S(1)}, u32[]{:S(2)}, u32[]{:S(2)}) %collective-permute-start.3) | collective-permute-done | bytes 180256 | tf_op jit(solution)/shard_map/ppermute | solution.py:55
  144.8 4.8 collective-permute-done.5.refs_5_
  149.6 17.5 %collective-permute-done.6.refs_6_ = bf16[2,64,704]{2,1,0:T(8,128)(2,1)S(1)} collective-permute-done((bf16[2,64,704]{2,1,0:T(8,128)(2,1)}, bf16[2,64,704]{2,1,0:T(8,128)(2,1)S(1)}, u32[]{:S(2)}, u32[]{:S(2)}) %collective-permute-start.6) | collective-permute-done | bytes 180256 | tf_op jit(solution)/shard_map/ppermute | solution.py:55
  167.2 16.2 %collective-permute-done.7.refs_7_ = bf16[2,64,704]{2,1,0:T(8,128)(2,1)S(1)} collective-permute-done((bf16[2,64,704]{2,1,0:T(8,128)(2,1)}, bf16[2,64,704]{2,1,0:T(8,128)(2,1)S(1)}, u32[]{:S(2)}, u32[]{:S(2)}) %collective-permute-start.7) | collective-permute-done | bytes 180256 | tf_op jit(solution)/shard_map/ppermute | solution.py:55
  189.7 16.5 %collective-permute-done.8.refs_2_ = bf16[8,64,704]{2,1,0:T(8,128)(2,1)S(1)} collective-permute-done((bf16[8,64,704]{2,1,0:T(8,128)(2,1)}, bf16[8,64,704]{2,1,0:T(8,128)(2,1)S(1)}, u32[]{:S(2)}, u32[]{:S(2)}) %collective-permute-start.8) | collective-permute-done | bytes 720928 | tf_op jit(solution)/shard_map/ppermute | solution.py:55
  207.4 15.7 %collective-permute-done.9.refs_3_ = bf16[8,64,704]{2,1,0:T(8,128)(2,1)S(1)} collective-permute-done((bf16[8,64,704]{2,1,0:T(8,128)(2,1)}, bf16[8,64,704]{2,1,0:T(8,128)(2,1)S(1)}, u32[]{:S(2)}, u32[]{:S(2)}) %collective-permute-start.9) | collective-permute-done | bytes 720928 | tf_op jit(solution)/shard_map/ppermute | solution.py:55
  223.5 16.9 %collective-permute-done.12.refs_6_ = bf16[8,64,704]{2,1,0:T(8,128)(2,1)S(1)} collective-permute-done((bf16[8,64,704]{2,1,0:T(8,128)(2,1)S(1)}, bf16[8,64,704]{2,1,0:T(8,128)(2,1)S(1)}, u32[]{:S(2)}, u32[]{:S(2)}) %collective-permute-start.12) | collective-permute-done | bytes 720928 | tf_op jit(solution)/shard_map/ppermute | solution.py:55
  242.2 5.8 shard_map.207
  248.0 7.3 %fusion.5.back_ref = f32[1024,704]{1,0:T(8,128)} fusion(bf16[1024,2048]{1,0:T(8,128)(2,1)} %all-gather.11.cloned.1.call-done, bf16[704,2048]{1,0:T(8,128)(2,1)S(1)} %copy-done), kind=kOutput, calls=%fused_computation.39 | convolution fusion | flops 2952790016 | bytes 9961472 | tf_op jit(solution)/shard_map/dot_general | solution.py:26
  255.3 12.1 %shard_map.208 = (bf16[1024,704]{1,0:T(8,128)(2,1)}, bf16[1024,704]{1,0:T(8,128)(2,1)}, bf16[1024,704]{1,0:T(8,128)(2,1)}) custom-call(bf16[1024,2048]{1,0:T(8,128)(2,1)} %all-gather.9.cloned.1.call-done.x_ref, f32[1024,704]{1,0:T(8,128)} %fusion.5.back_ref, bf16[2,2048,704]{2,1,0:T(8,128)(2,1)} %bitcast.30), custom_call_target="tpu_custom_call" | custom-call | tf_op jit(solution)/shard_map/pallas_call | solution.py:609
  267.3 8.2 %shard_map.209 = (bf16[8,64,704]{2,1,0:T(8,128)(2,1)}, bf16[8,64,704]{2,1,0:T(8,128)(2,1)}, bf16[8,64,704]{2,1,0:T(8,128)(2,1)}, bf16[8,64,704]{2,1,0:T(8,128)(2,1)}) custom-call(s32[2]{0:T(128)} %pad_add_fusion.id_ref, bf16[1024,2048]{1,0:T(8,128)(2,1)} %all-gather.9.cloned.1.call-done.x_ref, bf16[1024,704]{1,0:T(8,128)(2,1)} %get-tuple-element.89.grad_ref.gate_ref), custom_call_target="tpu_custom_call" | custom-call | tf_op jit(solution)/shard_map/pallas_call | solution.py:246
  275.5 11.4 %shard_map.210 = bf16[1024,2048]{1,0:T(8,128)(2,1)} custom-call(bf16[1024,704]{1,0:T(8,128)(2,1)} %get-tuple-element.89.grad_ref.gate_ref, bf16[1024,704]{1,0:T(8,128)(2,1)} %get-tuple-element.90.up_ref.grad_ref, bf16[2,2048,704]{2,1,0:T(8,128)(2,1)} %bitcast.31), custom_call_target="tpu_custom_call" | custom-call | tf_op jit(solution)/shard_map/pallas_call | solution.py:618
  287.0 47.2 %reduce-scatter.7.cloned.1.call-done.grad_ref = bf16[128,2048]{1,0:T(8,128)(2,1)} async-done(((bf16[1024,2048]{1,0:T(8,128)(2,1)}), bf16[128,2048]{1,0:T(8,128)(2,1)}) %reduce-scatter.7.cloned.1.call-update) | async-done | bytes 524304 | tf_op jit(solution)/shard_map/reduce_scatter | solution.py:626
  339.1 28.5 %all_to_all.32 = bf16[4,128,2048]{2,1,0:T(8,128)(2,1)S(1)} all-to-all(bf16[4,128,2048]{2,1,0:T(8,128)(2,1)S(1)} %broadcast_in_dim.19), channel_id=1, replica_groups=mesh['rep'=4,'shard'=8] {'rep'}, dimensions={0} | all-to-all | bytes 4194304 | tf_op jit(solution)/shard_map/all_to_all | solution.py:43
  371.0 21.3 %all_to_all.33 = bf16[4,512,128]{2,1,0:T(8,128)(2,1)} all-to-all(bf16[4,512,128]{2,1,0:T(8,128)(2,1)S(1)} %bitcast.41), channel_id=1, replica_groups=mesh['rep'=4,'shard'=8] {'rep'}, dimensions={0} | all-to-all | bytes 1048576 | tf_op jit(solution)/shard_map/all_to_all | solution.py:47
  392.3 8.3 %shard_map.213 = (bf16[4,128,512]{2,1,0:T(8,128)(2,1)}, f32[4,192,128]{2,1,0:T(8,128)}) custom-call(bf16[4,4,128,128]{3,2,1,0:T(8,128)(2,1)} %bitcast.35, f32[4,8,128,192]{3,2,1,0:T(8,128)} %get-tuple-element.94.probs_ref, bf16[4,128,512]{2,1,0:T(8,128)(2,1)} %get-tuple-element.68.q_ref, bf16[4,128,128]{2,1,0:T(8,128)(2,1)} %get-tuple-element.69.own_ref, ...), custom_call_target="tpu_custom_call" | custom-call | tf_op jit(solution)/shard_map/pallas_call | solution.py:678
  408.5 13.0 %shard_map.214 = (bf16[4,128,2048]{2,1,0:T(8,128)(2,1)}, bf16[2048,768]{1,0:T(8,128)(2,1)}) custom-call(bf16[4,128,512]{2,1,0:T(8,128)(2,1)} %get-tuple-element.95.dq_ref, f32[4,192,128]{2,1,0:T(8,128)} %get-tuple-element.96.dkv_ref, f32[4,64,128]{2,1,0:T(8,128)} %copy-done.31, f32[4,128,128]{2,1,0:T(8,128)} %get-tuple-element.132.cos_ref, ...), custom_call_target="tpu_custom_call" | custom-call | tf_op jit(solution)/shard_map/pallas_call | solution.py:697
  421.6 4.2 convolution_convert_fusion.2
  426.6 8.3 %shard_map.211 = (bf16[8,64,704]{2,1,0:T(8,128)(2,1)}, bf16[8,64,704]{2,1,0:T(8,128)(2,1)}, bf16[8,64,704]{2,1,0:T(8,128)(2,1)}, bf16[8,64,704]{2,1,0:T(8,128)(2,1)}) custom-call(s32[2]{0:T(128)} %pad_add_fusion.id_ref, bf16[1024,2048]{1,0:T(8,128)(2,1)} %all-gather.9.cloned.1.call-done.x_ref, bf16[1024,704]{1,0:T(8,128)(2,1)} %get-tuple-element.90.up_ref.grad_ref), custom_call_target="tpu_custom_call" | custom-call | tf_op jit(solution)/shard_map/pallas_call | solution.py:246
  434.8 4.9 convolution_convert_fusion
  442.8 16.9 %collective-permute-done.22 = bf16[8,64,704]{2,1,0:T(8,128)(2,1)} collective-permute-done((bf16[8,64,704]{2,1,0:T(8,128)(2,1)}, bf16[8,64,704]{2,1,0:T(8,128)(2,1)}, u32[]{:S(2)}, u32[]{:S(2)}) %collective-permute-start.22) | collective-permute-done | bytes 720928 | tf_op jit(solution)/shard_map/ppermute | solution.py:55
  466.2 5.7 convolution_convert_fusion.1
  477.5 16.8 %collective-permute-done.23.refs_2_ = bf16[8,64,704]{2,1,0:T(8,128)(2,1)} collective-permute-done((bf16[8,64,704]{2,1,0:T(8,128)(2,1)}, bf16[8,64,704]{2,1,0:T(8,128)(2,1)}, u32[]{:S(2)}, u32[]{:S(2)}) %collective-permute-start.23) | collective-permute-done | bytes 720928 | tf_op jit(solution)/shard_map/ppermute | solution.py:55
  494.3 3.9 shard_map.218
  511.5 4.4 collective-permute-done.30.refs_4_
  516.4 13.2 %collective-permute-done.31.refs_5_ = bf16[2,64,704]{2,1,0:T(8,128)(2,1)S(1)} collective-permute-done((bf16[2,64,704]{2,1,0:T(8,128)(2,1)}, bf16[2,64,704]{2,1,0:T(8,128)(2,1)S(1)}, u32[]{:S(2)}, u32[]{:S(2)}) %collective-permute-start.31) | collective-permute-done | bytes 180256 | tf_op jit(solution)/shard_map/ppermute | solution.py:55
  529.6 25.5 %collective-permute-done.32.refs_6_ = bf16[2,64,704]{2,1,0:T(8,128)(2,1)S(1)} collective-permute-done((bf16[2,64,704]{2,1,0:T(8,128)(2,1)}, bf16[2,64,704]{2,1,0:T(8,128)(2,1)S(1)}, u32[]{:S(2)}, u32[]{:S(2)}) %collective-permute-start.32) | collective-permute-done | bytes 180256 | tf_op jit(solution)/shard_map/ppermute | solution.py:55
  555.1 8.7 %collective-permute-done.33.refs_7_ = bf16[2,64,704]{2,1,0:T(8,128)(2,1)S(1)} collective-permute-done((bf16[2,64,704]{2,1,0:T(8,128)(2,1)}, bf16[2,64,704]{2,1,0:T(8,128)(2,1)S(1)}, u32[]{:S(2)}, u32[]{:S(2)}) %collective-permute-start.33) | collective-permute-done | bytes 180256 | tf_op jit(solution)/shard_map/ppermute | solution.py:55
  571.9 4.7 all-to-all-start.5
  576.6 28.5 %collective-permute-done.44 = bf16[80,2048]{1,0:T(8,128)(2,1)} collective-permute-done((bf16[80,2048]{1,0:T(8,128)(2,1)}, bf16[80,2048]{1,0:T(8,128)(2,1)}, u32[]{:S(2)}, u32[]{:S(2)}) %collective-permute-start.44) | collective-permute-done | bytes 327712 | tf_op jit(solution)/shard_map/ppermute | solution.py:55
  608.7 11.8 %collective-permute-done.35.refs_2_ = bf16[64,5632]{1,0:T(8,128)(2,1)} collective-permute-done((bf16[64,5632]{1,0:T(8,128)(2,1)}, bf16[64,5632]{1,0:T(8,128)(2,1)}, u32[]{:S(2)}, u32[]{:S(2)}) %collective-permute-start.35) | collective-permute-done | bytes 720928 | tf_op jit(solution)/shard_map/ppermute | solution.py:55
  620.5 10.4 %collective-permute-done.37.refs_1_ = bf16[64,5632]{1,0:T(8,128)(2,1)S(1)} collective-permute-done((bf16[64,5632]{1,0:T(8,128)(2,1)}, bf16[64,5632]{1,0:T(8,128)(2,1)S(1)}, u32[]{:S(2)}, u32[]{:S(2)}) %collective-permute-start.37) | collective-permute-done | bytes 720928 | tf_op jit(solution)/shard_map/ppermute | solution.py:55
  631.0 23.0 %collective-permute-done.46.refs_2_ = bf16[96,2048]{1,0:T(8,128)(2,1)} collective-permute-done((bf16[96,2048]{1,0:T(8,128)(2,1)S(1)}, bf16[96,2048]{1,0:T(8,128)(2,1)}, u32[]{:S(2)}, u32[]{:S(2)}) %collective-permute-start.46) | collective-permute-done | bytes 393248 | tf_op jit(solution)/shard_map/ppermute | solution.py:55
  656.5 4.6 shard_map.220
  661.1 4.7 shard_map.221
  673.1 3.6 collective-permute-done.18.refs_1_
  680.7 4.6 shard_map.222
  685.3 3.7 shard_map.215
  692.1 8.0 %collective-permute-done.17.refs_3_ = bf16[256,768]{1,0:T(8,128)(2,1)} collective-permute-done((bf16[256,768]{1,0:T(8,128)(2,1)}, bf16[256,768]{1,0:T(8,128)(2,1)}, u32[]{:S(2)}, u32[]{:S(2)}) %collective-permute-start.17) | collective-permute-done | bytes 393248 | tf_op jit(solution)/shard_map/ppermute | solution.py:55
  (226 shorter events, 126.4 us)
Async XLA Ops:
  7.2 40.5 %all-gather.5.cloned.1.call-start = ((), (), s32[]{:S(2)}) async-start(), calls=%async_computation.10 | async-start | bytes 2949120 | tf_op jit(solution)/shard_map/all_gather | solution.py:531
  10.2 71.3 %all-gather.7.cloned.1.call-start = ((), (), s32[]{:S(2)}) async-start(), calls=%async_computation.11 | async-start | bytes 2359296 | tf_op jit(solution)/shard_map/all_gather | solution.py:532
  12.0 236.0 %all-gather.11.cloned.1.call-start = ((), (), s32[]{:S(2)}) async-start(), calls=%async_computation.13 | async-start | bytes 4718592 | tf_op jit(solution)/shard_map/all_gather | solution.py:557
  14.7 30.5 %all-to-all-start = ((bf16[4,128,2176]{2,1,0:T(8,128)(2,1)}), bf16[4,128,2176]{2,1,0:T(8,128)(2,1)}, u32[]{:S(2)}, u32[]{:S(2)}) async-start(bf16[4,128,2176]{2,1,0:T(8,128)(2,1)} %broadcast_in_dim.18), calls=%async_computation | async-start | bytes 4456448 | tf_op jit(solution)/shard_map/all_to_all | solution.py:43
  19.3 235.9 %all-gather.9.cloned.1.call-start = ((), (), s32[]{:S(2)}) async-start(), calls=%async_computation.12 | async-start | bytes 4718592 | tf_op jit(solution)/shard_map/all_gather | solution.py:603
  114.1 220.1 %reduce-scatter.7.cloned.1.call-start = ((), (), s32[]{:S(2)}) async-start(), calls=%async_computation.15 | async-start | bytes 4718592 | tf_op jit(solution)/shard_map/reduce_scatter | solution.py:626
  122.0 22.8 %collective-permute-start.3 = (bf16[2,64,704]{2,1,0:T(8,128)(2,1)}, bf16[2,64,704]{2,1,0:T(8,128)(2,1)S(1)}, u32[]{:S(2)}, u32[]{:S(2)}) collective-permute-start(bf16[2,64,704]{2,1,0:T(8,128)(2,1)} %get-tuple-element.78), channel_id=1, source_target_pairs={{0,3},{1,2},{2,1},{3,0},{4,7},{5,6},{6,5},{7,4},{8,11},{9,10},{10,... | collective-permute-start | bytes 540680 | tf_op jit(solution)/shard_map/ppermute | solution.py:55
  123.6 21.2 %collective-permute-start.4 = (bf16[2,64,704]{2,1,0:T(8,128)(2,1)}, bf16[2,64,704]{2,1,0:T(8,128)(2,1)S(1)}, u32[]{:S(2)}, u32[]{:S(2)}) collective-permute-start(bf16[2,64,704]{2,1,0:T(8,128)(2,1)} %get-tuple-element.79), channel_id=1, source_target_pairs={{0,4},{1,5},{2,6},{3,7},{4,0},{5,1},{6,2},{7,3},{8,12},{9,13},{10,... | collective-permute-start | bytes 540680 | tf_op jit(solution)/shard_map/ppermute | solution.py:55
  124.1 25.5 %collective-permute-start.5 = (bf16[2,64,704]{2,1,0:T(8,128)(2,1)}, bf16[2,64,704]{2,1,0:T(8,128)(2,1)S(1)}, u32[]{:S(2)}, u32[]{:S(2)}) collective-permute-start(bf16[2,64,704]{2,1,0:T(8,128)(2,1)} %get-tuple-element.80), channel_id=1, source_target_pairs={{0,5},{1,4},{2,7},{3,6},{4,1},{5,0},{6,3},{7,2},{8,13},{9,12},{10,... | collective-permute-start | bytes 540680 | tf_op jit(solution)/shard_map/ppermute | solution.py:55
  126.4 40.8 %collective-permute-start.6 = (bf16[2,64,704]{2,1,0:T(8,128)(2,1)}, bf16[2,64,704]{2,1,0:T(8,128)(2,1)S(1)}, u32[]{:S(2)}, u32[]{:S(2)}) collective-permute-start(bf16[2,64,704]{2,1,0:T(8,128)(2,1)} %get-tuple-element.81), channel_id=1, source_target_pairs={{0,6},{1,7},{2,4},{3,5},{4,2},{5,3},{6,0},{7,1},{8,14},{9,15},{10,... | collective-permute-start | bytes 540680 | tf_op jit(solution)/shard_map/ppermute | solution.py:55
  135.6 47.8 %collective-permute-start.7 = (bf16[2,64,704]{2,1,0:T(8,128)(2,1)}, bf16[2,64,704]{2,1,0:T(8,128)(2,1)S(1)}, u32[]{:S(2)}, u32[]{:S(2)}) collective-permute-start(bf16[2,64,704]{2,1,0:T(8,128)(2,1)} %get-tuple-element.82), channel_id=1, source_target_pairs={{0,7},{1,6},{2,5},{3,4},{4,3},{5,2},{6,1},{7,0},{8,15},{9,14},{10,... | collective-permute-start | bytes 540680 | tf_op jit(solution)/shard_map/ppermute | solution.py:55
  187.6 35.4 %collective-permute-start.9 = (bf16[8,64,704]{2,1,0:T(8,128)(2,1)}, bf16[8,64,704]{2,1,0:T(8,128)(2,1)S(1)}, u32[]{:S(2)}, u32[]{:S(2)}) collective-permute-start(bf16[8,64,704]{2,1,0:T(8,128)(2,1)} %get-tuple-element.84.refs_1_), channel_id=1, source_target_pairs={{0,8},{8,0},{16,24},{24,16},{1,9},{9,1},{17,25},{25,17},{2,10},{10... | collective-permute-start | bytes 2162696 | tf_op jit(solution)/shard_map/ppermute | solution.py:55
  188.9 34.6 %collective-permute-start.10 = (bf16[8,64,704]{2,1,0:T(8,128)(2,1)}, bf16[8,64,704]{2,1,0:T(8,128)(2,1)S(1)}, u32[]{:S(2)}, u32[]{:S(2)}) collective-permute-start(bf16[8,64,704]{2,1,0:T(8,128)(2,1)} %get-tuple-element.83.refs_0_), channel_id=1, source_target_pairs={{0,16},{8,24},{16,0},{24,8},{1,17},{9,25},{17,1},{25,9},{2,18},{10... | collective-permute-start | bytes 2162696 | tf_op jit(solution)/shard_map/ppermute | solution.py:55
  206.2 34.2 %collective-permute-start.12 = (bf16[8,64,704]{2,1,0:T(8,128)(2,1)S(1)}, bf16[8,64,704]{2,1,0:T(8,128)(2,1)S(1)}, u32[]{:S(2)}, u32[]{:S(2)}) collective-permute-start(bf16[8,64,704]{2,1,0:T(8,128)(2,1)S(1)} %collective-permute-done.8.refs_2_), channel_id=1, source_target_pairs={{0,16},{8,24},{16,0},{24,8},{1,17},{9,25},{17,1},{25,9},{2,18},{10... | collective-permute-start | bytes 2162696 | tf_op jit(solution)/shard_map/ppermute | solution.py:55
  207.0 33.4 %collective-permute-start.13 = (bf16[8,64,704]{2,1,0:T(8,128)(2,1)S(1)}, bf16[8,64,704]{2,1,0:T(8,128)(2,1)S(1)}, u32[]{:S(2)}, u32[]{:S(2)}) collective-permute-start(bf16[8,64,704]{2,1,0:T(8,128)(2,1)S(1)} %collective-permute-done.11.refs_5_), channel_id=1, source_target_pairs={{0,8},{8,0},{16,24},{24,16},{1,9},{9,1},{17,25},{25,17},{2,10},{10... | collective-permute-start | bytes 2162696 | tf_op jit(solution)/shard_map/ppermute | solution.py:55
  286.9 368.6 %reduce-scatter.11.cloned.1.call-start = ((), (), s32[]{:S(2)}) async-start(), calls=%async_computation.17 | async-start | bytes 2359296 | tf_op jit(solution)/shard_map/reduce_scatter | solution.py:720
  425.8 245.3 %reduce-scatter.9.cloned.1.call-start = ((), (), s32[]{:S(2)}) async-start(), calls=%async_computation.16 | async-start | bytes 3538944 | tf_op jit(solution)/shard_map/reduce_scatter | solution.py:718
  426.5 251.9 %reduce-scatter.5.cloned.1.call-start = ((), (), s32[]{:S(2)}) async-start(), calls=%async_computation.14 | async-start | bytes 4718592 | tf_op jit(solution)/shard_map/reduce_scatter | solution.py:648
  440.7 22.7 %collective-permute-start.25 = (bf16[8,64,704]{2,1,0:T(8,128)(2,1)}, bf16[8,64,704]{2,1,0:T(8,128)(2,1)}, u32[]{:S(2)}, u32[]{:S(2)}) collective-permute-start(bf16[8,64,704]{2,1,0:T(8,128)(2,1)} %get-tuple-element.112), channel_id=1, source_target_pairs={{0,16},{8,24},{16,0},{24,8},{1,17},{9,25},{17,1},{25,9},{2,18},{10... | collective-permute-start | bytes 2162696 | tf_op jit(solution)/shard_map/ppermute | solution.py:55
  441.6 35.0 %collective-permute-start.21 = (bf16[8,64,704]{2,1,0:T(8,128)(2,1)}, bf16[8,64,704]{2,1,0:T(8,128)(2,1)}, u32[]{:S(2)}, u32[]{:S(2)}) collective-permute-start(bf16[8,64,704]{2,1,0:T(8,128)(2,1)} %get-tuple-element.107), channel_id=1, source_target_pairs={{0,8},{8,0},{16,24},{24,16},{1,9},{9,1},{17,25},{25,17},{2,10},{10... | collective-permute-start | bytes 2162696 | tf_op jit(solution)/shard_map/ppermute | solution.py:55
  442.5 35.0 %collective-permute-start.24 = (bf16[8,64,704]{2,1,0:T(8,128)(2,1)}, bf16[8,64,704]{2,1,0:T(8,128)(2,1)}, u32[]{:S(2)}, u32[]{:S(2)}) collective-permute-start(bf16[8,64,704]{2,1,0:T(8,128)(2,1)} %get-tuple-element.110), channel_id=1, source_target_pairs={{0,16},{8,24},{16,0},{24,8},{1,17},{9,25},{17,1},{25,9},{2,18},{10... | collective-permute-start | bytes 2162696 | tf_op jit(solution)/shard_map/ppermute | solution.py:55
  462.3 32.0 %collective-permute-start.23 = (bf16[8,64,704]{2,1,0:T(8,128)(2,1)}, bf16[8,64,704]{2,1,0:T(8,128)(2,1)}, u32[]{:S(2)}, u32[]{:S(2)}) collective-permute-start(bf16[8,64,704]{2,1,0:T(8,128)(2,1)} %add_convert_fusion.1), channel_id=1, source_target_pairs={{0,16},{8,24},{16,0},{24,8},{1,17},{9,25},{17,1},{25,9},{2,18},{10... | collective-permute-start | bytes 2162696 | tf_op jit(solution)/shard_map/ppermute | solution.py:55
  465.6 28.7 %collective-permute-start.26 = (bf16[8,64,704]{2,1,0:T(8,128)(2,1)}, bf16[8,64,704]{2,1,0:T(8,128)(2,1)}, u32[]{:S(2)}, u32[]{:S(2)}) collective-permute-start(bf16[8,64,704]{2,1,0:T(8,128)(2,1)} %add_convert_fusion), channel_id=1, source_target_pairs={{0,8},{8,0},{16,24},{24,16},{1,9},{9,1},{17,25},{25,17},{2,10},{10... | collective-permute-start | bytes 2162696 | tf_op jit(solution)/shard_map/ppermute | solution.py:55
  474.4 26.9 %collective-permute-start.42 = (bf16[80,2048]{1,0:T(8,128)(2,1)}, bf16[80,2048]{1,0:T(8,128)(2,1)}, u32[]{:S(2)}, u32[]{:S(2)}) collective-permute-start(bf16[80,2048]{1,0:T(8,128)(2,1)} %get-tuple-element.128), channel_id=1, source_target_pairs={{0,16},{8,24},{16,0},{24,8},{1,17},{9,25},{17,1},{25,9},{2,18},{10... | collective-permute-start | bytes 983048 | tf_op jit(solution)/shard_map/ppermute | solution.py:55
  476.6 27.4 %collective-permute-start.41 = (bf16[96,2048]{1,0:T(8,128)(2,1)S(1)}, bf16[96,2048]{1,0:T(8,128)(2,1)S(1)}, u32[]{:S(2)}, u32[]{:S(2)}) collective-permute-start(bf16[96,2048]{1,0:T(8,128)(2,1)S(1)} %get-tuple-element.130), channel_id=1, source_target_pairs={{0,8},{8,0},{16,24},{24,16},{1,9},{9,1},{17,25},{25,17},{2,10},{10... | collective-permute-start | bytes 1179656 | tf_op jit(solution)/shard_map/ppermute | solution.py:55
  504.0 25.6 %collective-permute-start.31 = (bf16[2,64,704]{2,1,0:T(8,128)(2,1)}, bf16[2,64,704]{2,1,0:T(8,128)(2,1)S(1)}, u32[]{:S(2)}, u32[]{:S(2)}) collective-permute-start(bf16[2,64,704]{2,1,0:T(8,128)(2,1)} %get-tuple-element.118), channel_id=1, source_target_pairs={{0,5},{1,4},{2,7},{3,6},{4,1},{5,0},{6,3},{7,2},{8,13},{9,12},{10,... | collective-permute-start | bytes 540680 | tf_op jit(solution)/shard_map/ppermute | solution.py:55
  506.1 49.0 %collective-permute-start.32 = (bf16[2,64,704]{2,1,0:T(8,128)(2,1)}, bf16[2,64,704]{2,1,0:T(8,128)(2,1)S(1)}, u32[]{:S(2)}, u32[]{:S(2)}) collective-permute-start(bf16[2,64,704]{2,1,0:T(8,128)(2,1)} %get-tuple-element.119), channel_id=1, source_target_pairs={{0,6},{1,7},{2,4},{3,5},{4,2},{5,3},{6,0},{7,1},{8,14},{9,15},{10,... | collective-permute-start | bytes 540680 | tf_op jit(solution)/shard_map/ppermute | solution.py:55
  506.2 57.6 %collective-permute-start.33 = (bf16[2,64,704]{2,1,0:T(8,128)(2,1)}, bf16[2,64,704]{2,1,0:T(8,128)(2,1)S(1)}, u32[]{:S(2)}, u32[]{:S(2)}) collective-permute-start(bf16[2,64,704]{2,1,0:T(8,128)(2,1)} %get-tuple-element.120), channel_id=1, source_target_pairs={{0,7},{1,6},{2,5},{3,4},{4,3},{5,2},{6,1},{7,0},{8,15},{9,14},{10,... | collective-permute-start | bytes 540680 | tf_op jit(solution)/shard_map/ppermute | solution.py:55
  511.5 58.3 %collective-permute-start.40 = (bf16[96,2048]{1,0:T(8,128)(2,1)S(1)}, bf16[96,2048]{1,0:T(8,128)(2,1)}, u32[]{:S(2)}, u32[]{:S(2)}) collective-permute-start(bf16[96,2048]{1,0:T(8,128)(2,1)S(1)} %get-tuple-element.129), channel_id=1, source_target_pairs={{0,8},{8,0},{16,24},{24,16},{1,9},{9,1},{17,25},{25,17},{2,10},{10... | collective-permute-start | bytes 1179656 | tf_op jit(solution)/shard_map/ppermute | solution.py:55
  515.9 53.9 %collective-permute-start.43 = (bf16[96,2048]{1,0:T(8,128)(2,1)}, bf16[96,2048]{1,0:T(8,128)(2,1)}, u32[]{:S(2)}, u32[]{:S(2)}) collective-permute-start(bf16[96,2048]{1,0:T(8,128)(2,1)} %add_convert_fusion.4), channel_id=1, source_target_pairs={{0,16},{8,24},{16,0},{24,8},{1,17},{9,25},{17,1},{25,9},{2,18},{10... | collective-permute-start | bytes 1179656 | tf_op jit(solution)/shard_map/ppermute | solution.py:55
  567.5 37.6 %collective-permute-start.34 = (bf16[64,5632]{1,0:T(8,128)(2,1)}, bf16[64,5632]{1,0:T(8,128)(2,1)}, u32[]{:S(2)}, u32[]{:S(2)}) collective-permute-start(bf16[64,5632]{1,0:T(8,128)(2,1)} %get-tuple-element.121.refs_0_), channel_id=1, source_target_pairs={{0,8},{8,0},{16,24},{24,16},{1,9},{9,1},{17,25},{25,17},{2,10},{10... | collective-permute-start | bytes 2162696 | tf_op jit(solution)/shard_map/ppermute | solution.py:55
  568.3 36.8 %collective-permute-start.38 = (bf16[64,5632]{1,0:T(8,128)(2,1)}, bf16[64,5632]{1,0:T(8,128)(2,1)}, u32[]{:S(2)}, u32[]{:S(2)}) collective-permute-start(bf16[64,5632]{1,0:T(8,128)(2,1)} %get-tuple-element.122.refs_0_), channel_id=1, source_target_pairs={{0,16},{8,24},{16,0},{24,8},{1,17},{9,25},{17,1},{25,9},{2,18},{10... | collective-permute-start | bytes 2162696 | tf_op jit(solution)/shard_map/ppermute | solution.py:55
  568.3 36.7 %collective-permute-start.44 = (bf16[80,2048]{1,0:T(8,128)(2,1)}, bf16[80,2048]{1,0:T(8,128)(2,1)}, u32[]{:S(2)}, u32[]{:S(2)}) collective-permute-start(bf16[80,2048]{1,0:T(8,128)(2,1)} %get-tuple-element.127), channel_id=1, source_target_pairs={{0,16},{8,24},{16,0},{24,8},{1,17},{9,25},{17,1},{25,9},{2,18},{10... | collective-permute-start | bytes 983048 | tf_op jit(solution)/shard_map/ppermute | solution.py:55
  569.8 50.7 %collective-permute-start.35 = (bf16[64,5632]{1,0:T(8,128)(2,1)}, bf16[64,5632]{1,0:T(8,128)(2,1)}, u32[]{:S(2)}, u32[]{:S(2)}) collective-permute-start(bf16[64,5632]{1,0:T(8,128)(2,1)} %get-tuple-element.121.refs_0_), channel_id=1, source_target_pairs={{0,16},{8,24},{16,0},{24,8},{1,17},{9,25},{17,1},{25,9},{2,18},{10... | collective-permute-start | bytes 2162696 | tf_op jit(solution)/shard_map/ppermute | solution.py:55
  569.8 36.8 %collective-permute-start.45 = (bf16[80,2048]{1,0:T(8,128)(2,1)}, bf16[80,2048]{1,0:T(8,128)(2,1)}, u32[]{:S(2)}, u32[]{:S(2)}) collective-permute-start(bf16[80,2048]{1,0:T(8,128)(2,1)} %add_convert_fusion.6), channel_id=1, source_target_pairs={{0,8},{8,0},{16,24},{24,16},{1,9},{9,1},{17,25},{25,17},{2,10},{10... | collective-permute-start | bytes 983048 | tf_op jit(solution)/shard_map/ppermute | solution.py:55
  571.9 113.4 %all-to-all-start.5 = ((bf16[4,128,2048]{2,1,0:T(8,128)(2,1)}), bf16[4,128,2048]{2,1,0:T(8,128)(2,1)}, u32[]{:S(2)}, u32[]{:S(2)}) async-start(bf16[4,128,2048]{2,1,0:T(8,128)(2,1)} %get-tuple-element.99), calls=%async_computation.7 | async-start | bytes 4194304 | tf_op jit(solution)/shard_map/all_to_all | solution.py:47
  605.1 25.9 %collective-permute-start.37 = (bf16[64,5632]{1,0:T(8,128)(2,1)}, bf16[64,5632]{1,0:T(8,128)(2,1)S(1)}, u32[]{:S(2)}, u32[]{:S(2)}) collective-permute-start(bf16[64,5632]{1,0:T(8,128)(2,1)} %get-tuple-element.122.refs_0_), channel_id=1, source_target_pairs={{0,8},{8,0},{16,24},{24,16},{1,9},{9,1},{17,25},{25,17},{2,10},{10... | collective-permute-start | bytes 2162696 | tf_op jit(solution)/shard_map/ppermute | solution.py:55
  605.1 48.9 %collective-permute-start.36 = (bf16[64,5632]{1,0:T(8,128)(2,1)}, bf16[64,5632]{1,0:T(8,128)(2,1)}, u32[]{:S(2)}, u32[]{:S(2)}) collective-permute-start(bf16[64,5632]{1,0:T(8,128)(2,1)} %collective-permute-done.34.refs_1_), channel_id=1, source_target_pairs={{0,16},{8,24},{16,0},{24,8},{1,17},{9,25},{17,1},{25,9},{2,18},{10... | collective-permute-start | bytes 2162696 | tf_op jit(solution)/shard_map/ppermute | solution.py:55
  605.1 50.4 %collective-permute-start.39 = (bf16[64,5632]{1,0:T(8,128)(2,1)}, bf16[64,5632]{1,0:T(8,128)(2,1)}, u32[]{:S(2)}, u32[]{:S(2)}) collective-permute-start(bf16[64,5632]{1,0:T(8,128)(2,1)} %collective-permute-done.38.refs_2_), channel_id=1, source_target_pairs={{0,8},{8,0},{16,24},{24,16},{1,9},{9,1},{17,25},{25,17},{2,10},{10... | collective-permute-start | bytes 2162696 | tf_op jit(solution)/shard_map/ppermute | solution.py:55
  606.6 47.3 %collective-permute-start.46 = (bf16[96,2048]{1,0:T(8,128)(2,1)S(1)}, bf16[96,2048]{1,0:T(8,128)(2,1)}, u32[]{:S(2)}, u32[]{:S(2)}) collective-permute-start(bf16[96,2048]{1,0:T(8,128)(2,1)S(1)} %add_convert_fusion.3.refs_0_), channel_id=1, source_target_pairs={{0,8},{8,0},{16,24},{24,16},{1,9},{9,1},{17,25},{25,17},{2,10},{10... | collective-permute-start | bytes 1179656 | tf_op jit(solution)/shard_map/ppermute | solution.py:55
  620.5 34.5 %collective-permute-start.49 = (bf16[80,2048]{1,0:T(8,128)(2,1)}, bf16[80,2048]{1,0:T(8,128)(2,1)}, u32[]{:S(2)}, u32[]{:S(2)}) collective-permute-start(bf16[80,2048]{1,0:T(8,128)(2,1)} %add_convert_fusion.5.refs_1_), channel_id=1, source_target_pairs={{0,16},{8,24},{16,0},{24,8},{1,17},{9,25},{17,1},{25,9},{2,18},{10... | collective-permute-start | bytes 983048 | tf_op jit(solution)/shard_map/ppermute | solution.py:55
  630.9 36.3 %collective-permute-start.48 = (bf16[96,2048]{1,0:T(8,128)(2,1)S(1)}, bf16[96,2048]{1,0:T(8,128)(2,1)}, u32[]{:S(2)}, u32[]{:S(2)}) collective-permute-start(bf16[96,2048]{1,0:T(8,128)(2,1)S(1)} %add_convert_fusion.3.refs_0_), channel_id=1, source_target_pairs={{0,16},{8,24},{16,0},{24,8},{1,17},{9,25},{17,1},{25,9},{2,18},{10... | collective-permute-start | bytes 1179656 | tf_op jit(solution)/shard_map/ppermute | solution.py:55
  655.5 21.2 %collective-permute-start.18 = (bf16[64,2048]{1,0:T(8,128)(2,1)}, bf16[64,2048]{1,0:T(8,128)(2,1)}, u32[]{:S(2)}, u32[]{:S(2)}) collective-permute-start(bf16[64,2048]{1,0:T(8,128)(2,1)} %reduce-scatter.11.cloned.1.call-done.refs_0_), channel_id=1, source_target_pairs={{0,8},{8,0},{16,24},{24,16},{1,9},{9,1},{17,25},{25,17},{2,10},{10... | collective-permute-start | bytes 786440 | tf_op jit(solution)/shard_map/ppermute | solution.py:55
  665.8 23.2 %collective-permute-start.19 = (bf16[64,2048]{1,0:T(8,128)(2,1)S(1)}, bf16[64,2048]{1,0:T(8,128)(2,1)}, u32[]{:S(2)}, u32[]{:S(2)}) collective-permute-start(bf16[64,2048]{1,0:T(8,128)(2,1)S(1)} %copy-done.16), channel_id=1, source_target_pairs={{0,16},{8,24},{16,0},{24,8},{1,17},{9,25},{17,1},{25,9},{2,18},{10... | collective-permute-start | bytes 786440 | tf_op jit(solution)/shard_map/ppermute | solution.py:55
  667.3 21.7 %collective-permute-start.20 = (bf16[64,2048]{1,0:T(8,128)(2,1)S(1)}, bf16[64,2048]{1,0:T(8,128)(2,1)}, u32[]{:S(2)}, u32[]{:S(2)}) collective-permute-start(bf16[64,2048]{1,0:T(8,128)(2,1)S(1)} %copy-done.16), channel_id=1, source_target_pairs={{0,24},{8,16},{16,8},{24,0},{1,25},{9,17},{17,9},{25,1},{2,26},{10... | collective-permute-start | bytes 786440 | tf_op jit(solution)/shard_map/ppermute | solution.py:55
  671.1 21.0 %collective-permute-start.15 = (bf16[256,768]{1,0:T(8,128)(2,1)}, bf16[256,768]{1,0:T(8,128)(2,1)S(1)}, u32[]{:S(2)}, u32[]{:S(2)}) collective-permute-start(bf16[256,768]{1,0:T(8,128)(2,1)} %reduce-scatter.9.cloned.1.call-done.refs_0_), channel_id=1, source_target_pairs={{0,8},{8,0},{16,24},{24,16},{1,9},{9,1},{17,25},{25,17},{2,10},{10... | collective-permute-start | bytes 1179656 | tf_op jit(solution)/shard_map/ppermute | solution.py:55
  671.3 20.8 %collective-permute-start.16 = (bf16[256,768]{1,0:T(8,128)(2,1)}, bf16[256,768]{1,0:T(8,128)(2,1)}, u32[]{:S(2)}, u32[]{:S(2)}) collective-permute-start(bf16[256,768]{1,0:T(8,128)(2,1)} %reduce-scatter.9.cloned.1.call-done.refs_0_), channel_id=1, source_target_pairs={{0,16},{8,24},{16,0},{24,8},{1,17},{9,25},{17,1},{25,9},{2,18},{10... | collective-permute-start | bytes 1179656 | tf_op jit(solution)/shard_map/ppermute | solution.py:55
  676.7 23.4 %collective-permute-start.17 = (bf16[256,768]{1,0:T(8,128)(2,1)}, bf16[256,768]{1,0:T(8,128)(2,1)}, u32[]{:S(2)}, u32[]{:S(2)}) collective-permute-start(bf16[256,768]{1,0:T(8,128)(2,1)} %reduce-scatter.9.cloned.1.call-done.refs_0_), channel_id=1, source_target_pairs={{0,24},{8,16},{16,8},{24,0},{1,25},{9,17},{17,9},{25,1},{2,26},{10... | collective-permute-start | bytes 1179656 | tf_op jit(solution)/shard_map/ppermute | solution.py:55
  (52 other events, 1211.5 us)
Sparse Core Ops, SparseCore 0:
  10.4 34.8 all-gather.4
  47.4 28.7 all-gather.6
  77.8 45.7 all-gather.10
  125.0 67.3 all-gather.8
  287.1 47.0 reduce-scatter.6
  425.9 28.4 reduce-scatter.10
  456.7 42.4 reduce-scatter.8
  502.1 80.5 reduce-scatter.4

commit v8 on v6

--- a/solution.py
+++ b/solution.py
@@ -72,8 +72,13 @@
     return [[chunks[0][0], first_one, last_one], [chunks[0][1], second_one, last_two]]
 
 
-def gather_direct(value, count):
-    return [value] + [send(value, "rep", count, k) for k in range(1, count)]
+def gather_two(value, count):
+    go = lambda value, step: send(value, "rep", count, step)
+    if count != 4:
+        return [(value,)] + [(go(value, k),) for k in range(1, count)]
+    half = value.shape[0] // 2
+    one, two = go(value, 1), go(value, 2)
+    return [(value,), (one,), (two,), (go(one[:half], 2), go(two[half:], 1))]
 
 
 def gather_rep(halves, count):
@@ -85,16 +90,16 @@
     return [halves, one, two, (go(one[0], 2), go(two[1], 1))]
 
 
-def place_kernel(count, me_ref, *refs):
-    parts, out_ref = refs[:-1], refs[-1]
+def place_kernel(sizes, me_ref, *refs):
+    parts, out_ref = list(refs[:-1]), refs[-1]
     at = pl.program_id(0)
-    size = len(parts) // count
-    for k in range(count):
+    for k, size in enumerate(sizes):
+        mine, parts = parts[:size], parts[size:]
 
         @pl.when(at == jnp.bitwise_xor(me_ref[0], k))
-        def _(k=k):
+        def _(mine=mine):
             row = 0
-            for part in parts[k * size : (k + 1) * size]:
+            for part in mine:
                 out_ref[0, row : row + part.shape[0]] = part[...].astype(F32)
                 row += part.shape[0]
 
@@ -114,7 +119,7 @@
         out_specs=pl.BlockSpec((1, rows, width), lambda g, me: (g, 0, 0)),
     )
     return pl.pallas_call(
-        partial(place_kernel, count),
+        partial(place_kernel, [len(piece) for piece in pieces]),
         out_shape=shape((count, rows, width), F32),
         grid_spec=grid,
         compiler_params=pltpu.CompilerParams(vmem_limit_bytes=56 * 1024 * 1024),
@@ -204,20 +209,25 @@
             ref[:, at * hidden : (at + 1) * hidden] = both[at, h]
 
 
-def qkv_kernel(share, id_ref, *refs):
+def qkv_kernel(share, sizes, id_ref, *refs):
     pieces = refs[:-6]
     q_ref, k_ref, v_ref, gain_ref, k_all, v_all = refs[-6:]
     count = k_all.shape[0]
     q_cols = q_ref.shape[1] // count
-    total = 0.0
-    for k, piece in enumerate(pieces):
+    gain_ref[...] = jnp.zeros_like(gain_ref)
+    pieces = list(pieces)
+    for k, size in enumerate(sizes):
         at = jnp.bitwise_xor(id_ref[0], k)
-        value = piece[...].astype(F32)
-        q_ref[:, pl.ds(pl.multiple_of(at * q_cols, LANES), q_cols)] = value[:, :q_cols]
-        k_all[at] = value[:, q_cols : q_cols + HD]
-        v_all[at] = value[:, q_cols + HD : q_cols + 2 * HD]
-        total += value[:, q_cols + 2 * HD :]
-    gain_ref[...] = total
+        row = 0
+        for piece in pieces[:size]:
+            value = piece[...].astype(F32)
+            rows = slice(row, row + value.shape[0])
+            q_ref[rows, pl.ds(pl.multiple_of(at * q_cols, LANES), q_cols)] = value[:, :q_cols]
+            k_all[at, rows] = value[:, q_cols : q_cols + HD]
+            v_all[at, rows] = value[:, q_cols + HD : q_cols + 2 * HD]
+            gain_ref[rows] += value[:, q_cols + 2 * HD :]
+            row = rows.stop
+        pieces = pieces[size:]
     for ref, both in ((k_ref, k_all), (v_ref, v_all)):
         for head in range(count // share):
             total = both[head * share]
@@ -256,6 +266,17 @@
         ),
         compiler_params=pltpu.CompilerParams(vmem_limit_bytes=56 * 1024 * 1024),
     )(ids, x, grad)
+
+
+def stack_kernel(sizes, id_ref, *refs):
+    parts, out_ref = list(refs[:-1]), refs[-1]
+    for k, size in enumerate(sizes):
+        at = jnp.bitwise_xor(id_ref[0], k)
+        row = 0
+        for part in parts[:size]:
+            out_ref[at, row : row + part.shape[0]] = part[...]
+            row += part.shape[0]
+        parts = parts[size:]
 
 
 def norm_scale(value):
@@ -364,7 +385,7 @@
 
 
 def in_back_kernel(
-    dq_ref, dkv_ref, back_ref, cos_ref, sin_ref, normed_ref, x_ref, two_ref, w_ref,
+    id_ref, dq_ref, dkv_ref, back_ref, cos_ref, sin_ref, normed_ref, x_ref, two_ref, w_ref,
     part_ref, grad_ref, total_ref,
 ):
     at = pl.program_id(0)
@@ -421,12 +442,18 @@
     low_ref[...] = out.astype(BF)
 
 
-def last_kernel(part_ref, x_ref, gain_ref, mid_ref, out_ref):
+def last_kernel(id_ref, *refs):
+    parts, (x_ref, gain_ref, mid_ref, out_ref) = refs[:-4], refs[-4:]
     x = x_ref[...].astype(F32)
     scale = norm_scale(x)
-    grad = part_ref[0].astype(F32)
-    for at in range(1, part_ref.shape[0]):
-        grad += part_ref[at].astype(F32)
+    half = len(parts) // 2
+    halves = []
+    for h in range(2):
+        total = parts[h * half][...].astype(F32)
+        for part in parts[h * half + 1 : (h + 1) * half]:
+            total += part[...].astype(F32)
+        halves.append(total)
+    grad = jnp.concatenate(halves, axis=0)
     scaled = grad * gain_ref[...]
     out = (
         mid_ref[...]
@@ -669,14 +696,20 @@
     gate_out = place([piece[:1] for piece in w_pair_grad], r)
     up_out = place([piece[1:] for piece in w_pair_grad], r)
 
-    branch_all = spread(branch, "rep", n_rep).reshape(all_rows, width)
+    branch = gather_two(branch, n_rep)
+    branch_all = flat_call(
+        partial(stack_kernel, [len(piece) for piece in branch]),
+        ids,
+        shape((n_rep, rows, width), BF),
+        [part for piece in branch for part in piece],
+    ).reshape(all_rows, width)
     in_grad = cols_cols(branch_all, w_o).astype(BF)
     branch_all, in_grad = lax.optimization_barrier((branch_all, in_grad))
     in_grad = in_grad.reshape(all_rows, n_rep, pair * fine).transpose(1, 0, 2)
     in_grad = swap(in_grad, "rep").reshape(n_rep, n_rep, rows, pair * fine)
     w_o_grad = rows_rows(out_in, branch_all).astype(BF)
     w_o_grad = lax.psum_scatter(w_o_grad, "shard", scatter_dimension=0, tiled=True)
-    o_out = place([(v,) for v in gather_direct(w_o_grad, n_rep)], r)
+    o_out = place(gather_two(w_o_grad, n_rep), r)
     query_grad, kv_grad = call(
         partial(attend_back_kernel, fine),
         (shape((n_rep, rows, q_cols), BF), shape((n_rep, span, LANES), F32)),
@@ -696,32 +729,58 @@
         kv_grad[:, :HALO], "shard", [(i + 1, i) for i in range(n_shard - 1)]
     )
     grad_cols = qkv_cols + LANES
-    one_grad_part, w_qkv_grad = call(
+    steady = lambda *dims: pl.BlockSpec(
+        dims, lambda g, ids: (0,) * len(dims), pipeline_mode=pl.Buffered(1)
+    )
+    block_of = lambda *dims: pl.BlockSpec(
+        (1,) + dims, lambda g, ids: (g,) + (0,) * len(dims)
+    )
+    one_grad_part, w_qkv_grad = pl.pallas_call(
         in_back_kernel,
-        (shape((n_rep, rows, width), BF), shape((width, grad_cols), BF)),
-        (n_rep,),
-        [
-            by_block((rows, q_cols)),
-            by_block((span, LANES)),
-            by_block((HALO, LANES)),
-            table,
-            table,
-            x_block,
-            x_block,
-            whole((rows, width)),
-            whole((width, qkv_cols)),
-        ],
-        (x_block, pl.BlockSpec((width, grad_cols), lambda g: (0, 0))),
-        [pltpu.VMEM((width, grad_cols), F32)],
+        out_shape=(shape((n_rep, rows, width), BF), shape((width, grad_cols), BF)),
+        grid_spec=pltpu.PrefetchScalarGridSpec(
+            num_scalar_prefetch=1,
+            grid=(n_rep,),
+            in_specs=[
+                block_of(rows, q_cols),
+                block_of(span, LANES),
+                block_of(HALO, LANES),
+                block_of(rows, LANES),
+                block_of(rows, LANES),
+                block_of(rows, width),
+                block_of(rows, width),
+                steady(rows, width),
+                steady(width, qkv_cols),
+            ],
+            out_specs=(
+                pl.BlockSpec(
+                    (1, rows, width), lambda g, ids: (jnp.bitwise_xor(g, ids[0]), 0, 0)
+                ),
+                pl.BlockSpec((width, grad_cols), lambda g, ids: (0, 0)),
+            ),
+            scratch_shapes=[pltpu.VMEM((width, grad_cols), F32)],
+        ),
+        name="attn_in_back",
+        compiler_params=pltpu.CompilerParams(vmem_limit_bytes=56 * 1024 * 1024),
     )(
-        query_grad, kv_grad, kv_back, cosine, sine, normed_one, x_all, gain_two_rows, w_qkv
+        ids, query_grad, kv_grad, kv_back, cosine, sine, normed_one, x_all, gain_two_rows,
+        w_qkv,
     )
     w_qkv_grad = lax.psum_scatter(w_qkv_grad, "shard", scatter_dimension=0, tiled=True)
-    input_grad = call(last_kernel, shape((rows, width), BF))(
-        swap(one_grad_part, "rep"), tokens, gain_one, mid_grad
-    )
+    one_grad = [one_grad_part[k] for k in range(n_rep)]
+    one_grad = [(part[: rows // 2], part[rows // 2 :]) for part in one_grad]
+    one_grad = parts_rep(one_grad, n_rep)
+    input_grad = flat_call(
+        last_kernel,
+        ids,
+        shape((rows, width), BF),
+        one_grad[0] + one_grad[1] + [tokens, gain_one, mid_grad],
+    )
+    w_qkv_grad = [(w_qkv_grad,)] + [
+        (send(w_qkv_grad, "rep", n_rep, k),) for k in range(1, n_rep)
+    ]
     q_out, k_out, v_out, gain_sums = flat_call(
-        partial(qkv_kernel, share),
+        partial(qkv_kernel, share, [len(piece) for piece in w_qkv_grad]),
         ids,
         (
             shape((own, width), F32),
@@ -729,7 +788,7 @@
             shape((own, KVH * HD), F32),
             shape((own, LANES), F32),
         ),
-        gather_direct(w_qkv_grad, n_rep),
+        [part for piece in w_qkv_grad for part in piece],
         [pltpu.VMEM((n_rep, own, HD), F32)] * 2,
     )
     return (

time: 698 us -> 697 us (level)
  blocking collectives: 89.5 us -> 61.8 us
  starting transfers between devices: 85.2 us -> 109 us
    ppermute x50 -> x61, starting transfers between devices: 71.9 us -> 99.8 us  [send(): return lax.ppermute(value, axis, pairs(count, step))]
    all_to_all x1 -> x0, blocking collectives: 27.6 us -> none  [spread(): return lax.all_to_all(wide, axis, split_axis=0, concat_axis=0, tiled=True)]
    pallas_call x5 -> x7, Pallas kernels: 18.4 us -> 24.8 us  [flat_call(): pl.pallas_call(kernel, out_shape=out_shape, in_specs=specs, scratch_shape...]
    pallas_call x6 -> x5, Pallas kernels: 33.8 us -> 30.9 us  [the longest x4 17.2 us: place(): pl.pallas_call(partial(place_kernel, [len(piece) for piece in pieces]), o...]
    ppermute x50 -> x61, waiting for transfers between devices: 237 us -> 235 us  [send(): return lax.ppermute(value, axis, pairs(count, step))]
  transfers between devices with their start and end apart: 62 -> 72, of which waited for: 29 -> 37; matrix products, arithmetic and copies ran while one was open for 6% -> 6% of each run, Pallas kernels for 12% -> 12%
where the time goes in v8:
time: 697 us; the launch traced here: 690 us
  waiting for transfers between devices  317 us (45%)
  Pallas kernels  127 us (18%)
  starting transfers between devices  109 us (16%)
  blocking collectives  61.8 us (9%)
  matrix products  26.9 us (4%)
  local copies, waits for them, and re-layouts  19.8 us (3%)
  between operations  15 us (2%)
  other arithmetic  14 us (2%)
    ppermute x61, waiting for transfers between devices, send(): return lax.ppermute(value, axis, pairs(count, step))  235 us
    ppermute x61, starting transfers between devices, send(): return lax.ppermute(value, axis, pairs(count, step))  99.8 us
    reduce_scatter x1, waiting for transfers between devices, body(): lax.psum_scatter(two_grad_part, 'shard', scatter_dimension=0, tiled=True)  65.2 us
    all_to_all x3, blocking collectives, swap(): return lax.all_to_all(value, axis, split_axis=0, concat_axis=0, tiled=True)  48.6 us
    dot_general x6, matrix products, dot(): lax.dot_general(left, right, (contract, ((), ())), preferred_element_type...  26.9 us
    pallas_call x7, Pallas kernels, flat_call(): pl.pallas_call(kernel, out_shape=out_shape, in_specs=specs, scratch_shape...  24.8 us
    pallas_call x4, Pallas kernels, place(): pl.pallas_call(partial(place_kernel, [len(piece) for piece in pieces]), o...  17.2 us
    pallas_call x2, Pallas kernels, pair_grad(): pl.pallas_call(partial(pair_grad_kernel, fine), out_shape=(shape((blocks,...  16.4 us
  transfers between devices with their start and end apart: 72, of which 37 were waited for; matrix products, arithmetic and copies ran while one was open for 6% of the time, Pallas kernels for 12%

profile of v8, /device:TPU:0, one launch (start us, length us, event | category | flops | bytes accessed | tf_op | source)
XLA Modules:
  0.0 689.9 jit_solution(10734562112228732859)
XLA Ops:
  14.7 5.3 all-to-all-start
  20.1 13.2 %all_gather.15 = bf16[2,2048]{1,0:T(2,128)(2,1)S(1)} all-gather(bf16[2,256]{1,0:T(2,128)(2,1)S(1)} %pad_maximum_fusion.2), channel_id=1, replica_groups=mesh['rep'=4,'shard'=8] {'shard'}, dimensions={1}, use_global_device_ids=true | all-gather | bytes 9216 | tf_op jit(solution)/shard_map/all_gather | solution.py:561
  34.0 13.2 %all-to-all-done.x_ref.pos_ref = bf16[4,128,2176]{2,1,0:T(8,128)(2,1)} async-done(((bf16[4,128,2176]{2,1,0:T(8,128)(2,1)}), bf16[4,128,2176]{2,1,0:T(8,128)(2,1)}, u32[]{:S(2)}, u32[]{:S(2)}) %all-to-all-start) | async-done | bytes 2228256 | tf_op jit(solution)/shard_map/all_to_all | solution.py:43
  49.7 6.2 shard_map.203
  59.6 6.4 shard_map.204
  66.0 10.6 %all_to_all.20 = bf16[4,4,128,128]{3,2,1,0:T(8,128)(2,1)S(1)} all-to-all(bf16[4,4,128,128]{3,2,1,0:T(8,128)(2,1)} %get-tuple-element.69), channel_id=1, replica_groups=mesh['rep'=4,'shard'=8] {'rep'}, dimensions={0} | all-to-all | bytes 1048576 | tf_op jit(solution)/shard_map/all_to_all | solution.py:47
  80.6 27.8 %all_to_all.21.part_ref = bf16[4,128,2048]{2,1,0:T(8,128)(2,1)} all-to-all(bf16[4,128,2048]{2,1,0:T(8,128)(2,1)S(1)} %bitcast.62), channel_id=1, replica_groups=mesh['rep'=4,'shard'=8] {'rep'}, dimensions={0} | all-to-all | bytes 4194304 | tf_op jit(solution)/shard_map/all_to_all | solution.py:47
  112.7 3.4 split_pair.1
  118.7 5.6 collective-permute-start.2
  128.8 10.4 %collective-permute-done.2.refs_2_ = bf16[2,64,704]{2,1,0:T(8,128)(2,1)S(1)} collective-permute-done((bf16[2,64,704]{2,1,0:T(8,128)(2,1)}, bf16[2,64,704]{2,1,0:T(8,128)(2,1)S(1)}, u32[]{:S(2)}, u32[]{:S(2)}) %collective-permute-start.2) | collective-permute-done | bytes 180256 | tf_op jit(solution)/shard_map/ppermute | solution.py:55
  139.7 8.8 %collective-permute-done.3.refs_3_ = bf16[2,64,704]{2,1,0:T(8,128)(2,1)S(1)} collective-permute-done((bf16[2,64,704]{2,1,0:T(8,128)(2,1)}, bf16[2,64,704]{2,1,0:T(8,128)(2,1)S(1)}, u32[]{:S(2)}, u32[]{:S(2)}) %collective-permute-start.3) | collective-permute-done | bytes 180256 | tf_op jit(solution)/shard_map/ppermute | solution.py:55
  150.4 9.4 %collective-permute-done.6.refs_6_ = bf16[2,64,704]{2,1,0:T(8,128)(2,1)S(1)} collective-permute-done((bf16[2,64,704]{2,1,0:T(8,128)(2,1)}, bf16[2,64,704]{2,1,0:T(8,128)(2,1)S(1)}, u32[]{:S(2)}, u32[]{:S(2)}) %collective-permute-start.6) | collective-permute-done | bytes 180256 | tf_op jit(solution)/shard_map/ppermute | solution.py:55
  159.9 7.0 %collective-permute-done.7.refs_7_ = bf16[2,64,704]{2,1,0:T(8,128)(2,1)S(1)} collective-permute-done((bf16[2,64,704]{2,1,0:T(8,128)(2,1)}, bf16[2,64,704]{2,1,0:T(8,128)(2,1)S(1)}, u32[]{:S(2)}, u32[]{:S(2)}) %collective-permute-start.7) | collective-permute-done | bytes 180256 | tf_op jit(solution)/shard_map/ppermute | solution.py:55
  174.3 16.6 %collective-permute-done.8.refs_2_ = bf16[8,64,704]{2,1,0:T(8,128)(2,1)S(1)} collective-permute-done((bf16[8,64,704]{2,1,0:T(8,128)(2,1)}, bf16[8,64,704]{2,1,0:T(8,128)(2,1)S(1)}, u32[]{:S(2)}, u32[]{:S(2)}) %collective-permute-start.8) | collective-permute-done | bytes 720928 | tf_op jit(solution)/shard_map/ppermute | solution.py:55
  192.9 14.8 %collective-permute-done.9.refs_3_ = bf16[8,64,704]{2,1,0:T(8,128)(2,1)S(1)} collective-permute-done((bf16[8,64,704]{2,1,0:T(8,128)(2,1)}, bf16[8,64,704]{2,1,0:T(8,128)(2,1)S(1)}, u32[]{:S(2)}, u32[]{:S(2)}) %collective-permute-start.9) | collective-permute-done | bytes 720928 | tf_op jit(solution)/shard_map/ppermute | solution.py:55
  207.9 16.6 %collective-permute-done.12.refs_6_ = bf16[8,64,704]{2,1,0:T(8,128)(2,1)S(1)} collective-permute-done((bf16[8,64,704]{2,1,0:T(8,128)(2,1)S(1)}, bf16[8,64,704]{2,1,0:T(8,128)(2,1)S(1)}, u32[]{:S(2)}, u32[]{:S(2)}) %collective-permute-start.12) | collective-permute-done | bytes 720928 | tf_op jit(solution)/shard_map/ppermute | solution.py:55
  226.3 5.8 shard_map.207
  232.1 7.3 %fusion.7.back_ref = f32[1024,704]{1,0:T(8,128)} fusion(bf16[1024,2048]{1,0:T(8,128)(2,1)} %all-gather.11.cloned.1.call-done, bf16[704,2048]{1,0:T(8,128)(2,1)S(1)} %copy-done), kind=kOutput, calls=%fused_computation.50 | convolution fusion | flops 2952790016 | bytes 9961472 | tf_op jit(solution)/shard_map/dot_general | solution.py:26
  239.4 12.1 %shard_map.208 = (bf16[1024,704]{1,0:T(8,128)(2,1)}, bf16[1024,704]{1,0:T(8,128)(2,1)}, bf16[1024,704]{1,0:T(8,128)(2,1)}) custom-call(bf16[1024,2048]{1,0:T(8,128)(2,1)} %all-gather.9.cloned.1.call-done.x_ref, f32[1024,704]{1,0:T(8,128)} %fusion.7.back_ref, bf16[2,2048,704]{2,1,0:T(8,128)(2,1)} %bitcast.53), custom_call_target="tpu_custom_call" | custom-call | tf_op jit(solution)/shard_map/pallas_call | solution.py:634
  251.5 8.1 %shard_map.209 = (bf16[8,64,704]{2,1,0:T(8,128)(2,1)}, bf16[8,64,704]{2,1,0:T(8,128)(2,1)}, bf16[8,64,704]{2,1,0:T(8,128)(2,1)}, bf16[8,64,704]{2,1,0:T(8,128)(2,1)}) custom-call(s32[2]{0:T(128)} %pad_add_fusion.id_ref, bf16[1024,2048]{1,0:T(8,128)(2,1)} %all-gather.9.cloned.1.call-done.x_ref, bf16[1024,704]{1,0:T(8,128)(2,1)} %get-tuple-element.88.grad_ref.gate_ref), custom_call_target="tpu_custom_call" | custom-call | tf_op jit(solution)/shard_map/pallas_call | solution.py:254
  259.7 11.4 %shard_map.210 = bf16[1024,2048]{1,0:T(8,128)(2,1)} custom-call(bf16[1024,704]{1,0:T(8,128)(2,1)} %get-tuple-element.88.grad_ref.gate_ref, bf16[1024,704]{1,0:T(8,128)(2,1)} %get-tuple-element.89.up_ref.grad_ref, bf16[2,2048,704]{2,1,0:T(8,128)(2,1)} %bitcast.54), custom_call_target="tpu_custom_call" | custom-call | tf_op jit(solution)/shard_map/pallas_call | solution.py:643
  271.7 65.2 %reduce-scatter.7.cloned.1.call-done.grad_ref = bf16[128,2048]{1,0:T(8,128)(2,1)} async-done(((bf16[1024,2048]{1,0:T(8,128)(2,1)}), bf16[128,2048]{1,0:T(8,128)(2,1)}) %reduce-scatter.7.cloned.1.call-update) | async-done | bytes 524304 | tf_op jit(solution)/shard_map/reduce_scatter | solution.py:651
  336.9 3.6 shard_map.212
  343.4 9.1 %collective-permute-done.14.refs_1_ = bf16[128,2048]{1,0:T(8,128)(2,1)S(1)} collective-permute-done((bf16[128,2048]{1,0:T(8,128)(2,1)}, bf16[128,2048]{1,0:T(8,128)(2,1)S(1)}, u32[]{:S(2)}, u32[]{:S(2)}) %collective-permute-start.14) | collective-permute-done | bytes 524320 | tf_op jit(solution)/shard_map/ppermute | solution.py:55
  355.6 3.7 collective-permute-done.16.refs_3_
  371.0 10.2 %all_to_all.22 = bf16[4,512,128]{2,1,0:T(8,128)(2,1)} all-to-all(bf16[4,512,128]{2,1,0:T(8,128)(2,1)S(1)} %bitcast_bitcast_fusion), channel_id=1, replica_groups=mesh['rep'=4,'shard'=8] {'rep'}, dimensions={0} | all-to-all | bytes 1048576 | tf_op jit(solution)/shard_map/all_to_all | solution.py:47
  381.2 8.2 %shard_map.214 = (bf16[4,128,512]{2,1,0:T(8,128)(2,1)}, f32[4,192,128]{2,1,0:T(8,128)}) custom-call(bf16[4,4,128,128]{3,2,1,0:T(8,128)(2,1)} %bitcast.58, f32[4,8,128,192]{3,2,1,0:T(8,128)} %get-tuple-element.94.probs_ref, bf16[4,128,512]{2,1,0:T(8,128)(2,1)} %get-tuple-element.67.q_ref, bf16[4,128,128]{2,1,0:T(8,128)(2,1)} %get-tuple-element.68.own_ref, ...), custom_call_target="tpu_custom_call" | custom-call | tf_op jit(solution)/shard_map/pallas_call | solution.py:713
  394.3 13.7 %attn_in_back.1 = (bf16[4,128,2048]{2,1,0:T(8,128)(2,1)}, bf16[2048,768]{1,0:T(8,128)(2,1)}) custom-call(s32[2]{0:T(128)} %pad_add_fusion.id_ref, bf16[4,128,512]{2,1,0:T(8,128)(2,1)} %get-tuple-element.95.dq_ref, f32[4,192,128]{2,1,0:T(8,128)} %get-tuple-element.96.dkv_ref, f32[4,64,128]{2,1,0:T(8,128)} %copy-done.42, ...), custom_call_target="tpu_custom_call" | custom-call | tf_op jit(solution)/shard_map/attn_in_back/pallas_call | solution.py:738
  408.3 8.3 %shard_map.211 = (bf16[8,64,704]{2,1,0:T(8,128)(2,1)}, bf16[8,64,704]{2,1,0:T(8,128)(2,1)}, bf16[8,64,704]{2,1,0:T(8,128)(2,1)}, bf16[8,64,704]{2,1,0:T(8,128)(2,1)}) custom-call(s32[2]{0:T(128)} %pad_add_fusion.id_ref, bf16[1024,2048]{1,0:T(8,128)(2,1)} %all-gather.9.cloned.1.call-done.x_ref, bf16[1024,704]{1,0:T(8,128)(2,1)} %get-tuple-element.89.up_ref.grad_ref), custom_call_target="tpu_custom_call" | custom-call | tf_op jit(solution)/shard_map/pallas_call | solution.py:254
  416.6 5.0 convolution_convert_fusion
  421.6 5.9 convolution_convert_fusion.1
  439.1 30.0 %collective-permute-done.52 = bf16[96,2048]{1,0:T(8,128)(2,1)S(1)} collective-permute-done((bf16[96,2048]{1,0:T(8,128)(2,1)S(1)}, bf16[96,2048]{1,0:T(8,128)(2,1)S(1)}, u32[]{:S(2)}, u32[]{:S(2)}) %collective-permute-start.52) | collective-permute-done | bytes 393248 | tf_op jit(solution)/shard_map/ppermute | solution.py:55
  478.8 5.8 collective-permute-done.56
  485.8 4.9 collective-permute-done.53
  493.7 13.9 %collective-permute-done.34.refs_2_ = bf16[8,64,704]{2,1,0:T(8,128)(2,1)} collective-permute-done((bf16[8,64,704]{2,1,0:T(8,128)(2,1)S(1)}, bf16[8,64,704]{2,1,0:T(8,128)(2,1)}, u32[]{:S(2)}, u32[]{:S(2)}) %collective-permute-start.34) | collective-permute-done | bytes 720928 | tf_op jit(solution)/shard_map/ppermute | solution.py:55
  507.6 3.9 shard_map.218
  511.5 17.7 %collective-permute-start.38 = (bf16[2,64,704]{2,1,0:T(8,128)(2,1)}, bf16[2,64,704]{2,1,0:T(8,128)(2,1)S(1)}, u32[]{:S(2)}, u32[]{:S(2)}) collective-permute-start(bf16[2,64,704]{2,1,0:T(8,128)(2,1)} %get-tuple-element.114), channel_id=1, source_target_pairs={{0,1},{1,0},{2,3},{3,2},{4,5},{5,4},{6,7},{7,6},{8,9},{9,8},{10,11... | collective-permute-start | bytes 540680 | tf_op jit(solution)/shard_map/ppermute | solution.py:55
  529.2 11.9 %collective-permute-start.39 = (bf16[2,64,704]{2,1,0:T(8,128)(2,1)}, bf16[2,64,704]{2,1,0:T(8,128)(2,1)S(1)}, u32[]{:S(2)}, u32[]{:S(2)}) collective-permute-start(bf16[2,64,704]{2,1,0:T(8,128)(2,1)} %get-tuple-element.115), channel_id=1, source_target_pairs={{0,2},{1,3},{2,0},{3,1},{4,6},{5,7},{6,4},{7,5},{8,10},{9,11},{10,... | collective-permute-start | bytes 540680 | tf_op jit(solution)/shard_map/ppermute | solution.py:55
  543.7 8.4 %collective-permute-done.39.refs_2_ = bf16[2,64,704]{2,1,0:T(8,128)(2,1)S(1)} collective-permute-done((bf16[2,64,704]{2,1,0:T(8,128)(2,1)}, bf16[2,64,704]{2,1,0:T(8,128)(2,1)S(1)}, u32[]{:S(2)}, u32[]{:S(2)}) %collective-permute-start.39) | collective-permute-done | bytes 180256 | tf_op jit(solution)/shard_map/ppermute | solution.py:55
  556.9 10.6 %collective-permute-done.41.refs_4_ = bf16[2,64,704]{2,1,0:T(8,128)(2,1)} collective-permute-done((bf16[2,64,704]{2,1,0:T(8,128)(2,1)}, bf16[2,64,704]{2,1,0:T(8,128)(2,1)}, u32[]{:S(2)}, u32[]{:S(2)}) %collective-permute-start.41) | collective-permute-done | bytes 180256 | tf_op jit(solution)/shard_map/ppermute | solution.py:55
  585.8 8.7 %collective-permute-done.45.refs_1_ = bf16[64,5632]{1,0:T(8,128)(2,1)} collective-permute-done((bf16[64,5632]{1,0:T(8,128)(2,1)}, bf16[64,5632]{1,0:T(8,128)(2,1)}, u32[]{:S(2)}, u32[]{:S(2)}) %collective-permute-start.45) | collective-permute-done | bytes 720928 | tf_op jit(solution)/shard_map/ppermute | solution.py:55
  609.0 11.3 %collective-permute-done.46.refs_2_ = bf16[64,5632]{1,0:T(8,128)(2,1)} collective-permute-done((bf16[64,5632]{1,0:T(8,128)(2,1)}, bf16[64,5632]{1,0:T(8,128)(2,1)}, u32[]{:S(2)}, u32[]{:S(2)}) %collective-permute-start.46) | collective-permute-done | bytes 720928 | tf_op jit(solution)/shard_map/ppermute | solution.py:55
  623.0 12.7 %collective-permute-done.47.refs_3_ = bf16[64,5632]{1,0:T(8,128)(2,1)} collective-permute-done((bf16[64,5632]{1,0:T(8,128)(2,1)}, bf16[64,5632]{1,0:T(8,128)(2,1)}, u32[]{:S(2)}, u32[]{:S(2)}) %collective-permute-start.47) | collective-permute-done | bytes 720928 | tf_op jit(solution)/shard_map/ppermute | solution.py:55
  639.9 4.6 shard_map.222
  644.6 4.6 shard_map.220
  649.2 4.9 shard_map.221
  662.0 3.5 shard_map.215
  669.8 8.2 %collective-permute-done.27.refs_3_ = bf16[256,768]{1,0:T(8,128)(2,1)} collective-permute-done((bf16[256,768]{1,0:T(8,128)(2,1)}, bf16[256,768]{1,0:T(8,128)(2,1)}, u32[]{:S(2)}, u32[]{:S(2)}) %collective-permute-start.27) | collective-permute-done | bytes 393248 | tf_op jit(solution)/shard_map/ppermute | solution.py:55
  (275 shorter events, 156.4 us)
Async XLA Ops:
  7.2 42.5 %all-gather.5.cloned.1.call-start = ((), (), s32[]{:S(2)}) async-start(), calls=%async_computation.8 | async-start | bytes 2949120 | tf_op jit(solution)/shard_map/all_gather | solution.py:556
  10.2 67.3 %all-gather.7.cloned.1.call-start = ((), (), s32[]{:S(2)}) async-start(), calls=%async_computation.9 | async-start | bytes 2359296 | tf_op jit(solution)/shard_map/all_gather | solution.py:557
  12.0 220.1 %all-gather.11.cloned.1.call-start = ((), (), s32[]{:S(2)}) async-start(), calls=%async_computation.11 | async-start | bytes 4718592 | tf_op jit(solution)/shard_map/all_gather | solution.py:582
  14.7 32.5 %all-to-all-start = ((bf16[4,128,2176]{2,1,0:T(8,128)(2,1)}), bf16[4,128,2176]{2,1,0:T(8,128)(2,1)}, u32[]{:S(2)}, u32[]{:S(2)}) async-start(bf16[4,128,2176]{2,1,0:T(8,128)(2,1)} %broadcast_in_dim.16), calls=%async_computation | async-start | bytes 4456448 | tf_op jit(solution)/shard_map/all_to_all | solution.py:43
  20.1 219.4 %all-gather.9.cloned.1.call-start = ((), (), s32[]{:S(2)}) async-start(), calls=%async_computation.10 | async-start | bytes 4718592 | tf_op jit(solution)/shard_map/all_gather | solution.py:628
  111.8 225.1 %reduce-scatter.7.cloned.1.call-start = ((), (), s32[]{:S(2)}) async-start(), calls=%async_computation.13 | async-start | bytes 4718592 | tf_op jit(solution)/shard_map/reduce_scatter | solution.py:651
  118.7 20.6 %collective-permute-start.2 = (bf16[2,64,704]{2,1,0:T(8,128)(2,1)}, bf16[2,64,704]{2,1,0:T(8,128)(2,1)S(1)}, u32[]{:S(2)}, u32[]{:S(2)}) collective-permute-start(bf16[2,64,704]{2,1,0:T(8,128)(2,1)} %get-tuple-element.76), channel_id=1, source_target_pairs={{0,2},{1,3},{2,0},{3,1},{4,6},{5,7},{6,4},{7,5},{8,10},{9,11},{10,... | collective-permute-start | bytes 540680 | tf_op jit(solution)/shard_map/ppermute | solution.py:55
  124.3 24.2 %collective-permute-start.3 = (bf16[2,64,704]{2,1,0:T(8,128)(2,1)}, bf16[2,64,704]{2,1,0:T(8,128)(2,1)S(1)}, u32[]{:S(2)}, u32[]{:S(2)}) collective-permute-start(bf16[2,64,704]{2,1,0:T(8,128)(2,1)} %get-tuple-element.77), channel_id=1, source_target_pairs={{0,3},{1,2},{2,1},{3,0},{4,7},{5,6},{6,5},{7,4},{8,11},{9,10},{10,... | collective-permute-start | bytes 540680 | tf_op jit(solution)/shard_map/ppermute | solution.py:55
  124.4 24.1 %collective-permute-start.4 = (bf16[2,64,704]{2,1,0:T(8,128)(2,1)}, bf16[2,64,704]{2,1,0:T(8,128)(2,1)S(1)}, u32[]{:S(2)}, u32[]{:S(2)}) collective-permute-start(bf16[2,64,704]{2,1,0:T(8,128)(2,1)} %get-tuple-element.78), channel_id=1, source_target_pairs={{0,4},{1,5},{2,6},{3,7},{4,0},{5,1},{6,2},{7,3},{8,12},{9,13},{10,... | collective-permute-start | bytes 540680 | tf_op jit(solution)/shard_map/ppermute | solution.py:55
  126.8 23.7 %collective-permute-start.5 = (bf16[2,64,704]{2,1,0:T(8,128)(2,1)}, bf16[2,64,704]{2,1,0:T(8,128)(2,1)S(1)}, u32[]{:S(2)}, u32[]{:S(2)}) collective-permute-start(bf16[2,64,704]{2,1,0:T(8,128)(2,1)} %get-tuple-element.79), channel_id=1, source_target_pairs={{0,5},{1,4},{2,7},{3,6},{4,1},{5,0},{6,3},{7,2},{8,13},{9,12},{10,... | collective-permute-start | bytes 540680 | tf_op jit(solution)/shard_map/ppermute | solution.py:55
  126.8 33.1 %collective-permute-start.6 = (bf16[2,64,704]{2,1,0:T(8,128)(2,1)}, bf16[2,64,704]{2,1,0:T(8,128)(2,1)S(1)}, u32[]{:S(2)}, u32[]{:S(2)}) collective-permute-start(bf16[2,64,704]{2,1,0:T(8,128)(2,1)} %get-tuple-element.80), channel_id=1, source_target_pairs={{0,6},{1,7},{2,4},{3,5},{4,2},{5,3},{6,0},{7,1},{8,14},{9,15},{10,... | collective-permute-start | bytes 540680 | tf_op jit(solution)/shard_map/ppermute | solution.py:55
  139.2 27.6 %collective-permute-start.7 = (bf16[2,64,704]{2,1,0:T(8,128)(2,1)}, bf16[2,64,704]{2,1,0:T(8,128)(2,1)S(1)}, u32[]{:S(2)}, u32[]{:S(2)}) collective-permute-start(bf16[2,64,704]{2,1,0:T(8,128)(2,1)} %get-tuple-element.81), channel_id=1, source_target_pairs={{0,7},{1,6},{2,5},{3,4},{4,3},{5,2},{6,1},{7,0},{8,15},{9,14},{10,... | collective-permute-start | bytes 540680 | tf_op jit(solution)/shard_map/ppermute | solution.py:55
  170.2 20.6 %collective-permute-start.8 = (bf16[8,64,704]{2,1,0:T(8,128)(2,1)}, bf16[8,64,704]{2,1,0:T(8,128)(2,1)S(1)}, u32[]{:S(2)}, u32[]{:S(2)}) collective-permute-start(bf16[8,64,704]{2,1,0:T(8,128)(2,1)} %get-tuple-element.82.refs_0_), channel_id=1, source_target_pairs={{0,8},{8,0},{16,24},{24,16},{1,9},{9,1},{17,25},{25,17},{2,10},{10... | collective-permute-start | bytes 2162696 | tf_op jit(solution)/shard_map/ppermute | solution.py:55
  170.4 20.6 %collective-permute-start.11 = (bf16[8,64,704]{2,1,0:T(8,128)(2,1)}, bf16[8,64,704]{2,1,0:T(8,128)(2,1)S(1)}, u32[]{:S(2)}, u32[]{:S(2)}) collective-permute-start(bf16[8,64,704]{2,1,0:T(8,128)(2,1)} %get-tuple-element.83.refs_1_), channel_id=1, source_target_pairs={{0,16},{8,24},{16,0},{24,8},{1,17},{9,25},{17,1},{25,9},{2,18},{10... | collective-permute-start | bytes 2162696 | tf_op jit(solution)/shard_map/ppermute | solution.py:55
  170.4 37.3 %collective-permute-start.9 = (bf16[8,64,704]{2,1,0:T(8,128)(2,1)}, bf16[8,64,704]{2,1,0:T(8,128)(2,1)S(1)}, u32[]{:S(2)}, u32[]{:S(2)}) collective-permute-start(bf16[8,64,704]{2,1,0:T(8,128)(2,1)} %get-tuple-element.83.refs_1_), channel_id=1, source_target_pairs={{0,8},{8,0},{16,24},{24,16},{1,9},{9,1},{17,25},{25,17},{2,10},{10... | collective-permute-start | bytes 2162696 | tf_op jit(solution)/shard_map/ppermute | solution.py:55
  172.4 35.5 %collective-permute-start.10 = (bf16[8,64,704]{2,1,0:T(8,128)(2,1)}, bf16[8,64,704]{2,1,0:T(8,128)(2,1)S(1)}, u32[]{:S(2)}, u32[]{:S(2)}) collective-permute-start(bf16[8,64,704]{2,1,0:T(8,128)(2,1)} %get-tuple-element.82.refs_0_), channel_id=1, source_target_pairs={{0,16},{8,24},{16,0},{24,8},{1,17},{9,25},{17,1},{25,9},{2,18},{10... | collective-permute-start | bytes 2162696 | tf_op jit(solution)/shard_map/ppermute | solution.py:55
  190.9 33.7 %collective-permute-start.12 = (bf16[8,64,704]{2,1,0:T(8,128)(2,1)S(1)}, bf16[8,64,704]{2,1,0:T(8,128)(2,1)S(1)}, u32[]{:S(2)}, u32[]{:S(2)}) collective-permute-start(bf16[8,64,704]{2,1,0:T(8,128)(2,1)S(1)} %collective-permute-done.8.refs_2_), channel_id=1, source_target_pairs={{0,16},{8,24},{16,0},{24,8},{1,17},{9,25},{17,1},{25,9},{2,18},{10... | collective-permute-start | bytes 2162696 | tf_op jit(solution)/shard_map/ppermute | solution.py:55
  191.0 33.5 %collective-permute-start.13 = (bf16[8,64,704]{2,1,0:T(8,128)(2,1)S(1)}, bf16[8,64,704]{2,1,0:T(8,128)(2,1)S(1)}, u32[]{:S(2)}, u32[]{:S(2)}) collective-permute-start(bf16[8,64,704]{2,1,0:T(8,128)(2,1)S(1)} %collective-permute-done.11.refs_5_), channel_id=1, source_target_pairs={{0,8},{8,0},{16,24},{24,16},{1,9},{9,1},{17,25},{25,17},{2,10},{10... | collective-permute-start | bytes 2162696 | tf_op jit(solution)/shard_map/ppermute | solution.py:55
  271.1 335.8 %reduce-scatter.11.cloned.1.call-start = ((), (), s32[]{:S(2)}) async-start(), calls=%async_computation.15 | async-start | bytes 2359296 | tf_op jit(solution)/shard_map/reduce_scatter | solution.py:711
  370.9 285.4 %reduce-scatter.9.cloned.1.call-start = ((), (), s32[]{:S(2)}) async-start(), calls=%async_computation.14 | async-start | bytes 3538944 | tf_op jit(solution)/shard_map/reduce_scatter | solution.py:769
  408.1 251.7 %reduce-scatter.5.cloned.1.call-start = ((), (), s32[]{:S(2)}) async-start(), calls=%async_computation.12 | async-start | bytes 4718592 | tf_op jit(solution)/shard_map/reduce_scatter | solution.py:673
  430.8 62.3 %collective-permute-start.32 = (bf16[8,64,704]{2,1,0:T(8,128)(2,1)}, bf16[8,64,704]{2,1,0:T(8,128)(2,1)S(1)}, u32[]{:S(2)}, u32[]{:S(2)}) collective-permute-start(bf16[8,64,704]{2,1,0:T(8,128)(2,1)} %get-tuple-element.107), channel_id=1, source_target_pairs={{0,8},{8,0},{16,24},{24,16},{1,9},{9,1},{17,25},{25,17},{2,10},{10... | collective-permute-start | bytes 2162696 | tf_op jit(solution)/shard_map/ppermute | solution.py:55
  431.2 40.2 %collective-permute-start.33 = (bf16[8,64,704]{2,1,0:T(8,128)(2,1)}, bf16[8,64,704]{2,1,0:T(8,128)(2,1)S(1)}, u32[]{:S(2)}, u32[]{:S(2)}) collective-permute-start(bf16[8,64,704]{2,1,0:T(8,128)(2,1)} %get-tuple-element.109), channel_id=1, source_target_pairs={{0,8},{8,0},{16,24},{24,16},{1,9},{9,1},{17,25},{25,17},{2,10},{10... | collective-permute-start | bytes 2162696 | tf_op jit(solution)/shard_map/ppermute | solution.py:55
  432.8 39.4 %collective-permute-start.36 = (bf16[8,64,704]{2,1,0:T(8,128)(2,1)}, bf16[8,64,704]{2,1,0:T(8,128)(2,1)S(1)}, u32[]{:S(2)}, u32[]{:S(2)}) collective-permute-start(bf16[8,64,704]{2,1,0:T(8,128)(2,1)} %get-tuple-element.112), channel_id=1, source_target_pairs={{0,16},{8,24},{16,0},{24,8},{1,17},{9,25},{17,1},{25,9},{2,18},{10... | collective-permute-start | bytes 2162696 | tf_op jit(solution)/shard_map/ppermute | solution.py:55
  435.1 34.0 %collective-permute-start.52 = (bf16[96,2048]{1,0:T(8,128)(2,1)S(1)}, bf16[96,2048]{1,0:T(8,128)(2,1)S(1)}, u32[]{:S(2)}, u32[]{:S(2)}) collective-permute-start(bf16[96,2048]{1,0:T(8,128)(2,1)S(1)} %get-tuple-element.128), channel_id=1, source_target_pairs={{0,8},{8,0},{16,24},{24,16},{1,9},{9,1},{17,25},{25,17},{2,10},{10... | collective-permute-start | bytes 1179656 | tf_op jit(solution)/shard_map/ppermute | solution.py:55
  437.2 40.4 %collective-permute-start.51 = (bf16[96,2048]{1,0:T(8,128)(2,1)S(1)}, bf16[96,2048]{1,0:T(8,128)(2,1)S(1)}, u32[]{:S(2)}, u32[]{:S(2)}) collective-permute-start(bf16[96,2048]{1,0:T(8,128)(2,1)S(1)} %get-tuple-element.127), channel_id=1, source_target_pairs={{0,8},{8,0},{16,24},{24,16},{1,9},{9,1},{17,25},{25,17},{2,10},{10... | collective-permute-start | bytes 1179656 | tf_op jit(solution)/shard_map/ppermute | solution.py:55
  472.3 21.5 %collective-permute-start.35 = (bf16[8,64,704]{2,1,0:T(8,128)(2,1)S(1)}, bf16[8,64,704]{2,1,0:T(8,128)(2,1)S(1)}, u32[]{:S(2)}, u32[]{:S(2)}) collective-permute-start(bf16[8,64,704]{2,1,0:T(8,128)(2,1)S(1)} %copy-done.46), channel_id=1, source_target_pairs={{0,16},{8,24},{16,0},{24,8},{1,17},{9,25},{17,1},{25,9},{2,18},{10... | collective-permute-start | bytes 2162696 | tf_op jit(solution)/shard_map/ppermute | solution.py:55
  477.6 30.0 %collective-permute-start.34 = (bf16[8,64,704]{2,1,0:T(8,128)(2,1)S(1)}, bf16[8,64,704]{2,1,0:T(8,128)(2,1)}, u32[]{:S(2)}, u32[]{:S(2)}) collective-permute-start(bf16[8,64,704]{2,1,0:T(8,128)(2,1)S(1)} %add_convert_fusion.1), channel_id=1, source_target_pairs={{0,16},{8,24},{16,0},{24,8},{1,17},{9,25},{17,1},{25,9},{2,18},{10... | collective-permute-start | bytes 2162696 | tf_op jit(solution)/shard_map/ppermute | solution.py:55
  484.6 23.0 %collective-permute-start.37 = (bf16[8,64,704]{2,1,0:T(8,128)(2,1)S(1)}, bf16[8,64,704]{2,1,0:T(8,128)(2,1)}, u32[]{:S(2)}, u32[]{:S(2)}) collective-permute-start(bf16[8,64,704]{2,1,0:T(8,128)(2,1)S(1)} %add_convert_fusion), channel_id=1, source_target_pairs={{0,8},{8,0},{16,24},{24,16},{1,9},{9,1},{17,25},{25,17},{2,10},{10... | collective-permute-start | bytes 2162696 | tf_op jit(solution)/shard_map/ppermute | solution.py:55
  490.6 50.4 %collective-permute-start.60 = (bf16[80,2048]{1,0:T(8,128)(2,1)S(1)}, bf16[80,2048]{1,0:T(8,128)(2,1)S(1)}, u32[]{:S(2)}, u32[]{:S(2)}) collective-permute-start(bf16[80,2048]{1,0:T(8,128)(2,1)S(1)} %add_convert_fusion.5.refs_1_), channel_id=1, source_target_pairs={{0,16},{8,24},{16,0},{24,8},{1,17},{9,25},{17,1},{25,9},{2,18},{10... | collective-permute-start | bytes 983048 | tf_op jit(solution)/shard_map/ppermute | solution.py:55
  493.1 48.5 %collective-permute-start.57 = (bf16[96,2048]{1,0:T(8,128)(2,1)S(1)}, bf16[96,2048]{1,0:T(8,128)(2,1)S(1)}, u32[]{:S(2)}, u32[]{:S(2)}) collective-permute-start(bf16[96,2048]{1,0:T(8,128)(2,1)S(1)} %add_convert_fusion.3.refs_0_), channel_id=1, source_target_pairs={{0,8},{8,0},{16,24},{24,16},{1,9},{9,1},{17,25},{25,17},{2,10},{10... | collective-permute-start | bytes 1179656 | tf_op jit(solution)/shard_map/ppermute | solution.py:55
  511.5 30.2 %collective-permute-start.38 = (bf16[2,64,704]{2,1,0:T(8,128)(2,1)}, bf16[2,64,704]{2,1,0:T(8,128)(2,1)S(1)}, u32[]{:S(2)}, u32[]{:S(2)}) collective-permute-start(bf16[2,64,704]{2,1,0:T(8,128)(2,1)} %get-tuple-element.114), channel_id=1, source_target_pairs={{0,1},{1,0},{2,3},{3,2},{4,5},{5,4},{6,7},{7,6},{8,9},{9,8},{10,11... | collective-permute-start | bytes 540680 | tf_op jit(solution)/shard_map/ppermute | solution.py:55
  529.2 23.0 %collective-permute-start.39 = (bf16[2,64,704]{2,1,0:T(8,128)(2,1)}, bf16[2,64,704]{2,1,0:T(8,128)(2,1)S(1)}, u32[]{:S(2)}, u32[]{:S(2)}) collective-permute-start(bf16[2,64,704]{2,1,0:T(8,128)(2,1)} %get-tuple-element.115), channel_id=1, source_target_pairs={{0,2},{1,3},{2,0},{3,1},{4,6},{5,7},{6,4},{7,5},{8,10},{9,11},{10,... | collective-permute-start | bytes 540680 | tf_op jit(solution)/shard_map/ppermute | solution.py:55
  541.1 34.8 %collective-permute-start.58 = (bf16[80,2048]{1,0:T(8,128)(2,1)S(1)}, bf16[80,2048]{1,0:T(8,128)(2,1)S(1)}, u32[]{:S(2)}, u32[]{:S(2)}) collective-permute-start(bf16[80,2048]{1,0:T(8,128)(2,1)S(1)} %add_convert_fusion.5.refs_1_), channel_id=1, source_target_pairs={{0,8},{8,0},{16,24},{24,16},{1,9},{9,1},{17,25},{25,17},{2,10},{10... | collective-permute-start | bytes 983048 | tf_op jit(solution)/shard_map/ppermute | solution.py:55
  541.7 25.8 %collective-permute-start.41 = (bf16[2,64,704]{2,1,0:T(8,128)(2,1)}, bf16[2,64,704]{2,1,0:T(8,128)(2,1)}, u32[]{:S(2)}, u32[]{:S(2)}) collective-permute-start(bf16[2,64,704]{2,1,0:T(8,128)(2,1)} %get-tuple-element.117), channel_id=1, source_target_pairs={{0,4},{1,5},{2,6},{3,7},{4,0},{5,1},{6,2},{7,3},{8,12},{9,13},{10,... | collective-permute-start | bytes 540680 | tf_op jit(solution)/shard_map/ppermute | solution.py:55
  541.7 27.7 %collective-permute-start.42 = (bf16[2,64,704]{2,1,0:T(8,128)(2,1)}, bf16[2,64,704]{2,1,0:T(8,128)(2,1)S(1)}, u32[]{:S(2)}, u32[]{:S(2)}) collective-permute-start(bf16[2,64,704]{2,1,0:T(8,128)(2,1)} %get-tuple-element.118), channel_id=1, source_target_pairs={{0,5},{1,4},{2,7},{3,6},{4,1},{5,0},{6,3},{7,2},{8,13},{9,12},{10,... | collective-permute-start | bytes 540680 | tf_op jit(solution)/shard_map/ppermute | solution.py:55
  575.9 23.4 %collective-permute-start.49 = (bf16[64,5632]{1,0:T(8,128)(2,1)}, bf16[64,5632]{1,0:T(8,128)(2,1)}, u32[]{:S(2)}, u32[]{:S(2)}) collective-permute-start(bf16[64,5632]{1,0:T(8,128)(2,1)} %get-tuple-element.122.refs_0_), channel_id=1, source_target_pairs={{0,16},{8,24},{16,0},{24,8},{1,17},{9,25},{17,1},{25,9},{2,18},{10... | collective-permute-start | bytes 2162696 | tf_op jit(solution)/shard_map/ppermute | solution.py:55
  577.6 27.2 %collective-permute-start.23 = (bf16[64,2048]{1,0:T(8,128)(2,1)S(1)}, bf16[64,2048]{1,0:T(8,128)(2,1)S(1)}, u32[]{:S(2)}, u32[]{:S(2)}) collective-permute-start(bf16[64,2048]{1,0:T(8,128)(2,1)S(1)} %get-tuple-element.133), channel_id=1, source_target_pairs={{0,16},{8,24},{16,0},{24,8},{1,17},{9,25},{17,1},{25,9},{2,18},{10... | collective-permute-start | bytes 786440 | tf_op jit(solution)/shard_map/ppermute | solution.py:55
  579.0 27.9 %collective-permute-start.20 = (bf16[64,2048]{1,0:T(8,128)(2,1)S(1)}, bf16[64,2048]{1,0:T(8,128)(2,1)}, u32[]{:S(2)}, u32[]{:S(2)}) collective-permute-start(bf16[64,2048]{1,0:T(8,128)(2,1)S(1)} %get-tuple-element.136), channel_id=1, source_target_pairs={{0,8},{8,0},{16,24},{24,16},{1,9},{9,1},{17,25},{25,17},{2,10},{10... | collective-permute-start | bytes 786440 | tf_op jit(solution)/shard_map/ppermute | solution.py:55
  583.7 36.6 %collective-permute-start.46 = (bf16[64,5632]{1,0:T(8,128)(2,1)}, bf16[64,5632]{1,0:T(8,128)(2,1)}, u32[]{:S(2)}, u32[]{:S(2)}) collective-permute-start(bf16[64,5632]{1,0:T(8,128)(2,1)} %get-tuple-element.121.refs_0_), channel_id=1, source_target_pairs={{0,16},{8,24},{16,0},{24,8},{1,17},{9,25},{17,1},{25,9},{2,18},{10... | collective-permute-start | bytes 2162696 | tf_op jit(solution)/shard_map/ppermute | solution.py:55
  594.5 28.0 %collective-permute-start.48 = (bf16[64,5632]{1,0:T(8,128)(2,1)}, bf16[64,5632]{1,0:T(8,128)(2,1)}, u32[]{:S(2)}, u32[]{:S(2)}) collective-permute-start(bf16[64,5632]{1,0:T(8,128)(2,1)} %get-tuple-element.122.refs_0_), channel_id=1, source_target_pairs={{0,8},{8,0},{16,24},{24,16},{1,9},{9,1},{17,25},{25,17},{2,10},{10... | collective-permute-start | bytes 2162696 | tf_op jit(solution)/shard_map/ppermute | solution.py:55
  599.2 36.5 %collective-permute-start.47 = (bf16[64,5632]{1,0:T(8,128)(2,1)}, bf16[64,5632]{1,0:T(8,128)(2,1)}, u32[]{:S(2)}, u32[]{:S(2)}) collective-permute-start(bf16[64,5632]{1,0:T(8,128)(2,1)} %collective-permute-done.45.refs_1_), channel_id=1, source_target_pairs={{0,16},{8,24},{16,0},{24,8},{1,17},{9,25},{17,1},{25,9},{2,18},{10... | collective-permute-start | bytes 2162696 | tf_op jit(solution)/shard_map/ppermute | solution.py:55
  604.8 33.1 %collective-permute-start.50 = (bf16[64,5632]{1,0:T(8,128)(2,1)}, bf16[64,5632]{1,0:T(8,128)(2,1)}, u32[]{:S(2)}, u32[]{:S(2)}) collective-permute-start(bf16[64,5632]{1,0:T(8,128)(2,1)} %collective-permute-done.49.refs_2_), channel_id=1, source_target_pairs={{0,8},{8,0},{16,24},{24,16},{1,9},{9,1},{17,25},{25,17},{2,10},{10... | collective-permute-start | bytes 2162696 | tf_op jit(solution)/shard_map/ppermute | solution.py:55
  606.9 31.0 %collective-permute-start.28 = (bf16[64,2048]{1,0:T(8,128)(2,1)}, bf16[64,2048]{1,0:T(8,128)(2,1)S(1)}, u32[]{:S(2)}, u32[]{:S(2)}) collective-permute-start(bf16[64,2048]{1,0:T(8,128)(2,1)} %reduce-scatter.11.cloned.1.call-done.refs_0_), channel_id=1, source_target_pairs={{0,8},{8,0},{16,24},{24,16},{1,9},{9,1},{17,25},{25,17},{2,10},{10... | collective-permute-start | bytes 786440 | tf_op jit(solution)/shard_map/ppermute | solution.py:55
  620.3 33.8 %collective-permute-start.29 = (bf16[64,2048]{1,0:T(8,128)(2,1)}, bf16[64,2048]{1,0:T(8,128)(2,1)S(1)}, u32[]{:S(2)}, u32[]{:S(2)}) collective-permute-start(bf16[64,2048]{1,0:T(8,128)(2,1)} %reduce-scatter.11.cloned.1.call-done.refs_0_), channel_id=1, source_target_pairs={{0,16},{8,24},{16,0},{24,8},{1,17},{9,25},{17,1},{25,9},{2,18},{10... | collective-permute-start | bytes 786440 | tf_op jit(solution)/shard_map/ppermute | solution.py:55
  622.5 32.3 %collective-permute-start.19 = (bf16[64,2048]{1,0:T(8,128)(2,1)}, bf16[64,2048]{1,0:T(8,128)(2,1)}, u32[]{:S(2)}, u32[]{:S(2)}) collective-permute-start(bf16[64,2048]{1,0:T(8,128)(2,1)} %get-tuple-element.137), channel_id=1, source_target_pairs={{0,8},{8,0},{16,24},{24,16},{1,9},{9,1},{17,25},{25,17},{2,10},{10... | collective-permute-start | bytes 786440 | tf_op jit(solution)/shard_map/ppermute | solution.py:55
  635.8 20.5 %collective-permute-start.22 = (bf16[64,2048]{1,0:T(8,128)(2,1)}, bf16[64,2048]{1,0:T(8,128)(2,1)}, u32[]{:S(2)}, u32[]{:S(2)}) collective-permute-start(bf16[64,2048]{1,0:T(8,128)(2,1)} %get-tuple-element.134), channel_id=1, source_target_pairs={{0,16},{8,24},{16,0},{24,8},{1,17},{9,25},{17,1},{25,9},{2,18},{10... | collective-permute-start | bytes 786440 | tf_op jit(solution)/shard_map/ppermute | solution.py:55
  637.9 20.4 %collective-permute-start.24 = (bf16[64,2048]{1,0:T(8,128)(2,1)}, bf16[64,2048]{1,0:T(8,128)(2,1)}, u32[]{:S(2)}, u32[]{:S(2)}) collective-permute-start(bf16[64,2048]{1,0:T(8,128)(2,1)} %get-tuple-element.131), channel_id=1, source_target_pairs={{0,8},{8,0},{16,24},{24,16},{1,9},{9,1},{17,25},{25,17},{2,10},{10... | collective-permute-start | bytes 786440 | tf_op jit(solution)/shard_map/ppermute | solution.py:55
  (74 other events, 1369.6 us)
Sparse Core Ops, SparseCore 0:
  10.4 36.4 all-gather.4
  49.1 28.2 all-gather.6
  79.0 46.9 all-gather.10
  127.4 69.7 all-gather.8
  271.2 65.6 reduce-scatter.6
  371.0 36.9 reduce-scatter.10
  410.3 43.6 reduce-scatter.8
  456.2 49.1 reduce-scatter.4

commit v9 on v8

--- a/solution.py
+++ b/solution.py
@@ -79,6 +79,10 @@
     half = value.shape[0] // 2
     one, two = go(value, 1), go(value, 2)
     return [(value,), (one,), (two,), (go(one[:half], 2), go(two[half:], 1))]
+
+
+def gather_direct(value, count):
+    return [(value,)] + [(send(value, "rep", count, k),) for k in range(1, count)]
 
 
 def gather_rep(halves, count):
@@ -704,12 +708,8 @@
         [part for piece in branch for part in piece],
     ).reshape(all_rows, width)
     in_grad = cols_cols(branch_all, w_o).astype(BF)
-    branch_all, in_grad = lax.optimization_barrier((branch_all, in_grad))
     in_grad = in_grad.reshape(all_rows, n_rep, pair * fine).transpose(1, 0, 2)
     in_grad = swap(in_grad, "rep").reshape(n_rep, n_rep, rows, pair * fine)
-    w_o_grad = rows_rows(out_in, branch_all).astype(BF)
-    w_o_grad = lax.psum_scatter(w_o_grad, "shard", scatter_dimension=0, tiled=True)
-    o_out = place(gather_two(w_o_grad, n_rep), r)
     query_grad, kv_grad = call(
         partial(attend_back_kernel, fine),
         (shape((n_rep, rows, q_cols), BF), shape((n_rep, span, LANES), F32)),
@@ -766,7 +766,11 @@
         ids, query_grad, kv_grad, kv_back, cosine, sine, normed_one, x_all, gain_two_rows,
         w_qkv,
     )
+    branch_all, _ = lax.optimization_barrier((branch_all, w_qkv_grad))
     w_qkv_grad = lax.psum_scatter(w_qkv_grad, "shard", scatter_dimension=0, tiled=True)
+    w_o_grad = rows_rows(out_in, branch_all).astype(BF)
+    w_o_grad = lax.psum_scatter(w_o_grad, "shard", scatter_dimension=0, tiled=True)
+    o_out = place(gather_direct(w_o_grad, n_rep), r)
     one_grad = [one_grad_part[k] for k in range(n_rep)]
     one_grad = [(part[: rows // 2], part[rows // 2 :]) for part in one_grad]
     one_grad = parts_rep(one_grad, n_rep)
@@ -776,9 +780,7 @@
         shape((rows, width), BF),
         one_grad[0] + one_grad[1] + [tokens, gain_one, mid_grad],
     )
-    w_qkv_grad = [(w_qkv_grad,)] + [
-        (send(w_qkv_grad, "rep", n_rep, k),) for k in range(1, n_rep)
-    ]
+    w_qkv_grad = gather_direct(w_qkv_grad, n_rep)
     q_out, k_out, v_out, gain_sums = flat_call(
         partial(qkv_kernel, share, [len(piece) for piece in w_qkv_grad]),
         ids,

time: 697 us -> 707 us (1.014)
  starting transfers between devices: 109 us -> 85.4 us
  waiting for transfers between devices: 317 us -> 337 us
    ppermute x61 -> x60, starting transfers between devices: 99.8 us -> 77 us  [send(): return lax.ppermute(value, axis, pairs(count, step))]
    ppermute x61 -> x60, waiting for transfers between devices: 235 us -> 254 us  [send(): return lax.ppermute(value, axis, pairs(count, step))]
  transfers between devices with their start and end apart: 72 -> 71, of which waited for: 37 -> 35; matrix products, arithmetic and copies ran while one was open for 6% -> 6% of each run, Pallas kernels for 12% -> 9%
where the time goes in v9:
time: 707 us; the launch traced here: 694 us
  waiting for transfers between devices  337 us (48%)
  Pallas kernels  127 us (18%)
  starting transfers between devices  85.4 us (12%)
  blocking collectives  62 us (9%)
  matrix products  29.1 us (4%)
  local copies, waits for them, and re-layouts  23.2 us (3%)
  other arithmetic  15.7 us (2%)
  between operations  15 us (2%)
    ppermute x60, waiting for transfers between devices, send(): return lax.ppermute(value, axis, pairs(count, step))  254 us
    ppermute x60, starting transfers between devices, send(): return lax.ppermute(value, axis, pairs(count, step))  77 us
    reduce_scatter x1, waiting for transfers between devices, body(): lax.psum_scatter(two_grad_part, 'shard', scatter_dimension=0, tiled=True)  65.9 us
    all_to_all x3, blocking collectives, swap(): return lax.all_to_all(value, axis, split_axis=0, concat_axis=0, tiled=True)  48.8 us
    dot_general x6, matrix products, dot(): lax.dot_general(left, right, (contract, ((), ())), preferred_element_type...  29.1 us
    pallas_call x7, Pallas kernels, flat_call(): pl.pallas_call(kernel, out_shape=out_shape, in_specs=specs, scratch_shape...  24.8 us
    pallas_call x4, Pallas kernels, place(): pl.pallas_call(partial(place_kernel, [len(piece) for piece in pieces]), o...  17 us
    pallas_call x2, Pallas kernels, pair_grad(): pl.pallas_call(partial(pair_grad_kernel, fine), out_shape=(shape((blocks,...  16.4 us
  transfers between devices with their start and end apart: 71, of which 35 were waited for; matrix products, arithmetic and copies ran while one was open for 6% of the time, Pallas kernels for 9%

profile of v9, /device:TPU:0, one launch (start us, length us, event | category | flops | bytes accessed | tf_op | source)
XLA Modules:
  0.0 694.5 jit_solution(12072522881101074552)
XLA Ops:
  14.7 5.3 all-to-all-start
  20.1 13.2 %all_gather.15 = bf16[2,2048]{1,0:T(2,128)(2,1)S(1)} all-gather(bf16[2,256]{1,0:T(2,128)(2,1)S(1)} %pad_maximum_fusion.2), channel_id=1, replica_groups=mesh['rep'=4,'shard'=8] {'shard'}, dimensions={1}, use_global_device_ids=true | all-gather | bytes 9216 | tf_op jit(solution)/shard_map/all_gather | solution.py:565
  34.0 13.2 %all-to-all-done.x_ref.pos_ref = bf16[4,128,2176]{2,1,0:T(8,128)(2,1)} async-done(((bf16[4,128,2176]{2,1,0:T(8,128)(2,1)}), bf16[4,128,2176]{2,1,0:T(8,128)(2,1)}, u32[]{:S(2)}, u32[]{:S(2)}) %all-to-all-start) | async-done | bytes 2228256 | tf_op jit(solution)/shard_map/all_to_all | solution.py:43
  49.7 6.2 shard_map.203
  59.6 6.4 shard_map.204
  66.0 10.6 %all_to_all.20 = bf16[4,4,128,128]{3,2,1,0:T(8,128)(2,1)S(1)} all-to-all(bf16[4,4,128,128]{3,2,1,0:T(8,128)(2,1)} %get-tuple-element.68), channel_id=1, replica_groups=mesh['rep'=4,'shard'=8] {'rep'}, dimensions={0} | all-to-all | bytes 1048576 | tf_op jit(solution)/shard_map/all_to_all | solution.py:47
  80.6 27.8 %all_to_all.21.part_ref = bf16[4,128,2048]{2,1,0:T(8,128)(2,1)} all-to-all(bf16[4,128,2048]{2,1,0:T(8,128)(2,1)S(1)} %bitcast.57), channel_id=1, replica_groups=mesh['rep'=4,'shard'=8] {'rep'}, dimensions={0} | all-to-all | bytes 4194304 | tf_op jit(solution)/shard_map/all_to_all | solution.py:47
  118.5 5.6 collective-permute-start.2
  128.7 10.3 %collective-permute-done.2.refs_2_ = bf16[2,64,704]{2,1,0:T(8,128)(2,1)S(1)} collective-permute-done((bf16[2,64,704]{2,1,0:T(8,128)(2,1)}, bf16[2,64,704]{2,1,0:T(8,128)(2,1)S(1)}, u32[]{:S(2)}, u32[]{:S(2)}) %collective-permute-start.2) | collective-permute-done | bytes 180256 | tf_op jit(solution)/shard_map/ppermute | solution.py:55
  139.5 8.6 %collective-permute-done.3.refs_3_ = bf16[2,64,704]{2,1,0:T(8,128)(2,1)S(1)} collective-permute-done((bf16[2,64,704]{2,1,0:T(8,128)(2,1)}, bf16[2,64,704]{2,1,0:T(8,128)(2,1)S(1)}, u32[]{:S(2)}, u32[]{:S(2)}) %collective-permute-start.3) | collective-permute-done | bytes 180256 | tf_op jit(solution)/shard_map/ppermute | solution.py:55
  150.2 9.4 %collective-permute-done.6.refs_6_ = bf16[2,64,704]{2,1,0:T(8,128)(2,1)S(1)} collective-permute-done((bf16[2,64,704]{2,1,0:T(8,128)(2,1)}, bf16[2,64,704]{2,1,0:T(8,128)(2,1)S(1)}, u32[]{:S(2)}, u32[]{:S(2)}) %collective-permute-start.6) | collective-permute-done | bytes 180256 | tf_op jit(solution)/shard_map/ppermute | solution.py:55
  159.7 6.9 %collective-permute-done.7.refs_7_ = bf16[2,64,704]{2,1,0:T(8,128)(2,1)S(1)} collective-permute-done((bf16[2,64,704]{2,1,0:T(8,128)(2,1)}, bf16[2,64,704]{2,1,0:T(8,128)(2,1)S(1)}, u32[]{:S(2)}, u32[]{:S(2)}) %collective-permute-start.7) | collective-permute-done | bytes 180256 | tf_op jit(solution)/shard_map/ppermute | solution.py:55
  174.1 16.6 %collective-permute-done.8.refs_2_ = bf16[8,64,704]{2,1,0:T(8,128)(2,1)S(1)} collective-permute-done((bf16[8,64,704]{2,1,0:T(8,128)(2,1)}, bf16[8,64,704]{2,1,0:T(8,128)(2,1)S(1)}, u32[]{:S(2)}, u32[]{:S(2)}) %collective-permute-start.8) | collective-permute-done | bytes 720928 | tf_op jit(solution)/shard_map/ppermute | solution.py:55
  192.7 14.8 %collective-permute-done.9.refs_3_ = bf16[8,64,704]{2,1,0:T(8,128)(2,1)S(1)} collective-permute-done((bf16[8,64,704]{2,1,0:T(8,128)(2,1)}, bf16[8,64,704]{2,1,0:T(8,128)(2,1)S(1)}, u32[]{:S(2)}, u32[]{:S(2)}) %collective-permute-start.9) | collective-permute-done | bytes 720928 | tf_op jit(solution)/shard_map/ppermute | solution.py:55
  207.7 16.7 %collective-permute-done.12.refs_6_ = bf16[8,64,704]{2,1,0:T(8,128)(2,1)S(1)} collective-permute-done((bf16[8,64,704]{2,1,0:T(8,128)(2,1)S(1)}, bf16[8,64,704]{2,1,0:T(8,128)(2,1)S(1)}, u32[]{:S(2)}, u32[]{:S(2)}) %collective-permute-start.12) | collective-permute-done | bytes 720928 | tf_op jit(solution)/shard_map/ppermute | solution.py:55
  226.1 5.8 shard_map.207
  231.9 7.3 %fusion.7.back_ref = f32[1024,704]{1,0:T(8,128)} fusion(bf16[1024,2048]{1,0:T(8,128)(2,1)} %all-gather.11.cloned.1.call-done, bf16[704,2048]{1,0:T(8,128)(2,1)S(1)} %copy-done), kind=kOutput, calls=%fused_computation.49 | convolution fusion | flops 2952790016 | bytes 9961472 | tf_op jit(solution)/shard_map/dot_general | solution.py:26
  239.2 12.1 %shard_map.208 = (bf16[1024,704]{1,0:T(8,128)(2,1)}, bf16[1024,704]{1,0:T(8,128)(2,1)}, bf16[1024,704]{1,0:T(8,128)(2,1)}) custom-call(bf16[1024,2048]{1,0:T(8,128)(2,1)} %all-gather.9.cloned.1.call-done.x_ref, f32[1024,704]{1,0:T(8,128)} %fusion.7.back_ref, bf16[2,2048,704]{2,1,0:T(8,128)(2,1)} %bitcast.48), custom_call_target="tpu_custom_call" | custom-call | tf_op jit(solution)/shard_map/pallas_call | solution.py:638
  251.3 8.1 %shard_map.209 = (bf16[8,64,704]{2,1,0:T(8,128)(2,1)}, bf16[8,64,704]{2,1,0:T(8,128)(2,1)}, bf16[8,64,704]{2,1,0:T(8,128)(2,1)}, bf16[8,64,704]{2,1,0:T(8,128)(2,1)}) custom-call(s32[2]{0:T(128)} %pad_add_fusion.id_ref, bf16[1024,2048]{1,0:T(8,128)(2,1)} %all-gather.9.cloned.1.call-done.x_ref, bf16[1024,704]{1,0:T(8,128)(2,1)} %get-tuple-element.87.grad_ref.gate_ref), custom_call_target="tpu_custom_call" | custom-call | tf_op jit(solution)/shard_map/pallas_call | solution.py:258
  259.4 11.4 %shard_map.210 = bf16[1024,2048]{1,0:T(8,128)(2,1)} custom-call(bf16[1024,704]{1,0:T(8,128)(2,1)} %get-tuple-element.87.grad_ref.gate_ref, bf16[1024,704]{1,0:T(8,128)(2,1)} %get-tuple-element.88.up_ref.grad_ref, bf16[2,2048,704]{2,1,0:T(8,128)(2,1)} %bitcast.49), custom_call_target="tpu_custom_call" | custom-call | tf_op jit(solution)/shard_map/pallas_call | solution.py:647
  270.9 65.9 %reduce-scatter.7.cloned.1.call-done.grad_ref = bf16[128,2048]{1,0:T(8,128)(2,1)} async-done(((bf16[1024,2048]{1,0:T(8,128)(2,1)}), bf16[128,2048]{1,0:T(8,128)(2,1)}) %reduce-scatter.7.cloned.1.call-update) | async-done | bytes 524304 | tf_op jit(solution)/shard_map/reduce_scatter | solution.py:655
  343.2 9.1 %collective-permute-done.14.refs_1_ = bf16[128,2048]{1,0:T(8,128)(2,1)S(1)} collective-permute-done((bf16[128,2048]{1,0:T(8,128)(2,1)}, bf16[128,2048]{1,0:T(8,128)(2,1)S(1)}, u32[]{:S(2)}, u32[]{:S(2)}) %collective-permute-start.14) | collective-permute-done | bytes 524320 | tf_op jit(solution)/shard_map/ppermute | solution.py:55
  370.1 10.4 %all_to_all.22 = bf16[4,512,128]{2,1,0:T(8,128)(2,1)} all-to-all(bf16[4,512,128]{2,1,0:T(8,128)(2,1)S(1)} %bitcast.59), channel_id=1, replica_groups=mesh['rep'=4,'shard'=8] {'rep'}, dimensions={0} | all-to-all | bytes 1048576 | tf_op jit(solution)/shard_map/all_to_all | solution.py:47
  380.5 8.2 %shard_map.214 = (bf16[4,128,512]{2,1,0:T(8,128)(2,1)}, f32[4,192,128]{2,1,0:T(8,128)}) custom-call(bf16[4,4,128,128]{3,2,1,0:T(8,128)(2,1)} %bitcast.53, f32[4,8,128,192]{3,2,1,0:T(8,128)} %get-tuple-element.92.probs_ref, bf16[4,128,512]{2,1,0:T(8,128)(2,1)} %get-tuple-element.66.q_ref, bf16[4,128,128]{2,1,0:T(8,128)(2,1)} %get-tuple-element.67.own_ref, ...), custom_call_target="tpu_custom_call" | custom-call | tf_op jit(solution)/shard_map/pallas_call | solution.py:713
  393.6 13.8 %attn_in_back.1 = (bf16[4,128,2048]{2,1,0:T(8,128)(2,1)}, bf16[2048,768]{1,0:T(8,128)(2,1)}) custom-call(s32[2]{0:T(128)} %pad_add_fusion.id_ref, bf16[4,128,512]{2,1,0:T(8,128)(2,1)} %get-tuple-element.93.dq_ref, f32[4,192,128]{2,1,0:T(8,128)} %get-tuple-element.94.dkv_ref, f32[4,64,128]{2,1,0:T(8,128)} %copy-done.48, ...), custom_call_target="tpu_custom_call" | custom-call | tf_op jit(solution)/shard_map/attn_in_back/pallas_call | solution.py:738
  407.4 4.2 convolution_convert_fusion.2
  412.4 8.3 %shard_map.211 = (bf16[8,64,704]{2,1,0:T(8,128)(2,1)}, bf16[8,64,704]{2,1,0:T(8,128)(2,1)}, bf16[8,64,704]{2,1,0:T(8,128)(2,1)}, bf16[8,64,704]{2,1,0:T(8,128)(2,1)}) custom-call(s32[2]{0:T(128)} %pad_add_fusion.id_ref, bf16[1024,2048]{1,0:T(8,128)(2,1)} %all-gather.9.cloned.1.call-done.x_ref, bf16[1024,704]{1,0:T(8,128)(2,1)} %get-tuple-element.88.up_ref.grad_ref), custom_call_target="tpu_custom_call" | custom-call | tf_op jit(solution)/shard_map/pallas_call | solution.py:258
  420.7 5.0 convolution_convert_fusion
  425.7 5.9 convolution_convert_fusion.1
  443.3 8.8 %collective-permute-done.32 = bf16[8,64,704]{2,1,0:T(8,128)(2,1)} collective-permute-done((bf16[8,64,704]{2,1,0:T(8,128)(2,1)}, bf16[8,64,704]{2,1,0:T(8,128)(2,1)}, u32[]{:S(2)}, u32[]{:S(2)}) %collective-permute-start.32) | collective-permute-done | bytes 720928 | tf_op jit(solution)/shard_map/ppermute | solution.py:55
  454.4 20.1 %collective-permute-done.35 = bf16[8,64,704]{2,1,0:T(8,128)(2,1)S(1)} collective-permute-done((bf16[8,64,704]{2,1,0:T(8,128)(2,1)}, bf16[8,64,704]{2,1,0:T(8,128)(2,1)S(1)}, u32[]{:S(2)}, u32[]{:S(2)}) %collective-permute-start.35) | collective-permute-done | bytes 720928 | tf_op jit(solution)/shard_map/ppermute | solution.py:55
  475.8 5.8 collective-permute-done.53
  490.3 8.8 %collective-permute-done.33.refs_2_ = bf16[8,64,704]{2,1,0:T(8,128)(2,1)S(1)} collective-permute-done((bf16[8,64,704]{2,1,0:T(8,128)(2,1)S(1)}, bf16[8,64,704]{2,1,0:T(8,128)(2,1)S(1)}, u32[]{:S(2)}, u32[]{:S(2)}) %collective-permute-start.33) | collective-permute-done | bytes 720928 | tf_op jit(solution)/shard_map/ppermute | solution.py:55
  499.2 3.8 collective-permute-done.36.refs_5_
  503.9 3.9 shard_map.218
  507.8 4.6 collective-permute-start.37
  522.7 9.1 %collective-permute-done.38.refs_2_ = bf16[2,64,704]{2,1,0:T(8,128)(2,1)} collective-permute-done((bf16[2,64,704]{2,1,0:T(8,128)(2,1)}, bf16[2,64,704]{2,1,0:T(8,128)(2,1)}, u32[]{:S(2)}, u32[]{:S(2)}) %collective-permute-start.38) | collective-permute-done | bytes 180256 | tf_op jit(solution)/shard_map/ppermute | solution.py:55
  531.8 12.7 %collective-permute-done.39.refs_3_ = bf16[2,64,704]{2,1,0:T(8,128)(2,1)} collective-permute-done((bf16[2,64,704]{2,1,0:T(8,128)(2,1)}, bf16[2,64,704]{2,1,0:T(8,128)(2,1)}, u32[]{:S(2)}, u32[]{:S(2)}) %collective-permute-start.39) | collective-permute-done | bytes 180256 | tf_op jit(solution)/shard_map/ppermute | solution.py:55
  546.8 4.8 collective-permute-done.41.refs_5_
  553.7 6.8 collective-permute-done.42.refs_6_
  561.4 5.0 collective-permute-done.43.refs_7_
  576.6 12.7 %collective-permute-done.44.refs_1_ = bf16[64,5632]{1,0:T(8,128)(2,1)S(1)} collective-permute-done((bf16[64,5632]{1,0:T(8,128)(2,1)}, bf16[64,5632]{1,0:T(8,128)(2,1)S(1)}, u32[]{:S(2)}, u32[]{:S(2)}) %collective-permute-start.44) | collective-permute-done | bytes 720928 | tf_op jit(solution)/shard_map/ppermute | solution.py:55
  592.2 4.2 collective-permute-done.23
  599.3 35.2 %collective-permute-done.60.refs_6_ = bf16[96,2048]{1,0:T(8,128)(2,1)S(1)} collective-permute-done((bf16[96,2048]{1,0:T(8,128)(2,1)S(1)}, bf16[96,2048]{1,0:T(8,128)(2,1)S(1)}, u32[]{:S(2)}, u32[]{:S(2)}) %collective-permute-start.60) | collective-permute-done | bytes 393248 | tf_op jit(solution)/shard_map/ppermute | solution.py:55
  639.6 4.6 shard_map.222
  644.2 4.6 shard_map.220
  648.9 4.6 shard_map.221
  672.8 9.6 %collective-permute-done.26.refs_2_ = bf16[256,768]{1,0:T(8,128)(2,1)} collective-permute-done((bf16[256,768]{1,0:T(8,128)(2,1)}, bf16[256,768]{1,0:T(8,128)(2,1)}, u32[]{:S(2)}, u32[]{:S(2)}) %collective-permute-start.26) | collective-permute-done | bytes 393248 | tf_op jit(solution)/shard_map/ppermute | solution.py:55
  (279 shorter events, 162.4 us)
Async XLA Ops:
  7.2 42.5 %all-gather.5.cloned.1.call-start = ((), (), s32[]{:S(2)}) async-start(), calls=%async_computation.8 | async-start | bytes 2949120 | tf_op jit(solution)/shard_map/all_gather | solution.py:560
  10.2 67.3 %all-gather.7.cloned.1.call-start = ((), (), s32[]{:S(2)}) async-start(), calls=%async_computation.9 | async-start | bytes 2359296 | tf_op jit(solution)/shard_map/all_gather | solution.py:561
  12.0 219.9 %all-gather.11.cloned.1.call-start = ((), (), s32[]{:S(2)}) async-start(), calls=%async_computation.11 | async-start | bytes 4718592 | tf_op jit(solution)/shard_map/all_gather | solution.py:586
  14.7 32.5 %all-to-all-start = ((bf16[4,128,2176]{2,1,0:T(8,128)(2,1)}), bf16[4,128,2176]{2,1,0:T(8,128)(2,1)}, u32[]{:S(2)}, u32[]{:S(2)}) async-start(bf16[4,128,2176]{2,1,0:T(8,128)(2,1)} %broadcast_in_dim.16), calls=%async_computation | async-start | bytes 4456448 | tf_op jit(solution)/shard_map/all_to_all | solution.py:43
  20.1 219.1 %all-gather.9.cloned.1.call-start = ((), (), s32[]{:S(2)}) async-start(), calls=%async_computation.10 | async-start | bytes 4718592 | tf_op jit(solution)/shard_map/all_gather | solution.py:632
  111.7 225.0 %reduce-scatter.7.cloned.1.call-start = ((), (), s32[]{:S(2)}) async-start(), calls=%async_computation.13 | async-start | bytes 4718592 | tf_op jit(solution)/shard_map/reduce_scatter | solution.py:655
  118.5 20.5 %collective-permute-start.2 = (bf16[2,64,704]{2,1,0:T(8,128)(2,1)}, bf16[2,64,704]{2,1,0:T(8,128)(2,1)S(1)}, u32[]{:S(2)}, u32[]{:S(2)}) collective-permute-start(bf16[2,64,704]{2,1,0:T(8,128)(2,1)} %get-tuple-element.75), channel_id=1, source_target_pairs={{0,2},{1,3},{2,0},{3,1},{4,6},{5,7},{6,4},{7,5},{8,10},{9,11},{10,... | collective-permute-start | bytes 540680 | tf_op jit(solution)/shard_map/ppermute | solution.py:55
  124.2 24.0 %collective-permute-start.3 = (bf16[2,64,704]{2,1,0:T(8,128)(2,1)}, bf16[2,64,704]{2,1,0:T(8,128)(2,1)S(1)}, u32[]{:S(2)}, u32[]{:S(2)}) collective-permute-start(bf16[2,64,704]{2,1,0:T(8,128)(2,1)} %get-tuple-element.76), channel_id=1, source_target_pairs={{0,3},{1,2},{2,1},{3,0},{4,7},{5,6},{6,5},{7,4},{8,11},{9,10},{10,... | collective-permute-start | bytes 540680 | tf_op jit(solution)/shard_map/ppermute | solution.py:55
  124.3 23.9 %collective-permute-start.4 = (bf16[2,64,704]{2,1,0:T(8,128)(2,1)}, bf16[2,64,704]{2,1,0:T(8,128)(2,1)S(1)}, u32[]{:S(2)}, u32[]{:S(2)}) collective-permute-start(bf16[2,64,704]{2,1,0:T(8,128)(2,1)} %get-tuple-element.77), channel_id=1, source_target_pairs={{0,4},{1,5},{2,6},{3,7},{4,0},{5,1},{6,2},{7,3},{8,12},{9,13},{10,... | collective-permute-start | bytes 540680 | tf_op jit(solution)/shard_map/ppermute | solution.py:55
  126.6 23.6 %collective-permute-start.5 = (bf16[2,64,704]{2,1,0:T(8,128)(2,1)}, bf16[2,64,704]{2,1,0:T(8,128)(2,1)S(1)}, u32[]{:S(2)}, u32[]{:S(2)}) collective-permute-start(bf16[2,64,704]{2,1,0:T(8,128)(2,1)} %get-tuple-element.78), channel_id=1, source_target_pairs={{0,5},{1,4},{2,7},{3,6},{4,1},{5,0},{6,3},{7,2},{8,13},{9,12},{10,... | collective-permute-start | bytes 540680 | tf_op jit(solution)/shard_map/ppermute | solution.py:55
  126.7 33.0 %collective-permute-start.6 = (bf16[2,64,704]{2,1,0:T(8,128)(2,1)}, bf16[2,64,704]{2,1,0:T(8,128)(2,1)S(1)}, u32[]{:S(2)}, u32[]{:S(2)}) collective-permute-start(bf16[2,64,704]{2,1,0:T(8,128)(2,1)} %get-tuple-element.79), channel_id=1, source_target_pairs={{0,6},{1,7},{2,4},{3,5},{4,2},{5,3},{6,0},{7,1},{8,14},{9,15},{10,... | collective-permute-start | bytes 540680 | tf_op jit(solution)/shard_map/ppermute | solution.py:55
  139.0 27.6 %collective-permute-start.7 = (bf16[2,64,704]{2,1,0:T(8,128)(2,1)}, bf16[2,64,704]{2,1,0:T(8,128)(2,1)S(1)}, u32[]{:S(2)}, u32[]{:S(2)}) collective-permute-start(bf16[2,64,704]{2,1,0:T(8,128)(2,1)} %get-tuple-element.80), channel_id=1, source_target_pairs={{0,7},{1,6},{2,5},{3,4},{4,3},{5,2},{6,1},{7,0},{8,15},{9,14},{10,... | collective-permute-start | bytes 540680 | tf_op jit(solution)/shard_map/ppermute | solution.py:55
  170.0 20.6 %collective-permute-start.8 = (bf16[8,64,704]{2,1,0:T(8,128)(2,1)}, bf16[8,64,704]{2,1,0:T(8,128)(2,1)S(1)}, u32[]{:S(2)}, u32[]{:S(2)}) collective-permute-start(bf16[8,64,704]{2,1,0:T(8,128)(2,1)} %get-tuple-element.81.refs_0_), channel_id=1, source_target_pairs={{0,8},{8,0},{16,24},{24,16},{1,9},{9,1},{17,25},{25,17},{2,10},{10... | collective-permute-start | bytes 2162696 | tf_op jit(solution)/shard_map/ppermute | solution.py:55
  170.2 20.6 %collective-permute-start.11 = (bf16[8,64,704]{2,1,0:T(8,128)(2,1)}, bf16[8,64,704]{2,1,0:T(8,128)(2,1)S(1)}, u32[]{:S(2)}, u32[]{:S(2)}) collective-permute-start(bf16[8,64,704]{2,1,0:T(8,128)(2,1)} %get-tuple-element.82.refs_1_), channel_id=1, source_target_pairs={{0,16},{8,24},{16,0},{24,8},{1,17},{9,25},{17,1},{25,9},{2,18},{10... | collective-permute-start | bytes 2162696 | tf_op jit(solution)/shard_map/ppermute | solution.py:55
  170.2 37.3 %collective-permute-start.9 = (bf16[8,64,704]{2,1,0:T(8,128)(2,1)}, bf16[8,64,704]{2,1,0:T(8,128)(2,1)S(1)}, u32[]{:S(2)}, u32[]{:S(2)}) collective-permute-start(bf16[8,64,704]{2,1,0:T(8,128)(2,1)} %get-tuple-element.82.refs_1_), channel_id=1, source_target_pairs={{0,8},{8,0},{16,24},{24,16},{1,9},{9,1},{17,25},{25,17},{2,10},{10... | collective-permute-start | bytes 2162696 | tf_op jit(solution)/shard_map/ppermute | solution.py:55
  172.2 35.5 %collective-permute-start.10 = (bf16[8,64,704]{2,1,0:T(8,128)(2,1)}, bf16[8,64,704]{2,1,0:T(8,128)(2,1)S(1)}, u32[]{:S(2)}, u32[]{:S(2)}) collective-permute-start(bf16[8,64,704]{2,1,0:T(8,128)(2,1)} %get-tuple-element.81.refs_0_), channel_id=1, source_target_pairs={{0,16},{8,24},{16,0},{24,8},{1,17},{9,25},{17,1},{25,9},{2,18},{10... | collective-permute-start | bytes 2162696 | tf_op jit(solution)/shard_map/ppermute | solution.py:55
  190.6 33.7 %collective-permute-start.12 = (bf16[8,64,704]{2,1,0:T(8,128)(2,1)S(1)}, bf16[8,64,704]{2,1,0:T(8,128)(2,1)S(1)}, u32[]{:S(2)}, u32[]{:S(2)}) collective-permute-start(bf16[8,64,704]{2,1,0:T(8,128)(2,1)S(1)} %collective-permute-done.8.refs_2_), channel_id=1, source_target_pairs={{0,16},{8,24},{16,0},{24,8},{1,17},{9,25},{17,1},{25,9},{2,18},{10... | collective-permute-start | bytes 2162696 | tf_op jit(solution)/shard_map/ppermute | solution.py:55
  190.8 33.5 %collective-permute-start.13 = (bf16[8,64,704]{2,1,0:T(8,128)(2,1)S(1)}, bf16[8,64,704]{2,1,0:T(8,128)(2,1)S(1)}, u32[]{:S(2)}, u32[]{:S(2)}) collective-permute-start(bf16[8,64,704]{2,1,0:T(8,128)(2,1)S(1)} %collective-permute-done.11.refs_5_), channel_id=1, source_target_pairs={{0,8},{8,0},{16,24},{24,16},{1,9},{9,1},{17,25},{25,17},{2,10},{10... | collective-permute-start | bytes 2162696 | tf_op jit(solution)/shard_map/ppermute | solution.py:55
  270.8 368.0 %reduce-scatter.11.cloned.1.call-start = ((), (), s32[]{:S(2)}) async-start(), calls=%async_computation.15 | async-start | bytes 2359296 | tf_op jit(solution)/shard_map/reduce_scatter | solution.py:772
  411.6 244.7 %reduce-scatter.9.cloned.1.call-start = ((), (), s32[]{:S(2)}) async-start(), calls=%async_computation.14 | async-start | bytes 3538944 | tf_op jit(solution)/shard_map/reduce_scatter | solution.py:770
  412.3 247.5 %reduce-scatter.5.cloned.1.call-start = ((), (), s32[]{:S(2)}) async-start(), calls=%async_computation.12 | async-start | bytes 4718592 | tf_op jit(solution)/shard_map/reduce_scatter | solution.py:677
  435.3 51.2 %collective-permute-start.31 = (bf16[8,64,704]{2,1,0:T(8,128)(2,1)}, bf16[8,64,704]{2,1,0:T(8,128)(2,1)S(1)}, u32[]{:S(2)}, u32[]{:S(2)}) collective-permute-start(bf16[8,64,704]{2,1,0:T(8,128)(2,1)} %get-tuple-element.105), channel_id=1, source_target_pairs={{0,8},{8,0},{16,24},{24,16},{1,9},{9,1},{17,25},{25,17},{2,10},{10... | collective-permute-start | bytes 2162696 | tf_op jit(solution)/shard_map/ppermute | solution.py:55
  437.0 52.4 %collective-permute-start.34 = (bf16[8,64,704]{2,1,0:T(8,128)(2,1)}, bf16[8,64,704]{2,1,0:T(8,128)(2,1)S(1)}, u32[]{:S(2)}, u32[]{:S(2)}) collective-permute-start(bf16[8,64,704]{2,1,0:T(8,128)(2,1)} %get-tuple-element.108), channel_id=1, source_target_pairs={{0,16},{8,24},{16,0},{24,8},{1,17},{9,25},{17,1},{25,9},{2,18},{10... | collective-permute-start | bytes 2162696 | tf_op jit(solution)/shard_map/ppermute | solution.py:55
  438.1 36.5 %collective-permute-start.35 = (bf16[8,64,704]{2,1,0:T(8,128)(2,1)}, bf16[8,64,704]{2,1,0:T(8,128)(2,1)S(1)}, u32[]{:S(2)}, u32[]{:S(2)}) collective-permute-start(bf16[8,64,704]{2,1,0:T(8,128)(2,1)} %get-tuple-element.110), channel_id=1, source_target_pairs={{0,16},{8,24},{16,0},{24,8},{1,17},{9,25},{17,1},{25,9},{2,18},{10... | collective-permute-start | bytes 2162696 | tf_op jit(solution)/shard_map/ppermute | solution.py:55
  441.3 41.3 %collective-permute-start.51 = (bf16[96,2048]{1,0:T(8,128)(2,1)S(1)}, bf16[96,2048]{1,0:T(8,128)(2,1)S(1)}, u32[]{:S(2)}, u32[]{:S(2)}) collective-permute-start(bf16[96,2048]{1,0:T(8,128)(2,1)S(1)} %get-tuple-element.126), channel_id=1, source_target_pairs={{0,8},{8,0},{16,24},{24,16},{1,9},{9,1},{17,25},{25,17},{2,10},{10... | collective-permute-start | bytes 1179656 | tf_op jit(solution)/shard_map/ppermute | solution.py:55
  452.1 29.5 %collective-permute-start.53 = (bf16[80,2048]{1,0:T(8,128)(2,1)S(1)}, bf16[80,2048]{1,0:T(8,128)(2,1)S(1)}, u32[]{:S(2)}, u32[]{:S(2)}) collective-permute-start(bf16[80,2048]{1,0:T(8,128)(2,1)S(1)} %get-tuple-element.123), channel_id=1, source_target_pairs={{0,16},{8,24},{16,0},{24,8},{1,17},{9,25},{17,1},{25,9},{2,18},{10... | collective-permute-start | bytes 983048 | tf_op jit(solution)/shard_map/ppermute | solution.py:55
  482.6 20.4 %collective-permute-start.36 = (bf16[8,64,704]{2,1,0:T(8,128)(2,1)S(1)}, bf16[8,64,704]{2,1,0:T(8,128)(2,1)S(1)}, u32[]{:S(2)}, u32[]{:S(2)}) collective-permute-start(bf16[8,64,704]{2,1,0:T(8,128)(2,1)S(1)} %add_convert_fusion), channel_id=1, source_target_pairs={{0,8},{8,0},{16,24},{24,16},{1,9},{9,1},{17,25},{25,17},{2,10},{10... | collective-permute-start | bytes 2162696 | tf_op jit(solution)/shard_map/ppermute | solution.py:55
  485.0 31.2 %collective-permute-start.50 = (bf16[96,2048]{1,0:T(8,128)(2,1)S(1)}, bf16[96,2048]{1,0:T(8,128)(2,1)S(1)}, u32[]{:S(2)}, u32[]{:S(2)}) collective-permute-start(bf16[96,2048]{1,0:T(8,128)(2,1)S(1)} %get-tuple-element.125), channel_id=1, source_target_pairs={{0,8},{8,0},{16,24},{24,16},{1,9},{9,1},{17,25},{25,17},{2,10},{10... | collective-permute-start | bytes 1179656 | tf_op jit(solution)/shard_map/ppermute | solution.py:55
  486.5 31.9 %collective-permute-start.52 = (bf16[96,2048]{1,0:T(8,128)(2,1)}, bf16[96,2048]{1,0:T(8,128)(2,1)S(1)}, u32[]{:S(2)}, u32[]{:S(2)}) collective-permute-start(bf16[96,2048]{1,0:T(8,128)(2,1)} %add_convert_fusion.4), channel_id=1, source_target_pairs={{0,16},{8,24},{16,0},{24,8},{1,17},{9,25},{17,1},{25,9},{2,18},{10... | collective-permute-start | bytes 1179656 | tf_op jit(solution)/shard_map/ppermute | solution.py:55
  489.3 29.7 %collective-permute-start.59 = (bf16[80,2048]{1,0:T(8,128)(2,1)}, bf16[80,2048]{1,0:T(8,128)(2,1)}, u32[]{:S(2)}, u32[]{:S(2)}) collective-permute-start(bf16[80,2048]{1,0:T(8,128)(2,1)} %add_convert_fusion.5.refs_1_), channel_id=1, source_target_pairs={{0,16},{8,24},{16,0},{24,8},{1,17},{9,25},{17,1},{25,9},{2,18},{10... | collective-permute-start | bytes 983048 | tf_op jit(solution)/shard_map/ppermute | solution.py:55
  516.9 27.5 %collective-permute-start.39 = (bf16[2,64,704]{2,1,0:T(8,128)(2,1)}, bf16[2,64,704]{2,1,0:T(8,128)(2,1)}, u32[]{:S(2)}, u32[]{:S(2)}) collective-permute-start(bf16[2,64,704]{2,1,0:T(8,128)(2,1)} %get-tuple-element.114), channel_id=1, source_target_pairs={{0,3},{1,2},{2,1},{3,0},{4,7},{5,6},{6,5},{7,4},{8,11},{9,10},{10,... | collective-permute-start | bytes 540680 | tf_op jit(solution)/shard_map/ppermute | solution.py:55
  518.4 53.1 %collective-permute-start.57 = (bf16[80,2048]{1,0:T(8,128)(2,1)}, bf16[80,2048]{1,0:T(8,128)(2,1)}, u32[]{:S(2)}, u32[]{:S(2)}) collective-permute-start(bf16[80,2048]{1,0:T(8,128)(2,1)} %add_convert_fusion.5.refs_1_), channel_id=1, source_target_pairs={{0,8},{8,0},{16,24},{24,16},{1,9},{9,1},{17,25},{25,17},{2,10},{10... | collective-permute-start | bytes 983048 | tf_op jit(solution)/shard_map/ppermute | solution.py:55
  519.0 26.9 %collective-permute-start.40 = (bf16[2,64,704]{2,1,0:T(8,128)(2,1)}, bf16[2,64,704]{2,1,0:T(8,128)(2,1)S(1)}, u32[]{:S(2)}, u32[]{:S(2)}) collective-permute-start(bf16[2,64,704]{2,1,0:T(8,128)(2,1)} %get-tuple-element.115), channel_id=1, source_target_pairs={{0,4},{1,5},{2,6},{3,7},{4,0},{5,1},{6,2},{7,3},{8,12},{9,13},{10,... | collective-permute-start | bytes 540680 | tf_op jit(solution)/shard_map/ppermute | solution.py:55
  522.7 29.0 %collective-permute-start.41 = (bf16[2,64,704]{2,1,0:T(8,128)(2,1)}, bf16[2,64,704]{2,1,0:T(8,128)(2,1)S(1)}, u32[]{:S(2)}, u32[]{:S(2)}) collective-permute-start(bf16[2,64,704]{2,1,0:T(8,128)(2,1)} %get-tuple-element.116), channel_id=1, source_target_pairs={{0,5},{1,4},{2,7},{3,6},{4,1},{5,0},{6,3},{7,2},{8,13},{9,12},{10,... | collective-permute-start | bytes 540680 | tf_op jit(solution)/shard_map/ppermute | solution.py:55
  531.8 28.7 %collective-permute-start.42 = (bf16[2,64,704]{2,1,0:T(8,128)(2,1)}, bf16[2,64,704]{2,1,0:T(8,128)(2,1)S(1)}, u32[]{:S(2)}, u32[]{:S(2)}) collective-permute-start(bf16[2,64,704]{2,1,0:T(8,128)(2,1)} %get-tuple-element.117), channel_id=1, source_target_pairs={{0,6},{1,7},{2,4},{3,5},{4,2},{5,3},{6,0},{7,1},{8,14},{9,15},{10,... | collective-permute-start | bytes 540680 | tf_op jit(solution)/shard_map/ppermute | solution.py:55
  544.5 22.0 %collective-permute-start.43 = (bf16[2,64,704]{2,1,0:T(8,128)(2,1)}, bf16[2,64,704]{2,1,0:T(8,128)(2,1)S(1)}, u32[]{:S(2)}, u32[]{:S(2)}) collective-permute-start(bf16[2,64,704]{2,1,0:T(8,128)(2,1)} %get-tuple-element.118), channel_id=1, source_target_pairs={{0,7},{1,6},{2,5},{3,4},{4,3},{5,2},{6,1},{7,0},{8,15},{9,14},{10,... | collective-permute-start | bytes 540680 | tf_op jit(solution)/shard_map/ppermute | solution.py:55
  545.9 28.0 %collective-permute-start.56 = (bf16[96,2048]{1,0:T(8,128)(2,1)S(1)}, bf16[96,2048]{1,0:T(8,128)(2,1)S(1)}, u32[]{:S(2)}, u32[]{:S(2)}) collective-permute-start(bf16[96,2048]{1,0:T(8,128)(2,1)S(1)} %add_convert_fusion.3.refs_0_), channel_id=1, source_target_pairs={{0,8},{8,0},{16,24},{24,16},{1,9},{9,1},{17,25},{25,17},{2,10},{10... | collective-permute-start | bytes 1179656 | tf_op jit(solution)/shard_map/ppermute | solution.py:55
  551.6 22.9 %collective-permute-start.58 = (bf16[96,2048]{1,0:T(8,128)(2,1)S(1)}, bf16[96,2048]{1,0:T(8,128)(2,1)}, u32[]{:S(2)}, u32[]{:S(2)}) collective-permute-start(bf16[96,2048]{1,0:T(8,128)(2,1)S(1)} %add_convert_fusion.3.refs_0_), channel_id=1, source_target_pairs={{0,16},{8,24},{16,0},{24,8},{1,17},{9,25},{17,1},{25,9},{2,18},{10... | collective-permute-start | bytes 1179656 | tf_op jit(solution)/shard_map/ppermute | solution.py:55
  573.9 22.5 %collective-permute-start.23 = (bf16[64,2048]{1,0:T(8,128)(2,1)S(1)}, bf16[64,2048]{1,0:T(8,128)(2,1)S(1)}, u32[]{:S(2)}, u32[]{:S(2)}) collective-permute-start(bf16[64,2048]{1,0:T(8,128)(2,1)S(1)} %get-tuple-element.131), channel_id=1, source_target_pairs={{0,16},{8,24},{16,0},{24,8},{1,17},{9,25},{17,1},{25,9},{2,18},{10... | collective-permute-start | bytes 786440 | tf_op jit(solution)/shard_map/ppermute | solution.py:55
  574.6 22.4 %collective-permute-start.20 = (bf16[64,2048]{1,0:T(8,128)(2,1)S(1)}, bf16[64,2048]{1,0:T(8,128)(2,1)S(1)}, u32[]{:S(2)}, u32[]{:S(2)}) collective-permute-start(bf16[64,2048]{1,0:T(8,128)(2,1)S(1)} %get-tuple-element.134), channel_id=1, source_target_pairs={{0,8},{8,0},{16,24},{24,16},{1,9},{9,1},{17,25},{25,17},{2,10},{10... | collective-permute-start | bytes 786440 | tf_op jit(solution)/shard_map/ppermute | solution.py:55
  575.1 60.0 %collective-permute-start.45 = (bf16[64,5632]{1,0:T(8,128)(2,1)S(1)}, bf16[64,5632]{1,0:T(8,128)(2,1)S(1)}, u32[]{:S(2)}, u32[]{:S(2)}) collective-permute-start(bf16[64,5632]{1,0:T(8,128)(2,1)S(1)} %copy-done.20), channel_id=1, source_target_pairs={{0,16},{8,24},{16,0},{24,8},{1,17},{9,25},{17,1},{25,9},{2,18},{10... | collective-permute-start | bytes 2162696 | tf_op jit(solution)/shard_map/ppermute | solution.py:55
  589.3 47.3 %collective-permute-start.47 = (bf16[64,5632]{1,0:T(8,128)(2,1)S(1)}, bf16[64,5632]{1,0:T(8,128)(2,1)S(1)}, u32[]{:S(2)}, u32[]{:S(2)}) collective-permute-start(bf16[64,5632]{1,0:T(8,128)(2,1)S(1)} %copy-done.19), channel_id=1, source_target_pairs={{0,8},{8,0},{16,24},{24,16},{1,9},{9,1},{17,25},{25,17},{2,10},{10... | collective-permute-start | bytes 2162696 | tf_op jit(solution)/shard_map/ppermute | solution.py:55
  590.8 46.5 %collective-permute-start.46 = (bf16[64,5632]{1,0:T(8,128)(2,1)S(1)}, bf16[64,5632]{1,0:T(8,128)(2,1)S(1)}, u32[]{:S(2)}, u32[]{:S(2)}) collective-permute-start(bf16[64,5632]{1,0:T(8,128)(2,1)S(1)} %collective-permute-done.44.refs_1_), channel_id=1, source_target_pairs={{0,16},{8,24},{16,0},{24,8},{1,17},{9,25},{17,1},{25,9},{2,18},{10... | collective-permute-start | bytes 2162696 | tf_op jit(solution)/shard_map/ppermute | solution.py:55
  596.4 42.4 %collective-permute-start.49 = (bf16[64,5632]{1,0:T(8,128)(2,1)S(1)}, bf16[64,5632]{1,0:T(8,128)(2,1)}, u32[]{:S(2)}, u32[]{:S(2)}) collective-permute-start(bf16[64,5632]{1,0:T(8,128)(2,1)S(1)} %collective-permute-done.48.refs_2_), channel_id=1, source_target_pairs={{0,8},{8,0},{16,24},{24,16},{1,9},{9,1},{17,25},{25,17},{2,10},{10... | collective-permute-start | bytes 2162696 | tf_op jit(solution)/shard_map/ppermute | solution.py:55
  597.0 37.6 %collective-permute-start.60 = (bf16[96,2048]{1,0:T(8,128)(2,1)S(1)}, bf16[96,2048]{1,0:T(8,128)(2,1)S(1)}, u32[]{:S(2)}, u32[]{:S(2)}) collective-permute-start(bf16[96,2048]{1,0:T(8,128)(2,1)S(1)} %collective-permute-done.56.refs_2_), channel_id=1, source_target_pairs={{0,16},{8,24},{16,0},{24,8},{1,17},{9,25},{17,1},{25,9},{2,18},{10... | collective-permute-start | bytes 1179656 | tf_op jit(solution)/shard_map/ppermute | solution.py:55
  635.1 19.8 %collective-permute-start.22 = (bf16[64,2048]{1,0:T(8,128)(2,1)S(1)}, bf16[64,2048]{1,0:T(8,128)(2,1)}, u32[]{:S(2)}, u32[]{:S(2)}) collective-permute-start(bf16[64,2048]{1,0:T(8,128)(2,1)S(1)} %get-tuple-element.132), channel_id=1, source_target_pairs={{0,16},{8,24},{16,0},{24,8},{1,17},{9,25},{17,1},{25,9},{2,18},{10... | collective-permute-start | bytes 786440 | tf_op jit(solution)/shard_map/ppermute | solution.py:55
  657.0 25.3 %collective-permute-start.26 = (bf16[256,768]{1,0:T(8,128)(2,1)}, bf16[256,768]{1,0:T(8,128)(2,1)}, u32[]{:S(2)}, u32[]{:S(2)}) collective-permute-start(bf16[256,768]{1,0:T(8,128)(2,1)} %reduce-scatter.9.cloned.1.call-done.refs_0_), channel_id=1, source_target_pairs={{0,16},{8,24},{16,0},{24,8},{1,17},{9,25},{17,1},{25,9},{2,18},{10... | collective-permute-start | bytes 1179656 | tf_op jit(solution)/shard_map/ppermute | solution.py:55
  658.5 23.9 %collective-permute-start.27 = (bf16[256,768]{1,0:T(8,128)(2,1)}, bf16[256,768]{1,0:T(8,128)(2,1)}, u32[]{:S(2)}, u32[]{:S(2)}) collective-permute-start(bf16[256,768]{1,0:T(8,128)(2,1)} %reduce-scatter.9.cloned.1.call-done.refs_0_), channel_id=1, source_target_pairs={{0,24},{8,16},{16,8},{24,0},{1,25},{9,17},{17,9},{25,1},{2,26},{10... | collective-permute-start | bytes 1179656 | tf_op jit(solution)/shard_map/ppermute | solution.py:55
  (77 other events, 1338.2 us)
Sparse Core Ops, SparseCore 0:
  10.4 36.4 all-gather.4
  49.1 28.2 all-gather.6
  79.0 46.9 all-gather.10
  127.4 69.6 all-gather.8
  271.0 65.7 reduce-scatter.6
  411.7 37.6 reduce-scatter.10
  451.7 38.9 reduce-scatter.8
  492.9 71.1 reduce-scatter.4

commit v10 on v9

--- a/solution.py
+++ b/solution.py
@@ -72,11 +72,11 @@
     return [[chunks[0][0], first_one, last_one], [chunks[0][1], second_one, last_two]]
 
 
-def gather_two(value, count):
+def gather_two(value, count, half=None):
     go = lambda value, step: send(value, "rep", count, step)
     if count != 4:
         return [(value,)] + [(go(value, k),) for k in range(1, count)]
-    half = value.shape[0] // 2
+    half = half or value.shape[0] // 2
     one, two = go(value, 1), go(value, 2)
     return [(value,), (one,), (two,), (go(one[:half], 2), go(two[half:], 1))]
 
@@ -213,25 +213,26 @@
             ref[:, at * hidden : (at + 1) * hidden] = both[at, h]
 
 
-def qkv_kernel(share, sizes, id_ref, *refs):
-    pieces = refs[:-6]
-    q_ref, k_ref, v_ref, gain_ref, k_all, v_all = refs[-6:]
+def attn_kernel(share, fine, id_ref, *refs):
+    pieces = refs[:-7]
+    q_ref, k_ref, v_ref, o_ref, gain_ref, k_all, v_all = refs[-7:]
     count = k_all.shape[0]
     q_cols = q_ref.shape[1] // count
-    gain_ref[...] = jnp.zeros_like(gain_ref)
-    pieces = list(pieces)
-    for k, size in enumerate(sizes):
+    o_at = q_cols + 2 * HD + LANES
+    total = 0.0
+    for k, piece in enumerate(pieces):
         at = jnp.bitwise_xor(id_ref[0], k)
-        row = 0
-        for piece in pieces[:size]:
-            value = piece[...].astype(F32)
-            rows = slice(row, row + value.shape[0])
-            q_ref[rows, pl.ds(pl.multiple_of(at * q_cols, LANES), q_cols)] = value[:, :q_cols]
-            k_all[at, rows] = value[:, q_cols : q_cols + HD]
-            v_all[at, rows] = value[:, q_cols + HD : q_cols + 2 * HD]
-            gain_ref[rows] += value[:, q_cols + 2 * HD :]
-            row = rows.stop
-        pieces = pieces[size:]
+        value = piece[...].astype(F32)
+        q_ref[:, pl.ds(pl.multiple_of(at * q_cols, LANES), q_cols)] = value[:, :q_cols]
+        k_all[at] = value[:, q_cols : q_cols + HD]
+        v_all[at] = value[:, q_cols + HD : q_cols + 2 * HD]
+        total += value[:, q_cols + 2 * HD : o_at]
+        rows = pl.ds(pl.multiple_of(at * fine, fine), fine)
+        for block in range(count):
+            o_ref[rows, block * q_cols : (block + 1) * q_cols] = value[
+                block * fine : (block + 1) * fine, o_at:
+            ]
+    gain_ref[...] = total
     for ref, both in ((k_ref, k_all), (v_ref, v_all)):
         for head in range(count // share):
             total = both[head * share]
@@ -389,8 +390,8 @@
 
 
 def in_back_kernel(
-    id_ref, dq_ref, dkv_ref, back_ref, cos_ref, sin_ref, normed_ref, x_ref, two_ref, w_ref,
-    part_ref, grad_ref, total_ref,
+    id_ref, dq_ref, dkv_ref, back_ref, cos_ref, sin_ref, normed_ref, x_ref, two_ref, o_ref,
+    w_ref, part_ref, grad_ref, qkv_all, one_all,
 ):
     at = pl.program_id(0)
     rows = dq_ref.shape[1]
@@ -402,25 +403,19 @@
     normed_grad = cols_cols(qkv_grad, w_ref[...])
     part_ref[0] = normed_grad.astype(BF)
     x = x_ref[0].astype(F32)
-    one = (normed_grad * x * norm_scale(x)).astype(BF)
-    cols = qkv_grad.shape[1]
-    lane = lax.broadcasted_iota(jnp.int32, (rows, LANES), 1)
-
-    @pl.when(at == 0)
-    def _():
-        total_ref[:, :cols] = rows_rows(normed_ref[0], qkv_grad)
-        total_ref[:, cols:] = rows_rows(one, (lane < HD).astype(BF)) + rows_rows(
-            two_ref[...], (lane >= HD).astype(BF)
-        )
-
-    @pl.when(at > 0)
-    def _():
-        total_ref[:, :cols] += rows_rows(normed_ref[0], qkv_grad)
-        total_ref[:, cols:] += rows_rows(one, (lane < HD).astype(BF))
+    mine = pl.ds(pl.multiple_of(at * rows, rows), rows)
+    qkv_all[mine] = qkv_grad
+    one_all[mine] = (normed_grad * x * norm_scale(x)).astype(BF)
 
     @pl.when(at == pl.num_programs(0) - 1)
     def _():
-        grad_ref[...] = total_ref[...].astype(BF)
+        cols = qkv_all.shape[1]
+        lane = lambda count: lax.broadcasted_iota(jnp.int32, (count, LANES), 1)
+        gains = rows_rows(one_all[...], (lane(one_all.shape[0]) < HD).astype(BF))
+        gains += rows_rows(two_ref[...], (lane(rows) >= HD).astype(BF))
+        grad_ref[:, :cols] = rows_rows(normed_ref[...], qkv_all[...]).astype(BF)
+        grad_ref[:, cols : cols + LANES] = gains.astype(BF)
+        grad_ref[:, cols + LANES :] = o_ref[...]
 
 
 def middle_kernel(part_ref, x_ref, gain_ref, mid_ref, normed_ref):
@@ -677,10 +672,10 @@
     down_rows = lax.psum_scatter(down_part, "shard", scatter_dimension=0, tiled=True)
     layer_out = (x_mid + down_rows.astype(F32)).astype(BF)
     w_down_grad = parts_rep(down_chunks, n_rep)
-    w_down_grad = tuple(
-        sum(part.astype(F32) for part in parts).astype(BF) for parts in w_down_grad
-    )
-    down_out = place(gather_rep(w_down_grad, n_rep), r)
+    w_down_grad = jnp.concatenate(
+        [sum(part.astype(F32) for part in parts).astype(BF) for parts in w_down_grad], axis=0
+    )
+    down_out = place(gather_two(w_down_grad, n_rep, cut), r)
     w_pair_grad = parts_rep(pair_chunks, n_rep)
     w_pair_grad = flat_call(
         sum_kernel,
@@ -708,6 +703,10 @@
         [part for piece in branch for part in piece],
     ).reshape(all_rows, width)
     in_grad = cols_cols(branch_all, w_o).astype(BF)
+    branch_all, in_grad = lax.optimization_barrier((branch_all, in_grad))
+    w_o_grad = rows_rows(out_in, branch_all).astype(BF)
+    w_o_grad = w_o_grad.reshape(n_shard, fine, n_rep, q_cols).transpose(0, 2, 1, 3)
+    w_o_grad = w_o_grad.reshape(width, q_cols)
     in_grad = in_grad.reshape(all_rows, n_rep, pair * fine).transpose(1, 0, 2)
     in_grad = swap(in_grad, "rep").reshape(n_rep, n_rep, rows, pair * fine)
     query_grad, kv_grad = call(
@@ -728,7 +727,7 @@
     kv_back = lax.ppermute(
         kv_grad[:, :HALO], "shard", [(i + 1, i) for i in range(n_shard - 1)]
     )
-    grad_cols = qkv_cols + LANES
+    grad_cols = qkv_cols + LANES + q_cols
     steady = lambda *dims: pl.BlockSpec(
         dims, lambda g, ids: (0,) * len(dims), pipeline_mode=pl.Buffered(1)
     )
@@ -747,9 +746,10 @@
                 block_of(HALO, LANES),
                 block_of(rows, LANES),
                 block_of(rows, LANES),
-                block_of(rows, width),
+                steady(all_rows, width),
                 block_of(rows, width),
                 steady(rows, width),
+                steady(width, q_cols),
                 steady(width, qkv_cols),
             ],
             out_specs=(
@@ -758,19 +758,18 @@
                 ),
                 pl.BlockSpec((width, grad_cols), lambda g, ids: (0, 0)),
             ),
-            scratch_shapes=[pltpu.VMEM((width, grad_cols), F32)],
+            scratch_shapes=[
+                pltpu.VMEM((all_rows, qkv_cols), BF),
+                pltpu.VMEM((all_rows, width), BF),
+            ],
         ),
         name="attn_in_back",
         compiler_params=pltpu.CompilerParams(vmem_limit_bytes=56 * 1024 * 1024),
     )(
-        ids, query_grad, kv_grad, kv_back, cosine, sine, normed_one, x_all, gain_two_rows,
-        w_qkv,
-    )
-    branch_all, _ = lax.optimization_barrier((branch_all, w_qkv_grad))
+        ids, query_grad, kv_grad, kv_back, cosine, sine,
+        normed_one.reshape(all_rows, width), x_all, gain_two_rows, w_o_grad, w_qkv,
+    )
     w_qkv_grad = lax.psum_scatter(w_qkv_grad, "shard", scatter_dimension=0, tiled=True)
-    w_o_grad = rows_rows(out_in, branch_all).astype(BF)
-    w_o_grad = lax.psum_scatter(w_o_grad, "shard", scatter_dimension=0, tiled=True)
-    o_out = place(gather_direct(w_o_grad, n_rep), r)
     one_grad = [one_grad_part[k] for k in range(n_rep)]
     one_grad = [(part[: rows // 2], part[rows // 2 :]) for part in one_grad]
     one_grad = parts_rep(one_grad, n_rep)
@@ -780,17 +779,17 @@
         shape((rows, width), BF),
         one_grad[0] + one_grad[1] + [tokens, gain_one, mid_grad],
     )
-    w_qkv_grad = gather_direct(w_qkv_grad, n_rep)
-    q_out, k_out, v_out, gain_sums = flat_call(
-        partial(qkv_kernel, share, [len(piece) for piece in w_qkv_grad]),
+    q_out, k_out, v_out, o_out, gain_sums = flat_call(
+        partial(attn_kernel, share, fine),
         ids,
         (
             shape((own, width), F32),
             shape((own, KVH * HD), F32),
             shape((own, KVH * HD), F32),
+            shape((own, width), F32),
             shape((own, LANES), F32),
         ),
-        [part for piece in w_qkv_grad for part in piece],
+        [piece[0] for piece in gather_direct(w_qkv_grad, n_rep)],
         [pltpu.VMEM((n_rep, own, HD), F32)] * 2,
     )
     return (

time: 707 us -> 713 us (level)
  waiting for transfers between devices: 337 us -> 354 us
  starting transfers between devices: 85.4 us -> 74.2 us
  local copies, waits for them, and re-layouts: 23.2 us -> 30.5 us
    ppermute x60 -> x55, waiting for transfers between devices: 254 us -> 273 us  [send(): return lax.ppermute(value, axis, pairs(count, step))]
    ppermute x60 -> x55, starting transfers between devices: 77 us -> 65.5 us  [send(): return lax.ppermute(value, axis, pairs(count, step))]
    pallas_call x4 -> x3, Pallas kernels: 17 us -> 14.2 us  [place(): pl.pallas_call(partial(place_kernel, [len(piece) for piece in pieces]), o...]
  transfers between devices with their start and end apart: 71 -> 65, of which waited for: 35 -> 31; matrix products, arithmetic and copies ran while one was open for 6% -> 8% of each run, Pallas kernels for 9% -> 9%
where the time goes in v10:
time: 713 us; the launch traced here: 702 us
  waiting for transfers between devices  354 us (50%)
  Pallas kernels  125 us (18%)
  starting transfers between devices  74.2 us (10%)
  blocking collectives  62.4 us (9%)
  local copies, waits for them, and re-layouts  30.5 us (4%)
  matrix products  26.7 us (4%)
  between operations  15 us (2%)
  other arithmetic  14.1 us (2%)
    ppermute x55, waiting for transfers between devices, send(): return lax.ppermute(value, axis, pairs(count, step))  273 us
    reduce_scatter x1, waiting for transfers between devices, body(): lax.psum_scatter(two_grad_part, 'shard', scatter_dimension=0, tiled=True)  65.7 us
    ppermute x55, starting transfers between devices, send(): return lax.ppermute(value, axis, pairs(count, step))  65.5 us
    all_to_all x3, blocking collectives, swap(): return lax.all_to_all(value, axis, split_axis=0, concat_axis=0, tiled=True)  49.1 us
    dot_general x6, matrix products, dot(): lax.dot_general(left, right, (contract, ((), ())), preferred_element_type...  26.7 us
    pallas_call x7, Pallas kernels, flat_call(): pl.pallas_call(kernel, out_shape=out_shape, in_specs=specs, scratch_shape...  25.9 us
    pallas_call x2, Pallas kernels, pair_grad(): pl.pallas_call(partial(pair_grad_kernel, fine), out_shape=(shape((blocks,...  16.4 us
  transfers between devices with their start and end apart: 65, of which 31 were waited for; matrix products, arithmetic and copies ran while one was open for 8% of the time, Pallas kernels for 9%

profile of v10, /device:TPU:0, one launch (start us, length us, event | category | flops | bytes accessed | tf_op | source)
XLA Modules:
  0.0 701.9 jit_solution(3098405623072741757)
XLA Ops:
  14.7 5.3 all-to-all-start
  20.1 13.2 %all_gather.15 = bf16[2,2048]{1,0:T(2,128)(2,1)S(1)} all-gather(bf16[2,256]{1,0:T(2,128)(2,1)S(1)} %pad_maximum_fusion.3), channel_id=1, replica_groups=mesh['rep'=4,'shard'=8] {'shard'}, dimensions={1}, use_global_device_ids=true | all-gather | bytes 9216 | tf_op jit(solution)/shard_map/all_gather | solution.py:560
  34.0 13.2 %all-to-all-done.x_ref.pos_ref = bf16[4,128,2176]{2,1,0:T(8,128)(2,1)} async-done(((bf16[4,128,2176]{2,1,0:T(8,128)(2,1)}), bf16[4,128,2176]{2,1,0:T(8,128)(2,1)}, u32[]{:S(2)}, u32[]{:S(2)}) %all-to-all-start) | async-done | bytes 2228256 | tf_op jit(solution)/shard_map/all_to_all | solution.py:43
  49.7 6.2 shard_map.203
  59.6 6.4 shard_map.204
  66.0 10.6 %all_to_all.20 = bf16[4,4,128,128]{3,2,1,0:T(8,128)(2,1)S(1)} all-to-all(bf16[4,4,128,128]{3,2,1,0:T(8,128)(2,1)} %get-tuple-element.70), channel_id=1, replica_groups=mesh['rep'=4,'shard'=8] {'rep'}, dimensions={0} | all-to-all | bytes 1048576 | tf_op jit(solution)/shard_map/all_to_all | solution.py:47
  80.6 27.8 %all_to_all.21.part_ref = bf16[4,128,2048]{2,1,0:T(8,128)(2,1)} all-to-all(bf16[4,128,2048]{2,1,0:T(8,128)(2,1)S(1)} %bitcast.65), channel_id=1, replica_groups=mesh['rep'=4,'shard'=8] {'rep'}, dimensions={0} | all-to-all | bytes 4194304 | tf_op jit(solution)/shard_map/all_to_all | solution.py:47
  118.6 5.6 collective-permute-start.2
  128.8 10.4 %collective-permute-done.2.refs_2_ = bf16[2,64,704]{2,1,0:T(8,128)(2,1)S(1)} collective-permute-done((bf16[2,64,704]{2,1,0:T(8,128)(2,1)}, bf16[2,64,704]{2,1,0:T(8,128)(2,1)S(1)}, u32[]{:S(2)}, u32[]{:S(2)}) %collective-permute-start.2) | collective-permute-done | bytes 180256 | tf_op jit(solution)/shard_map/ppermute | solution.py:55
  139.7 8.7 %collective-permute-done.3.refs_3_ = bf16[2,64,704]{2,1,0:T(8,128)(2,1)S(1)} collective-permute-done((bf16[2,64,704]{2,1,0:T(8,128)(2,1)}, bf16[2,64,704]{2,1,0:T(8,128)(2,1)S(1)}, u32[]{:S(2)}, u32[]{:S(2)}) %collective-permute-start.3) | collective-permute-done | bytes 180256 | tf_op jit(solution)/shard_map/ppermute | solution.py:55
  150.4 9.4 %collective-permute-done.6.refs_6_ = bf16[2,64,704]{2,1,0:T(8,128)(2,1)S(1)} collective-permute-done((bf16[2,64,704]{2,1,0:T(8,128)(2,1)}, bf16[2,64,704]{2,1,0:T(8,128)(2,1)S(1)}, u32[]{:S(2)}, u32[]{:S(2)}) %collective-permute-start.6) | collective-permute-done | bytes 180256 | tf_op jit(solution)/shard_map/ppermute | solution.py:55
  159.8 7.0 collective-permute-done.7.refs_7_
  174.2 16.6 %collective-permute-done.8.refs_2_ = bf16[8,64,704]{2,1,0:T(8,128)(2,1)S(1)} collective-permute-done((bf16[8,64,704]{2,1,0:T(8,128)(2,1)}, bf16[8,64,704]{2,1,0:T(8,128)(2,1)S(1)}, u32[]{:S(2)}, u32[]{:S(2)}) %collective-permute-start.8) | collective-permute-done | bytes 720928 | tf_op jit(solution)/shard_map/ppermute | solution.py:55
  192.8 14.8 %collective-permute-done.9.refs_3_ = bf16[8,64,704]{2,1,0:T(8,128)(2,1)S(1)} collective-permute-done((bf16[8,64,704]{2,1,0:T(8,128)(2,1)}, bf16[8,64,704]{2,1,0:T(8,128)(2,1)S(1)}, u32[]{:S(2)}, u32[]{:S(2)}) %collective-permute-start.9) | collective-permute-done | bytes 720928 | tf_op jit(solution)/shard_map/ppermute | solution.py:55
  207.8 16.7 %collective-permute-done.12.refs_6_ = bf16[8,64,704]{2,1,0:T(8,128)(2,1)S(1)} collective-permute-done((bf16[8,64,704]{2,1,0:T(8,128)(2,1)S(1)}, bf16[8,64,704]{2,1,0:T(8,128)(2,1)S(1)}, u32[]{:S(2)}, u32[]{:S(2)}) %collective-permute-start.12) | collective-permute-done | bytes 720928 | tf_op jit(solution)/shard_map/ppermute | solution.py:55
  226.3 5.8 shard_map.207
  232.1 7.3 %fusion.7.back_ref = f32[1024,704]{1,0:T(8,128)} fusion(bf16[1024,2048]{1,0:T(8,128)(2,1)} %all-gather.11.cloned.1.call-done, bf16[704,2048]{1,0:T(8,128)(2,1)S(1)} %copy-done), kind=kOutput, calls=%fused_computation.51 | convolution fusion | flops 2952790016 | bytes 9961472 | tf_op jit(solution)/shard_map/dot_general | solution.py:26
  239.4 12.1 %shard_map.208 = (bf16[1024,704]{1,0:T(8,128)(2,1)}, bf16[1024,704]{1,0:T(8,128)(2,1)}, bf16[1024,704]{1,0:T(8,128)(2,1)}) custom-call(bf16[1024,2048]{1,0:T(8,128)(2,1)} %all-gather.9.cloned.1.call-done.x_ref, f32[1024,704]{1,0:T(8,128)} %fusion.7.back_ref, bf16[2,2048,704]{2,1,0:T(8,128)(2,1)} %bitcast.56), custom_call_target="tpu_custom_call" | custom-call | tf_op jit(solution)/shard_map/pallas_call | solution.py:633
  251.5 8.2 %shard_map.209 = (bf16[8,64,704]{2,1,0:T(8,128)(2,1)}, bf16[8,64,704]{2,1,0:T(8,128)(2,1)}, bf16[8,64,704]{2,1,0:T(8,128)(2,1)}, bf16[8,64,704]{2,1,0:T(8,128)(2,1)}) custom-call(s32[2]{0:T(128)} %pad_add_fusion.id_ref, bf16[1024,2048]{1,0:T(8,128)(2,1)} %all-gather.9.cloned.1.call-done.x_ref, bf16[1024,704]{1,0:T(8,128)(2,1)} %get-tuple-element.89.grad_ref.gate_ref), custom_call_target="tpu_custom_call" | custom-call | tf_op jit(solution)/shard_map/pallas_call | solution.py:259
  259.7 11.4 %shard_map.210 = bf16[1024,2048]{1,0:T(8,128)(2,1)} custom-call(bf16[1024,704]{1,0:T(8,128)(2,1)} %get-tuple-element.89.grad_ref.gate_ref, bf16[1024,704]{1,0:T(8,128)(2,1)} %get-tuple-element.90.up_ref.grad_ref, bf16[2,2048,704]{2,1,0:T(8,128)(2,1)} %bitcast.57), custom_call_target="tpu_custom_call" | custom-call | tf_op jit(solution)/shard_map/pallas_call | solution.py:642
  271.1 65.7 %reduce-scatter.6.cloned.1.call-done.grad_ref = bf16[128,2048]{1,0:T(8,128)(2,1)} async-done(((bf16[1024,2048]{1,0:T(8,128)(2,1)}), bf16[128,2048]{1,0:T(8,128)(2,1)}) %reduce-scatter.6.cloned.1.call-update) | async-done | bytes 524304 | tf_op jit(solution)/shard_map/reduce_scatter | solution.py:650
  336.9 3.6 shard_map.212
  343.4 9.0 %collective-permute-done.14.refs_1_ = bf16[128,2048]{1,0:T(8,128)(2,1)S(1)} collective-permute-done((bf16[128,2048]{1,0:T(8,128)(2,1)}, bf16[128,2048]{1,0:T(8,128)(2,1)S(1)}, u32[]{:S(2)}, u32[]{:S(2)}) %collective-permute-start.14) | collective-permute-done | bytes 524320 | tf_op jit(solution)/shard_map/ppermute | solution.py:55
  355.6 3.7 collective-permute-done.16.refs_3_
  368.2 10.7 %all_to_all.22 = bf16[4,512,128]{2,1,0:T(8,128)(2,1)} all-to-all(bf16[4,512,128]{2,1,0:T(8,128)(2,1)S(1)} %bitcast_bitcast_fusion), channel_id=1, replica_groups=mesh['rep'=4,'shard'=8] {'rep'}, dimensions={0} | all-to-all | bytes 1048576 | tf_op jit(solution)/shard_map/all_to_all | solution.py:47
  379.0 8.4 %shard_map.214 = (bf16[4,128,512]{2,1,0:T(8,128)(2,1)}, f32[4,192,128]{2,1,0:T(8,128)}) custom-call(bf16[4,4,128,128]{3,2,1,0:T(8,128)(2,1)} %bitcast.62, f32[4,8,128,192]{3,2,1,0:T(8,128)} %get-tuple-element.95.probs_ref, bf16[4,128,512]{2,1,0:T(8,128)(2,1)} %get-tuple-element.68.q_ref, bf16[4,128,128]{2,1,0:T(8,128)(2,1)} %get-tuple-element.69.own_ref, ...), custom_call_target="tpu_custom_call" | custom-call | tf_op jit(solution)/shard_map/pallas_call | solution.py:712
  392.2 4.5 reshape.115
  400.8 13.8 %attn_in_back.1 = (bf16[4,128,2048]{2,1,0:T(8,128)(2,1)}, bf16[2048,1280]{1,0:T(8,128)(2,1)}) custom-call(s32[2]{0:T(128)} %pad_add_fusion.id_ref, bf16[4,128,512]{2,1,0:T(8,128)(2,1)} %get-tuple-element.96.dq_ref, f32[4,192,128]{2,1,0:T(8,128)} %get-tuple-element.97.dkv_ref, f32[4,64,128]{2,1,0:T(8,128)} %copy-done.43, ...), custom_call_target="tpu_custom_call" | custom-call | tf_op jit(solution)/shard_map/attn_in_back/pallas_call | solution.py:737
  414.8 8.3 %shard_map.211 = (bf16[8,64,704]{2,1,0:T(8,128)(2,1)}, bf16[8,64,704]{2,1,0:T(8,128)(2,1)}, bf16[8,64,704]{2,1,0:T(8,128)(2,1)}, bf16[8,64,704]{2,1,0:T(8,128)(2,1)}) custom-call(s32[2]{0:T(128)} %pad_add_fusion.id_ref, bf16[1024,2048]{1,0:T(8,128)(2,1)} %all-gather.9.cloned.1.call-done.x_ref, bf16[1024,704]{1,0:T(8,128)(2,1)} %get-tuple-element.90.up_ref.grad_ref), custom_call_target="tpu_custom_call" | custom-call | tf_op jit(solution)/shard_map/pallas_call | solution.py:259
  423.1 5.0 convolution_convert_fusion
  428.1 5.9 convolution_convert_fusion.1
  442.5 4.2 collective-permute-done.51
  449.0 34.1 %collective-permute-done.48 = bf16[96,2048]{1,0:T(8,128)(2,1)S(1)} collective-permute-done((bf16[96,2048]{1,0:T(8,128)(2,1)S(1)}, bf16[96,2048]{1,0:T(8,128)(2,1)S(1)}, u32[]{:S(2)}, u32[]{:S(2)}) %collective-permute-start.48) | collective-permute-done | bytes 393248 | tf_op jit(solution)/shard_map/ppermute | solution.py:55
  488.9 6.2 collective-permute-done.47
  496.2 4.9 collective-permute-done.52
  502.6 12.8 %collective-permute-done.49 = bf16[96,2048]{1,0:T(8,128)(2,1)S(1)} collective-permute-done((bf16[96,2048]{1,0:T(8,128)(2,1)S(1)}, bf16[96,2048]{1,0:T(8,128)(2,1)S(1)}, u32[]{:S(2)}, u32[]{:S(2)}) %collective-permute-start.49) | collective-permute-done | bytes 393248 | tf_op jit(solution)/shard_map/ppermute | solution.py:55
  516.6 14.1 %collective-permute-done.30.refs_2_ = bf16[8,64,704]{2,1,0:T(8,128)(2,1)S(1)} collective-permute-done((bf16[8,64,704]{2,1,0:T(8,128)(2,1)S(1)}, bf16[8,64,704]{2,1,0:T(8,128)(2,1)S(1)}, u32[]{:S(2)}, u32[]{:S(2)}) %collective-permute-start.30) | collective-permute-done | bytes 720928 | tf_op jit(solution)/shard_map/ppermute | solution.py:55
  532.5 3.9 shard_map.217
  543.0 9.2 %collective-permute-done.35.refs_2_ = bf16[2,64,704]{2,1,0:T(8,128)(2,1)S(1)} collective-permute-done((bf16[2,64,704]{2,1,0:T(8,128)(2,1)}, bf16[2,64,704]{2,1,0:T(8,128)(2,1)S(1)}, u32[]{:S(2)}, u32[]{:S(2)}) %collective-permute-start.35) | collective-permute-done | bytes 180256 | tf_op jit(solution)/shard_map/ppermute | solution.py:55
  558.4 10.1 %collective-permute-done.38.refs_5_ = bf16[2,64,704]{2,1,0:T(8,128)(2,1)S(1)} collective-permute-done((bf16[2,64,704]{2,1,0:T(8,128)(2,1)}, bf16[2,64,704]{2,1,0:T(8,128)(2,1)S(1)}, u32[]{:S(2)}, u32[]{:S(2)}) %collective-permute-start.38) | collective-permute-done | bytes 180256 | tf_op jit(solution)/shard_map/ppermute | solution.py:55
  577.5 19.9 %collective-permute-done.56.refs_4_ = bf16[80,2048]{1,0:T(8,128)(2,1)S(1)} collective-permute-done((bf16[80,2048]{1,0:T(8,128)(2,1)S(1)}, bf16[80,2048]{1,0:T(8,128)(2,1)S(1)}, u32[]{:S(2)}, u32[]{:S(2)}) %collective-permute-start.56) | collective-permute-done | bytes 327712 | tf_op jit(solution)/shard_map/ppermute | solution.py:55
  602.2 13.4 %collective-permute-done.55.refs_3_ = bf16[96,2048]{1,0:T(8,128)(2,1)S(1)} collective-permute-done((bf16[96,2048]{1,0:T(8,128)(2,1)S(1)}, bf16[96,2048]{1,0:T(8,128)(2,1)S(1)}, u32[]{:S(2)}, u32[]{:S(2)}) %collective-permute-start.55) | collective-permute-done | bytes 393248 | tf_op jit(solution)/shard_map/ppermute | solution.py:55
  617.6 4.7 shard_map.221
  622.3 8.9 %collective-permute-done.43.refs_3_ = bf16[64,5632]{1,0:T(8,128)(2,1)} collective-permute-done((bf16[64,5632]{1,0:T(8,128)(2,1)}, bf16[64,5632]{1,0:T(8,128)(2,1)}, u32[]{:S(2)}, u32[]{:S(2)}) %collective-permute-start.43) | collective-permute-done | bytes 720928 | tf_op jit(solution)/shard_map/ppermute | solution.py:55
  631.2 4.6 shard_map.219
  635.8 4.9 shard_map.220
  654.3 30.2 %collective-permute-done.21.refs_2_ = bf16[64,2048]{1,0:T(8,128)(2,1)} collective-permute-done((bf16[64,2048]{1,0:T(8,128)(2,1)}, bf16[64,2048]{1,0:T(8,128)(2,1)}, u32[]{:S(2)}, u32[]{:S(2)}) %collective-permute-start.21) | collective-permute-done | bytes 262176 | tf_op jit(solution)/shard_map/ppermute | solution.py:55
  688.9 4.2 shard_map.216
  (262 shorter events, 141.3 us)
Async XLA Ops:
  7.2 42.5 %all-gather.5.cloned.1.call-start = ((), (), s32[]{:S(2)}) async-start(), calls=%async_computation.7 | async-start | bytes 2949120 | tf_op jit(solution)/shard_map/all_gather | solution.py:555
  10.2 67.3 %all-gather.7.cloned.1.call-start = ((), (), s32[]{:S(2)}) async-start(), calls=%async_computation.8 | async-start | bytes 2359296 | tf_op jit(solution)/shard_map/all_gather | solution.py:556
  12.0 220.1 %all-gather.11.cloned.1.call-start = ((), (), s32[]{:S(2)}) async-start(), calls=%async_computation.10 | async-start | bytes 4718592 | tf_op jit(solution)/shard_map/all_gather | solution.py:581
  14.7 32.5 %all-to-all-start = ((bf16[4,128,2176]{2,1,0:T(8,128)(2,1)}), bf16[4,128,2176]{2,1,0:T(8,128)(2,1)}, u32[]{:S(2)}, u32[]{:S(2)}) async-start(bf16[4,128,2176]{2,1,0:T(8,128)(2,1)} %broadcast_in_dim.16), calls=%async_computation | async-start | bytes 4456448 | tf_op jit(solution)/shard_map/all_to_all | solution.py:43
  20.1 219.3 %all-gather.9.cloned.1.call-start = ((), (), s32[]{:S(2)}) async-start(), calls=%async_computation.9 | async-start | bytes 4718592 | tf_op jit(solution)/shard_map/all_gather | solution.py:627
  111.7 225.1 %reduce-scatter.6.cloned.1.call-start = ((), (), s32[]{:S(2)}) async-start(), calls=%async_computation.12 | async-start | bytes 4718592 | tf_op jit(solution)/shard_map/reduce_scatter | solution.py:650
  118.6 20.6 %collective-permute-start.2 = (bf16[2,64,704]{2,1,0:T(8,128)(2,1)}, bf16[2,64,704]{2,1,0:T(8,128)(2,1)S(1)}, u32[]{:S(2)}, u32[]{:S(2)}) collective-permute-start(bf16[2,64,704]{2,1,0:T(8,128)(2,1)} %get-tuple-element.77), channel_id=1, source_target_pairs={{0,2},{1,3},{2,0},{3,1},{4,6},{5,7},{6,4},{7,5},{8,10},{9,11},{10,... | collective-permute-start | bytes 540680 | tf_op jit(solution)/shard_map/ppermute | solution.py:55
  124.2 24.2 %collective-permute-start.3 = (bf16[2,64,704]{2,1,0:T(8,128)(2,1)}, bf16[2,64,704]{2,1,0:T(8,128)(2,1)S(1)}, u32[]{:S(2)}, u32[]{:S(2)}) collective-permute-start(bf16[2,64,704]{2,1,0:T(8,128)(2,1)} %get-tuple-element.78), channel_id=1, source_target_pairs={{0,3},{1,2},{2,1},{3,0},{4,7},{5,6},{6,5},{7,4},{8,11},{9,10},{10,... | collective-permute-start | bytes 540680 | tf_op jit(solution)/shard_map/ppermute | solution.py:55
  124.4 24.1 %collective-permute-start.4 = (bf16[2,64,704]{2,1,0:T(8,128)(2,1)}, bf16[2,64,704]{2,1,0:T(8,128)(2,1)S(1)}, u32[]{:S(2)}, u32[]{:S(2)}) collective-permute-start(bf16[2,64,704]{2,1,0:T(8,128)(2,1)} %get-tuple-element.79), channel_id=1, source_target_pairs={{0,4},{1,5},{2,6},{3,7},{4,0},{5,1},{6,2},{7,3},{8,12},{9,13},{10,... | collective-permute-start | bytes 540680 | tf_op jit(solution)/shard_map/ppermute | solution.py:55
  126.7 23.7 %collective-permute-start.5 = (bf16[2,64,704]{2,1,0:T(8,128)(2,1)}, bf16[2,64,704]{2,1,0:T(8,128)(2,1)S(1)}, u32[]{:S(2)}, u32[]{:S(2)}) collective-permute-start(bf16[2,64,704]{2,1,0:T(8,128)(2,1)} %get-tuple-element.80), channel_id=1, source_target_pairs={{0,5},{1,4},{2,7},{3,6},{4,1},{5,0},{6,3},{7,2},{8,13},{9,12},{10,... | collective-permute-start | bytes 540680 | tf_op jit(solution)/shard_map/ppermute | solution.py:55
  126.8 33.1 %collective-permute-start.6 = (bf16[2,64,704]{2,1,0:T(8,128)(2,1)}, bf16[2,64,704]{2,1,0:T(8,128)(2,1)S(1)}, u32[]{:S(2)}, u32[]{:S(2)}) collective-permute-start(bf16[2,64,704]{2,1,0:T(8,128)(2,1)} %get-tuple-element.81), channel_id=1, source_target_pairs={{0,6},{1,7},{2,4},{3,5},{4,2},{5,3},{6,0},{7,1},{8,14},{9,15},{10,... | collective-permute-start | bytes 540680 | tf_op jit(solution)/shard_map/ppermute | solution.py:55
  139.2 27.6 %collective-permute-start.7 = (bf16[2,64,704]{2,1,0:T(8,128)(2,1)}, bf16[2,64,704]{2,1,0:T(8,128)(2,1)S(1)}, u32[]{:S(2)}, u32[]{:S(2)}) collective-permute-start(bf16[2,64,704]{2,1,0:T(8,128)(2,1)} %get-tuple-element.82), channel_id=1, source_target_pairs={{0,7},{1,6},{2,5},{3,4},{4,3},{5,2},{6,1},{7,0},{8,15},{9,14},{10,... | collective-permute-start | bytes 540680 | tf_op jit(solution)/shard_map/ppermute | solution.py:55
  170.2 20.6 %collective-permute-start.8 = (bf16[8,64,704]{2,1,0:T(8,128)(2,1)}, bf16[8,64,704]{2,1,0:T(8,128)(2,1)S(1)}, u32[]{:S(2)}, u32[]{:S(2)}) collective-permute-start(bf16[8,64,704]{2,1,0:T(8,128)(2,1)} %get-tuple-element.83.refs_0_), channel_id=1, source_target_pairs={{0,8},{8,0},{16,24},{24,16},{1,9},{9,1},{17,25},{25,17},{2,10},{10... | collective-permute-start | bytes 2162696 | tf_op jit(solution)/shard_map/ppermute | solution.py:55
  170.3 20.6 %collective-permute-start.11 = (bf16[8,64,704]{2,1,0:T(8,128)(2,1)}, bf16[8,64,704]{2,1,0:T(8,128)(2,1)S(1)}, u32[]{:S(2)}, u32[]{:S(2)}) collective-permute-start(bf16[8,64,704]{2,1,0:T(8,128)(2,1)} %get-tuple-element.84.refs_1_), channel_id=1, source_target_pairs={{0,16},{8,24},{16,0},{24,8},{1,17},{9,25},{17,1},{25,9},{2,18},{10... | collective-permute-start | bytes 2162696 | tf_op jit(solution)/shard_map/ppermute | solution.py:55
  170.3 37.3 %collective-permute-start.9 = (bf16[8,64,704]{2,1,0:T(8,128)(2,1)}, bf16[8,64,704]{2,1,0:T(8,128)(2,1)S(1)}, u32[]{:S(2)}, u32[]{:S(2)}) collective-permute-start(bf16[8,64,704]{2,1,0:T(8,128)(2,1)} %get-tuple-element.84.refs_1_), channel_id=1, source_target_pairs={{0,8},{8,0},{16,24},{24,16},{1,9},{9,1},{17,25},{25,17},{2,10},{10... | collective-permute-start | bytes 2162696 | tf_op jit(solution)/shard_map/ppermute | solution.py:55
  172.4 35.5 %collective-permute-start.10 = (bf16[8,64,704]{2,1,0:T(8,128)(2,1)}, bf16[8,64,704]{2,1,0:T(8,128)(2,1)S(1)}, u32[]{:S(2)}, u32[]{:S(2)}) collective-permute-start(bf16[8,64,704]{2,1,0:T(8,128)(2,1)} %get-tuple-element.83.refs_0_), channel_id=1, source_target_pairs={{0,16},{8,24},{16,0},{24,8},{1,17},{9,25},{17,1},{25,9},{2,18},{10... | collective-permute-start | bytes 2162696 | tf_op jit(solution)/shard_map/ppermute | solution.py:55
  190.8 33.7 %collective-permute-start.12 = (bf16[8,64,704]{2,1,0:T(8,128)(2,1)S(1)}, bf16[8,64,704]{2,1,0:T(8,128)(2,1)S(1)}, u32[]{:S(2)}, u32[]{:S(2)}) collective-permute-start(bf16[8,64,704]{2,1,0:T(8,128)(2,1)S(1)} %collective-permute-done.8.refs_2_), channel_id=1, source_target_pairs={{0,16},{8,24},{16,0},{24,8},{1,17},{9,25},{17,1},{25,9},{2,18},{10... | collective-permute-start | bytes 2162696 | tf_op jit(solution)/shard_map/ppermute | solution.py:55
  191.0 33.5 %collective-permute-start.13 = (bf16[8,64,704]{2,1,0:T(8,128)(2,1)S(1)}, bf16[8,64,704]{2,1,0:T(8,128)(2,1)S(1)}, u32[]{:S(2)}, u32[]{:S(2)}) collective-permute-start(bf16[8,64,704]{2,1,0:T(8,128)(2,1)S(1)} %collective-permute-done.11.refs_5_), channel_id=1, source_target_pairs={{0,8},{8,0},{16,24},{24,16},{1,9},{9,1},{17,25},{25,17},{2,10},{10... | collective-permute-start | bytes 2162696 | tf_op jit(solution)/shard_map/ppermute | solution.py:55
  271.1 371.7 %reduce-scatter.8.cloned.1.call-start = ((), (), s32[]{:S(2)}) async-start(), calls=%async_computation.13 | async-start | bytes 5898240 | tf_op jit(solution)/shard_map/reduce_scatter | solution.py:772
  414.6 237.5 %reduce-scatter.4.cloned.1.call-start = ((), (), s32[]{:S(2)}) async-start(), calls=%async_computation.11 | async-start | bytes 4718592 | tf_op jit(solution)/shard_map/reduce_scatter | solution.py:672
  437.3 79.3 %collective-permute-start.28 = (bf16[8,64,704]{2,1,0:T(8,128)(2,1)}, bf16[8,64,704]{2,1,0:T(8,128)(2,1)S(1)}, u32[]{:S(2)}, u32[]{:S(2)}) collective-permute-start(bf16[8,64,704]{2,1,0:T(8,128)(2,1)} %get-tuple-element.109), channel_id=1, source_target_pairs={{0,8},{8,0},{16,24},{24,16},{1,9},{9,1},{17,25},{25,17},{2,10},{10... | collective-permute-start | bytes 2162696 | tf_op jit(solution)/shard_map/ppermute | solution.py:55
  437.7 46.9 %collective-permute-start.29 = (bf16[8,64,704]{2,1,0:T(8,128)(2,1)}, bf16[8,64,704]{2,1,0:T(8,128)(2,1)S(1)}, u32[]{:S(2)}, u32[]{:S(2)}) collective-permute-start(bf16[8,64,704]{2,1,0:T(8,128)(2,1)} %get-tuple-element.111), channel_id=1, source_target_pairs={{0,8},{8,0},{16,24},{24,16},{1,9},{9,1},{17,25},{25,17},{2,10},{10... | collective-permute-start | bytes 2162696 | tf_op jit(solution)/shard_map/ppermute | solution.py:55
  439.3 47.2 %collective-permute-start.32 = (bf16[8,64,704]{2,1,0:T(8,128)(2,1)}, bf16[8,64,704]{2,1,0:T(8,128)(2,1)S(1)}, u32[]{:S(2)}, u32[]{:S(2)}) collective-permute-start(bf16[8,64,704]{2,1,0:T(8,128)(2,1)} %get-tuple-element.114), channel_id=1, source_target_pairs={{0,16},{8,24},{16,0},{24,8},{1,17},{9,25},{17,1},{25,9},{2,18},{10... | collective-permute-start | bytes 2162696 | tf_op jit(solution)/shard_map/ppermute | solution.py:55
  440.4 47.4 %collective-permute-start.50 = (bf16[80,2048]{1,0:T(8,128)(2,1)S(1)}, bf16[80,2048]{1,0:T(8,128)(2,1)S(1)}, u32[]{:S(2)}, u32[]{:S(2)}) collective-permute-start(bf16[80,2048]{1,0:T(8,128)(2,1)S(1)} %get-tuple-element.129), channel_id=1, source_target_pairs={{0,16},{8,24},{16,0},{24,8},{1,17},{9,25},{17,1},{25,9},{2,18},{10... | collective-permute-start | bytes 983048 | tf_op jit(solution)/shard_map/ppermute | solution.py:55
  446.8 36.3 %collective-permute-start.48 = (bf16[96,2048]{1,0:T(8,128)(2,1)S(1)}, bf16[96,2048]{1,0:T(8,128)(2,1)S(1)}, u32[]{:S(2)}, u32[]{:S(2)}) collective-permute-start(bf16[96,2048]{1,0:T(8,128)(2,1)S(1)} %get-tuple-element.128), channel_id=1, source_target_pairs={{0,8},{8,0},{16,24},{24,16},{1,9},{9,1},{17,25},{25,17},{2,10},{10... | collective-permute-start | bytes 1179656 | tf_op jit(solution)/shard_map/ppermute | solution.py:55
  486.5 30.1 %collective-permute-start.31 = (bf16[8,64,704]{2,1,0:T(8,128)(2,1)S(1)}, bf16[8,64,704]{2,1,0:T(8,128)(2,1)S(1)}, u32[]{:S(2)}, u32[]{:S(2)}) collective-permute-start(bf16[8,64,704]{2,1,0:T(8,128)(2,1)S(1)} %copy-done.46), channel_id=1, source_target_pairs={{0,16},{8,24},{16,0},{24,8},{1,17},{9,25},{17,1},{25,9},{2,18},{10... | collective-permute-start | bytes 2162696 | tf_op jit(solution)/shard_map/ppermute | solution.py:55
  487.9 27.5 %collective-permute-start.49 = (bf16[96,2048]{1,0:T(8,128)(2,1)S(1)}, bf16[96,2048]{1,0:T(8,128)(2,1)S(1)}, u32[]{:S(2)}, u32[]{:S(2)}) collective-permute-start(bf16[96,2048]{1,0:T(8,128)(2,1)S(1)} %add_convert_fusion.4), channel_id=1, source_target_pairs={{0,16},{8,24},{16,0},{24,8},{1,17},{9,25},{17,1},{25,9},{2,18},{10... | collective-permute-start | bytes 1179656 | tf_op jit(solution)/shard_map/ppermute | solution.py:55
  495.1 35.7 %collective-permute-start.30 = (bf16[8,64,704]{2,1,0:T(8,128)(2,1)S(1)}, bf16[8,64,704]{2,1,0:T(8,128)(2,1)S(1)}, u32[]{:S(2)}, u32[]{:S(2)}) collective-permute-start(bf16[8,64,704]{2,1,0:T(8,128)(2,1)S(1)} %add_convert_fusion.1), channel_id=1, source_target_pairs={{0,16},{8,24},{16,0},{24,8},{1,17},{9,25},{17,1},{25,9},{2,18},{10... | collective-permute-start | bytes 2162696 | tf_op jit(solution)/shard_map/ppermute | solution.py:55
  501.1 29.6 %collective-permute-start.33 = (bf16[8,64,704]{2,1,0:T(8,128)(2,1)S(1)}, bf16[8,64,704]{2,1,0:T(8,128)(2,1)S(1)}, u32[]{:S(2)}, u32[]{:S(2)}) collective-permute-start(bf16[8,64,704]{2,1,0:T(8,128)(2,1)S(1)} %add_convert_fusion), channel_id=1, source_target_pairs={{0,8},{8,0},{16,24},{24,16},{1,9},{9,1},{17,25},{25,17},{2,10},{10... | collective-permute-start | bytes 2162696 | tf_op jit(solution)/shard_map/ppermute | solution.py:55
  539.7 34.2 %collective-permute-start.54 = (bf16[176,2048]{1,0:T(8,128)(2,1)S(1)}, bf16[176,2048]{1,0:T(8,128)(2,1)S(1)}, u32[]{:S(2)}, u32[]{:S(2)}) collective-permute-start(bf16[176,2048]{1,0:T(8,128)(2,1)S(1)} %pad_maximum_fusion.refs_0_), channel_id=1, source_target_pairs={{0,16},{8,24},{16,0},{24,8},{1,17},{9,25},{17,1},{25,9},{2,18},{10... | collective-permute-start | bytes 2162696 | tf_op jit(solution)/shard_map/ppermute | solution.py:55
  540.6 17.1 %collective-permute-start.37 = (bf16[2,64,704]{2,1,0:T(8,128)(2,1)}, bf16[2,64,704]{2,1,0:T(8,128)(2,1)S(1)}, u32[]{:S(2)}, u32[]{:S(2)}) collective-permute-start(bf16[2,64,704]{2,1,0:T(8,128)(2,1)} %get-tuple-element.119), channel_id=1, source_target_pairs={{0,4},{1,5},{2,6},{3,7},{4,0},{5,1},{6,2},{7,3},{8,12},{9,13},{10,... | collective-permute-start | bytes 540680 | tf_op jit(solution)/shard_map/ppermute | solution.py:55
  542.9 25.5 %collective-permute-start.38 = (bf16[2,64,704]{2,1,0:T(8,128)(2,1)}, bf16[2,64,704]{2,1,0:T(8,128)(2,1)S(1)}, u32[]{:S(2)}, u32[]{:S(2)}) collective-permute-start(bf16[2,64,704]{2,1,0:T(8,128)(2,1)} %get-tuple-element.120), channel_id=1, source_target_pairs={{0,5},{1,4},{2,7},{3,6},{4,1},{5,0},{6,3},{7,2},{8,13},{9,12},{10,... | collective-permute-start | bytes 540680 | tf_op jit(solution)/shard_map/ppermute | solution.py:55
  557.6 18.5 %collective-permute-start.53 = (bf16[176,2048]{1,0:T(8,128)(2,1)S(1)}, bf16[176,2048]{1,0:T(8,128)(2,1)S(1)}, u32[]{:S(2)}, u32[]{:S(2)}) collective-permute-start(bf16[176,2048]{1,0:T(8,128)(2,1)S(1)} %pad_maximum_fusion.refs_0_), channel_id=1, source_target_pairs={{0,8},{8,0},{16,24},{24,16},{1,9},{9,1},{17,25},{25,17},{2,10},{10... | collective-permute-start | bytes 2162696 | tf_op jit(solution)/shard_map/ppermute | solution.py:55
  572.0 26.5 %collective-permute-start.41 = (bf16[64,5632]{1,0:T(8,128)(2,1)}, bf16[64,5632]{1,0:T(8,128)(2,1)}, u32[]{:S(2)}, u32[]{:S(2)}) collective-permute-start(bf16[64,5632]{1,0:T(8,128)(2,1)} %get-tuple-element.123.refs_0_), channel_id=1, source_target_pairs={{0,8},{8,0},{16,24},{24,16},{1,9},{9,1},{17,25},{25,17},{2,10},{10... | collective-permute-start | bytes 2162696 | tf_op jit(solution)/shard_map/ppermute | solution.py:55
  573.2 26.9 %collective-permute-start.45 = (bf16[64,5632]{1,0:T(8,128)(2,1)}, bf16[64,5632]{1,0:T(8,128)(2,1)S(1)}, u32[]{:S(2)}, u32[]{:S(2)}) collective-permute-start(bf16[64,5632]{1,0:T(8,128)(2,1)} %get-tuple-element.124.refs_0_), channel_id=1, source_target_pairs={{0,16},{8,24},{16,0},{24,8},{1,17},{9,25},{17,1},{25,9},{2,18},{10... | collective-permute-start | bytes 2162696 | tf_op jit(solution)/shard_map/ppermute | solution.py:55
  573.9 23.5 %collective-permute-start.56 = (bf16[80,2048]{1,0:T(8,128)(2,1)S(1)}, bf16[80,2048]{1,0:T(8,128)(2,1)S(1)}, u32[]{:S(2)}, u32[]{:S(2)}) collective-permute-start(bf16[80,2048]{1,0:T(8,128)(2,1)S(1)} %slice.120), channel_id=1, source_target_pairs={{0,8},{8,0},{16,24},{24,16},{1,9},{9,1},{17,25},{25,17},{2,10},{10... | collective-permute-start | bytes 983048 | tf_op jit(solution)/shard_map/ppermute | solution.py:55
  575.3 41.1 %collective-permute-start.42 = (bf16[64,5632]{1,0:T(8,128)(2,1)}, bf16[64,5632]{1,0:T(8,128)(2,1)}, u32[]{:S(2)}, u32[]{:S(2)}) collective-permute-start(bf16[64,5632]{1,0:T(8,128)(2,1)} %get-tuple-element.123.refs_0_), channel_id=1, source_target_pairs={{0,16},{8,24},{16,0},{24,8},{1,17},{9,25},{17,1},{25,9},{2,18},{10... | collective-permute-start | bytes 2162696 | tf_op jit(solution)/shard_map/ppermute | solution.py:55
  576.2 39.4 %collective-permute-start.55 = (bf16[96,2048]{1,0:T(8,128)(2,1)S(1)}, bf16[96,2048]{1,0:T(8,128)(2,1)S(1)}, u32[]{:S(2)}, u32[]{:S(2)}) collective-permute-start(bf16[96,2048]{1,0:T(8,128)(2,1)S(1)} %slice.119), channel_id=1, source_target_pairs={{0,16},{8,24},{16,0},{24,8},{1,17},{9,25},{17,1},{25,9},{2,18},{10... | collective-permute-start | bytes 1179656 | tf_op jit(solution)/shard_map/ppermute | solution.py:55
  597.4 38.5 %collective-permute-start.44 = (bf16[64,5632]{1,0:T(8,128)(2,1)}, bf16[64,5632]{1,0:T(8,128)(2,1)}, u32[]{:S(2)}, u32[]{:S(2)}) collective-permute-start(bf16[64,5632]{1,0:T(8,128)(2,1)} %get-tuple-element.124.refs_0_), channel_id=1, source_target_pairs={{0,8},{8,0},{16,24},{24,16},{1,9},{9,1},{17,25},{25,17},{2,10},{10... | collective-permute-start | bytes 2162696 | tf_op jit(solution)/shard_map/ppermute | solution.py:55
  598.5 32.7 %collective-permute-start.43 = (bf16[64,5632]{1,0:T(8,128)(2,1)}, bf16[64,5632]{1,0:T(8,128)(2,1)}, u32[]{:S(2)}, u32[]{:S(2)}) collective-permute-start(bf16[64,5632]{1,0:T(8,128)(2,1)} %collective-permute-done.41.refs_1_), channel_id=1, source_target_pairs={{0,16},{8,24},{16,0},{24,8},{1,17},{9,25},{17,1},{25,9},{2,18},{10... | collective-permute-start | bytes 2162696 | tf_op jit(solution)/shard_map/ppermute | solution.py:55
  600.2 35.7 %collective-permute-start.46 = (bf16[64,5632]{1,0:T(8,128)(2,1)S(1)}, bf16[64,5632]{1,0:T(8,128)(2,1)}, u32[]{:S(2)}, u32[]{:S(2)}) collective-permute-start(bf16[64,5632]{1,0:T(8,128)(2,1)S(1)} %collective-permute-done.45.refs_2_), channel_id=1, source_target_pairs={{0,8},{8,0},{16,24},{24,16},{1,9},{9,1},{17,25},{25,17},{2,10},{10... | collective-permute-start | bytes 2162696 | tf_op jit(solution)/shard_map/ppermute | solution.py:55
  615.6 28.0 %collective-permute-start.23 = (bf16[64,2048]{1,0:T(8,128)(2,1)}, bf16[64,2048]{1,0:T(8,128)(2,1)}, u32[]{:S(2)}, u32[]{:S(2)}) collective-permute-start(bf16[64,2048]{1,0:T(8,128)(2,1)} %get-tuple-element.135), channel_id=1, source_target_pairs={{0,16},{8,24},{16,0},{24,8},{1,17},{9,25},{17,1},{25,9},{2,18},{10... | collective-permute-start | bytes 786440 | tf_op jit(solution)/shard_map/ppermute | solution.py:55
  616.4 28.4 %collective-permute-start.20 = (bf16[64,2048]{1,0:T(8,128)(2,1)}, bf16[64,2048]{1,0:T(8,128)(2,1)}, u32[]{:S(2)}, u32[]{:S(2)}) collective-permute-start(bf16[64,2048]{1,0:T(8,128)(2,1)} %get-tuple-element.138), channel_id=1, source_target_pairs={{0,8},{8,0},{16,24},{24,16},{1,9},{9,1},{17,25},{25,17},{2,10},{10... | collective-permute-start | bytes 786440 | tf_op jit(solution)/shard_map/ppermute | solution.py:55
  642.8 45.3 %collective-permute-start.25 = (bf16[256,1280]{1,0:T(8,128)(2,1)}, bf16[256,1280]{1,0:T(8,128)(2,1)S(1)}, u32[]{:S(2)}, u32[]{:S(2)}) collective-permute-start(bf16[256,1280]{1,0:T(8,128)(2,1)} %reduce-scatter.8.cloned.1.call-done.refs_0_), channel_id=1, source_target_pairs={{0,8},{8,0},{16,24},{24,16},{1,9},{9,1},{17,25},{25,17},{2,10},{10... | collective-permute-start | bytes 1966088 | tf_op jit(solution)/shard_map/ppermute | solution.py:55
  643.6 44.5 %collective-permute-start.26 = (bf16[256,1280]{1,0:T(8,128)(2,1)}, bf16[256,1280]{1,0:T(8,128)(2,1)}, u32[]{:S(2)}, u32[]{:S(2)}) collective-permute-start(bf16[256,1280]{1,0:T(8,128)(2,1)} %reduce-scatter.8.cloned.1.call-done.refs_0_), channel_id=1, source_target_pairs={{0,16},{8,24},{16,0},{24,8},{1,17},{9,25},{17,1},{25,9},{2,18},{10... | collective-permute-start | bytes 1966088 | tf_op jit(solution)/shard_map/ppermute | solution.py:55
  644.8 43.2 %collective-permute-start.27 = (bf16[256,1280]{1,0:T(8,128)(2,1)}, bf16[256,1280]{1,0:T(8,128)(2,1)}, u32[]{:S(2)}, u32[]{:S(2)}) collective-permute-start(bf16[256,1280]{1,0:T(8,128)(2,1)} %reduce-scatter.8.cloned.1.call-done.refs_0_), channel_id=1, source_target_pairs={{0,24},{8,16},{16,8},{24,0},{1,25},{9,17},{17,9},{25,1},{2,26},{10... | collective-permute-start | bytes 1966088 | tf_op jit(solution)/shard_map/ppermute | solution.py:55
  649.8 34.8 %collective-permute-start.21 = (bf16[64,2048]{1,0:T(8,128)(2,1)}, bf16[64,2048]{1,0:T(8,128)(2,1)}, u32[]{:S(2)}, u32[]{:S(2)}) collective-permute-start(bf16[64,2048]{1,0:T(8,128)(2,1)} %get-tuple-element.134), channel_id=1, source_target_pairs={{0,16},{8,24},{16,0},{24,8},{1,17},{9,25},{17,1},{25,9},{2,18},{10... | collective-permute-start | bytes 786440 | tf_op jit(solution)/shard_map/ppermute | solution.py:55
  650.9 33.6 %collective-permute-start.24 = (bf16[64,2048]{1,0:T(8,128)(2,1)}, bf16[64,2048]{1,0:T(8,128)(2,1)}, u32[]{:S(2)}, u32[]{:S(2)}) collective-permute-start(bf16[64,2048]{1,0:T(8,128)(2,1)} %get-tuple-element.133), channel_id=1, source_target_pairs={{0,8},{8,0},{16,24},{24,16},{1,9},{9,1},{17,25},{25,17},{2,10},{10... | collective-permute-start | bytes 786440 | tf_op jit(solution)/shard_map/ppermute | solution.py:55
  (67 other events, 1175.0 us)
Sparse Core Ops, SparseCore 0:
  10.4 36.4 all-gather.4
  49.1 28.2 all-gather.6
  79.0 46.9 all-gather.10
  127.4 69.7 all-gather.8
  271.2 65.6 reduce-scatter.5
  414.7 60.5 reduce-scatter.7
  477.6 48.3 reduce-scatter.3
